TPU v7x, 32 devices: a whole 2x2x4 slice. The times are simulated.
32 devices in a mesh: dp: 16 (over z, y, x), tensor: 2 (over core).
Axes of the slice: x: 2, y: 2, z: 4, core: 2. Of those that a mesh axis runs over, the one named last changes fastest.
Arguments:
- tokens: bfloat16 [32, 1024, 768], P(None, ('dp', 'tensor')), may hold values from -6 to 6
- encoder: bfloat16 [32, 128, 768], P('dp', 'tensor'), may hold values from -6 to 6
- lengths: int32 [32], replicated, may hold values from 256 to 1024, as said below
- deal: int32 [32], replicated, may hold values from 0 to 31, as said below
- self_project: bfloat16 [768, 3, 768], P('dp', None, 'tensor'), may hold values from -0.21875 to 0.21875
- self_output: bfloat16 [768, 768], P('tensor', 'dp'), may hold values from -1.75 to 1.75
- cross_query: bfloat16 [768, 768], P('dp', 'tensor'), may hold values from -0.21875 to 0.21875
- cross_memory: bfloat16 [768, 2, 768], P('dp', None, 'tensor'), may hold values from -0.21875 to 0.21875
- cross_output: bfloat16 [768, 768], P('tensor', 'dp'), may hold values from -1.75 to 1.75
- hidden_in: bfloat16 [768, 3072], P('dp', 'tensor'), may hold values from -0.21875 to 0.21875
- hidden_out: bfloat16 [3072, 768], P('tensor', 'dp'), may hold values from -0.109375 to 0.109375
- in_bias: float32 [4, 768], P(None, 'tensor'), may hold values from -3 to 3
- out_bias: float32 [3, 768], replicated, may hold values from -3 to 3
- hidden_bias: float32 [3072], P('tensor'), may hold values from -3 to 3
- norm_gain: float32 [3, 768], replicated, may hold values from 0.5 to 1.5
- norm_bias: float32 [3, 768], replicated, may hold values from -2 to 2
- cotangent: bfloat16 [32, 1024, 768], P(None, ('dp', 'tensor')), may hold values from -6 to 6
Outputs:
- output: bfloat16 [32, 1024, 768], P(None, ('dp', 'tensor'))
- grad_tokens: bfloat16 [32, 1024, 768], P(None, ('dp', 'tensor'))
- grad_encoder: bfloat16 [32, 128, 768], P('dp', 'tensor')
- grad_self_project: float32 [768, 3, 768], P('dp', None, 'tensor')
- grad_self_output: float32 [768, 768], P('tensor', 'dp')
- grad_cross_query: float32 [768, 768], P('dp', 'tensor')
- grad_cross_memory: float32 [768, 2, 768], P('dp', None, 'tensor')
- grad_cross_output: float32 [768, 768], P('tensor', 'dp')
- grad_hidden_in: float32 [768, 3072], P('dp', 'tensor')
- grad_hidden_out: float32 [3072, 768], P('tensor', 'dp')
- grad_in_bias: float32 [4, 768], P(None, 'tensor')
- grad_out_bias: float32 [3, 768], replicated
- grad_hidden_bias: float32 [3072], P('tensor')
- grad_norm_gain: float32 [3, 768], replicated
- grad_norm_bias: float32 [3, 768], replicated
Inputs may be any that keep to these rules, and one draw needn't show every extreme that they name: A permutation: dealt slot t holds initial sequence deal[t]; slots 2 i and 2 i + 1 belong to index i of dp; the lengths of those two sequences sum to at most 1536, and to exactly 1536 for some i. `lengths`: 1024 is reached.
All inputs are finite; a program needn't handle non-finite values.
Results may differ from a plain program's by a relative error of at most 0.022.
Values may be sent and summed in bfloat16 or wider, within the bound.
No kernel may reach another device: no remote copies, remote signals or barrier semaphores. Data moves between devices by JAX's collectives and lax.ppermute only.
A program may use at most 256 MiB of HBM per device.

v0:
```python
import math

import jax
import jax.numpy as jnp
from jax import lax
from jax.sharding import PartitionSpec as P

HD = 64


EPSILON = 1e-05
MASKED = -1e30


def layer_norm(hidden, gain_row, shift_row):
    center = hidden - jnp.mean(hidden, -1, keepdims=True)
    spread = jnp.mean(center * center, -1, keepdims=True)
    return center * lax.rsqrt(spread + EPSILON) * gain_row + shift_row


def exact_gelu(values_in):
    return jax.nn.gelu(values_in, approximate=False)


def contract_rows(left_side, right_side):
    return lax.dot_general(
        left_side, right_side, (((0,), (0,)), ((), ())), preferred_element_type=jnp.float32
    )


def times_transpose(left_side, right_side):
    return lax.dot_general(
        left_side, right_side, (((1,), (1,)), ((), ())), preferred_element_type=jnp.float32
    )


def rows_full(half_rows):
    return lax.all_gather(half_rows, "tensor", axis=0, tiled=True)


def rows_sum(partial_rows):
    return lax.psum_scatter(partial_rows, "tensor", scatter_dimension=0, tiled=True)


def pack_slots(slot_rows, first_len, second_len, capacity):
    longest = slot_rows.shape[1]
    row_ids = jnp.arange(longest, dtype=jnp.int32)
    zero_value = jnp.zeros((), slot_rows.dtype)
    first_part = jnp.where((row_ids < first_len)[:, None], slot_rows[0], zero_value)
    second_part = jnp.where((row_ids < second_len)[:, None], slot_rows[1], zero_value)
    buffer = jnp.zeros((capacity + longest, slot_rows.shape[2]), slot_rows.dtype)
    buffer = lax.dynamic_update_slice_in_dim(buffer, first_part, 0, 0)
    buffer = lax.dynamic_update_slice_in_dim(buffer, second_part, first_len, 0)
    return buffer[:capacity]


def unpack_rows(packed, first_len, second_len, longest):
    buffer = jnp.concatenate([packed, jnp.zeros((longest, packed.shape[1]), packed.dtype)], 0)
    row_ids = jnp.arange(longest, dtype=jnp.int32)
    zero_value = jnp.zeros((), packed.dtype)
    first_part = jnp.where((row_ids < first_len)[:, None], buffer[:longest], zero_value)
    second_slice = lax.dynamic_slice_in_dim(buffer, first_len, longest, 0)
    second_part = jnp.where((row_ids < second_len)[:, None], second_slice, zero_value)
    return jnp.stack([first_part, second_part])


def attend_forward(queries, keys_in, values_in, allowed, causal, head_dim):
    query_count, head_width = queries.shape
    key_count = keys_in.shape[0]
    head_count = head_width // head_dim
    block_rows = min(512, query_count)

    def one_head(head_idx, state_in):
        out_buffer, lse_buffer = state_in
        col_start = head_idx * head_dim
        head_keys = lax.dynamic_slice_in_dim(keys_in, col_start, head_dim, 1)
        head_values = lax.dynamic_slice_in_dim(values_in, col_start, head_dim, 1)
        for block_idx in range(query_count // block_rows):
            low_row = block_idx * block_rows
            key_end = low_row + block_rows if causal else key_count
            head_query = lax.dynamic_slice(queries, (low_row, col_start), (block_rows, head_dim))
            scores = times_transpose(head_query, head_keys[:key_end])
            scores = jnp.where(allowed(low_row, block_rows, key_end), scores, MASKED)
            row_top = jnp.max(scores, -1, keepdims=True)
            exps = jnp.exp(scores - row_top)
            row_total = jnp.sum(exps, -1, keepdims=True)
            probability = (exps / row_total).astype(jnp.bfloat16)
            block_out = jnp.dot(
                probability, head_values[:key_end], preferred_element_type=jnp.float32
            )
            out_buffer = lax.dynamic_update_slice(
                out_buffer, block_out.astype(jnp.bfloat16), (low_row, col_start)
            )
            lse_rows = (row_top + jnp.log(row_total)).reshape(1, block_rows)
            lse_buffer = lax.dynamic_update_slice(lse_buffer, lse_rows, (head_idx, low_row))
        return (out_buffer, lse_buffer)

    start_state = (
        jnp.zeros((query_count, head_width), jnp.bfloat16),
        jnp.zeros((head_count, query_count), jnp.float32),
    )
    return lax.fori_loop(0, head_count, one_head, start_state)


def attend_backward(queries, keys_in, values_in, grad_out, lse_buffer, allowed, causal, head_dim):
    query_count, head_width = queries.shape
    key_count = keys_in.shape[0]
    head_count = head_width // head_dim
    block_rows = min(512, query_count)

    def one_head(head_idx, state_in):
        grad_query, grad_keys, grad_values = state_in
        col_start = head_idx * head_dim
        head_keys = lax.dynamic_slice_in_dim(keys_in, col_start, head_dim, 1)
        head_values = lax.dynamic_slice_in_dim(values_in, col_start, head_dim, 1)
        keys_total = jnp.zeros((key_count, head_dim), jnp.float32)
        values_total = jnp.zeros((key_count, head_dim), jnp.float32)
        for block_idx in range(query_count // block_rows):
            low_row = block_idx * block_rows
            key_end = low_row + block_rows if causal else key_count
            head_query = lax.dynamic_slice(queries, (low_row, col_start), (block_rows, head_dim))
            head_grad = lax.dynamic_slice(grad_out, (low_row, col_start), (block_rows, head_dim))
            lse_rows = lax.dynamic_slice(lse_buffer, (head_idx, low_row), (1, block_rows)).reshape(
                block_rows, 1
            )
            scores = times_transpose(head_query, head_keys[:key_end])
            scores = jnp.where(allowed(low_row, block_rows, key_end), scores, MASKED)
            probability = jnp.exp(scores - lse_rows)
            values_total = values_total.at[:key_end].add(
                contract_rows(probability.astype(jnp.bfloat16), head_grad)
            )
            grad_prob = times_transpose(head_grad, head_values[:key_end])
            row_dot = jnp.sum(probability * grad_prob, -1, keepdims=True)
            grad_score = (probability * (grad_prob - row_dot)).astype(jnp.bfloat16)
            block_query = jnp.dot(
                grad_score, head_keys[:key_end], preferred_element_type=jnp.float32
            )
            grad_query = lax.dynamic_update_slice(
                grad_query, block_query.astype(jnp.bfloat16), (low_row, col_start)
            )
            keys_total = keys_total.at[:key_end].add(contract_rows(grad_score, head_query))
        grad_keys = lax.dynamic_update_slice(
            grad_keys, keys_total.astype(jnp.bfloat16), (0, col_start)
        )
        grad_values = lax.dynamic_update_slice(
            grad_values, values_total.astype(jnp.bfloat16), (0, col_start)
        )
        return (grad_query, grad_keys, grad_values)

    start_state = (
        jnp.zeros((query_count, head_width), jnp.bfloat16),
        jnp.zeros((key_count, head_width), jnp.bfloat16),
        jnp.zeros((key_count, head_width), jnp.bfloat16),
    )
    return lax.fori_loop(0, head_count, one_head, start_state)


def body(
    tokens,
    encoder,
    lengths,
    deal,
    self_project,
    self_output,
    cross_query,
    cross_memory,
    cross_output,
    hidden_in,
    hidden_out,
    in_bias,
    out_bias,
    hidden_bias,
    norm_gain,
    norm_bias,
    cotangent,
):
    score_scale = 1.0 / math.sqrt(HD)
    dp_count = lax.axis_size("dp")
    dp_index = lax.axis_index("dp")
    tensor_index = lax.axis_index("tensor")
    piece_rows = tokens.shape[1]
    model_width = tokens.shape[2]
    ordered = jnp.take(tokens, deal, axis=0)
    ordered_cot = jnp.take(cotangent, deal, axis=0)
    arrived, arrived_cot = (
        lax.all_to_all(ordered, "dp", split_axis=0, concat_axis=1, tiled=True),
        lax.all_to_all(ordered_cot, "dp", split_axis=0, concat_axis=1, tiled=True),
    )
    arrived = arrived.reshape(2, dp_count, piece_rows, model_width)
    arrived_cot = arrived_cot.reshape(2, dp_count, piece_rows, model_width)
    full_tok, full_cot, memory = (
        lax.all_gather(arrived, "tensor", axis=2, tiled=True),
        lax.all_gather(arrived_cot, "tensor", axis=2, tiled=True),
        lax.all_gather(encoder, "tensor", axis=1, tiled=True),
    )
    longest = full_tok.shape[1] * full_tok.shape[2]
    capacity = longest + longest // 2
    half_rows = capacity // 2
    own_start = tensor_index * half_rows
    pair_ids = lax.dynamic_slice_in_dim(deal, 2 * dp_index, 2)
    pair_len = jnp.take(lengths, pair_ids)
    first_len = pair_len[0]
    second_len = pair_len[1]
    inputs_full = pack_slots(
        full_tok.reshape(2, longest, model_width), first_len, second_len, capacity
    )
    inputs_half = lax.dynamic_slice_in_dim(inputs_full, own_start, half_rows, 0).astype(jnp.float32)
    cot_packed = pack_slots(
        full_cot.reshape(2, longest, model_width), first_len, second_len, capacity
    )
    cot_half = lax.dynamic_slice_in_dim(cot_packed, own_start, half_rows, 0).astype(jnp.float32)
    row_ids = jnp.arange(capacity, dtype=jnp.int32)
    segment = (row_ids >= first_len).astype(jnp.int32) + (row_ids >= first_len + second_len).astype(
        jnp.int32
    )
    query_segment = jnp.minimum(segment, 1)
    memory_rows = memory.shape[1]
    memory_flat = memory.reshape(2 * memory_rows, model_width)
    memory_segment = jnp.arange(2 * memory_rows, dtype=jnp.int32) // memory_rows

    def self_allowed(low_row, count_rows, key_end):
        query_pos = row_ids[low_row : low_row + count_rows]
        key_pos = row_ids[:key_end]
        same_seq = segment[low_row : low_row + count_rows][:, None] == segment[:key_end][None, :]
        return same_seq & (key_pos[None, :] <= query_pos[:, None])

    def cross_allowed(low_row, count_rows, key_end):
        return query_segment[low_row : low_row + count_rows][:, None] == memory_segment[None, :]

    gathered = (
        lax.all_gather(self_project, "dp", axis=0, tiled=True),
        lax.all_gather(cross_query, "dp", axis=0, tiled=True),
        lax.all_gather(cross_memory, "dp", axis=0, tiled=True),
        lax.all_gather(hidden_in, "dp", axis=0, tiled=True),
        lax.all_gather(self_output, "dp", axis=1, tiled=True),
        lax.all_gather(cross_output, "dp", axis=1, tiled=True),
        lax.all_gather(hidden_out, "dp", axis=1, tiled=True),
    )
    (
        project_weight,
        query_weight,
        memory_weight,
        expand_weight,
        self_out_weight,
        cross_out_weight,
        reduce_weight,
    ) = gathered
    heads_width = project_weight.shape[2]
    mixed_proj = jnp.dot(
        inputs_full,
        project_weight.reshape(model_width, 3 * heads_width),
        preferred_element_type=jnp.float32,
    ).reshape(capacity, 3, heads_width)
    queries = ((mixed_proj[:, 0] + in_bias[0]) * score_scale).astype(jnp.bfloat16)
    keys_self = mixed_proj[:, 1].astype(jnp.bfloat16)
    values_self = (mixed_proj[:, 2] + in_bias[1]).astype(jnp.bfloat16)
    attn_self, lse_self = attend_forward(queries, keys_self, values_self, self_allowed, True, HD)
    branch_self = (
        rows_sum(jnp.dot(attn_self, self_out_weight, preferred_element_type=jnp.float32))
        + out_bias[0]
    )
    normed_one, norm_back_one = jax.vjp(
        layer_norm, inputs_half + branch_self, norm_gain[0], norm_bias[0]
    )
    cross_in = rows_full(normed_one.astype(jnp.bfloat16))
    cross_queries = (
        (jnp.dot(cross_in, query_weight, preferred_element_type=jnp.float32) + in_bias[2])
        * score_scale
    ).astype(jnp.bfloat16)
    memory_kv = jnp.dot(
        memory_flat,
        memory_weight.reshape(model_width, 2 * heads_width),
        preferred_element_type=jnp.float32,
    ).reshape(2 * memory_rows, 2, heads_width)
    keys_cross = memory_kv[:, 0].astype(jnp.bfloat16)
    values_cross = (memory_kv[:, 1] + in_bias[3]).astype(jnp.bfloat16)
    attn_cross, lse_cross = attend_forward(
        cross_queries, keys_cross, values_cross, cross_allowed, False, HD
    )
    branch_cross = (
        rows_sum(jnp.dot(attn_cross, cross_out_weight, preferred_element_type=jnp.float32))
        + out_bias[1]
    )
    normed_two, norm_back_two = jax.vjp(
        layer_norm, normed_one + branch_cross, norm_gain[1], norm_bias[1]
    )
    hidden_rows = rows_full(normed_two.astype(jnp.bfloat16))
    pre_act = jnp.dot(hidden_rows, expand_weight, preferred_element_type=jnp.float32) + hidden_bias
    activated, gelu_back = jax.vjp(exact_gelu, pre_act)
    act_values = activated.astype(jnp.bfloat16)
    branch_ffn = (
        rows_sum(jnp.dot(act_values, reduce_weight, preferred_element_type=jnp.float32))
        + out_bias[2]
    )
    final_rows, norm_back_three = jax.vjp(
        layer_norm, normed_two + branch_ffn, norm_gain[2], norm_bias[2]
    )
    final_full = rows_full(final_rows.astype(jnp.bfloat16))
    out_slots = unpack_rows(final_full, first_len, second_len, longest)
    out_mine = lax.dynamic_index_in_dim(
        out_slots.reshape(2, dp_count, 2, piece_rows, model_width), tensor_index, 2, keepdims=False
    )
    gathered = (
        lax.all_gather(self_project, "dp", axis=0, tiled=True),
        lax.all_gather(cross_query, "dp", axis=0, tiled=True),
        lax.all_gather(cross_memory, "dp", axis=0, tiled=True),
        lax.all_gather(hidden_in, "dp", axis=0, tiled=True),
        lax.all_gather(self_output, "dp", axis=1, tiled=True),
        lax.all_gather(cross_output, "dp", axis=1, tiled=True),
        lax.all_gather(hidden_out, "dp", axis=1, tiled=True),
    )
    (
        project_weight,
        query_weight,
        memory_weight,
        expand_weight,
        self_out_weight,
        cross_out_weight,
        reduce_weight,
    ) = gathered
    grad_three, gain_grad_three, shift_grad_three = norm_back_three(cot_half)
    grad_branch_ffn = grad_three.astype(jnp.bfloat16)
    grad_ffn_full = rows_full(grad_branch_ffn)
    grad_reduce = contract_rows(act_values, grad_ffn_full)
    grad_act = times_transpose(grad_ffn_full, reduce_weight)
    grad_pre = gelu_back(grad_act)[0].astype(jnp.bfloat16)
    grad_expand = contract_rows(hidden_rows, grad_pre)
    grad_normed_two = grad_three + rows_sum(times_transpose(grad_pre, expand_weight))
    grad_two, gain_grad_two, shift_grad_two = norm_back_two(grad_normed_two)
    grad_branch_cross = grad_two.astype(jnp.bfloat16)
    grad_cross_full = rows_full(grad_branch_cross)
    grad_cross_out = contract_rows(attn_cross, grad_cross_full)
    grad_attn_cross = times_transpose(grad_cross_full, cross_out_weight).astype(jnp.bfloat16)
    grad_cq, grad_ck, grad_cv = attend_backward(
        cross_queries,
        keys_cross,
        values_cross,
        grad_attn_cross,
        lse_cross,
        cross_allowed,
        False,
        HD,
    )
    grad_query_weight = contract_rows(cross_in, grad_cq) * score_scale
    grad_memory_both = jnp.concatenate([grad_ck, grad_cv], 1)
    grad_memory_weight = contract_rows(memory_flat, grad_memory_both).reshape(
        model_width, 2, heads_width
    )
    grad_memory = times_transpose(
        grad_memory_both, memory_weight.reshape(model_width, 2 * heads_width)
    )
    grad_normed_one = grad_two + rows_sum(times_transpose(grad_cq, query_weight) * score_scale)
    grad_one, gain_grad_one, shift_grad_one = norm_back_one(grad_normed_one)
    grad_branch_self = grad_one.astype(jnp.bfloat16)
    grad_self_full = rows_full(grad_branch_self)
    grad_self_out = contract_rows(attn_self, grad_self_full)
    grad_attn_self = times_transpose(grad_self_full, self_out_weight).astype(jnp.bfloat16)
    grad_sq, grad_sk, grad_sv = attend_backward(
        queries, keys_self, values_self, grad_attn_self, lse_self, self_allowed, True, HD
    )
    grad_mixed = jnp.concatenate([grad_sq, grad_sk, grad_sv], 1)
    factors = jnp.array([score_scale, 1.0, 1.0], jnp.float32)[None, :, None]
    grad_project = (
        contract_rows(inputs_full, grad_mixed).reshape(model_width, 3, heads_width) * factors
    )
    grad_inputs = (
        times_transpose(grad_sq, project_weight[:, 0]) * score_scale
        + times_transpose(grad_sk, project_weight[:, 1])
        + times_transpose(grad_sv, project_weight[:, 2])
    )
    own_grad = lax.dynamic_slice_in_dim(grad_inputs, own_start, half_rows, 0) + grad_one
    grad_inputs = lax.dynamic_update_slice_in_dim(grad_inputs, own_grad, own_start, 0)
    grad_slots = unpack_rows(grad_inputs, first_len, second_len, longest).reshape(
        2, dp_count, 2 * piece_rows, model_width
    )
    grad_tok_mine, grad_mem_mine = (
        lax.psum_scatter(
            grad_slots.astype(jnp.bfloat16), "tensor", scatter_dimension=2, tiled=True
        ).astype(jnp.float32),
        lax.psum_scatter(
            grad_memory.reshape(2, memory_rows, model_width).astype(jnp.bfloat16),
            "tensor",
            scatter_dimension=1,
            tiled=True,
        ).astype(jnp.float32),
    )
    back_out, back_grad = (
        lax.all_to_all(out_mine, "dp", split_axis=1, concat_axis=0, tiled=True),
        lax.all_to_all(
            grad_tok_mine.astype(jnp.bfloat16), "dp", split_axis=1, concat_axis=0, tiled=True
        ),
    )
    inverse = jnp.zeros_like(deal).at[deal].set(jnp.arange(deal.shape[0], dtype=jnp.int32))
    output = jnp.take(back_out.reshape(-1, piece_rows, model_width), inverse, axis=0)
    grad_tokens = jnp.take(back_grad.reshape(-1, piece_rows, model_width), inverse, axis=0)
    grad_encoder = grad_mem_mine.astype(jnp.bfloat16)
    (
        grad_project,
        grad_query_weight,
        grad_memory_weight,
        grad_expand,
        grad_self_out,
        grad_cross_out,
        grad_reduce,
    ) = (
        lax.psum_scatter(grad_project, "dp", scatter_dimension=0, tiled=True),
        lax.psum_scatter(grad_query_weight, "dp", scatter_dimension=0, tiled=True),
        lax.psum_scatter(grad_memory_weight, "dp", scatter_dimension=0, tiled=True),
        lax.psum_scatter(grad_expand, "dp", scatter_dimension=0, tiled=True),
        lax.psum_scatter(grad_self_out, "dp", scatter_dimension=1, tiled=True),
        lax.psum_scatter(grad_cross_out, "dp", scatter_dimension=1, tiled=True),
        lax.psum_scatter(grad_reduce, "dp", scatter_dimension=1, tiled=True),
    )
    in_rows = jnp.stack(
        [
            score_scale * jnp.sum(grad_sq, 0, dtype=jnp.float32),
            jnp.sum(grad_sv, 0, dtype=jnp.float32),
            score_scale * jnp.sum(grad_cq, 0, dtype=jnp.float32),
            jnp.sum(grad_cv, 0, dtype=jnp.float32),
        ]
    )
    in_full = lax.dynamic_update_slice(
        jnp.zeros((4, model_width), jnp.float32), in_rows, (0, tensor_index * heads_width)
    )
    out_rows = jnp.stack(
        [
            jnp.sum(grad_branch_self, 0, dtype=jnp.float32),
            jnp.sum(grad_branch_cross, 0, dtype=jnp.float32),
            jnp.sum(grad_branch_ffn, 0, dtype=jnp.float32),
        ]
    )
    units_half = expand_weight.shape[1]
    hidden_full = lax.dynamic_update_slice_in_dim(
        jnp.zeros((2 * units_half,), jnp.float32),
        jnp.sum(grad_pre, 0, dtype=jnp.float32),
        tensor_index * units_half,
        0,
    )
    gain_rows = jnp.stack([gain_grad_one, gain_grad_two, gain_grad_three])
    shift_rows = jnp.stack([shift_grad_one, shift_grad_two, shift_grad_three])
    in_total, out_total, hidden_total, gain_total, shift_total = lax.psum(
        (in_full, out_rows, hidden_full, gain_rows, shift_rows), ("dp", "tensor")
    )
    grad_in_bias = lax.dynamic_slice_in_dim(in_total, tensor_index * heads_width, heads_width, 1)
    grad_hidden_bias = lax.dynamic_slice_in_dim(
        hidden_total, tensor_index * units_half, units_half, 0
    )
    return (
        output,
        grad_tokens,
        grad_encoder,
        grad_project,
        grad_self_out,
        grad_query_weight,
        grad_memory_weight,
        grad_cross_out,
        grad_expand,
        grad_reduce,
        grad_in_bias,
        out_total,
        grad_hidden_bias,
        gain_total,
        shift_total,
    )


def solution(mesh):
    in_specs = (
        P(None, ("dp", "tensor"), None),
        P("dp", "tensor", None),
        P(),
        P(),
        P("dp", None, "tensor"),
        P("tensor", "dp"),
        P("dp", "tensor"),
        P("dp", None, "tensor"),
        P("tensor", "dp"),
        P("dp", "tensor"),
        P("tensor", "dp"),
        P(None, "tensor"),
        P(),
        P("tensor"),
        P(),
        P(),
        P(None, ("dp", "tensor"), None),
    )
    out_specs = (
        P(None, ("dp", "tensor"), None),
        P(None, ("dp", "tensor"), None),
        P("dp", "tensor", None),
        P("dp", None, "tensor"),
        P("tensor", "dp"),
        P("dp", "tensor"),
        P("dp", None, "tensor"),
        P("tensor", "dp"),
        P("dp", "tensor"),
        P("tensor", "dp"),
        P(None, "tensor"),
        P(),
        P("tensor"),
        P(),
        P(),
    )
    return jax.shard_map(body, mesh=mesh, in_specs=in_specs, out_specs=out_specs, check_vma=False)
```

profile of v0, /device:TPU:0, one launch (start us, length us, event | category | flops | bytes accessed | tf_op | source)
XLA Modules:
  0.0 1893.3 jit_solution(11829577460795265645)
XLA Ops:
  10.0 3.2 gather_fusion.3
  14.9 56.7 %all_to_all.60 = bf16[32,32,768]{2,1,0:T(8,128)(2,1)S(1)} all-to-all(bf16[32,32,768]{2,1,0:T(8,128)(2,1)S(1)} %get-tuple-element.1525), channel_id=1, replica_groups=mesh['dp'=16,'tensor'=2] {'dp'}, dimensions={0} | all-to-all | bytes 3145728 | tf_op jit(solution)/shard_map/all_to_all | solution.py:187
  73.0 42.0 %all_to_all.61 = bf16[32,32,768]{2,1,0:T(8,128)(2,1)S(1)} all-to-all(bf16[32,32,768]{2,1,0:T(8,128)(2,1)S(1)} %get-tuple-element.1526), channel_id=1, replica_groups=mesh['dp'=16,'tensor'=2] {'dp'}, dimensions={0} | all-to-all | bytes 3145728 | tf_op jit(solution)/shard_map/all_to_all | solution.py:186
  123.0 43.5 %all_gather.57 = bf16[384,768]{0,1:T(8,128)(2,1)} all-gather(bf16[384,48]{0,1:T(8,128)(2,1)S(1)} %copy-done.60), channel_id=1, replica_groups=mesh['dp'=16,'tensor'=2] {'dp'}, dimensions={1}, use_global_device_ids=true | all-gather | bytes 626688 | tf_op jit(solution)/shard_map/all_gather | solution.py:235
  166.5 3.8 copy.51
  170.4 3.3 fusion.248
  180.8 8.1 dynamic_update_slice.196
  188.9 4.9 fusion.208
  198.0 81.0 %while.133 = (s32[]{:T(128)}, bf16[1536,384]{0,1:T(8,128)(2,1)}, f32[6,1536]{1,0:T(8,128)S(1)}, s32[1536]{0:T(1024)S(1)}, s32[1536]{0:T(1024)S(1)}, /*index=5*/b...) while((s32[]{:T(128)}, bf16[1536,384]{0,1:T(8,128)(2,1)}, ...), condition=%wide.region_7.9_spmd.clone, body=%wide.region_0.8_spmd.clone.sunk | while | flops 418478592 | bytes 46872876 | solution.py:102
  279.0 5.0 fusion.251
  286.6 3.4 slice.688
  300.8 47.3 %all_gather.59 = bf16[768,384]{1,0:T(8,128)(2,1)} all-gather(bf16[48,384]{1,0:T(8,128)(2,1)S(1)} %copy-done.61), channel_id=1, replica_groups=mesh['dp'=16,'tensor'=2] {'dp'}, dimensions={0}, use_global_device_ids=true | all-gather | bytes 626688 | tf_op jit(solution)/shard_map/all_gather | solution.py:232
  348.1 41.6 %all_gather.62 = bf16[384,768]{0,1:T(8,128)(2,1)} all-gather(bf16[384,48]{0,1:T(8,128)(2,1)S(1)} %copy-done.62), channel_id=1, replica_groups=mesh['dp'=16,'tensor'=2] {'dp'}, dimensions={1}, use_global_device_ids=true | all-gather | bytes 626688 | tf_op jit(solution)/shard_map/all_gather | solution.py:236
  395.4 4.3 fusion.200
  400.8 46.4 %while.135 = (s32[]{:T(128)}, bf16[1536,384]{0,1:T(8,128)(2,1)}, f32[6,1536]{1,0:T(8,128)S(1)}, s32[1536]{0:T(1024)S(1)}, bf16[1536,384]{1,0:T(8,128)(2,1)}, /*i...) while((s32[]{:T(128)}, bf16[1536,384]{0,1:T(8,128)(2,1)}, ...), condition=%wide.region_18.20_spmd.clone.clone, body=%wide.region_11.19_spmd.clone.clone.sunk | while | flops 103907840 | bytes 5791927 | solution.py:102
  447.2 4.8 fusion.253
  452.9 9.5 reduce-scatter.15.cloned.1.call-done
  468.4 60.3 %all-gather.23.cloned.1.call-done = bf16[768,1536]{1,0:T(8,128)(2,1)} async-done(((bf16[48,1536]{1,0:T(8,128)(2,1)}), bf16[768,1536]{1,0:T(8,128)(2,1)}) %all-gather.23.cloned.1.call-update) | async-done | bytes 2359312 | tf_op jit(solution)/shard_map/all_gather | solution.py:234
  528.7 11.4 all-gather.21.cloned.1.call-done
  540.0 27.1 %multiply_convert_fusion.6 = (bf16[1536,1536]{1,0:T(8,128)(2,1)}, f32[1536,1536]{1,0:T(8,128)}, f32[1536,1536]{1,0:T(8,128)}) fusion(f32[1536]{0:T(1024)S(1)} %copy-done.91, bf16[1536,768]{1,0:T(8,128)(2,1)} %all-gather.21.cloned.1.call-done, bf16[768,1536]{1,0:T(8,128)(2,1)} %all-gather.23.cloned.1.call-done), kind=kOutput, calls=%fused_computation.265 | convolution fusion | flops 3779592192 | bytes 28317696 | tf_op jit(solution)/shard_map/dot_general | solution.py:288
  567.1 39.1 %all-gather.25.cloned.1.call-done = bf16[1536,768]{0,1:T(8,128)(2,1)} async-done(((bf16[1536,48]{0,1:T(8,128)(2,1)}), bf16[1536,768]{0,1:T(8,128)(2,1)}) %all-gather.25.cloned.1.call-update) | async-done | bytes 2359312 | tf_op jit(solution)/shard_map/all_gather | solution.py:237
  606.2 9.2 fusion.254
  615.5 3.7 dynamic_update_slice.197
  619.2 8.0 dynamic_update_slice.198
  627.2 3.4 slice.697
  641.8 10.1 all-gather.31.cloned.1.call-done
  651.9 13.9 convert_reduce_fusion
  667.9 5.5 fusion.255
  673.5 13.9 reduce-scatter.19.cloned.1.call-done
  687.4 3.6 multiply_reduce_fusion.6
  695.3 12.2 all-gather.33.cloned.1.call-done
  707.6 4.1 convolution_convert_fusion.12
  712.4 44.9 %while.136 = (s32[]{:T(128)}, bf16[1536,384]{0,1:T(8,128)(2,1)S(1)}, bf16[256,384]{0,1:T(8,128)(2,1)}, bf16[256,384]{0,1:T(8,128)(2,1)S(1)}, s32[1536]{0:T(1024)...) while((s32[]{:T(128)}, bf16[1536,384]{0,1:T(8,128)(2,1)S(1)}, ...), condition=%wide.region_35.37_spmd.clone.clone, body=%wide.region_31.36_spmd.clone.clone.sunk | while | flops 255394304 | bytes 19528932 | solution.py:155
  757.3 3.6 convolution_multiply_fusion
  761.1 13.9 reduce-scatter.21.cloned.1.call-done
  775.0 3.8 multiply_reduce_fusion.7
  783.6 11.7 all-gather.35.cloned.1.call-done
  795.3 4.1 convolution_convert_fusion.11
  801.6 83.5 %while.134 = (s32[]{:T(128)}, bf16[1536,384]{0,1:T(8,128)(2,1)S(1)}, bf16[1536,384]{0,1:T(8,128)(2,1)}, bf16[1536,384]{0,1:T(8,128)(2,1)}, s32[1536]{0:T(1024)S(...) while((s32[]{:T(128)}, bf16[1536,384]{0,1:T(8,128)(2,1)S(1)}, ...), condition=%wide.region_43.45_spmd.clone, body=%wide.region_39.44_spmd.clone.sunk | while | flops 1024555520 | bytes 64415000 | solution.py:155
  889.2 5.0 add_add_fusion
  894.3 3.4 add_dynamic-update-slice_fusion
  897.7 5.3 fusion.214
  908.3 3.1 copy.60
  911.3 6.3 fusion.188
  919.8 6.2 copy.59
  927.7 7.9 fusion.260
  937.2 8.1 fusion.259
  952.0 4.1 fusion.258
  956.2 2.7 copy_bitcast_fusion.1
  958.9 7.7 all-to-all-start.1
  966.7 4.2 convolution_multiply_fusion.1
  970.9 51.4 %all-to-all-done.1 = bf16[2,16,32,768]{3,2,0,1:T(8,128)(2,1)} async-done(((bf16[2,16,32,768]{3,2,0,1:T(8,128)(2,1)}), bf16[2,16,32,768]{3,2,0,1:T(8,128)(2,1)}, u32[]{:S(2)}, u32[]{:S(2)}) %all-to-all-start.1) | async-done | bytes 1572896 | tf_op jit(solution)/shard_map/all_to_all | solution.py:388
  1022.3 9.9 all-to-all-start.3
  1035.4 4.2 fusion.256
  1045.0 60.6 %all-reduce.8 = (f32[4,768]{1,0:T(4,128)S(1)}, f32[3,768]{1,0:T(4,128)}, f32[3072]{0:T(1024)S(1)}, f32[3,768]{1,0:T(4,128)}, f32[3,768]{1,0:T(4,128)}) all-reduce(f32[4,768]{1,0:T(4,128)S(1)} %maximum_dynamic-update-slice_fusion, f32[3,768]{1,0:T(4,128)S(1)} %pad_maximum_fusion.1, ...), channel_id=1, replica_groups=mesh['dp'=16,'tensor'=2] {'dp','tensor'}, use_global_device_ids=true, to_apply=%region_57.59 | all-reduce | flops 13056 | bytes 104448 | tf_op jit(solution)/shard_map/psum | solution.py:441
  1108.9 95.9 %all-reduce.12.cloned.1.call-done = (f32[768,3,384]{2,1,0:T(4,128)}, f32[768,2,384]{2,1,0:T(2,128)}) async-done(((f32[768,3,384]{2,1,0:T(4,128)}, f32[768,2,384]{2,1,0:T(2,128)}), (f32[768,3,384]{2,1,0:T(4,128)}, f32[768,2,384]{2,1,0:T(2,128)})) %all-reduce.12.cloned.1.call-update) | async-done | bytes 5898256
  1208.1 3.4 gather_fusion.4
  1211.5 3.4 broadcast_select_fusion
  1215.0 131.4 %reduce-scatter.35.cloned.1.call-done = f32[1536,48]{0,1:T(8,128)} async-done(((f32[1536,768]{0,1:T(8,128)}), f32[1536,48]{0,1:T(8,128)}) %reduce-scatter.35.cloned.1.call-update) | async-done | bytes 294928 | tf_op jit(solution)/shard_map/reduce_scatter | solution.py:412
  1346.3 142.3 %reduce-scatter.33.cloned.1.call-done = f32[48,1536]{1,0:T(8,128)} async-done(((f32[768,1536]{1,0:T(8,128)}), f32[48,1536]{1,0:T(8,128)}) %reduce-scatter.33.cloned.1.call-update) | async-done | bytes 294928 | tf_op jit(solution)/shard_map/reduce_scatter | solution.py:409
  1488.6 9.7 reduce-scatter.25.cloned.1.call-done
  1498.3 130.9 %reduce-scatter.31.cloned.1.call-done = f32[384,48]{0,1:T(8,128)} async-done(((f32[384,768]{0,1:T(8,128)}), f32[384,48]{0,1:T(8,128)}) %reduce-scatter.31.cloned.1.call-update) | async-done | bytes 73744 | tf_op jit(solution)/shard_map/reduce_scatter | solution.py:411
  1629.2 128.5 %reduce-scatter.29.cloned.1.call-done = f32[48,384]{1,0:T(8,128)} async-done(((f32[768,384]{1,0:T(8,128)}), f32[48,384]{1,0:T(8,128)}) %reduce-scatter.29.cloned.1.call-update) | async-done | bytes 73744 | tf_op jit(solution)/shard_map/reduce_scatter | solution.py:407
  1757.7 128.6 %reduce-scatter.27.cloned.1.call-done = f32[384,48]{0,1:T(8,128)} async-done(((f32[384,768]{0,1:T(8,128)}), f32[384,48]{0,1:T(8,128)}) %reduce-scatter.27.cloned.1.call-update) | async-done | bytes 73744 | tf_op jit(solution)/shard_map/reduce_scatter | solution.py:410
  (916 shorter events, 363.4 us)
Async XLA Ops:
  7.2 159.3 %all-gather.15.cloned.1.call-start = ((), (), s32[]{:S(2)}) async-start(), calls=%async_computation.17 | async-start | bytes 1880064 | tf_op jit(solution)/shard_map/all_gather | solution.py:231
  7.9 162.5 %all-gather.29.cloned.1.call-start = ((), (), s32[]{:S(2)}) async-start(), calls=%async_computation.27 | async-start | bytes 4718592 | tf_op jit(solution)/shard_map/all_gather | solution.py:193
  72.9 100.8 %all-gather.13.cloned.1.call-start = ((), (), s32[]{:S(2)}) async-start(), calls=%async_computation.16 | async-start | bytes 4718592 | tf_op jit(solution)/shard_map/all_gather | solution.py:192
  114.9 7.5 copy-start.79
  114.9 8.1 copy-start.60
  116.2 176.5 %reduce-scatter.13.cloned.1.call-start = ((), (), s32[]{:S(2)}) async-start(), calls=%async_computation.18 | async-start | bytes 7077888 | tf_op jit(solution)/shard_map/reduce_scatter | solution.py:42
  121.1 54.8 %copy-start.80 = (pred[1024]{0:T(1024)(128)(4,1)}, pred[1024]{0:T(1024)(128)(4,1)S(1)}, u32[]{:S(2)}) copy-start(pred[1024]{0:T(1024)(128)(4,1)S(1)} %iota_compare_fusion.3) | copy-start | bytes 3076
  121.8 54.1 %copy-start.82 = (pred[1024]{0:T(1024)(128)(4,1)}, pred[1024]{0:T(1024)(128)(4,1)S(1)}, u32[]{:S(2)}) copy-start(pred[1024]{0:T(1024)(128)(4,1)S(1)} %iota_compare_fusion.2) | copy-start | bytes 3076
  180.8 8.1 copy-start.35
  284.1 105.5 %all-gather.19.cloned.1.call-start = ((), (), s32[]{:S(2)}) async-start(), calls=%async_computation.20 | async-start | bytes 1253376 | tf_op jit(solution)/shard_map/all_gather | solution.py:233
  284.7 110.7 %all-gather.17.cloned.1.call-start = ((), (), s32[]{:S(2)}) async-start(), calls=%async_computation.19 | async-start | bytes 3538944 | tf_op jit(solution)/shard_map/all_gather | solution.py:38
  286.0 10.4 copy-start.49
  286.6 9.8 copy-start.56
  295.1 167.3 %copy-start.3 = (f32[768,768]{1,0:T(8,128)}, f32[768,768]{1,0:T(8,128)S(1)}, u32[]{:S(2)}) copy-start(f32[768,768]{1,0:T(8,128)S(1)} %get-tuple-element.1451) | copy-start | bytes 7077892
  295.1 167.3 %copy-start.43 = (f32[768]{0:T(1024)}, f32[768]{0:T(1024)S(1)}, u32[]{:S(2)}) copy-start(f32[768]{0:T(1024)S(1)} %broadcast_multiply_fusion.3) | copy-start | bytes 9220
  295.6 166.8 %copy-start.47 = (f32[768]{0:T(1024)}, f32[768]{0:T(1024)S(1)}, u32[]{:S(2)}) copy-start(f32[768]{0:T(1024)S(1)} %fusion.221) | copy-start | bytes 9220
  296.5 51.6 %copy-start.62 = (bf16[384,48]{0,1:T(8,128)(2,1)S(1)}, bf16[384,48]{0,1:T(8,128)(2,1)}, u32[]{:S(2)}) copy-start(bf16[384,48]{0,1:T(8,128)(2,1)} %param.76) | copy-start | bytes 110596
  297.9 164.5 %reduce-scatter.15.cloned.1.call-start = ((), (), s32[]{:S(2)}) async-start(), calls=%async_computation.21 | async-start | bytes 7077888 | tf_op jit(solution)/shard_map/reduce_scatter | solution.py:42
  400.8 46.4 %copy-start.34 = (bf16[384,768]{0,1:T(8,128)(2,1)S(1)}, bf16[384,768]{0,1:T(8,128)(2,1)}, u32[]{:S(2)}) copy-start(bf16[384,768]{0,1:T(8,128)(2,1)} %all_gather.62) | copy-start | bytes 1769476
  452.0 10.4 copy-start.50
  452.0 10.4 copy-start.57
  452.0 10.4 copy-start.73
  452.1 76.6 %all-gather.23.cloned.1.call-start = ((), (), s32[]{:S(2)}) async-start(), calls=%async_computation.23 | async-start | bytes 2506752 | tf_op jit(solution)/shard_map/all_gather | solution.py:234
  452.8 87.2 %all-gather.21.cloned.1.call-start = ((), (), s32[]{:S(2)}) async-start(), calls=%async_computation.22 | async-start | bytes 3538944 | tf_op jit(solution)/shard_map/all_gather | solution.py:38
  466.3 73.8 %copy-start.91 = (f32[1536]{0:T(1024)S(1)}, f32[1536]{0:T(1024)}, u32[]{:S(2)}) copy-start(f32[1536]{0:T(1024)} %param.81) | copy-start | bytes 18436
  467.8 138.4 %all-gather.25.cloned.1.call-start = ((), (), s32[]{:S(2)}) async-start(), calls=%async_computation.24 | async-start | bytes 2506752 | tf_op jit(solution)/shard_map/all_gather | solution.py:237
  468.4 162.2 %reduce-scatter.17.cloned.1.call-start = ((), (), s32[]{:S(2)}) async-start(), calls=%async_computation.25 | async-start | bytes 7077888 | tf_op jit(solution)/shard_map/reduce_scatter | solution.py:42
  615.4 36.5 %all-gather.31.cloned.1.call-start = ((), (), s32[]{:S(2)}) async-start(), calls=%async_computation.28 | async-start | bytes 3538944 | tf_op jit(solution)/shard_map/all_gather | solution.py:38
  641.7 45.7 %reduce-scatter.19.cloned.1.call-start = ((), (), s32[]{:S(2)}) async-start(), calls=%async_computation.29 | async-start | bytes 7077888 | tf_op jit(solution)/shard_map/reduce_scatter | solution.py:42
  651.9 16.0 copy-start.90
  673.5 34.1 %all-gather.33.cloned.1.call-start = ((), (), s32[]{:S(2)}) async-start(), calls=%async_computation.30 | async-start | bytes 3538944 | tf_op jit(solution)/shard_map/all_gather | solution.py:38
  695.3 79.7 %reduce-scatter.21.cloned.1.call-start = ((), (), s32[]{:S(2)}) async-start(), calls=%async_computation.31 | async-start | bytes 7077888 | tf_op jit(solution)/shard_map/reduce_scatter | solution.py:42
  695.3 17.1 copy-start.9
  712.4 44.9 %copy-start.33 = (bf16[768,384]{1,0:T(8,128)(2,1)S(1)}, bf16[768,384]{1,0:T(8,128)(2,1)}, u32[]{:S(2)}) copy-start(bf16[768,384]{1,0:T(8,128)(2,1)} %all_gather.59) | copy-start | bytes 1769476
  761.0 14.0 copy-start.4
  761.0 14.0 copy-start.44
  761.0 14.0 copy-start.48
  761.0 14.0 copy-start.51
  761.0 17.7 copy-start.59
  761.0 34.2 %all-gather.35.cloned.1.call-start = ((), (), s32[]{:S(2)}) async-start(), calls=%async_computation.32 | async-start | bytes 3538944 | tf_op jit(solution)/shard_map/all_gather | solution.py:38
  781.1 14.2 copy-start.32
  783.0 114.7 %all-gather.27.cloned.1.call-start = ((), (), s32[]{:S(2)}) async-start(), calls=%async_computation.26 | async-start | bytes 3538944 | tf_op jit(solution)/shard_map/all_gather | solution.py:38
  783.6 238.7 %reduce-scatter.23.cloned.1.call-start = ((), (), s32[]{:S(2)}) async-start(), calls=%async_computation.33 | async-start | bytes 4718592 | tf_op jit(solution)/shard_map/reduce_scatter | solution.py:377
  905.0 299.7 %all-reduce.12.cloned.1.call-start = ((), (), s32[]{:S(2)}) async-start(), calls=%async_computation.40 | async-start | bytes 14155776
  911.3 6.3 copy-start.84
  926.0 420.3 %reduce-scatter.35.cloned.1.call-start = ((), (), s32[]{:S(2)}) async-start(), calls=%async_computation.39 | async-start | bytes 5013504 | tf_op jit(solution)/shard_map/reduce_scatter | solution.py:412
  935.6 553.0 %reduce-scatter.33.cloned.1.call-start = ((), (), s32[]{:S(2)}) async-start(), calls=%async_computation.38 | async-start | bytes 5013504 | tf_op jit(solution)/shard_map/reduce_scatter | solution.py:409
  945.4 6.6 copy-start.25
  945.4 552.9 %reduce-scatter.25.cloned.1.call-start = ((), (), s32[]{:S(2)}) async-start(), calls=%async_computation.34 | async-start | bytes 589824 | tf_op jit(solution)/shard_map/reduce_scatter | solution.py:380
  952.0 677.2 %reduce-scatter.31.cloned.1.call-start = ((), (), s32[]{:S(2)}) async-start(), calls=%async_computation.37 | async-start | bytes 1253376 | tf_op jit(solution)/shard_map/reduce_scatter | solution.py:411
  958.9 7.8 copy-start.19
  958.9 63.4 %all-to-all-start.1 = ((bf16[2,16,32,768]{3,2,0,1:T(8,128)(2,1)}), bf16[2,16,32,768]{3,2,0,1:T(8,128)(2,1)}, u32[]{:S(2)}, u32[]{:S(2)}) async-start(bf16[2,16,32,768]{3,2,0,1:T(8,128)(2,1)} %copy_bitcast_fusion.1), calls=%async_computation.4 | async-start | bytes 3145728 | tf_op jit(solution)/shard_map/all_to_all | solution.py:388
  966.6 791.0 %reduce-scatter.29.cloned.1.call-start = ((), (), s32[]{:S(2)}) async-start(), calls=%async_computation.36 | async-start | bytes 1253376 | tf_op jit(solution)/shard_map/reduce_scatter | solution.py:407
  970.8 62.2 %copy-start.92 = (u32[32]{0:T(128)S(1)}, u32[32]{0:T(128)}, u32[]{:S(2)}) copy-start(u32[32]{0:T(128)} %constant.878) | copy-start | bytes 388
  970.8 64.5 %copy-start.24 = (bf16[1536,384]{0,1:T(8,128)(2,1)S(1)}, bf16[1536,384]{0,1:T(8,128)(2,1)}, u32[]{:S(2)}) copy-start(bf16[1536,384]{0,1:T(8,128)(2,1)} %get-tuple-element.1155) | copy-start | bytes 3538948
  1022.3 185.8 %all-to-all-start.3 = ((bf16[2,16,32,768]{3,2,0,1:T(8,128)(2,1)}), bf16[2,16,32,768]{3,2,0,1:T(8,128)(2,1)}, u32[]{:S(2)}, u32[]{:S(2)}) async-start(bf16[2,16,32,768]{3,2,0,1:T(8,128)(2,1)} %reduce-scatter.23.cloned.1.call-done), calls=%async_computation.9 | async-start | bytes 3145728 | tf_op jit(solution)/shard_map/all_to_all | solution.py:389
  1032.2 854.1 %reduce-scatter.27.cloned.1.call-start = ((), (), s32[]{:S(2)}) async-start(), calls=%async_computation.35 | async-start | bytes 1253376 | tf_op jit(solution)/shard_map/reduce_scatter | solution.py:410
  1035.3 6.3 copy-start.68
  1035.3 7.2 copy-start.65
  1035.4 7.3 copy-start.64
  1035.4 7.3 copy-start.69
  1040.3 68.6 %copy-start.78 = (s32[1024]{0:T(1024)}, s32[1024]{0:T(1024)S(1)}, u32[]{:S(2)}) copy-start(s32[1024]{0:T(1024)S(1)} %pad_clamp_fusion) | copy-start | bytes 12292
  1108.9 102.7 %copy-start.85 = (pred[32]{0:T(512)(128)(4,1)S(1)}, pred[32]{0:T(512)(128)(4,1)}, u32[]{:S(2)}) copy-start(pred[32]{0:T(512)(128)(4,1)} %compare_and_fusion) | copy-start | bytes 100
  1208.1 678.2 %copy-start.1 = (bf16[32,32,768]{2,1,0:T(8,128)(2,1)S(1)}, bf16[32,32,768]{2,1,0:T(8,128)(2,1)}, u32[]{:S(2)}) copy-start(bf16[32,32,768]{2,1,0:T(8,128)(2,1)} %param.68) | copy-start | bytes 4718596
  (92 other events, 210.1 us)
Sparse Core Ops, SparseCore 0:
  10.7 66.5 all-gather.14
  79.4 10.8 all-gather.28
  116.3 10.4 all-gather.12
  284.2 8.4 reduce-scatter.12
  295.8 58.8 all-gather.18
  356.1 9.3 all-gather.16
  452.2 10.1 reduce-scatter.14
  465.2 63.4 all-gather.22
  530.2 9.7 all-gather.20
  542.7 63.4 all-gather.24
  615.5 11.4 reduce-scatter.16
  641.9 10.0 all-gather.30
  673.6 13.7 reduce-scatter.18
  695.4 12.1 all-gather.32
  761.1 13.7 reduce-scatter.20
  783.1 12.1 all-gather.34
  797.3 12.1 all-gather.26
  905.2 12.5 reduce-scatter.22
  926.2 278.5 all-reduce.11
  1210.4 135.9 reduce-scatter.34
  1352.9 135.6 reduce-scatter.32
  1491.4 6.8 reduce-scatter.24
  1504.4 124.7 reduce-scatter.30
  1635.1 122.5 reduce-scatter.28
  1763.7 122.5 reduce-scatter.26
where the time goes:
time: 1910 us; the launch traced here: 1890 us
  waiting for transfers between devices  1010 us (53%)
  matrix products  342 us (18%)
  blocking collectives  294 us (15%)
  local copies, waits for them, and re-layouts  131 us (7%)
  other arithmetic  79.8 us (4%)
  between operations  19.2 us (1%)
    dot_general x117, matrix products, times_transpose(): lax.dot_general(left_side, right_side, (((1,), (1,)), ((), ())), preferre...  148 us
    reduce_scatter x1, waiting for transfers between devices, body(): lax.psum_scatter(grad_expand, 'dp', scatter_dimension=0, tiled=True)  142 us
    reduce_scatter x1, waiting for transfers between devices, body(): lax.psum_scatter(grad_reduce, 'dp', scatter_dimension=1, tiled=True)  131 us
    reduce_scatter x1, waiting for transfers between devices, body(): lax.psum_scatter(grad_cross_out, 'dp', scatter_dimension=1, tiled=True)  131 us
    reduce_scatter x1, waiting for transfers between devices, body(): lax.psum_scatter(grad_self_out, 'dp', scatter_dimension=1, tiled=True)  129 us
    reduce_scatter x1, waiting for transfers between devices, body(): lax.psum_scatter(grad_query_weight, 'dp', scatter_dimension=0, tiled=True)  128 us
    unnamed x26, waiting for transfers between devices  99.2 us
    dot_general x79, matrix products, contract_rows(): lax.dot_general(left_side, right_side, (((0,), (0,)), ((), ())), preferre...  74.2 us
  transfers between devices with their start and end apart: 27, of which 18 were waited for; matrix products, arithmetic and copies ran while one was open for 13% of the time, Pallas kernels for 0%

commit v1 on v0

v1 whole, which is shorter than its diff:
```python
import functools
import math

import jax
import jax.numpy as jnp
from jax import lax
from jax.experimental import pallas as pl
from jax.experimental.pallas import tpu as pltpu
from jax.sharding import PartitionSpec as P

HD = 64
EPSILON = 1e-05
MASKED = -1e30
BLOCK = 128
F32 = jnp.float32
BF16 = jnp.bfloat16


def dot_nn(left, right):
    return lax.dot_general(left, right, (((1,), (0,)), ((), ())), preferred_element_type=F32)


def dot_nt(left, right):
    return lax.dot_general(left, right, (((1,), (1,)), ((), ())), preferred_element_type=F32)


def dot_tn(left, right):
    return lax.dot_general(left, right, (((0,), (0,)), ((), ())), preferred_element_type=F32)


def lane_low(shape):
    return lax.broadcasted_iota(jnp.int32, shape, 1) < HD


def stack_heads(rows):
    low = lane_low(rows.shape)
    zero = jnp.zeros_like(rows)
    return jnp.concatenate([jnp.where(low, rows, zero), jnp.where(low, zero, rows)], 0)


def unstack_heads(transposed):
    both = transposed.T
    low = lane_low((BLOCK, 2 * HD))
    return jnp.where(low, both[:BLOCK], both[BLOCK:])


def block_place(meta):
    block = pl.program_id(1)
    first_blocks = meta[0]
    second = block >= first_blocks
    start = jnp.where(second, first_blocks, 0)
    return block, block - start, start, second.astype(jnp.int32), block < meta[1]


def diagonal_mask(own, piece, tensor_index):
    key = lax.broadcasted_iota(jnp.int32, (BLOCK, 2 * BLOCK), 0)
    query = lax.broadcasted_iota(jnp.int32, (BLOCK, 2 * BLOCK), 1) & (BLOCK - 1)
    if own:
        return key <= query
    shift = piece.bit_length() - 1
    return (key >> shift) < (query >> shift) + tensor_index


def mask_scores(scores, mask):
    keys = scores.shape[0]
    last = jnp.where(mask, scores[keys - BLOCK :], MASKED)
    if keys == BLOCK:
        return last
    return jnp.concatenate([scores[: keys - BLOCK], last], 0)


def forward_kernel(parts, causal, piece, spans, meta, q_ref, *refs):
    keys = refs[:parts]
    values = refs[parts : 2 * parts]
    out_ref, lse_ref = refs[2 * parts : 2 * parts + 2]
    flipped = refs[2 * parts + 2 :]
    block, local, start, second, active = block_place(meta)

    @pl.when(block == 0)
    def _():
        for part in range(parts):
            flipped[part][...] = values[part][...].astype(F32).T.astype(BF16)

    def run(base, span):
        stacked = stack_heads(q_ref[...])
        scores = []
        for part in range(parts):
            tile = dot_nt(keys[part][pl.ds(base, span), :], stacked)
            if causal:
                tile = mask_scores(tile, diagonal_mask(part == 0, piece, meta[2]))
            scores.append(tile)
        top = functools.reduce(
            jnp.maximum, [jnp.max(tile, 0, keepdims=True) for tile in scores]
        )
        exps = [jnp.exp(tile - top) for tile in scores]
        total = functools.reduce(jnp.add, [jnp.sum(tile, 0, keepdims=True) for tile in exps])
        result = functools.reduce(
            jnp.add,
            [
                dot_nn(flipped[part][:, pl.ds(base, span)], exps[part].astype(BF16))
                for part in range(parts)
            ],
        )
        out_ref[...] = unstack_heads(result / total).astype(BF16)
        lse_ref[...] = jnp.broadcast_to(top + jnp.log(total), (1, 1, 8, 2 * BLOCK))

    if causal:
        base = pl.multiple_of(start * BLOCK, BLOCK)
        for step in range(spans):
            pl.when(active & (local == step))(functools.partial(run, base, (step + 1) * BLOCK))
    else:
        pl.when(active)(functools.partial(run, pl.multiple_of(second * BLOCK, BLOCK), BLOCK))

    @pl.when(jnp.logical_not(active))
    def _():
        out_ref[...] = jnp.zeros_like(out_ref)
        lse_ref[...] = jnp.zeros_like(lse_ref)


def backward_kernel(parts, causal, piece, spans, meta, q_ref, g_ref, lse_ref, *refs):
    keys = refs[:parts]
    values = refs[parts : 2 * parts]
    dq_ref = refs[2 * parts]
    dk_out = refs[2 * parts + 1 : 3 * parts + 1]
    dv_out = refs[3 * parts + 1 : 4 * parts + 1]
    flipped = refs[4 * parts + 1 : 5 * parts + 1]
    dk_sum = refs[5 * parts + 1 : 6 * parts + 1]
    dv_sum = refs[6 * parts + 1 : 7 * parts + 1]
    block, local, start, second, active = block_place(meta)

    @pl.when(block == 0)
    def _():
        for part in range(parts):
            flipped[part][...] = keys[part][...].astype(F32).T.astype(BF16)
            dk_sum[part][...] = jnp.zeros_like(dk_sum[part])
            dv_sum[part][...] = jnp.zeros_like(dv_sum[part])

    def run(base, span):
        queries = stack_heads(q_ref[...])
        grads = stack_heads(g_ref[...])
        lse = lse_ref[0, 0, 0:1, :]
        probs = []
        grad_probs = []
        for part in range(parts):
            tile = dot_nt(keys[part][pl.ds(base, span), :], queries)
            if causal:
                tile = mask_scores(tile, diagonal_mask(part == 0, piece, meta[2]))
            probs.append(jnp.exp(tile - lse))
            grad_probs.append(dot_nt(values[part][pl.ds(base, span), :], grads))
        row_dot = functools.reduce(
            jnp.add,
            [jnp.sum(p * g, 0, keepdims=True) for p, g in zip(probs, grad_probs)],
        )
        grad_query = None
        for part in range(parts):
            grad_score = (probs[part] * (grad_probs[part] - row_dot)).astype(BF16)
            place = pl.ds(base, span)
            dv_sum[part][place, :] += dot_nn(probs[part].astype(BF16), grads)
            dk_sum[part][place, :] += dot_nn(grad_score, queries)
            term = dot_nn(flipped[part][:, place], grad_score)
            grad_query = term if grad_query is None else grad_query + term
        dq_ref[...] = unstack_heads(grad_query).astype(BF16)

    if causal:
        base = pl.multiple_of(start * BLOCK, BLOCK)
        for step in range(spans):
            pl.when(active & (local == step))(functools.partial(run, base, (step + 1) * BLOCK))
    else:
        pl.when(active)(functools.partial(run, pl.multiple_of(second * BLOCK, BLOCK), BLOCK))

    @pl.when(jnp.logical_not(active))
    def _():
        dq_ref[...] = jnp.zeros_like(dq_ref)

    @pl.when(block == pl.num_programs(1) - 1)
    def _():
        for part in range(parts):
            dk_out[part][...] = dk_sum[part][...].astype(dk_out[part].dtype)
            dv_out[part][...] = dv_sum[part][...].astype(dv_out[part].dtype)


def row_spec():
    return pl.BlockSpec((BLOCK, 2 * HD), lambda pair, block, meta: (block, pair))


def whole_spec(rows):
    return pl.BlockSpec((rows, 2 * HD), lambda pair, block, meta: (0, pair))


def lse_spec():
    return pl.BlockSpec((1, 1, 8, 2 * BLOCK), lambda pair, block, meta: (pair, block, 0, 0))


def attend_forward(meta, queries, keys, values, causal, piece, spans):
    rows, width = queries.shape
    parts = len(keys)
    pairs, blocks = width // (2 * HD), rows // BLOCK
    key_rows = keys[0].shape[0]
    work = pairs * blocks * parts * 4 * BLOCK * 2 * BLOCK * (2 * BLOCK if causal else BLOCK)
    return pl.pallas_call(
        functools.partial(forward_kernel, parts, causal, piece, spans),
        grid_spec=pltpu.PrefetchScalarGridSpec(
            num_scalar_prefetch=1,
            grid=(pairs, blocks),
            in_specs=[row_spec()] + [whole_spec(key_rows)] * (2 * parts),
            out_specs=[row_spec(), lse_spec()],
            scratch_shapes=[pltpu.VMEM((2 * HD, key_rows), BF16)] * parts,
        ),
        out_shape=[
            jax.ShapeDtypeStruct((rows, width), BF16),
            jax.ShapeDtypeStruct((pairs, blocks, 8, 2 * BLOCK), F32),
        ],
        cost_estimate=pl.CostEstimate(
            flops=4 * work, bytes_accessed=8 * rows * width, transcendentals=work // 256
        ),
        name="attend_forward",
    )(meta, queries, *keys, *values)


def attend_backward(meta, queries, grads, lse, keys, values, causal, piece, spans, kinds):
    rows, width = queries.shape
    parts = len(keys)
    pairs, blocks = width // (2 * HD), rows // BLOCK
    key_rows = keys[0].shape[0]
    work = pairs * blocks * parts * 4 * BLOCK * 2 * BLOCK * (2 * BLOCK if causal else BLOCK)
    results = pl.pallas_call(
        functools.partial(backward_kernel, parts, causal, piece, spans),
        grid_spec=pltpu.PrefetchScalarGridSpec(
            num_scalar_prefetch=1,
            grid=(pairs, blocks),
            in_specs=[row_spec(), row_spec(), lse_spec()] + [whole_spec(key_rows)] * (2 * parts),
            out_specs=[row_spec()] + [whole_spec(key_rows)] * (2 * parts),
            scratch_shapes=[pltpu.VMEM((2 * HD, key_rows), BF16)] * parts
            + [pltpu.VMEM((key_rows, 2 * HD), F32)] * (2 * parts),
        ),
        out_shape=[jax.ShapeDtypeStruct((rows, width), BF16)]
        + [jax.ShapeDtypeStruct((key_rows, width), kind) for kind in kinds + kinds],
        cost_estimate=pl.CostEstimate(
            flops=10 * work, bytes_accessed=16 * rows * width, transcendentals=work // 256
        ),
        name="attend_backward",
    )(meta, queries, grads, lse, *keys, *values)
    return results[0], results[1 : 1 + parts], results[1 + parts :]


def norm_forward(hidden, gain, shift):
    center = hidden - jnp.mean(hidden, -1, keepdims=True)
    spread = jnp.mean(center * center, -1, keepdims=True)
    scale = lax.rsqrt(spread + EPSILON)
    unit = center * scale
    return unit * gain + shift, unit, scale


def norm_backward(grad, unit, scale, gain):
    gain_grad = jnp.sum(grad * unit, 0)
    shift_grad = jnp.sum(grad, 0)
    inner = grad * gain
    mean_inner = jnp.mean(inner, -1, keepdims=True)
    mean_unit = jnp.mean(inner * unit, -1, keepdims=True)
    return scale * (inner - mean_inner - unit * mean_unit), gain_grad, shift_grad


def swap(value):
    return lax.ppermute(value, "tensor", [(0, 1), (1, 0)])


def body(
    tokens,
    encoder,
    lengths,
    deal,
    self_project,
    self_output,
    cross_query,
    cross_memory,
    cross_output,
    hidden_in,
    hidden_out,
    in_bias,
    out_bias,
    hidden_bias,
    norm_gain,
    norm_bias,
    cotangent,
):
    score_scale = 1.0 / math.sqrt(HD)
    dp_count = lax.axis_size("dp")
    dp_index = lax.axis_index("dp")
    tensor_index = lax.axis_index("tensor")
    piece = tokens.shape[1]
    width = tokens.shape[2]
    slots = piece * dp_count
    half = self_project.shape[2]
    units = hidden_in.shape[1]
    shard = self_project.shape[0]
    memory_rows = encoder.shape[1]
    spans = slots // BLOCK
    blocks = (slots + slots // 2) // BLOCK + 1
    rows = blocks * BLOCK
    per_block = BLOCK // piece

    pair_ids = lax.dynamic_slice_in_dim(deal, 2 * dp_index, 2)
    pair_len = jnp.take(lengths, pair_ids)
    pieces_used = (pair_len + 2 * piece - 1) // (2 * piece)
    blocks_used = (pieces_used * piece + BLOCK - 1) // BLOCK
    first_blocks = blocks_used[0]
    all_blocks = first_blocks + blocks_used[1]
    meta = jnp.stack([first_blocks, all_blocks, tensor_index]).astype(jnp.int32)

    block_ids = jnp.arange(blocks, dtype=jnp.int32)
    block_seq = (block_ids >= first_blocks).astype(jnp.int32)
    block_local = jnp.minimum(block_ids - block_seq * first_blocks, spans - 1)
    piece_ids = (
        (block_local[:, None] * per_block + jnp.arange(per_block, dtype=jnp.int32)[None, :]) * 2
        + block_seq[:, None]
    ).reshape(-1)
    slot_ids = block_local[:, None] * BLOCK + jnp.arange(BLOCK, dtype=jnp.int32)[None, :]
    positions = ((slot_ids // piece) * 2 + tensor_index) * piece + slot_ids % piece
    row_valid = (
        (positions < jnp.where(block_seq == 1, pair_len[1], pair_len[0])[:, None])
        & (block_ids < all_blocks)[:, None]
    ).reshape(rows, 1)

    def exchange(value):
        ordered = jnp.take(value, deal, axis=0)
        arrived = lax.all_to_all(ordered, "dp", split_axis=0, concat_axis=0, tiled=True)
        return jnp.take(arrived, piece_ids, axis=0).reshape(rows, width)

    send_piece = jnp.arange(dp_count, dtype=jnp.int32)
    send_block = send_piece // per_block
    send_ids = jnp.stack(
        [
            jnp.minimum(send_block, blocks_used[0] - 1) * per_block,
            (first_blocks + jnp.minimum(send_block, blocks_used[1] - 1)) * per_block,
        ],
        1,
    ) + (send_piece % per_block)[:, None]
    send_pos = (send_piece[:, None, None] * 2 + tensor_index) * piece + jnp.arange(
        piece, dtype=jnp.int32
    )[None, None, :]
    send_valid = (send_pos < pair_len[None, :, None]).reshape(2 * dp_count, piece, 1)
    inverse = jnp.zeros_like(deal).at[deal].set(jnp.arange(deal.shape[0], dtype=jnp.int32))

    def send_home(value):
        pieces = value.reshape(rows // piece, piece, width)
        outgoing = jnp.where(
            send_valid, jnp.take(pieces, send_ids.reshape(-1), axis=0), jnp.zeros((), value.dtype)
        )
        back = lax.all_to_all(outgoing, "dp", split_axis=0, concat_axis=0, tiled=True)
        return jnp.take(back, inverse, axis=0)

    inputs = exchange(tokens)

    def gather(value):
        own = lax.all_gather(value, "dp", axis=0, tiled=True)
        return (own, swap(own))

    qkv_weight = gather(self_project.reshape(shard, 3 * half))
    mid_weight = gather(
        jnp.concatenate(
            [self_output.T, cross_query, cross_memory.reshape(shard, 2 * half), cross_output.T], 1
        )
    )
    ffn_weight = gather(jnp.concatenate([hidden_in, hidden_out.T], 1))
    both = (0, 1)

    def columns(pair, start, count):
        return [lax.slice_in_dim(pair[h], start, start + count, axis=1) for h in both]

    project_q = columns(qkv_weight, 0, half)
    project_k = columns(qkv_weight, half, half)
    project_v = columns(qkv_weight, 2 * half, half)
    self_out = columns(mid_weight, 0, half)
    query_w = columns(mid_weight, half, half)
    memory_k = columns(mid_weight, 2 * half, half)
    memory_v = columns(mid_weight, 3 * half, half)
    cross_out = columns(mid_weight, 4 * half, half)
    expand = columns(ffn_weight, 0, units)
    reduce = columns(ffn_weight, units, units)

    biases = jnp.concatenate([in_bias.reshape(-1), hidden_bias])
    bias_pair = (biases, swap(biases))
    in_pair = [b[: 4 * half].reshape(4, half) for b in bias_pair]
    hidden_pair = [b[4 * half :] for b in bias_pair]

    cot = jnp.where(row_valid, exchange(cotangent), jnp.zeros((), BF16)).astype(F32)

    memory_full = jnp.concatenate([encoder, swap(encoder)], 1).reshape(4 * memory_rows, width)

    queries = [
        ((dot_nn(inputs, project_q[h]) + in_pair[h][0]) * score_scale).astype(BF16) for h in both
    ]
    keys = [dot_nn(inputs, project_k[h]).astype(BF16) for h in both]
    values = [(dot_nn(inputs, project_v[h]) + in_pair[h][1]).astype(BF16) for h in both]
    keys_far = [swap(keys[1 - h]) for h in both]
    values_far = [swap(values[1 - h]) for h in both]
    attn = []
    lse = []
    for h in both:
        result = attend_forward(
            meta, queries[h], [keys[h], keys_far[h]], [values[h], values_far[h]], True, piece, spans
        )
        attn.append(result[0])
        lse.append(result[1])
    branch = dot_nt(attn[0], self_out[0]) + dot_nt(attn[1], self_out[1]) + out_bias[0]
    n1, unit1, scale1 = norm_forward(inputs.astype(F32) + branch, norm_gain[0], norm_bias[0])
    cross_in = n1.astype(BF16)
    cqs = [
        ((dot_nn(cross_in, query_w[h]) + in_pair[h][2]) * score_scale).astype(BF16) for h in both
    ]
    cks = [dot_nn(memory_full, memory_k[h]).astype(BF16) for h in both]
    cvs = [(dot_nn(memory_full, memory_v[h]) + in_pair[h][3]).astype(BF16) for h in both]
    cattn = []
    clse = []
    for h in both:
        result = attend_forward(meta, cqs[h], [cks[h]], [cvs[h]], False, piece, spans)
        cattn.append(result[0])
        clse.append(result[1])
    branch = dot_nt(cattn[0], cross_out[0]) + dot_nt(cattn[1], cross_out[1]) + out_bias[1]
    n2, unit2, scale2 = norm_forward(n1 + branch, norm_gain[1], norm_bias[1])
    hidden = n2.astype(BF16)
    act = []
    slope = []
    for h in both:
        pre = dot_nn(hidden, expand[h]) + hidden_pair[h]
        phi = 0.5 * (1.0 + lax.erf(pre * (1.0 / math.sqrt(2.0))))
        act.append((pre * phi).astype(BF16))
        density = jnp.exp(-0.5 * pre * pre) * (1.0 / math.sqrt(2.0 * math.pi))
        slope.append((phi + pre * density).astype(BF16))
    branch = dot_nt(act[0], reduce[0]) + dot_nt(act[1], reduce[1]) + out_bias[2]
    n3, unit3, scale3 = norm_forward(n2 + branch, norm_gain[2], norm_bias[2])
    output = send_home(n3.astype(BF16))

    def scatter(grads):
        mine = grads[0] + swap(grads[1].astype(BF16)).astype(F32)
        return lax.psum_scatter(mine.astype(BF16), "dp", scatter_dimension=0, tiled=True).astype(F32)

    dh3, gain3, shift3 = norm_backward(cot, unit3, scale3, norm_gain[2])
    dz = dh3.astype(BF16)
    grad_reduce = [dot_tn(dz, act[h]) for h in both]
    du = [(dot_nn(dz, reduce[h]) * slope[h].astype(F32)).astype(BF16) for h in both]
    grad_expand = [dot_tn(hidden, du[h]) for h in both]
    ffn_shard = scatter(
        [jnp.concatenate([grad_expand[h], grad_reduce[h]], 1) for h in both]
    )
    dn2 = dh3 + dot_nt(du[0], expand[0]) + dot_nt(du[1], expand[1])
    dh2, gain2, shift2 = norm_backward(dn2, unit2, scale2, norm_gain[1])
    dy2 = dh2.astype(BF16)
    grad_cross_out = [dot_tn(dy2, cattn[h]) for h in both]
    dca = [dot_nn(dy2, cross_out[h]).astype(BF16) for h in both]
    dcq = []
    dck = []
    dcv = []
    for h in both:
        result = attend_backward(
            meta, cqs[h], dca[h], clse[h], [cks[h]], [cvs[h]], False, piece, spans, [F32]
        )
        dcq.append(result[0])
        dck.append(result[1][0].reshape(2, 2, memory_rows, half))
        dcv.append(result[2][0].reshape(2, 2, memory_rows, half))
    dck_sum = [
        (dck[h][:, 0] + swap(dck[1 - h][:, 1].astype(BF16)).astype(F32))
        .astype(BF16)
        .reshape(2 * memory_rows, half)
        for h in both
    ]
    dcv_sum = [
        (dcv[h][:, 0] + swap(dcv[1 - h][:, 1].astype(BF16)).astype(F32))
        .astype(BF16)
        .reshape(2 * memory_rows, half)
        for h in both
    ]
    memory_own = encoder.reshape(2 * memory_rows, width)
    grad_query_w = [dot_tn(cross_in, dcq[h]) * score_scale for h in both]
    grad_memory_k = [dot_tn(memory_own, dck_sum[h]) for h in both]
    grad_memory_v = [dot_tn(memory_own, dcv_sum[h]) for h in both]
    grad_memory = (
        dot_nt(dck_sum[0], memory_k[0])
        + dot_nt(dck_sum[1], memory_k[1])
        + dot_nt(dcv_sum[0], memory_v[0])
        + dot_nt(dcv_sum[1], memory_v[1])
    )
    grad_encoder = grad_memory.astype(BF16).reshape(2, memory_rows, width)
    dn1 = dh2 + (dot_nt(dcq[0], query_w[0]) + dot_nt(dcq[1], query_w[1])) * score_scale
    dh1, gain1, shift1 = norm_backward(dn1, unit1, scale1, norm_gain[0])
    dy = dh1.astype(BF16)
    grad_self_out = [dot_tn(dy, attn[h]) for h in both]
    da = [dot_nn(dy, self_out[h]).astype(BF16) for h in both]
    mid_shard = scatter(
        [
            jnp.concatenate(
                [
                    grad_self_out[h],
                    grad_query_w[h],
                    grad_memory_k[h],
                    grad_memory_v[h],
                    grad_cross_out[h],
                ],
                1,
            )
            for h in both
        ]
    )
    dq = []
    dk = []
    dv = []
    for h in both:
        result = attend_backward(
            meta,
            queries[h],
            da[h],
            lse[h],
            [keys[h], keys_far[h]],
            [values[h], values_far[h]],
            True,
            piece,
            spans,
            [F32, BF16],
        )
        dq.append(result[0])
        dk.append(result[1])
        dv.append(result[2])
    dk = [(dk[h][0] + swap(dk[1 - h][1]).astype(F32)).astype(BF16) for h in both]
    dv = [(dv[h][0] + swap(dv[1 - h][1]).astype(F32)).astype(BF16) for h in both]
    qkv_shard = scatter(
        [
            jnp.concatenate(
                [
                    dot_tn(inputs, dq[h]) * score_scale,
                    dot_tn(inputs, dk[h]),
                    dot_tn(inputs, dv[h]),
                ],
                1,
            )
            for h in both
        ]
    )
    grad_inputs = (
        dh1
        + (dot_nt(dq[0], project_q[0]) + dot_nt(dq[1], project_q[1])) * score_scale
        + dot_nt(dk[0], project_k[0])
        + dot_nt(dk[1], project_k[1])
        + dot_nt(dv[0], project_v[0])
        + dot_nt(dv[1], project_v[1])
    )
    grad_tokens = send_home(grad_inputs.astype(BF16))

    def rows_sum(value):
        return jnp.sum(value, 0, dtype=F32)

    def global_order(pair):
        own_first = jnp.concatenate(pair, -1)
        other_first = jnp.concatenate(pair[::-1], -1)
        return jnp.where(tensor_index == 0, own_first, other_first)

    in_rows = global_order(
        [
            jnp.stack(
                [
                    score_scale * rows_sum(dq[h]),
                    rows_sum(dv[h]),
                    score_scale * rows_sum(dcq[h]),
                    rows_sum(dcv_sum[h]),
                ]
            )
            for h in both
        ]
    )
    hidden_row = global_order([rows_sum(du[h]) for h in both])
    out_rows = jnp.stack([rows_sum(dy), rows_sum(dy2), rows_sum(dz)])
    gain_rows = jnp.stack([gain1, gain2, gain3])
    shift_rows = jnp.stack([shift1, shift2, shift3])
    small = lax.psum(
        jnp.concatenate(
            [
                in_rows.reshape(-1),
                hidden_row,
                out_rows.reshape(-1),
                gain_rows.reshape(-1),
                shift_rows.reshape(-1),
            ]
        ),
        ("dp", "tensor"),
    )
    in_end = 8 * half
    hidden_end = in_end + 2 * units
    in_total = small[:in_end].reshape(4, 2 * half)
    hidden_total = small[in_end:hidden_end]
    rest = small[hidden_end:].reshape(3, 3, width)
    return (
        output,
        grad_tokens,
        grad_encoder,
        qkv_shard.reshape(shard, 3, half),
        mid_shard[:, :half].T,
        mid_shard[:, half : 2 * half],
        mid_shard[:, 2 * half : 4 * half].reshape(shard, 2, half),
        mid_shard[:, 4 * half :].T,
        ffn_shard[:, :units],
        ffn_shard[:, units:].T,
        lax.dynamic_slice_in_dim(in_total, tensor_index * half, half, 1),
        rest[0],
        lax.dynamic_slice_in_dim(hidden_total, tensor_index * units, units, 0),
        rest[1],
        rest[2],
    )


def solution(mesh):
    in_specs = (
        P(None, ("dp", "tensor"), None),
        P("dp", "tensor", None),
        P(),
        P(),
        P("dp", None, "tensor"),
        P("tensor", "dp"),
        P("dp", "tensor"),
        P("dp", None, "tensor"),
        P("tensor", "dp"),
        P("dp", "tensor"),
        P("tensor", "dp"),
        P(None, "tensor"),
        P(),
        P("tensor"),
        P(),
        P(),
        P(None, ("dp", "tensor"), None),
    )
    out_specs = (
        P(None, ("dp", "tensor"), None),
        P(None, ("dp", "tensor"), None),
        P("dp", "tensor", None),
        P("dp", None, "tensor"),
        P("tensor", "dp"),
        P("dp", "tensor"),
        P("dp", None, "tensor"),
        P("tensor", "dp"),
        P("dp", "tensor"),
        P("tensor", "dp"),
        P(None, "tensor"),
        P(),
        P("tensor"),
        P(),
        P(),
    )
    return jax.shard_map(body, mesh=mesh, in_specs=in_specs, out_specs=out_specs, check_vma=False)
```

time: 1910 us -> 919 us (0.48)
  waiting for transfers between devices: 1010 us -> 361 us
  blocking collectives: 294 us -> 45.2 us
  matrix products: 342 us -> 147 us
  Pallas kernels: 0 us -> 150 us
  local copies, waits for them, and re-layouts: 131 us -> 71.2 us
    reduce_scatter x12 -> x1, waiting for transfers between devices: 711 us -> 137 us  [scatter(): lax.psum_scatter(mine.astype(BF16), 'dp', scatter_dimension=0, tiled=True)]
    dot_general x275 -> x60, matrix products: 342 us -> 147 us  [the longest x20 60.4 us: dot_nn(): lax.dot_general(left, right, (((1,), (0,)), ((), ())), preferred_element_...]
    pallas_call x0 -> x8, Pallas kernels: none -> 150 us  [the longest x4 79.2 us: attend_backward(): pl.pallas_call(functools.partial(backward_kernel, parts, causal, piece, s...]
    all_gather x4 -> x0, blocking collectives: 135 us -> none  [the longest x1 47.3 us: body(): lax.all_gather(cross_query, 'dp', axis=0, tiled=True)]
    all_to_all x2 -> x0, blocking collectives: 98.6 us -> none  [the longest x1 56.7 us: body(): lax.all_to_all(ordered_cot, 'dp', split_axis=0, concat_axis=1, tiled=True)]
    all_gather x12 -> x3, waiting for transfers between devices: 145 us -> 74.9 us  [gather(): own = lax.all_gather(value, 'dp', axis=0, tiled=True)]
    dynamic_update_slice x41 -> x0, local copies, waits for them, and re-layouts: 32.6 us -> none  [the longest x2 16.2 us: pack_slots(): buffer = lax.dynamic_update_slice_in_dim(buffer, second_part, first_len, 0)]
    unnamed x26 -> x8, waiting for transfers between devices: 99.2 us -> 77.1 us
  transfers between devices with their start and end apart: 27 -> 30, of which waited for: 18 -> 8; matrix products, arithmetic and copies ran while one was open for 13% -> 24% of each run, Pallas kernels for 0% -> 11%
where the time goes in v1:
time: 919 us; the launch traced here: 901 us
  waiting for transfers between devices  361 us (39%)
  Pallas kernels  150 us (16%)
  matrix products  147 us (16%)
  local copies, waits for them, and re-layouts  71.2 us (8%)
  other arithmetic  70.5 us (8%)
  blocking collectives  45.2 us (5%)
  starting transfers between devices  36.3 us (4%)
  between operations  18.8 us (2%)
    reduce_scatter x1, waiting for transfers between devices, scatter(): lax.psum_scatter(mine.astype(BF16), 'dp', scatter_dimension=0, tiled=True)  137 us
    pallas_call x4, Pallas kernels, attend_backward(): pl.pallas_call(functools.partial(backward_kernel, parts, causal, piece, s...  79.2 us
    unnamed x8, waiting for transfers between devices  77.1 us
    all_gather x3, waiting for transfers between devices, gather(): own = lax.all_gather(value, 'dp', axis=0, tiled=True)  74.9 us
    pallas_call x4, Pallas kernels, attend_forward(): pl.pallas_call(functools.partial(forward_kernel, parts, causal, piece, sp...  71.1 us
    dot_general x20, matrix products, dot_nn(): lax.dot_general(left, right, (((1,), (0,)), ((), ())), preferred_element_...  60.4 us
    dot_general x20, matrix products, dot_nt(): lax.dot_general(left, right, (((1,), (1,)), ((), ())), preferred_element_...  46.6 us
    psum x1, blocking collectives, body(): lax.psum(jnp.concatenate([in_rows.reshape(-1), hidden_row, out_rows.resha...  45.2 us
  transfers between devices with their start and end apart: 30, of which 8 were waited for; matrix products, arithmetic and copies ran while one was open for 24% of the time, Pallas kernels for 11%

profile of v1, /device:TPU:0, one launch (start us, length us, event | category | flops | bytes accessed | tf_op | source)
XLA Modules:
  0.0 900.8 jit_solution(16297032937059540039)
XLA Ops:
  17.4 8.5 all-to-all-start.2
  31.3 33.9 %all-to-all-done.2 = bf16[32,32,768]{2,1,0:T(8,128)(2,1)S(1)} async-done(((bf16[32,32,768]{2,1,0:T(8,128)(2,1)}), bf16[32,32,768]{2,1,0:T(8,128)(2,1)S(1)}, u32[]{:S(2)}, u32[]{:S(2)}) %all-to-all-start.2) | async-done | bytes 1572896 | tf_op jit(solution)/shard_map/all_to_all | solution.py:326
  65.2 8.5 all-to-all-start
  93.9 5.1 all-gather.4.cloned.1.call-done
  101.8 3.8 convert_reduce_fusion.2
  105.8 6.7 all-to-all-done
  116.0 3.2 convolution_convert_fusion.7.refs_0_
  119.3 49.8 %all-gather.6.cloned.1.call-done = bf16[768,1920]{1,0:T(8,128)(2,1)} async-done(((bf16[48,1920]{1,0:T(8,128)(2,1)}), bf16[768,1920]{1,0:T(8,128)(2,1)}) %all-gather.6.cloned.1.call-update) | async-done | bytes 2949136 | tf_op jit(solution)/shard_map/all_gather | solution.py:355
  172.2 2.8 convolution_convert_fusion.6.refs_0_
  175.1 2.8 fusion.45.refs_2_
  178.4 2.8 fusion.48.q_ref
  181.3 20.1 %attend_forward.5 = (bf16[896,384]{1,0:T(8,128)(2,1)}, f32[3,7,8,256]{3,2,1,0:T(8,128)}) custom-call(s32[3]{0:T(128)} %pad_add_fusion.meta, bf16[896,384]{1,0:T(8,128)(2,1)} %fusion.48.q_ref, bf16[896,384]{1,0:T(8,128)(2,1)} %convolution_convert_fusion.6.refs_0_, bf16[896,384]{1,0:T(8,128)(2,1)} %collective-permute-done.4.refs_1_, ...), custom_call_target="tpu_custom_call" | custom-call | flops 5637144576 | bytes 2752512 | tf_op jit(solution)/shard_map/attend_forward/pallas_call | solution.py:200
  201.3 2.1 convolution_convert_fusion.13.refs_0_
  207.2 20.0 %attend_forward.4 = (bf16[896,384]{1,0:T(8,128)(2,1)}, f32[3,7,8,256]{3,2,1,0:T(8,128)}) custom-call(s32[3]{0:T(128)} %pad_add_fusion.meta, bf16[896,384]{1,0:T(8,128)(2,1)} %fusion.49.q_ref, bf16[896,384]{1,0:T(8,128)(2,1)} %convolution_convert_fusion.7.refs_0_, bf16[896,384]{1,0:T(8,128)(2,1)} %copy-done.116, bf16[896,384]{1,0:T(8,128)(2,1)} %copy-done.115, ...), custom_call_target="tpu_custom_call" | custom-call | flops 5637144576 | bytes 2752512 | tf_op jit(solution)/shard_map/attend_forward/pallas_call | solution.py:200
  229.4 2.2 fusion.157
  232.1 20.0 %all-gather.8.cloned.1.call-done = bf16[768,3072]{1,0:T(8,128)(2,1)} async-done(((bf16[48,3072]{1,0:T(8,128)(2,1)}), bf16[768,3072]{1,0:T(8,128)(2,1)}) %all-gather.8.cloned.1.call-update) | async-done | bytes 4718608 | tf_op jit(solution)/shard_map/all_gather | solution.py:355
  253.7 2.8 fusion.47.q_ref
  256.5 15.3 %attend_forward.6 = (bf16[896,384]{1,0:T(8,128)(2,1)}, f32[3,7,8,256]{3,2,1,0:T(8,128)}) custom-call(s32[3]{0:T(128)} %pad_add_fusion.meta, bf16[896,384]{1,0:T(8,128)(2,1)} %fusion.47.q_ref, bf16[256,384]{1,0:T(8,128)(2,1)} %convolution_convert_fusion.13.refs_0_, bf16[256,384]{1,0:T(8,128)(2,1)} %fusion.63.refs_1_), custom_call_target="tpu_custom_call" | custom-call | flops 1409286144 | bytes 2752512 | tf_op jit(solution)/shard_map/attend_forward/pallas_call | solution.py:200
  271.8 2.2 convolution_convert_fusion.12.refs_0_
  276.1 2.8 fusion.46.q_ref
  278.9 15.8 %attend_forward.7 = (bf16[896,384]{1,0:T(8,128)(2,1)}, f32[3,7,8,256]{3,2,1,0:T(8,128)}) custom-call(s32[3]{0:T(128)} %pad_add_fusion.meta, bf16[896,384]{1,0:T(8,128)(2,1)} %fusion.46.q_ref, bf16[256,384]{1,0:T(8,128)(2,1)} %convolution_convert_fusion.12.refs_0_, bf16[256,384]{1,0:T(8,128)(2,1)} %fusion.64.refs_1_), custom_call_target="tpu_custom_call" | custom-call | flops 1409286144 | bytes 2752512 | tf_op jit(solution)/shard_map/attend_forward/pallas_call | solution.py:200
  294.8 2.1 fusion.76
  296.9 2.6 fusion.158
  300.7 3.4 multiply_convert_fusion.3
  304.2 2.4 fusion.29
  306.6 5.1 multiply_convert_fusion.2
  311.7 5.4 fusion.159
  320.3 3.2 convert_reduce_fusion.3
  323.5 6.1 convert_reduce_fusion
  329.5 5.8 convert_reduce_fusion.1
  335.3 2.3 fusion.31
  337.6 5.4 multiply_reduce_fusion
  343.0 2.7 convert_reduce_fusion.4
  346.9 2.8 convolution_convert_fusion.5.g_ref
  349.7 15.7 %attend_backward.4 = (bf16[896,384]{1,0:T(8,128)(2,1)}, f32[256,384]{1,0:T(8,128)}, f32[256,384]{1,0:T(8,128)}) custom-call(s32[3]{0:T(128)} %pad_add_fusion.meta, bf16[896,384]{1,0:T(8,128)(2,1)} %fusion.47.q_ref, bf16[896,384]{1,0:T(8,128)(2,1)} %convolution_convert_fusion.5.g_ref, f32[3,7,8,256]{3,2,1,0:T(8,128)} %get-tuple-element.46.lse_ref, ...), custom_call_target="tpu_custom_call" | custom-call | flops 3523215360 | bytes 5505024 | tf_op jit(solution)/shard_map/attend_backward/pallas_call | solution.py:226
  365.4 3.2 convolution_convert_fusion.4.g_ref
  368.6 15.9 %attend_backward.5 = (bf16[896,384]{1,0:T(8,128)(2,1)}, f32[256,384]{1,0:T(8,128)}, f32[256,384]{1,0:T(8,128)}) custom-call(s32[3]{0:T(128)} %pad_add_fusion.meta, bf16[896,384]{1,0:T(8,128)(2,1)} %fusion.46.q_ref, bf16[896,384]{1,0:T(8,128)(2,1)} %convolution_convert_fusion.4.g_ref, f32[3,7,8,256]{3,2,1,0:T(8,128)} %get-tuple-element.48.lse_ref, ...), custom_call_target="tpu_custom_call" | custom-call | flops 3523215360 | bytes 5505024 | tf_op jit(solution)/shard_map/attend_backward/pallas_call | solution.py:226
  384.5 2.1 fusion.82
  386.6 3.4 multiply_reduce_fusion.1
  390.1 2.2 convert_reduce_fusion.5
  395.8 2.9 convolution_convert_fusion.2.g_ref
  398.7 23.7 %attend_backward.7 = (bf16[896,384]{1,0:T(8,128)(2,1)}, f32[896,384]{1,0:T(8,128)}, bf16[896,384]{1,0:T(8,128)(2,1)}, f32[896,384]{1,0:T(8,128)}, bf16[896,384]{1,0:T(8,128)(2,1)}) custom-call(s32[3]{0:T(128)} %pad_add_fusion.meta, bf16[896,384]{1,0:T(8,128)(2,1)} %fusion.48.q_ref, bf16[896,384]{1,0:T(8,128)(2,1)} %convolution_convert_fusion.2.g_ref, ...), custom_call_target="tpu_custom_call" | custom-call | flops 14092861440 | bytes 5505024 | tf_op jit(solution)/shard_map/attend_backward/pallas_call | solution.py:226
  422.9 2.8 convolution_convert_fusion.3.g_ref
  425.7 23.9 %attend_backward.6 = (bf16[896,384]{1,0:T(8,128)(2,1)}, f32[896,384]{1,0:T(8,128)}, bf16[896,384]{1,0:T(8,128)(2,1)}, f32[896,384]{1,0:T(8,128)}, bf16[896,384]{1,0:T(8,128)(2,1)}) custom-call(s32[3]{0:T(128)} %pad_add_fusion.meta, bf16[896,384]{1,0:T(8,128)(2,1)} %fusion.49.q_ref, bf16[896,384]{1,0:T(8,128)(2,1)} %convolution_convert_fusion.3.g_ref, ...), custom_call_target="tpu_custom_call" | custom-call | flops 14092861440 | bytes 5505024 | tf_op jit(solution)/shard_map/attend_backward/pallas_call | solution.py:226
  472.0 2.2 copy.74
  475.9 6.2 convolution_convert_fusion
  482.1 4.2 convolution_convert_fusion.1
  489.6 2.5 add_convert_fusion
  492.1 3.9 copy.76
  496.1 5.2 pad_maximum_fusion
  504.6 7.2 fusion.162
  511.8 4.6 fusion.161
  516.4 9.0 %fusion = bf16[768,3072]{1,0:T(8,128)(2,1)} fusion(f32[768,1536]{1,0:T(8,128)} %fusion.162, f32[768,1536]{1,0:T(8,128)} %fusion.161, bf16[768,3072]{1,0:T(8,128)(2,1)} %collective-permute-done.19), kind=kLoop, calls=%fused_computation.11 | loop fusion | flops 9437184 | bytes 18874368 | tf_op jit(solution)/shard_map/convert_element_type | solution.py:436
  528.6 2.1 fusion.88
  532.3 2.1 fusion.101
  536.4 2.3 add_convert_fusion.1
  540.5 3.5 select_select_fusion
  544.0 4.3 all-to-all-start.3
  554.3 31.3 %all-to-all-done.3 = bf16[32,32,768]{2,1,0:T(8,128)(2,1)S(1)} async-done(((bf16[32,32,768]{2,1,0:T(8,128)(2,1)}), bf16[32,32,768]{2,1,0:T(8,128)(2,1)S(1)}, u32[]{:S(2)}, u32[]{:S(2)}) %all-to-all-start.3) | async-done | bytes 1572896 | tf_op jit(solution)/shard_map/all_to_all | solution.py:349
  585.6 9.8 %all-to-all-start.1 = ((bf16[32,32,768]{2,1,0:T(8,128)(2,1)}), bf16[32,32,768]{2,1,0:T(8,128)(2,1)S(1)}, u32[]{:S(2)}, u32[]{:S(2)}) async-start(bf16[32,32,768]{2,1,0:T(8,128)(2,1)} %get-tuple-element.169), calls=%async_computation.1 | async-start | bytes 3145728 | tf_op jit(solution)/shard_map/all_to_all | solution.py:349
  613.7 45.2 %psum.7 = f32[13056]{0:T(1024)S(1)} all-reduce(f32[13056]{0:T(1024)S(1)} %constant_dynamic-update-slice_fusion.1), channel_id=1, replica_groups=mesh['dp'=16,'tensor'=2] {'dp','tensor'}, use_global_device_ids=true, to_apply=%region_35.39 | all-reduce | flops 13056 | bytes 104448 | tf_op jit(solution)/shard_map/psum | solution.py:573
  666.2 3.4 broadcast_select_fusion
  671.6 77.0 %reduce-scatter.12.cloned.1.call-done = bf16[48,1920]{1,0:T(8,128)(2,1)} async-done(((bf16[768,1920]{1,0:T(8,128)(2,1)}), bf16[48,1920]{1,0:T(8,128)(2,1)}) %reduce-scatter.12.cloned.1.call-update) | async-done | bytes 184336
  753.0 137.3 %reduce-scatter.8.cloned.1.call-done = bf16[48,3072]{1,0:T(8,128)(2,1)} async-done(((bf16[768,3072]{1,0:T(8,128)(2,1)}), bf16[48,3072]{1,0:T(8,128)(2,1)}) %reduce-scatter.8.cloned.1.call-update) | async-done | bytes 294928 | tf_op jit(solution)/shard_map/reduce_scatter | solution.py:436
  (496 shorter events, 142.5 us)
Async XLA Ops:
  7.2 91.8 %all-gather.4.cloned.1.call-start = ((), (), s32[]{:S(2)}) async-start(), calls=%async_computation.7 | async-start | bytes 1880064 | tf_op jit(solution)/shard_map/all_gather | solution.py:355
  8.9 160.1 %all-gather.6.cloned.1.call-start = ((), (), s32[]{:S(2)}) async-start(), calls=%async_computation.8 | async-start | bytes 3133440 | tf_op jit(solution)/shard_map/all_gather | solution.py:355
  17.3 8.6 copy-start.72
  17.3 8.6 copy-start.73
  17.3 9.3 %copy-start.77 = (f32[4,384]{1,0:T(4,128)S(1)}, f32[4,384]{1,0:T(4,128)}, u32[]{:S(2)}) copy-start(f32[4,384]{1,0:T(4,128)} %param.34) | copy-start | bytes 18436
  17.3 9.3 %copy-start.88 = (f32[1536]{0:T(1024)S(1)}, f32[1536]{0:T(1024)}, u32[]{:S(2)}) copy-start(f32[1536]{0:T(1024)} %param.36) | copy-start | bytes 18436
  17.3 10.0 %copy-start.42 = (bf16[2,64,768]{2,1,0:T(8,128)(2,1)S(1)}, bf16[2,64,768]{2,1,0:T(8,128)(2,1)}, u32[]{:S(2)}) copy-start(bf16[2,64,768]{2,1,0:T(8,128)(2,1)} %param.24) | copy-start | bytes 589828
  17.3 10.5 %copy-start.2 = (s32[32]{0:T(128)S(1)}, s32[32]{0:T(128)}, u32[]{:S(2)}) copy-start(s32[32]{0:T(128)} %param.25) | copy-start | bytes 388
  17.4 47.8 %all-to-all-start.2 = ((bf16[32,32,768]{2,1,0:T(8,128)(2,1)}), bf16[32,32,768]{2,1,0:T(8,128)(2,1)S(1)}, u32[]{:S(2)}, u32[]{:S(2)}) async-start(bf16[32,32,768]{2,1,0:T(8,128)(2,1)} %get-tuple-element.172), calls=%async_computation.2 | async-start | bytes 3145728 | tf_op jit(solution)/shard_map/all_to_all | solution.py:326
  25.8 226.3 %all-gather.8.cloned.1.call-start = ((), (), s32[]{:S(2)}) async-start(), calls=%async_computation.9 | async-start | bytes 5013504 | tf_op jit(solution)/shard_map/all_gather | solution.py:355
  27.3 63.9 %collective-permute-start.2 = (f32[3072]{0:T(1024)}, f32[3072]{0:T(1024)}, u32[]{:S(2)}, u32[]{:S(2)}) collective-permute-start(f32[3072]{0:T(1024)} %pad_maximum_fusion.5), channel_id=1, source_target_pairs={{0,1},{1,0},{2,3},{3,2},{4,5},{5,4},{6,7},{7,6},{8,9},{9,8},{10,11... | collective-permute-start | bytes 36872 | tf_op jit(solution)/shard_map/ppermute | solution.py:264
  27.3 71.8 %collective-permute-start.7 = (bf16[2,64,768]{2,1,0:T(8,128)(2,1)S(1)}, bf16[2,64,768]{2,1,0:T(8,128)(2,1)S(1)}, u32[]{:S(2)}, u32[]{:S(2)}) collective-permute-start(bf16[2,64,768]{2,1,0:T(8,128)(2,1)S(1)} %copy-done.42), channel_id=1, source_target_pairs={{0,1},{1,0},{2,3},{3,2},{4,5},{5,4},{6,7},{7,6},{8,9},{9,8},{10,11... | collective-permute-start | bytes 589832 | tf_op jit(solution)/shard_map/ppermute | solution.py:264
  28.6 36.6 %copy-start.93 = (s32[2]{0:T(128)}, s32[2]{0:T(128)S(1)}, u32[]{:S(2)}) copy-start(s32[2]{0:T(128)S(1)} %get-tuple-element.155) | copy-start | bytes 28
  65.2 47.3 %all-to-all-start = ((bf16[32,32,768]{2,1,0:T(8,128)(2,1)}), bf16[32,32,768]{2,1,0:T(8,128)(2,1)S(1)}, u32[]{:S(2)}, u32[]{:S(2)}) async-start(bf16[32,32,768]{2,1,0:T(8,128)(2,1)} %get-tuple-element.173), calls=%async_computation | async-start | bytes 3145728 | tf_op jit(solution)/shard_map/all_to_all | solution.py:326
  73.6 595.9 %reduce-scatter.10.cloned.1.call-start = ((), (), s32[]{:S(2)}) async-start(), calls=%async_computation.11 | async-start | bytes 1880064
  74.6 9.0 %copy-start.114 = (s32[28]{0:T(128)}, s32[28]{0:T(128)S(1)}, u32[]{:S(2)}) copy-start(s32[28]{0:T(128)S(1)} %add.523) | copy-start | bytes 340
  99.0 73.3 %collective-permute-start = (bf16[768,1152]{1,0:T(8,128)(2,1)}, bf16[768,1152]{1,0:T(8,128)(2,1)}, u32[]{:S(2)}, u32[]{:S(2)}) collective-permute-start(bf16[768,1152]{1,0:T(8,128)(2,1)} %all-gather.4.cloned.1.call-done), channel_id=1, source_target_pairs={{0,1},{1,0},{2,3},{3,2},{4,5},{5,4},{6,7},{7,6},{8,9},{9,8},{10,11... | collective-permute-start | bytes 5308424 | tf_op jit(solution)/shard_map/ppermute | solution.py:264
  114.3 54.7 %copy-start.40 = (bf16[768,1152]{1,0:T(8,128)(2,1)S(1)}, bf16[768,1152]{1,0:T(8,128)(2,1)}, u32[]{:S(2)}) copy-start(bf16[768,1152]{1,0:T(8,128)(2,1)} %all-gather.4.cloned.1.call-done) | copy-start | bytes 5308420
  114.3 54.7 %copy-start.105 = (f32[384]{0:T(512)S(1)}, f32[384]{0:T(512)}, u32[]{:S(2)}) copy-start(f32[384]{0:T(512)} %get-tuple-element.133) | copy-start | bytes 4612
  116.0 62.4 %copy-start.3 = (bf16[28,32,768]{2,1,0:T(8,128)(2,1)}, bf16[28,32,768]{2,1,0:T(8,128)(2,1)S(1)}, u32[]{:S(2)}) copy-start(bf16[28,32,768]{2,1,0:T(8,128)(2,1)S(1)} %broadcast_select_fusion.5) | copy-start | bytes 4128772
  119.3 51.3 %copy-start.104 = (f32[384]{0:T(512)S(1)}, f32[384]{0:T(512)}, u32[]{:S(2)}) copy-start(f32[384]{0:T(512)} %get-tuple-element.134) | copy-start | bytes 4612
  119.3 62.0 %collective-permute-start.4 = (bf16[896,384]{1,0:T(8,128)(2,1)}, bf16[896,384]{1,0:T(8,128)(2,1)}, u32[]{:S(2)}, u32[]{:S(2)}) collective-permute-start(bf16[896,384]{1,0:T(8,128)(2,1)} %convolution_convert_fusion.7.refs_0_), channel_id=1, source_target_pairs={{0,1},{1,0},{2,3},{3,2},{4,5},{5,4},{6,7},{7,6},{8,9},{9,8},{10,11... | collective-permute-start | bytes 2064392 | tf_op jit(solution)/shard_map/ppermute | solution.py:264
  169.0 58.2 %collective-permute-start.6 = (bf16[768,1920]{1,0:T(8,128)(2,1)}, bf16[768,1920]{1,0:T(8,128)(2,1)}, u32[]{:S(2)}, u32[]{:S(2)}) collective-permute-start(bf16[768,1920]{1,0:T(8,128)(2,1)} %all-gather.6.cloned.1.call-done), channel_id=1, source_target_pairs={{0,1},{1,0},{2,3},{3,2},{4,5},{5,4},{6,7},{7,6},{8,9},{9,8},{10,11... | collective-permute-start | bytes 8847368 | tf_op jit(solution)/shard_map/ppermute | solution.py:264
  169.9 11.3 %collective-permute-start.5 = (bf16[896,384]{1,0:T(8,128)(2,1)S(1)}, bf16[896,384]{1,0:T(8,128)(2,1)}, u32[]{:S(2)}, u32[]{:S(2)}) collective-permute-start(bf16[896,384]{1,0:T(8,128)(2,1)S(1)} %fusion.44.refs_2_), channel_id=1, source_target_pairs={{0,1},{1,0},{2,3},{3,2},{4,5},{5,4},{6,7},{7,6},{8,9},{9,8},{10,11... | collective-permute-start | bytes 2064392 | tf_op jit(solution)/shard_map/ppermute | solution.py:264
  175.1 30.5 %collective-permute-start.1 = (bf16[896,384]{1,0:T(8,128)(2,1)}, bf16[896,384]{1,0:T(8,128)(2,1)S(1)}, u32[]{:S(2)}, u32[]{:S(2)}) collective-permute-start(bf16[896,384]{1,0:T(8,128)(2,1)} %convolution_convert_fusion.6.refs_0_), channel_id=1, source_target_pairs={{0,1},{1,0},{2,3},{3,2},{4,5},{5,4},{6,7},{7,6},{8,9},{9,8},{10,11... | collective-permute-start | bytes 2064392 | tf_op jit(solution)/shard_map/ppermute | solution.py:264
  177.9 27.6 %collective-permute-start.3 = (bf16[896,384]{1,0:T(8,128)(2,1)}, bf16[896,384]{1,0:T(8,128)(2,1)S(1)}, u32[]{:S(2)}, u32[]{:S(2)}) collective-permute-start(bf16[896,384]{1,0:T(8,128)(2,1)} %fusion.45.refs_2_), channel_id=1, source_target_pairs={{0,1},{1,0},{2,3},{3,2},{4,5},{5,4},{6,7},{7,6},{8,9},{9,8},{10,11... | collective-permute-start | bytes 2064392 | tf_op jit(solution)/shard_map/ppermute | solution.py:264
  181.2 20.1 %copy-start.63 = (bf16[2,128,768]{2,1,0:T(8,128)(2,1)S(1)}, bf16[2,128,768]{2,1,0:T(8,128)(2,1)}, u32[]{:S(2)}) copy-start(bf16[2,128,768]{2,1,0:T(8,128)(2,1)} %pad_maximum_fusion.2) | copy-start | bytes 1179652
  181.2 22.2 %copy-start.103 = (f32[384]{0:T(512)S(1)}, f32[384]{0:T(512)}, u32[]{:S(2)}) copy-start(f32[384]{0:T(512)} %get-tuple-element.132) | copy-start | bytes 4612
  205.5 21.7 %copy-start.57 = (bf16[896,384]{1,0:T(8,128)(2,1)S(1)}, bf16[896,384]{1,0:T(8,128)(2,1)}, u32[]{:S(2)}) copy-start(bf16[896,384]{1,0:T(8,128)(2,1)} %get-tuple-element.43) | copy-start | bytes 2064388
  231.6 20.5 %copy-start.76 = (f32[768]{0:T(1024)S(1)}, f32[768]{0:T(1024)}, u32[]{:S(2)}) copy-start(f32[768]{0:T(1024)} %get-tuple-element.127) | copy-start | bytes 9220
  232.0 21.6 %copy-start.102 = (f32[384]{0:T(512)S(1)}, f32[384]{0:T(512)}, u32[]{:S(2)}) copy-start(f32[384]{0:T(512)} %get-tuple-element.135) | copy-start | bytes 4612
  252.1 54.5 %collective-permute-start.8 = (bf16[768,3072]{1,0:T(8,128)(2,1)}, bf16[768,3072]{1,0:T(8,128)(2,1)}, u32[]{:S(2)}, u32[]{:S(2)}) collective-permute-start(bf16[768,3072]{1,0:T(8,128)(2,1)} %all-gather.8.cloned.1.call-done), channel_id=1, source_target_pairs={{0,1},{1,0},{2,3},{3,2},{4,5},{5,4},{6,7},{7,6},{8,9},{9,8},{10,11... | collective-permute-start | bytes 14155784 | tf_op jit(solution)/shard_map/ppermute | solution.py:264
  256.5 17.5 %copy-start.108 = (f32[384]{0:T(512)S(1)}, f32[384]{0:T(512)}, u32[]{:S(2)}) copy-start(f32[384]{0:T(512)} %get-tuple-element.164) | copy-start | bytes 4612
  256.5 19.6 %copy-start.107 = (f32[384]{0:T(512)S(1)}, f32[384]{0:T(512)}, u32[]{:S(2)}) copy-start(f32[384]{0:T(512)} %get-tuple-element.165) | copy-start | bytes 4612
  278.9 15.8 %copy-start.55 = (bf16[896,384]{1,0:T(8,128)(2,1)S(1)}, bf16[896,384]{1,0:T(8,128)(2,1)}, u32[]{:S(2)}) copy-start(bf16[896,384]{1,0:T(8,128)(2,1)} %get-tuple-element.44) | copy-start | bytes 2064388
  329.5 8.1 copy-start.118
  368.6 15.9 %copy-start.27 = (bf16[896,384]{1,0:T(8,128)(2,1)S(1)}, bf16[896,384]{1,0:T(8,128)(2,1)}, u32[]{:S(2)}) copy-start(bf16[896,384]{1,0:T(8,128)(2,1)} %get-tuple-element.47) | copy-start | bytes 2064388
  398.7 24.2 %copy-start.54 = (bf16[896,768]{1,0:T(8,128)(2,1)S(1)}, bf16[896,768]{1,0:T(8,128)(2,1)}, u32[]{:S(2)}) copy-start(bf16[896,768]{1,0:T(8,128)(2,1)} %copy-done.53) | copy-start | bytes 4128772
  422.4 45.5 %collective-permute-start.11 = (bf16[896,384]{1,0:T(8,128)(2,1)}, bf16[896,384]{1,0:T(8,128)(2,1)}, u32[]{:S(2)}, u32[]{:S(2)}) collective-permute-start(bf16[896,384]{1,0:T(8,128)(2,1)} %get-tuple-element.59), channel_id=1, source_target_pairs={{0,1},{1,0},{2,3},{3,2},{4,5},{5,4},{6,7},{7,6},{8,9},{9,8},{10,11... | collective-permute-start | bytes 2064392 | tf_op jit(solution)/shard_map/ppermute | solution.py:264
  425.7 26.0 %copy-start.5 = (bf16[28,32,768]{2,1,0:T(8,128)(2,1)S(1)}, bf16[28,32,768]{2,1,0:T(8,128)(2,1)}, u32[]{:S(2)}) copy-start(bf16[28,32,768]{2,1,0:T(8,128)(2,1)} %copy-done.3) | copy-start | bytes 4128772
  449.6 10.4 %collective-permute-start.10 = (bf16[896,384]{1,0:T(8,128)(2,1)}, bf16[896,384]{1,0:T(8,128)(2,1)S(1)}, u32[]{:S(2)}, u32[]{:S(2)}) collective-permute-start(bf16[896,384]{1,0:T(8,128)(2,1)} %get-tuple-element.57), channel_id=1, source_target_pairs={{0,1},{1,0},{2,3},{3,2},{4,5},{5,4},{6,7},{7,6},{8,9},{9,8},{10,11... | collective-permute-start | bytes 2064392 | tf_op jit(solution)/shard_map/ppermute | solution.py:264
  449.7 20.9 %collective-permute-start.9 = (bf16[896,384]{1,0:T(8,128)(2,1)}, bf16[896,384]{1,0:T(8,128)(2,1)S(1)}, u32[]{:S(2)}, u32[]{:S(2)}) collective-permute-start(bf16[896,384]{1,0:T(8,128)(2,1)} %get-tuple-element.55), channel_id=1, source_target_pairs={{0,1},{1,0},{2,3},{3,2},{4,5},{5,4},{6,7},{7,6},{8,9},{9,8},{10,11... | collective-permute-start | bytes 2064392 | tf_op jit(solution)/shard_map/ppermute | solution.py:264
  450.2 7.3 collective-permute-start.12
  451.2 6.1 collective-permute-start.14
  457.3 6.6 collective-permute-start.16
  461.9 9.7 %collective-permute-start.17 = (bf16[768,1152]{0,1:T(8,128)(2,1)S(1)}, bf16[768,1152]{0,1:T(8,128)(2,1)S(1)}, u32[]{:S(2)}, u32[]{:S(2)}) collective-permute-start(bf16[768,1152]{0,1:T(8,128)(2,1)S(1)} %pad_maximum_fusion.1), channel_id=1, source_target_pairs={{0,1},{1,0},{2,3},{3,2},{4,5},{5,4},{6,7},{7,6},{8,9},{9,8},{10,11... | collective-permute-start | bytes 5308424 | tf_op jit(solution)/shard_map/ppermute | solution.py:264
  467.4 22.2 %collective-permute-start.18 = (bf16[768,1920]{0,1:T(8,128)(2,1)}, bf16[768,1920]{0,1:T(8,128)(2,1)}, u32[]{:S(2)}, u32[]{:S(2)}) collective-permute-start(bf16[768,1920]{0,1:T(8,128)(2,1)} %fusion.53), channel_id=1, source_target_pairs={{0,1},{1,0},{2,3},{3,2},{4,5},{5,4},{6,7},{7,6},{8,9},{9,8},{10,11... | collective-permute-start | bytes 8847368 | tf_op jit(solution)/shard_map/ppermute | solution.py:264
  474.3 274.3 %reduce-scatter.12.cloned.1.call-start = ((), (), s32[]{:S(2)}) async-start(), calls=%async_computation.12 | async-start | bytes 3133440
  475.3 11.9 %collective-permute-start.13 = (bf16[2,64,384]{2,1,0:T(8,128)(2,1)S(1)}, bf16[2,64,384]{2,1,0:T(8,128)(2,1)S(1)}, u32[]{:S(2)}, u32[]{:S(2)}) collective-permute-start(bf16[2,64,384]{2,1,0:T(8,128)(2,1)S(1)} %fusion.118), channel_id=1, source_target_pairs={{0,1},{1,0},{2,3},{3,2},{4,5},{5,4},{6,7},{7,6},{8,9},{9,8},{10,11... | collective-permute-start | bytes 294920 | tf_op jit(solution)/shard_map/ppermute | solution.py:264
  475.5 11.9 %collective-permute-start.15 = (bf16[2,64,384]{2,1,0:T(8,128)(2,1)S(1)}, bf16[2,64,384]{2,1,0:T(8,128)(2,1)S(1)}, u32[]{:S(2)}, u32[]{:S(2)}) collective-permute-start(bf16[2,64,384]{2,1,0:T(8,128)(2,1)S(1)} %fusion.120), channel_id=1, source_target_pairs={{0,1},{1,0},{2,3},{3,2},{4,5},{5,4},{6,7},{7,6},{8,9},{9,8},{10,11... | collective-permute-start | bytes 294920 | tf_op jit(solution)/shard_map/ppermute | solution.py:264
  475.9 10.4 %slice-start = ((s8[5898240]{0:T(1024)(128)(4,1)}), s8[4194304]{0:T(1024)(128)(4,1)S(1)}, s32[]{:S(2)}) async-start(s8[5898240]{0:T(1024)(128)(4,1)} %bitcast.244), calls=%async_computation.13 | async-start | bytes 8388608
  496.0 7.9 copy-start.9
  496.0 394.2 %reduce-scatter.8.cloned.1.call-start = ((), (), s32[]{:S(2)}) async-start(), calls=%async_computation.10 | async-start | bytes 5013504 | tf_op jit(solution)/shard_map/reduce_scatter | solution.py:436
  501.3 15.1 %collective-permute-start.19 = (bf16[768,3072]{1,0:T(8,128)(2,1)}, bf16[768,3072]{1,0:T(8,128)(2,1)}, u32[]{:S(2)}, u32[]{:S(2)}) collective-permute-start(bf16[768,3072]{1,0:T(8,128)(2,1)} %pad_maximum_fusion), channel_id=1, source_target_pairs={{0,1},{1,0},{2,3},{3,2},{4,5},{5,4},{6,7},{7,6},{8,9},{9,8},{10,11... | collective-permute-start | bytes 14155784 | tf_op jit(solution)/shard_map/ppermute | solution.py:264
  544.0 9.5 %copy-start.29 = (bf16[896,384]{1,0:T(8,128)(2,1)S(1)}, bf16[896,384]{1,0:T(8,128)(2,1)}, u32[]{:S(2)}) copy-start(bf16[896,384]{1,0:T(8,128)(2,1)} %get-tuple-element.47) | copy-start | bytes 2064388
  544.0 41.6 %all-to-all-start.3 = ((bf16[32,32,768]{2,1,0:T(8,128)(2,1)}), bf16[32,32,768]{2,1,0:T(8,128)(2,1)S(1)}, u32[]{:S(2)}, u32[]{:S(2)}) async-start(bf16[32,32,768]{2,1,0:T(8,128)(2,1)} %get-tuple-element.168), calls=%async_computation.3 | async-start | bytes 3145728 | tf_op jit(solution)/shard_map/all_to_all | solution.py:349
  551.0 46.2 %copy-start.79 = (f32[768]{0:T(1024)S(1)}, f32[768]{0:T(1024)}, u32[]{:S(2)}) copy-start(f32[768]{0:T(1024)} %get-tuple-element.142) | copy-start | bytes 9220
  551.0 46.2 %copy-start.80 = (f32[768]{0:T(1024)S(1)}, f32[768]{0:T(1024)}, u32[]{:S(2)}) copy-start(f32[768]{0:T(1024)} %get-tuple-element.139) | copy-start | bytes 9220
  551.1 56.1 %copy-start.65 = (bf16[2,64,384]{2,1,0:T(8,128)(2,1)S(1)}, bf16[2,64,384]{2,1,0:T(8,128)(2,1)}, u32[]{:S(2)}) copy-start(bf16[2,64,384]{2,1,0:T(8,128)(2,1)} %copy-done.64) | copy-start | bytes 294916
  585.6 78.5 %all-to-all-start.1 = ((bf16[32,32,768]{2,1,0:T(8,128)(2,1)}), bf16[32,32,768]{2,1,0:T(8,128)(2,1)S(1)}, u32[]{:S(2)}, u32[]{:S(2)}) async-start(bf16[32,32,768]{2,1,0:T(8,128)(2,1)} %get-tuple-element.169), calls=%async_computation.1 | async-start | bytes 3145728 | tf_op jit(solution)/shard_map/all_to_all | solution.py:349
  595.4 16.0 %copy-start.67 = (bf16[2,64,384]{2,1,0:T(8,128)(2,1)S(1)}, bf16[2,64,384]{2,1,0:T(8,128)(2,1)}, u32[]{:S(2)}) copy-start(bf16[2,64,384]{2,1,0:T(8,128)(2,1)} %copy-done.66) | copy-start | bytes 294916
  603.3 10.2 %copy-start.86 = (f32[384]{0:T(512)S(1)}, f32[384]{0:T(512)}, u32[]{:S(2)}) copy-start(f32[384]{0:T(512)} %get-tuple-element.149) | copy-start | bytes 4612
  605.9 7.6 copy-start.98
  749.8 143.9 %copy-start.1 = (bf16[32,32,768]{2,1,0:T(8,128)(2,1)S(1)}, bf16[32,32,768]{2,1,0:T(8,128)(2,1)}, u32[]{:S(2)}) copy-start(bf16[32,32,768]{2,1,0:T(8,128)(2,1)} %param.39) | copy-start | bytes 4718596
  (91 other events, 290.5 us)
Sparse Core Ops, SparseCore 0:
  11.4 87.5 all-gather.3
  102.4 66.6 all-gather.5
  172.4 79.6 all-gather.7
  474.4 137.5 reduce-scatter.9
  616.9 131.6 reduce-scatter.11
  753.6 136.6 reduce-scatter.7

commit v2 on v1

--- a/solution.py
+++ b/solution.py
@@ -12,6 +12,7 @@
 EPSILON = 1e-05
 MASKED = -1e30
 BLOCK = 128
+PAIR = 2 * HD
 F32 = jnp.float32
 BF16 = jnp.bfloat16
 
@@ -40,12 +41,12 @@
 
 def unstack_heads(transposed):
     both = transposed.T
-    low = lane_low((BLOCK, 2 * HD))
+    low = lane_low((BLOCK, PAIR))
     return jnp.where(low, both[:BLOCK], both[BLOCK:])
 
 
 def block_place(meta):
-    block = pl.program_id(1)
+    block = pl.program_id(0)
     first_blocks = meta[0]
     second = block >= first_blocks
     start = jnp.where(second, first_blocks, 0)
@@ -69,41 +70,11 @@
     return jnp.concatenate([scores[: keys - BLOCK], last], 0)
 
 
-def forward_kernel(parts, causal, piece, spans, meta, q_ref, *refs):
-    keys = refs[:parts]
-    values = refs[parts : 2 * parts]
-    out_ref, lse_ref = refs[2 * parts : 2 * parts + 2]
-    flipped = refs[2 * parts + 2 :]
-    block, local, start, second, active = block_place(meta)
-
-    @pl.when(block == 0)
-    def _():
-        for part in range(parts):
-            flipped[part][...] = values[part][...].astype(F32).T.astype(BF16)
-
-    def run(base, span):
-        stacked = stack_heads(q_ref[...])
-        scores = []
-        for part in range(parts):
-            tile = dot_nt(keys[part][pl.ds(base, span), :], stacked)
-            if causal:
-                tile = mask_scores(tile, diagonal_mask(part == 0, piece, meta[2]))
-            scores.append(tile)
-        top = functools.reduce(
-            jnp.maximum, [jnp.max(tile, 0, keepdims=True) for tile in scores]
-        )
-        exps = [jnp.exp(tile - top) for tile in scores]
-        total = functools.reduce(jnp.add, [jnp.sum(tile, 0, keepdims=True) for tile in exps])
-        result = functools.reduce(
-            jnp.add,
-            [
-                dot_nn(flipped[part][:, pl.ds(base, span)], exps[part].astype(BF16))
-                for part in range(parts)
-            ],
-        )
-        out_ref[...] = unstack_heads(result / total).astype(BF16)
-        lse_ref[...] = jnp.broadcast_to(top + jnp.log(total), (1, 1, 8, 2 * BLOCK))
-
+def pair_columns(pair):
+    return slice(pair * PAIR, (pair + 1) * PAIR)
+
+
+def run_spans(causal, spans, local, start, second, active, run):
     if causal:
         base = pl.multiple_of(start * BLOCK, BLOCK)
         for step in range(spans):
@@ -111,13 +82,52 @@
     else:
         pl.when(active)(functools.partial(run, pl.multiple_of(second * BLOCK, BLOCK), BLOCK))
 
+
+def forward_kernel(parts, pairs, causal, piece, spans, meta, q_ref, *refs):
+    keys = refs[:parts]
+    values = refs[parts : 2 * parts]
+    out_ref, lse_ref = refs[2 * parts : 2 * parts + 2]
+    flipped = refs[2 * parts + 2 :]
+    block, local, start, second, active = block_place(meta)
+
+    @pl.when(block == 0)
+    def _():
+        for part in range(parts):
+            flipped[part][...] = values[part][...].astype(F32).T.astype(BF16)
+
+    def run(base, span):
+        masks = [diagonal_mask(part == 0, piece, meta[2]) for part in range(parts)]
+        for pair in range(pairs):
+            cols = pair_columns(pair)
+            stacked = stack_heads(q_ref[:, cols])
+            scores = []
+            for part in range(parts):
+                tile = dot_nt(keys[part][pl.ds(base, span), cols], stacked)
+                scores.append(mask_scores(tile, masks[part]) if causal else tile)
+            top = functools.reduce(
+                jnp.maximum, [jnp.max(tile, 0, keepdims=True) for tile in scores]
+            )
+            exps = [jnp.exp(tile - top) for tile in scores]
+            total = functools.reduce(jnp.add, [jnp.sum(tile, 0, keepdims=True) for tile in exps])
+            result = functools.reduce(
+                jnp.add,
+                [
+                    dot_nn(flipped[part][cols, pl.ds(base, span)], exps[part].astype(BF16))
+                    for part in range(parts)
+                ],
+            )
+            out_ref[:, cols] = unstack_heads(result / total).astype(BF16)
+            lse_ref[0, pair : pair + 1, :] = top + jnp.log(total)
+
+    run_spans(causal, spans, local, start, second, active, run)
+
     @pl.when(jnp.logical_not(active))
     def _():
         out_ref[...] = jnp.zeros_like(out_ref)
         lse_ref[...] = jnp.zeros_like(lse_ref)
 
 
-def backward_kernel(parts, causal, piece, spans, meta, q_ref, g_ref, lse_ref, *refs):
+def backward_kernel(parts, pairs, causal, piece, spans, meta, q_ref, g_ref, lse_ref, *refs):
     keys = refs[:parts]
     values = refs[parts : 2 * parts]
     dq_ref = refs[2 * parts]
@@ -136,79 +146,77 @@
             dv_sum[part][...] = jnp.zeros_like(dv_sum[part])
 
     def run(base, span):
-        queries = stack_heads(q_ref[...])
-        grads = stack_heads(g_ref[...])
-        lse = lse_ref[0, 0, 0:1, :]
-        probs = []
-        grad_probs = []
-        for part in range(parts):
-            tile = dot_nt(keys[part][pl.ds(base, span), :], queries)
-            if causal:
-                tile = mask_scores(tile, diagonal_mask(part == 0, piece, meta[2]))
-            probs.append(jnp.exp(tile - lse))
-            grad_probs.append(dot_nt(values[part][pl.ds(base, span), :], grads))
-        row_dot = functools.reduce(
-            jnp.add,
-            [jnp.sum(p * g, 0, keepdims=True) for p, g in zip(probs, grad_probs)],
-        )
-        grad_query = None
-        for part in range(parts):
-            grad_score = (probs[part] * (grad_probs[part] - row_dot)).astype(BF16)
-            place = pl.ds(base, span)
-            dv_sum[part][place, :] += dot_nn(probs[part].astype(BF16), grads)
-            dk_sum[part][place, :] += dot_nn(grad_score, queries)
-            term = dot_nn(flipped[part][:, place], grad_score)
-            grad_query = term if grad_query is None else grad_query + term
-        dq_ref[...] = unstack_heads(grad_query).astype(BF16)
-
-    if causal:
-        base = pl.multiple_of(start * BLOCK, BLOCK)
-        for step in range(spans):
-            pl.when(active & (local == step))(functools.partial(run, base, (step + 1) * BLOCK))
-    else:
-        pl.when(active)(functools.partial(run, pl.multiple_of(second * BLOCK, BLOCK), BLOCK))
+        place = pl.ds(base, span)
+        masks = [diagonal_mask(part == 0, piece, meta[2]) for part in range(parts)]
+        for pair in range(pairs):
+            cols = pair_columns(pair)
+            queries = stack_heads(q_ref[:, cols])
+            grads = stack_heads(g_ref[:, cols])
+            lse = lse_ref[0, pair : pair + 1, :]
+            probs = []
+            grad_probs = []
+            for part in range(parts):
+                tile = dot_nt(keys[part][place, cols], queries)
+                if causal:
+                    tile = mask_scores(tile, masks[part])
+                probs.append(jnp.exp(tile - lse))
+                grad_probs.append(dot_nt(values[part][place, cols], grads))
+            row_dot = functools.reduce(
+                jnp.add,
+                [jnp.sum(p * g, 0, keepdims=True) for p, g in zip(probs, grad_probs)],
+            )
+            grad_query = None
+            for part in range(parts):
+                grad_score = (probs[part] * (grad_probs[part] - row_dot)).astype(BF16)
+                dv_sum[part][place, cols] += dot_nn(probs[part].astype(BF16), grads)
+                dk_sum[part][place, cols] += dot_nn(grad_score, queries)
+                term = dot_nn(flipped[part][cols, place], grad_score)
+                grad_query = term if grad_query is None else grad_query + term
+            dq_ref[:, cols] = unstack_heads(grad_query).astype(BF16)
+
+    run_spans(causal, spans, local, start, second, active, run)
 
     @pl.when(jnp.logical_not(active))
     def _():
         dq_ref[...] = jnp.zeros_like(dq_ref)
 
-    @pl.when(block == pl.num_programs(1) - 1)
+    @pl.when(block == pl.num_programs(0) - 1)
     def _():
         for part in range(parts):
             dk_out[part][...] = dk_sum[part][...].astype(dk_out[part].dtype)
             dv_out[part][...] = dv_sum[part][...].astype(dv_out[part].dtype)
 
 
-def row_spec():
-    return pl.BlockSpec((BLOCK, 2 * HD), lambda pair, block, meta: (block, pair))
-
-
-def whole_spec(rows):
-    return pl.BlockSpec((rows, 2 * HD), lambda pair, block, meta: (0, pair))
+def row_spec(width):
+    return pl.BlockSpec((BLOCK, width), lambda block, meta: (block, 0))
+
+
+def whole_spec(rows, width):
+    return pl.BlockSpec((rows, width), lambda block, meta: (0, 0))
 
 
 def lse_spec():
-    return pl.BlockSpec((1, 1, 8, 2 * BLOCK), lambda pair, block, meta: (pair, block, 0, 0))
+    return pl.BlockSpec((1, 8, 2 * BLOCK), lambda block, meta: (block, 0, 0))
 
 
 def attend_forward(meta, queries, keys, values, causal, piece, spans):
     rows, width = queries.shape
     parts = len(keys)
-    pairs, blocks = width // (2 * HD), rows // BLOCK
+    pairs, blocks = width // PAIR, rows // BLOCK
     key_rows = keys[0].shape[0]
     work = pairs * blocks * parts * 4 * BLOCK * 2 * BLOCK * (2 * BLOCK if causal else BLOCK)
     return pl.pallas_call(
-        functools.partial(forward_kernel, parts, causal, piece, spans),
+        functools.partial(forward_kernel, parts, pairs, causal, piece, spans),
         grid_spec=pltpu.PrefetchScalarGridSpec(
             num_scalar_prefetch=1,
-            grid=(pairs, blocks),
-            in_specs=[row_spec()] + [whole_spec(key_rows)] * (2 * parts),
-            out_specs=[row_spec(), lse_spec()],
-            scratch_shapes=[pltpu.VMEM((2 * HD, key_rows), BF16)] * parts,
+            grid=(blocks,),
+            in_specs=[row_spec(width)] + [whole_spec(key_rows, width)] * (2 * parts),
+            out_specs=[row_spec(width), lse_spec()],
+            scratch_shapes=[pltpu.VMEM((width, key_rows), BF16)] * parts,
         ),
         out_shape=[
             jax.ShapeDtypeStruct((rows, width), BF16),
-            jax.ShapeDtypeStruct((pairs, blocks, 8, 2 * BLOCK), F32),
+            jax.ShapeDtypeStruct((blocks, 8, 2 * BLOCK), F32),
         ],
         cost_estimate=pl.CostEstimate(
             flops=4 * work, bytes_accessed=8 * rows * width, transcendentals=work // 256
@@ -220,18 +228,19 @@
 def attend_backward(meta, queries, grads, lse, keys, values, causal, piece, spans, kinds):
     rows, width = queries.shape
     parts = len(keys)
-    pairs, blocks = width // (2 * HD), rows // BLOCK
+    pairs, blocks = width // PAIR, rows // BLOCK
     key_rows = keys[0].shape[0]
     work = pairs * blocks * parts * 4 * BLOCK * 2 * BLOCK * (2 * BLOCK if causal else BLOCK)
     results = pl.pallas_call(
-        functools.partial(backward_kernel, parts, causal, piece, spans),
+        functools.partial(backward_kernel, parts, pairs, causal, piece, spans),
         grid_spec=pltpu.PrefetchScalarGridSpec(
             num_scalar_prefetch=1,
-            grid=(pairs, blocks),
-            in_specs=[row_spec(), row_spec(), lse_spec()] + [whole_spec(key_rows)] * (2 * parts),
-            out_specs=[row_spec()] + [whole_spec(key_rows)] * (2 * parts),
-            scratch_shapes=[pltpu.VMEM((2 * HD, key_rows), BF16)] * parts
-            + [pltpu.VMEM((key_rows, 2 * HD), F32)] * (2 * parts),
+            grid=(blocks,),
+            in_specs=[row_spec(width), row_spec(width), lse_spec()]
+            + [whole_spec(key_rows, width)] * (2 * parts),
+            out_specs=[row_spec(width)] + [whole_spec(key_rows, width)] * (2 * parts),
+            scratch_shapes=[pltpu.VMEM((width, key_rows), BF16)] * parts
+            + [pltpu.VMEM((key_rows, width), F32)] * (2 * parts),
         ),
         out_shape=[jax.ShapeDtypeStruct((rows, width), BF16)]
         + [jax.ShapeDtypeStruct((key_rows, width), kind) for kind in kinds + kinds],
@@ -243,6 +252,85 @@
     return results[0], results[1 : 1 + parts], results[1 + parts :]
 
 
+def grads_kernel(sides, counts, factors, extra, grouped, meta, *refs):
+    lefts = refs[: max(sides) + 1]
+    rights = refs[len(lefts) : len(lefts) + len(counts)]
+    rest = refs[len(lefts) + len(counts) :]
+    extra_ref = rest[0] if extra else None
+    out_ref = rest[1] if extra else rest[0]
+    flipped = rest[2:] if extra else rest[1:]
+    step = pl.program_id(0)
+
+    @pl.when(step == 0)
+    def _():
+        for left, flip in zip(lefts, flipped):
+            flip[...] = left[...].astype(F32).T.astype(BF16)
+
+    begin = 0
+    for index, count in enumerate(counts):
+
+        @pl.when((step >= begin) & (step < begin + count))
+        def _(index=index):
+            result = dot_nn(flipped[sides[index]][...], rights[index][...])
+            if factors[index] != 1.0:
+                result = result * factors[index]
+            if not grouped:
+                if extra:
+                    result = result + extra_ref[...].astype(F32)
+                out_ref[...] = result.astype(BF16)
+                return
+            size = out_ref.shape[2]
+            for plane in range(4):
+                for low in range(4):
+                    row = (plane * 4 + low) * size
+                    place = pl.ds(meta[0] ^ low, 1)
+                    part = result[row : row + size]
+                    if extra:
+                        part = part + extra_ref[place, plane].astype(F32)[0]
+                    out_ref[place, plane] = part.astype(BF16)[None]
+
+        begin += count
+
+
+def weight_grads(meta, lefts, rights, sides, factors, extra, grouped):
+    chunk = 384
+    counts = [right.shape[1] // chunk for right in rights]
+    width = lefts[0].shape[1]
+    total = sum(counts) * chunk
+    begins = [sum(counts[:i]) for i in range(len(counts))]
+
+    def right_spec(index):
+        return pl.BlockSpec(
+            (rights[index].shape[0], chunk),
+            lambda step, meta: (0, jnp.clip(step - begins[index], 0, counts[index] - 1)),
+        )
+
+    if grouped:
+        shape = (4, 4, width // 16, total)
+        out_spec = pl.BlockSpec((4, 4, width // 16, chunk), lambda step, meta: (0, 0, 0, step))
+    else:
+        shape = (width, total)
+        out_spec = pl.BlockSpec((width, chunk), lambda step, meta: (0, step))
+    flops = sum(2 * right.shape[0] * width * right.shape[1] for right in rights)
+    return pl.pallas_call(
+        functools.partial(grads_kernel, sides, counts, factors, extra is not None, grouped),
+        grid_spec=pltpu.PrefetchScalarGridSpec(
+            num_scalar_prefetch=1,
+            grid=(sum(counts),),
+            in_specs=[pl.BlockSpec(left.shape, lambda step, meta: (0, 0)) for left in lefts]
+            + [right_spec(index) for index in range(len(rights))]
+            + ([out_spec] if extra is not None else []),
+            out_specs=out_spec,
+            scratch_shapes=[pltpu.VMEM((width, left.shape[0]), BF16) for left in lefts],
+        ),
+        out_shape=jax.ShapeDtypeStruct(shape, BF16),
+        cost_estimate=pl.CostEstimate(
+            flops=flops, bytes_accessed=flops // 256, transcendentals=0
+        ),
+        name="weight_grads",
+    )(meta, *lefts, *rights, *([extra] if extra is not None else []))
+
+
 def norm_forward(hidden, gain, shift):
     center = hidden - jnp.mean(hidden, -1, keepdims=True)
     spread = jnp.mean(center * center, -1, keepdims=True)
@@ -262,6 +350,76 @@
 
 def swap(value):
     return lax.ppermute(value, "tensor", [(0, 1), (1, 0)])
+
+
+def hop(value, bits):
+    return lax.ppermute(value, "dp", [(i, i ^ bits) for i in range(16)])
+
+
+def assemble_kernel(meta, own_ref, first_ref, second_ref, third_ref, out_ref):
+    for low, ref in enumerate((own_ref, first_ref, second_ref, third_ref)):
+        out_ref[0, pl.ds(meta[1] ^ low, 1)] = ref[...]
+
+
+def quick_gather(value):
+    if lax.axis_size("dp") != 16:
+        return lax.all_gather(value, "dp", axis=0, tiled=True)
+    rows, count = value.shape
+    line = jnp.stack([value, hop(value, 4), hop(value, 8), hop(value, 12)])
+    index = lax.axis_index("dp")
+    meta = jnp.stack([index // 4, index % 4]).astype(jnp.int32)
+    spec = pl.BlockSpec((1, rows, count), lambda i, meta: (i ^ meta[0], 0, 0))
+    full = pl.pallas_call(
+        assemble_kernel,
+        grid_spec=pltpu.PrefetchScalarGridSpec(
+            num_scalar_prefetch=1,
+            grid=(4,),
+            in_specs=[spec] * 4,
+            out_specs=pl.BlockSpec((1, 4, rows, count), lambda i, meta: (i, 0, 0, 0)),
+        ),
+        out_shape=jax.ShapeDtypeStruct((4, 4, rows, count), value.dtype),
+        cost_estimate=pl.CostEstimate(
+            flops=0, bytes_accessed=64 * rows * count, transcendentals=0
+        ),
+        name="assemble",
+    )(meta, line, hop(line, 1), hop(line, 2), hop(line, 3))
+    return full.reshape(16 * rows, count)
+
+
+def total_of(parts):
+    return functools.reduce(jnp.add, [part.astype(F32) for part in parts])
+
+
+def scatter_low(groups):
+    received = [hop(groups[low], low) for low in (1, 2, 3)]
+    return total_of([groups[0]] + received).astype(BF16)
+
+
+def scatter_plane(line):
+    plane = lax.axis_index("dp") // 4
+
+    def pick(other):
+        return lax.dynamic_index_in_dim(line, plane ^ other, 0, keepdims=False)
+
+    received = [hop(pick(other), 4 * other) for other in (1, 2, 3)]
+    return total_of([pick(0)] + received)
+
+
+def slow_scatter(value):
+    return lax.psum_scatter(value, "dp", scatter_dimension=0, tiled=True).astype(F32)
+
+
+def sum_everywhere(value):
+    if lax.axis_size("dp") != 16:
+        return lax.psum(value, ("dp", "tensor"))
+    value = value + swap(value)
+    for unit in (1, 4):
+        value = total_of([value] + [hop(value, unit * bits) for bits in (1, 2, 3)])
+    return value
+
+
+def tie(*values):
+    return lax.optimization_barrier(values)
 
 
 def body(
@@ -321,11 +479,6 @@
         & (block_ids < all_blocks)[:, None]
     ).reshape(rows, 1)
 
-    def exchange(value):
-        ordered = jnp.take(value, deal, axis=0)
-        arrived = lax.all_to_all(ordered, "dp", split_axis=0, concat_axis=0, tiled=True)
-        return jnp.take(arrived, piece_ids, axis=0).reshape(rows, width)
-
     send_piece = jnp.arange(dp_count, dtype=jnp.int32)
     send_block = send_piece // per_block
     send_ids = jnp.stack(
@@ -346,16 +499,30 @@
         outgoing = jnp.where(
             send_valid, jnp.take(pieces, send_ids.reshape(-1), axis=0), jnp.zeros((), value.dtype)
         )
-        back = lax.all_to_all(outgoing, "dp", split_axis=0, concat_axis=0, tiled=True)
-        return jnp.take(back, inverse, axis=0)
-
-    inputs = exchange(tokens)
+        return lax.all_to_all(outgoing, "dp", split_axis=0, concat_axis=0, tiled=True)
+
+    def order(value):
+        return jnp.take(value, deal, axis=0)
+
+    def arrive(ordered):
+        return lax.all_to_all(ordered, "dp", split_axis=0, concat_axis=0, tiled=True)
+
+    def pack(arrived):
+        return jnp.take(arrived, piece_ids, axis=0).reshape(rows, width)
+
+    arrived = arrive(order(tokens))
+    ordered_cot, arrived = tie(order(cotangent), arrived)
+    inputs = pack(arrived)
+    arrived_cot = arrive(ordered_cot)
+
+    quick = dp_count == 16
 
     def gather(value):
         own = lax.all_gather(value, "dp", axis=0, tiled=True)
         return (own, swap(own))
 
-    qkv_weight = gather(self_project.reshape(shard, 3 * half))
+    qkv_own = quick_gather(self_project.reshape(shard, 3 * half))
+    qkv_weight = (qkv_own, swap(qkv_own))
     mid_weight = gather(
         jnp.concatenate(
             [self_output.T, cross_query, cross_memory.reshape(shard, 2 * half), cross_output.T], 1
@@ -383,7 +550,7 @@
     in_pair = [b[: 4 * half].reshape(4, half) for b in bias_pair]
     hidden_pair = [b[4 * half :] for b in bias_pair]
 
-    cot = jnp.where(row_valid, exchange(cotangent), jnp.zeros((), BF16)).astype(F32)
+    cot = jnp.where(row_valid, pack(arrived_cot), jnp.zeros((), BF16)).astype(F32)
 
     memory_full = jnp.concatenate([encoder, swap(encoder)], 1).reshape(4 * memory_rows, width)
 
@@ -429,25 +596,26 @@
         slope.append((phi + pre * density).astype(BF16))
     branch = dot_nt(act[0], reduce[0]) + dot_nt(act[1], reduce[1]) + out_bias[2]
     n3, unit3, scale3 = norm_forward(n2 + branch, norm_gain[2], norm_bias[2])
-    output = send_home(n3.astype(BF16))
-
-    def scatter(grads):
-        mine = grads[0] + swap(grads[1].astype(BF16)).astype(F32)
-        return lax.psum_scatter(mine.astype(BF16), "dp", scatter_dimension=0, tiled=True).astype(F32)
+    output_back = send_home(n3.astype(BF16))
+
+    low_meta = jnp.reshape(dp_index % 4, (1,)).astype(jnp.int32)
+
+    def chip_grads(lefts, rights, sides, factors, grouped):
+        far = weight_grads(low_meta, lefts, rights[1], sides, factors, None, grouped)
+        return weight_grads(low_meta, lefts, rights[0], sides, factors, swap(far), grouped)
 
     dh3, gain3, shift3 = norm_backward(cot, unit3, scale3, norm_gain[2])
     dz = dh3.astype(BF16)
-    grad_reduce = [dot_tn(dz, act[h]) for h in both]
     du = [(dot_nn(dz, reduce[h]) * slope[h].astype(F32)).astype(BF16) for h in both]
-    grad_expand = [dot_tn(hidden, du[h]) for h in both]
-    ffn_shard = scatter(
-        [jnp.concatenate([grad_expand[h], grad_reduce[h]], 1) for h in both]
+    ffn_grads = chip_grads(
+        [hidden, dz], [[du[h], act[h]] for h in both], (0, 1), (1.0, 1.0), False
     )
     dn2 = dh3 + dot_nt(du[0], expand[0]) + dot_nt(du[1], expand[1])
     dh2, gain2, shift2 = norm_backward(dn2, unit2, scale2, norm_gain[1])
     dy2 = dh2.astype(BF16)
-    grad_cross_out = [dot_tn(dy2, cattn[h]) for h in both]
     dca = [dot_nn(dy2, cross_out[h]).astype(BF16) for h in both]
+    ffn_grads, dca[0] = tie(ffn_grads, dca[0])
+    ffn_shard = slow_scatter(ffn_grads)
     dcq = []
     dck = []
     dcv = []
@@ -471,9 +639,6 @@
         for h in both
     ]
     memory_own = encoder.reshape(2 * memory_rows, width)
-    grad_query_w = [dot_tn(cross_in, dcq[h]) * score_scale for h in both]
-    grad_memory_k = [dot_tn(memory_own, dck_sum[h]) for h in both]
-    grad_memory_v = [dot_tn(memory_own, dcv_sum[h]) for h in both]
     grad_memory = (
         dot_nt(dck_sum[0], memory_k[0])
         + dot_nt(dck_sum[1], memory_k[1])
@@ -484,23 +649,17 @@
     dn1 = dh2 + (dot_nt(dcq[0], query_w[0]) + dot_nt(dcq[1], query_w[1])) * score_scale
     dh1, gain1, shift1 = norm_backward(dn1, unit1, scale1, norm_gain[0])
     dy = dh1.astype(BF16)
-    grad_self_out = [dot_tn(dy, attn[h]) for h in both]
     da = [dot_nn(dy, self_out[h]).astype(BF16) for h in both]
-    mid_shard = scatter(
-        [
-            jnp.concatenate(
-                [
-                    grad_self_out[h],
-                    grad_query_w[h],
-                    grad_memory_k[h],
-                    grad_memory_v[h],
-                    grad_cross_out[h],
-                ],
-                1,
-            )
-            for h in both
-        ]
-    )
+    mid_grads = chip_grads(
+        [dy, cross_in, memory_own, dy2],
+        [[attn[h], dcq[h], dck_sum[h], dcv_sum[h], cattn[h]] for h in both],
+        (0, 1, 2, 2, 3),
+        (1.0, score_scale, 1.0, 1.0, 1.0),
+        quick,
+    )
+    mid_grads, da[0], output_back = tie(mid_grads, da[0], output_back)
+    output = jnp.take(output_back, inverse, axis=0)
+    mid_line = scatter_low(mid_grads) if quick else None
     dq = []
     dk = []
     dv = []
@@ -517,24 +676,24 @@
             spans,
             [F32, BF16],
         )
+        if h == 0 and quick:
+            mid_line, dq_first = tie(mid_line, result[0])
+            result = (dq_first, result[1], result[2])
+            da[1], mid_line = tie(da[1], mid_line)
         dq.append(result[0])
         dk.append(result[1])
         dv.append(result[2])
+    mid_shard = scatter_plane(mid_line) if quick else slow_scatter(mid_grads)
     dk = [(dk[h][0] + swap(dk[1 - h][1]).astype(F32)).astype(BF16) for h in both]
     dv = [(dv[h][0] + swap(dv[1 - h][1]).astype(F32)).astype(BF16) for h in both]
-    qkv_shard = scatter(
-        [
-            jnp.concatenate(
-                [
-                    dot_tn(inputs, dq[h]) * score_scale,
-                    dot_tn(inputs, dk[h]),
-                    dot_tn(inputs, dv[h]),
-                ],
-                1,
-            )
-            for h in both
-        ]
-    )
+    qkv_grads = chip_grads(
+        [inputs],
+        [[dq[h], dk[h], dv[h]] for h in both],
+        (0, 0, 0),
+        (score_scale, 1.0, 1.0),
+        quick,
+    )
+    qkv_shard = scatter_plane(scatter_low(qkv_grads)) if quick else slow_scatter(qkv_grads)
     grad_inputs = (
         dh1
         + (dot_nt(dq[0], project_q[0]) + dot_nt(dq[1], project_q[1])) * score_scale
@@ -543,7 +702,7 @@
         + dot_nt(dv[0], project_v[0])
         + dot_nt(dv[1], project_v[1])
     )
-    grad_tokens = send_home(grad_inputs.astype(BF16))
+    grad_tokens = jnp.take(send_home(grad_inputs.astype(BF16)), inverse, axis=0)
 
     def rows_sum(value):
         return jnp.sum(value, 0, dtype=F32)
@@ -570,7 +729,7 @@
     out_rows = jnp.stack([rows_sum(dy), rows_sum(dy2), rows_sum(dz)])
     gain_rows = jnp.stack([gain1, gain2, gain3])
     shift_rows = jnp.stack([shift1, shift2, shift3])
-    small = lax.psum(
+    small = sum_everywhere(
         jnp.concatenate(
             [
                 in_rows.reshape(-1),
@@ -579,8 +738,7 @@
                 gain_rows.reshape(-1),
                 shift_rows.reshape(-1),
             ]
-        ),
-        ("dp", "tensor"),
+        )
     )
     in_end = 8 * half
     hidden_end = in_end + 2 * units

time: 919 us -> 610 us (0.66); the launches traced: 901 us -> 602 us
  waiting for transfers between devices: 361 us -> 118 us
  blocking collectives: 45.2 us -> 0 us
  starting transfers between devices: 36.3 us -> 68.1 us
  matrix products: 147 us -> 117 us
  local copies, waits for them, and re-layouts: 71.2 us -> 61.7 us
    reduce_scatter x1, waiting for transfers between devices: 137 us -> 0.01 us  [slow_scatter(): lax.psum_scatter(value, 'dp', scatter_dimension=0, tiled=True).astype(F32)]
    ppermute x0 -> x24, waiting for transfers between devices: none -> 89.6 us  [hop(): return lax.ppermute(value, 'dp', [(i, i ^ bits) for i in range(16)])]
    unnamed x8 -> x3, waiting for transfers between devices: 77.1 us -> 0.05 us
    all_gather x3 -> x2, waiting for transfers between devices: 74.9 us -> 23.1 us  [gather(): own = lax.all_gather(value, 'dp', axis=0, tiled=True)]
    psum x1 -> x0, blocking collectives: 45.2 us -> none  [body(): lax.psum(jnp.concatenate([in_rows.reshape(-1), hidden_row, out_rows.resha...]
    dot_general x20 -> x0, matrix products: 40 us -> none  [dot_tn(): lax.dot_general(left, right, (((0,), (0,)), ((), ())), preferred_element_...]
    all_to_all x2, waiting for transfers between devices: 40.6 us -> 4.98 us  [arrive(): lax.all_to_all(ordered, 'dp', split_axis=0, concat_axis=0, tiled=True)]
    ppermute x0 -> x24, starting transfers between devices: none -> 34.7 us  [hop(): return lax.ppermute(value, 'dp', [(i, i ^ bits) for i in range(16)])]
  transfers between devices with their start and end apart: 30 -> 52, of which waited for: 8 -> 11; matrix products, arithmetic and copies ran while one was open for 24% -> 35% of each run, Pallas kernels for 11% -> 24%
where the time goes in v2:
time: 610 us; the launch traced here: 602 us
  Pallas kernels  154 us (25%)
  waiting for transfers between devices  118 us (19%)
  matrix products  117 us (19%)
  starting transfers between devices  68.1 us (11%)
  other arithmetic  64.5 us (11%)
  local copies, waits for them, and re-layouts  61.7 us (10%)
  between operations  18.1 us (3%)
    ppermute x24, waiting for transfers between devices, hop(): return lax.ppermute(value, 'dp', [(i, i ^ bits) for i in range(16)])  89.6 us
    dot_general x20, matrix products, dot_nn(): lax.dot_general(left, right, (((1,), (0,)), ((), ())), preferred_element_...  64.3 us
    pallas_call x6, Pallas kernels, weight_grads(): pl.pallas_call(functools.partial(grads_kernel, sides, counts, factors, ex...  58.9 us
    dot_general x20, matrix products, dot_nt(): lax.dot_general(left, right, (((1,), (1,)), ((), ())), preferred_element_...  52.8 us
    pallas_call x4, Pallas kernels, attend_backward(): pl.pallas_call(functools.partial(backward_kernel, parts, pairs, causal, p...  51.5 us
    pallas_call x4, Pallas kernels, attend_forward(): pl.pallas_call(functools.partial(forward_kernel, parts, pairs, causal, pi...  39.5 us
    ppermute x24, starting transfers between devices, hop(): return lax.ppermute(value, 'dp', [(i, i ^ bits) for i in range(16)])  34.7 us
    all_gather x2, waiting for transfers between devices, gather(): own = lax.all_gather(value, 'dp', axis=0, tiled=True)  23.1 us
  transfers between devices with their start and end apart: 52, of which 11 were waited for; matrix products, arithmetic and copies ran while one was open for 35% of the time, Pallas kernels for 24%

profile of v2, /device:TPU:0, one launch (start us, length us, event | category | flops | bytes accessed | tf_op | source)
XLA Modules:
  0.0 601.6 jit_solution(15535223798939019100)
XLA Ops:
  10.7 5.1 collective-permute-start.2
  27.9 7.1 %all-to-all-start = ((bf16[32,32,768]{2,1,0:T(8,128)(2,1)}), bf16[32,32,768]{2,1,0:T(8,128)(2,1)S(1)}, u32[]{:S(2)}, u32[]{:S(2)}) async-start(bf16[32,32,768]{2,1,0:T(8,128)(2,1)} %get-tuple-element.207), calls=%async_computation | async-start | bytes 3145728 | tf_op jit(solution)/shard_map/all_to_all | solution.py:508
  57.8 18.9 %collective-permute-done.3.first_ref = bf16[4,48,1152]{2,1,0:T(8,128)(2,1)S(1)} collective-permute-done((bf16[4,48,1152]{2,1,0:T(8,128)(2,1)S(1)}, bf16[4,48,1152]{2,1,0:T(8,128)(2,1)S(1)}, u32[]{:S(2)}, u32[]{:S(2)}) %collective-permute-start.3) | collective-permute-done | bytes 442400 | tf_op jit(solution)/shard_map/ppermute | solution.py:356
  76.6 20.1 %collective-permute-done.5.third_ref = bf16[4,48,1152]{2,1,0:T(8,128)(2,1)S(1)} collective-permute-done((bf16[4,48,1152]{2,1,0:T(8,128)(2,1)S(1)}, bf16[4,48,1152]{2,1,0:T(8,128)(2,1)S(1)}, u32[]{:S(2)}, u32[]{:S(2)}) %collective-permute-start.5) | collective-permute-done | bytes 442400 | tf_op jit(solution)/shard_map/ppermute | solution.py:356
  97.5 4.4 assemble.1
  110.6 3.4 gather_fusion.3
  117.8 6.6 %all-to-all-start.1 = ((bf16[32,32,768]{2,1,0:T(8,128)(2,1)}), bf16[32,32,768]{2,1,0:T(8,128)(2,1)}, u32[]{:S(2)}, u32[]{:S(2)}) async-start(bf16[32,32,768]{2,1,0:T(8,128)(2,1)} %get-tuple-element.58), calls=%async_computation.1 | async-start | bytes 3145728 | tf_op jit(solution)/shard_map/all_to_all | solution.py:508
  126.9 2.8 convolution_convert_fusion.4.refs_0_
  130.3 2.8 fusion.43.refs_2_
  135.3 2.9 fusion.46.q_ref
  138.1 11.7 %attend_forward.5 = (bf16[896,384]{1,0:T(8,128)(2,1)}, f32[7,8,256]{2,1,0:T(8,128)}) custom-call(s32[3]{0:T(128)} %pad_add_fusion.meta, bf16[896,384]{1,0:T(8,128)(2,1)} %fusion.46.q_ref, bf16[896,384]{1,0:T(8,128)(2,1)} %convolution_convert_fusion.4.refs_0_, bf16[896,384]{1,0:T(8,128)(2,1)} %collective-permute-done.10.refs_1_, ...), custom_call_target="tpu_custom_call" | custom-call | flops 5637144576 | bytes 2752512 | tf_op jit(solution)/shard_map/attend_forward/pallas_call | solution.py:208
  149.9 12.0 %attend_forward.4 = (bf16[896,384]{1,0:T(8,128)(2,1)}, f32[7,8,256]{2,1,0:T(8,128)}) custom-call(s32[3]{0:T(128)} %pad_add_fusion.meta, bf16[896,384]{1,0:T(8,128)(2,1)} %fusion.47.q_ref, bf16[896,384]{1,0:T(8,128)(2,1)} %convolution_convert_fusion.5.refs_0_, bf16[896,384]{1,0:T(8,128)(2,1)} %collective-permute-done.7.refs_1_, ...), custom_call_target="tpu_custom_call" | custom-call | flops 5637144576 | bytes 2752512 | tf_op jit(solution)/shard_map/attend_forward/pallas_call | solution.py:208
  166.1 5.0 all-to-all-done.1
  177.3 2.7 fusion.150
  180.5 23.1 %all-gather.5.cloned.1.call-done = bf16[768,3072]{1,0:T(8,128)(2,1)} async-done(((bf16[48,3072]{1,0:T(8,128)(2,1)}), bf16[768,3072]{1,0:T(8,128)(2,1)}) %all-gather.5.cloned.1.call-update) | async-done | bytes 4718608 | tf_op jit(solution)/shard_map/all_gather | solution.py:521
  205.2 2.8 fusion.45.q_ref
  208.0 7.7 %attend_forward.6 = (bf16[896,384]{1,0:T(8,128)(2,1)}, f32[7,8,256]{2,1,0:T(8,128)}) custom-call(s32[3]{0:T(128)} %pad_add_fusion.meta, bf16[896,384]{1,0:T(8,128)(2,1)} %fusion.45.q_ref, bf16[256,384]{1,0:T(8,128)(2,1)} %convolution_convert_fusion.7.refs_0_, bf16[256,384]{1,0:T(8,128)(2,1)} %fusion.50.refs_1_), custom_call_target="tpu_custom_call" | custom-call | flops 1409286144 | bytes 2752512 | tf_op jit(solution)/shard_map/attend_forward/pallas_call | solution.py:208
  220.0 2.8 fusion.44.q_ref
  222.8 8.1 %attend_forward.7 = (bf16[896,384]{1,0:T(8,128)(2,1)}, f32[7,8,256]{2,1,0:T(8,128)}) custom-call(s32[3]{0:T(128)} %pad_add_fusion.meta, bf16[896,384]{1,0:T(8,128)(2,1)} %fusion.44.q_ref, bf16[256,384]{1,0:T(8,128)(2,1)} %convolution_convert_fusion.6.refs_0_, bf16[256,384]{1,0:T(8,128)(2,1)} %fusion.51.refs_1_), custom_call_target="tpu_custom_call" | custom-call | flops 1409286144 | bytes 2752512 | tf_op jit(solution)/shard_map/attend_forward/pallas_call | solution.py:208
  233.1 2.6 fusion.151
  236.9 4.7 multiply_convert_fusion.3
  244.0 5.1 multiply_convert_fusion.2
  249.1 5.4 fusion.152
  260.6 7.2 %convert_reduce_fusion = (f32[1536]{0:T(1024)}, bf16[896,1536]{1,0:T(8,128)(2,1)}) fusion(f32[896,1536]{1,0:T(8,128)S(1)} %get-tuple-element.218, f32[1536]{0:T(1024)S(1)} %copy-done.65, bf16[896,768]{1,0:T(8,128)(2,1)S(1)} %get-tuple-element.165.refs_1_, bf16[768,3072]{1,0:T(8,128)(2,1)} %collective-permute-done.14), kind=kOutput, calls=%fused_computation.22 | convolution fusion | flops 2134571520 | bytes 12005376 | tf_op jit(solution)/shard_map/dot_general | solution.py:21
  267.8 12.6 %weight_grads.6 = bf16[768,3072]{1,0:T(8,128)(2,1)} custom-call(s32[1]{0:T(128)} %bitcast.meta, bf16[896,768]{1,0:T(8,128)(2,1)} %copy-done.22, bf16[896,768]{1,0:T(8,128)(2,1)} %copy-done.21, bf16[896,1536]{1,0:T(8,128)(2,1)} %get-tuple-element.224.refs_2_, bf16[896,1536]{1,0:T(8,128)(2,1)} %copy-done.84), custom_call_target="tpu_custom_call" | custom-call | flops 4227858432 | bytes 16515072 | tf_op jit(solution)/shard_map/weight_grads/pallas_call | solution.py:315
  281.0 6.8 %convert_reduce_fusion.1 = (f32[1536]{0:T(1024)}, bf16[896,1536]{1,0:T(8,128)(2,1)S(1)}) fusion(f32[896,1536]{1,0:T(8,128)} %get-tuple-element.216, f32[1536]{0:T(1024)S(1)} %copy-done.62, bf16[896,768]{1,0:T(8,128)(2,1)} %copy-done.21, bf16[768,3072]{1,0:T(8,128)(2,1)} %all-gather.5.cloned.1.call-done), kind=kOutput, calls=%fused_computation.23 | convolution fusion | flops 2134571520 | bytes 12005376 | tf_op jit(solution)/shard_map/dot_general | solution.py:21
  287.8 5.0 fusion.29
  292.9 4.8 multiply_reduce_fusion
  297.8 2.5 convert_reduce_fusion.4
  300.3 3.2 convolution_convert_fusion.2.g_ref
  303.5 8.7 %attend_backward.5 = (bf16[896,384]{1,0:T(8,128)(2,1)}, f32[256,384]{1,0:T(8,128)}, f32[256,384]{1,0:T(8,128)}) custom-call(s32[3]{0:T(128)} %pad_add_fusion.meta, bf16[896,384]{1,0:T(8,128)(2,1)} %fusion.44.q_ref, bf16[896,384]{1,0:T(8,128)(2,1)} %convolution_convert_fusion.2.g_ref, f32[7,8,256]{2,1,0:T(8,128)} %get-tuple-element.62.lse_ref, ...), custom_call_target="tpu_custom_call" | custom-call | flops 3523215360 | bytes 5505024 | tf_op jit(solution)/shard_map/attend_backward/pallas_call | solution.py:234
  315.9 3.2 gather_fusion.5
  319.1 2.9 select_select_fusion.1
  322.0 6.6 %all-to-all-start.2 = ((bf16[32,32,768]{2,1,0:T(8,128)(2,1)}), bf16[32,32,768]{2,1,0:T(8,128)(2,1)}, u32[]{:S(2)}, u32[]{:S(2)}) async-start(bf16[32,32,768]{2,1,0:T(8,128)(2,1)} %select_select_fusion.1), calls=%async_computation.2 | async-start | bytes 3145728 | tf_op jit(solution)/shard_map/all_to_all | solution.py:502
  328.8 3.2 convolution_convert_fusion.3.g_ref
  332.0 13.9 %weight_grads.7 = bf16[768,3072]{1,0:T(8,128)(2,1)} custom-call(s32[1]{0:T(128)} %bitcast.meta, bf16[896,768]{1,0:T(8,128)(2,1)} %copy-done.22, bf16[896,768]{1,0:T(8,128)(2,1)} %copy-done.21, bf16[896,1536]{1,0:T(8,128)(2,1)} %copy-done.25, bf16[896,1536]{1,0:T(8,128)(2,1)} %copy-done.24, bf16[768,3072]{1,0:T(8,128)(2,1)} %collective-permute-done.15.refs_4_), custom_call_target="tpu_custom_call" | custom-call | flops 4227858432 | bytes 16515072 | tf_op jit(solution)/shard_map/weight_grads/pallas_call | solution.py:315
  345.8 8.7 %attend_backward.4 = (bf16[896,384]{1,0:T(8,128)(2,1)}, f32[256,384]{1,0:T(8,128)}, f32[256,384]{1,0:T(8,128)}) custom-call(s32[3]{0:T(128)} %pad_add_fusion.meta, bf16[896,384]{1,0:T(8,128)(2,1)} %fusion.45.q_ref, bf16[896,384]{1,0:T(8,128)(2,1)} %convolution_convert_fusion.3.g_ref, f32[7,8,256]{2,1,0:T(8,128)} %get-tuple-element.60.lse_ref, ...), custom_call_target="tpu_custom_call" | custom-call | flops 3523215360 | bytes 5505024 | tf_op jit(solution)/shard_map/attend_backward/pallas_call | solution.py:234
  356.9 2.9 multiply_reduce_fusion.1
  366.1 9.1 %weight_grads.8 = bf16[4,4,48,1920]{3,2,1,0:T(8,128)(2,1)} custom-call(s32[1]{0:T(128)} %bitcast.meta, bf16[896,768]{1,0:T(8,128)(2,1)} %get-tuple-element.159.refs_0_, bf16[896,768]{1,0:T(8,128)(2,1)} %copy-done.4, bf16[128,768]{1,0:T(8,128)(2,1)} %bitcast.219, bf16[896,768]{1,0:T(8,128)(2,1)} %get-tuple-element.162.refs_3_, ...), custom_call_target="tpu_custom_call" | custom-call | flops 1736441856 | bytes 6782976 | tf_op jit(solution)/shard_map/weight_grads/pallas_call | solution.py:315
  379.6 2.8 convolution_convert_fusion.1.g_ref
  382.5 2.8 convolution_convert_fusion.g_ref
  392.1 10.3 %weight_grads.9 = bf16[4,4,48,1920]{3,2,1,0:T(8,128)(2,1)} custom-call(s32[1]{0:T(128)} %bitcast.meta, bf16[896,768]{1,0:T(8,128)(2,1)} %get-tuple-element.159.refs_0_, bf16[896,768]{1,0:T(8,128)(2,1)} %copy-done.4, bf16[128,768]{1,0:T(8,128)(2,1)} %bitcast.220, bf16[896,768]{1,0:T(8,128)(2,1)} %get-tuple-element.162.refs_3_, ...), custom_call_target="tpu_custom_call" | custom-call | flops 1736441856 | bytes 6782976 | tf_op jit(solution)/shard_map/weight_grads/pallas_call | solution.py:315
  402.3 2.8 slice_bitcast_fusion.2
  405.2 2.8 collective-permute-start.23
  408.7 16.9 %attend_backward.6 = (bf16[896,384]{1,0:T(8,128)(2,1)}, f32[896,384]{1,0:T(8,128)}, bf16[896,384]{1,0:T(8,128)(2,1)}, f32[896,384]{1,0:T(8,128)}, bf16[896,384]{1,0:T(8,128)(2,1)}) custom-call(s32[3]{0:T(128)} %pad_add_fusion.meta, bf16[896,384]{1,0:T(8,128)(2,1)} %fusion.47.q_ref, bf16[896,384]{1,0:T(8,128)(2,1)} %convolution_convert_fusion.1.g_ref, ...), custom_call_target="tpu_custom_call" | custom-call | flops 14092861440 | bytes 5505024 | tf_op jit(solution)/shard_map/attend_backward/pallas_call | solution.py:234
  426.2 3.3 gather_fusion.6
  429.5 16.2 %collective-permute-done.22 = bf16[4,48,1920]{2,1,0:T(8,128)(2,1)S(1)} collective-permute-done((bf16[4,48,1920]{2,1,0:T(8,128)(2,1)}, bf16[4,48,1920]{2,1,0:T(8,128)(2,1)S(1)}, u32[]{:S(2)}, u32[]{:S(2)}) %collective-permute-start.22) | collective-permute-done | bytes 737312 | tf_op jit(solution)/shard_map/ppermute | solution.py:356
  447.4 17.2 %attend_backward.7 = (bf16[896,384]{1,0:T(8,128)(2,1)}, f32[896,384]{1,0:T(8,128)}, bf16[896,384]{1,0:T(8,128)(2,1)}, f32[896,384]{1,0:T(8,128)}, bf16[896,384]{1,0:T(8,128)(2,1)}) custom-call(s32[3]{0:T(128)} %pad_add_fusion.meta, bf16[896,384]{1,0:T(8,128)(2,1)} %fusion.46.q_ref, bf16[896,384]{1,0:T(8,128)(2,1)} %convolution_convert_fusion.g_ref, ...), custom_call_target="tpu_custom_call" | custom-call | flops 14092861440 | bytes 5505024 | tf_op jit(solution)/shard_map/attend_backward/pallas_call | solution.py:234
  465.9 3.7 collective-permute-start.37
  477.8 3.5 fusion.78
  481.3 3.6 fusion.91
  486.6 6.4 %weight_grads.10 = bf16[4,4,48,1152]{3,2,1,0:T(8,128)(2,1)} custom-call(s32[1]{0:T(128)} %bitcast.meta, bf16[896,768]{1,0:T(8,128)(2,1)} %bitcast.208, bf16[896,384]{1,0:T(8,128)(2,1)} %get-tuple-element.77.refs_1_, bf16[896,384]{1,0:T(8,128)(2,1)} %copy-done.28, bf16[896,384]{1,0:T(8,128)(2,1)} %get-tuple-element.172.refs_3_), custom_call_target="tpu_custom_call" | custom-call | flops 1585446912 | bytes 6193152 | tf_op jit(solution)/shard_map/weight_grads/pallas_call | solution.py:315
  504.7 3.4 collective-permute-start.41
  508.7 3.6 add_convert_fusion
  514.4 3.9 collective-permute-start.44
  520.4 7.4 %all-to-all-start.3 = ((bf16[32,32,768]{2,1,0:T(8,128)(2,1)}), bf16[32,32,768]{2,1,0:T(8,128)(2,1)S(1)}, u32[]{:S(2)}, u32[]{:S(2)}) async-start(bf16[32,32,768]{2,1,0:T(8,128)(2,1)} %select_select_fusion), calls=%async_computation.3 | async-start | bytes 3145728 | tf_op jit(solution)/shard_map/all_to_all | solution.py:502
  527.9 6.7 %weight_grads.11 = bf16[4,4,48,1152]{3,2,1,0:T(8,128)(2,1)} custom-call(s32[1]{0:T(128)} %bitcast.meta, bf16[896,768]{1,0:T(8,128)(2,1)} %bitcast.209, bf16[896,384]{1,0:T(8,128)(2,1)} %get-tuple-element.73.refs_1_, bf16[896,384]{1,0:T(8,128)(2,1)} %copy-done.19, bf16[896,384]{1,0:T(8,128)(2,1)} %copy-done.17, ...), custom_call_target="tpu_custom_call" | custom-call | flops 1585446912 | bytes 6193152 | tf_op jit(solution)/shard_map/weight_grads/pallas_call | solution.py:315
  537.0 2.8 collective-permute-start.31
  543.0 21.3 %collective-permute-done.31 = bf16[4,48,1152]{2,1,0:T(8,128)(2,1)S(1)} collective-permute-done((bf16[4,48,1152]{2,1,0:T(8,128)(2,1)}, bf16[4,48,1152]{2,1,0:T(8,128)(2,1)S(1)}, u32[]{:S(2)}, u32[]{:S(2)}) %collective-permute-start.31) | collective-permute-done | bytes 442400 | tf_op jit(solution)/shard_map/ppermute | solution.py:356
  564.2 2.6 collective-permute-done.30
  566.9 4.3 collective-permute-done.29
  572.6 3.0 collective-permute-start.34
  580.3 4.2 collective-permute-done.33
  587.3 3.9 broadcast_select_fusion
  (449 shorter events, 155.0 us)
Async XLA Ops:
  7.2 15.3 %copy-start = (bf16[32,32,768]{2,1,0:T(8,128)(2,1)S(1)}, bf16[32,32,768]{2,1,0:T(8,128)(2,1)}, u32[]{:S(2)}) copy-start(bf16[32,32,768]{2,1,0:T(8,128)(2,1)} %param.23) | copy-start | bytes 4718596
  7.2 123.0 %all-gather.3.cloned.1.call-start = ((), (), s32[]{:S(2)}) async-start(), calls=%async_computation.5 | async-start | bytes 3133440 | tf_op jit(solution)/shard_map/all_gather | solution.py:521
  10.7 40.6 %collective-permute-start.2 = (bf16[48,1152]{1,0:T(8,128)(2,1)S(1)}, bf16[48,1152]{1,0:T(8,128)(2,1)S(1)}, u32[]{:S(2)}, u32[]{:S(2)}) collective-permute-start(bf16[48,1152]{1,0:T(8,128)(2,1)S(1)} %bitcast.248), channel_id=1, source_target_pairs={{0,24},{2,26},{4,28},{6,30},{8,16},{10,18},{12,20},{14,22},{16,8},... | collective-permute-start | bytes 331784 | tf_op jit(solution)/shard_map/ppermute | solution.py:356
  15.8 35.5 %collective-permute-start.1 = (bf16[48,1152]{1,0:T(8,128)(2,1)S(1)}, bf16[48,1152]{1,0:T(8,128)(2,1)S(1)}, u32[]{:S(2)}, u32[]{:S(2)}) collective-permute-start(bf16[48,1152]{1,0:T(8,128)(2,1)S(1)} %bitcast.249), channel_id=1, source_target_pairs={{0,16},{2,18},{4,20},{6,22},{8,24},{10,26},{12,28},{14,30},{16,0},... | collective-permute-start | bytes 331784 | tf_op jit(solution)/shard_map/ppermute | solution.py:356
  15.8 35.5 %collective-permute-start = (bf16[48,1152]{1,0:T(8,128)(2,1)S(1)}, bf16[48,1152]{1,0:T(8,128)(2,1)}, u32[]{:S(2)}, u32[]{:S(2)}) collective-permute-start(bf16[48,1152]{1,0:T(8,128)(2,1)S(1)} %bitcast.250), channel_id=1, source_target_pairs={{0,8},{2,10},{4,12},{6,14},{8,0},{10,2},{12,4},{14,6},{16,24},{18,... | collective-permute-start | bytes 331784 | tf_op jit(solution)/shard_map/ppermute | solution.py:356
  27.9 20.8 %copy-start.66 = (f32[3,768]{1,0:T(4,128)S(1)}, f32[3,768]{1,0:T(4,128)}, u32[]{:S(2)}) copy-start(f32[3,768]{1,0:T(4,128)} %param.35) | copy-start | bytes 27652
  27.9 21.5 %copy-start.67 = (f32[3,768]{1,0:T(4,128)S(1)}, f32[3,768]{1,0:T(4,128)}, u32[]{:S(2)}) copy-start(f32[3,768]{1,0:T(4,128)} %param.38) | copy-start | bytes 27652
  27.9 21.4 %copy-start.68 = (f32[3,768]{1,0:T(4,128)S(1)}, f32[3,768]{1,0:T(4,128)}, u32[]{:S(2)}) copy-start(f32[3,768]{1,0:T(4,128)} %param.37) | copy-start | bytes 27652
  27.9 81.5 %all-to-all-start = ((bf16[32,32,768]{2,1,0:T(8,128)(2,1)}), bf16[32,32,768]{2,1,0:T(8,128)(2,1)S(1)}, u32[]{:S(2)}, u32[]{:S(2)}) async-start(bf16[32,32,768]{2,1,0:T(8,128)(2,1)} %get-tuple-element.207), calls=%async_computation | async-start | bytes 3145728 | tf_op jit(solution)/shard_map/all_to_all | solution.py:508
  35.1 168.5 %all-gather.5.cloned.1.call-start = ((), (), s32[]{:S(2)}) async-start(), calls=%async_computation.6 | async-start | bytes 5013504 | tf_op jit(solution)/shard_map/all_gather | solution.py:521
  35.7 70.0 %collective-permute-start.8 = (f32[3072]{0:T(1024)}, f32[3072]{0:T(1024)}, u32[]{:S(2)}, u32[]{:S(2)}) collective-permute-start(f32[3072]{0:T(1024)} %pad_maximum_fusion.4), channel_id=1, source_target_pairs={{0,1},{1,0},{2,3},{3,2},{4,5},{5,4},{6,7},{7,6},{8,9},{9,8},{10,11... | collective-permute-start | bytes 36872 | tf_op jit(solution)/shard_map/ppermute | solution.py:352
  35.7 72.7 %collective-permute-start.13 = (bf16[2,64,768]{2,1,0:T(8,128)(2,1)S(1)}, bf16[2,64,768]{2,1,0:T(8,128)(2,1)}, u32[]{:S(2)}, u32[]{:S(2)}) collective-permute-start(bf16[2,64,768]{2,1,0:T(8,128)(2,1)S(1)} %copy-done.34), channel_id=1, source_target_pairs={{0,1},{1,0},{2,3},{3,2},{4,5},{5,4},{6,7},{7,6},{8,9},{9,8},{10,11... | collective-permute-start | bytes 589832 | tf_op jit(solution)/shard_map/ppermute | solution.py:352
  52.3 44.5 %copy-start.33 = (bf16[4,48,1152]{2,1,0:T(8,128)(2,1)}, bf16[4,48,1152]{2,1,0:T(8,128)(2,1)S(1)}, u32[]{:S(2)}) copy-start(bf16[4,48,1152]{2,1,0:T(8,128)(2,1)S(1)} %pad_maximum_fusion.own_ref) | copy-start | bytes 1327108
  52.3 24.3 %collective-permute-start.3 = (bf16[4,48,1152]{2,1,0:T(8,128)(2,1)S(1)}, bf16[4,48,1152]{2,1,0:T(8,128)(2,1)S(1)}, u32[]{:S(2)}, u32[]{:S(2)}) collective-permute-start(bf16[4,48,1152]{2,1,0:T(8,128)(2,1)S(1)} %pad_maximum_fusion.own_ref), channel_id=1, source_target_pairs={{0,2},{2,0},{4,6},{6,4},{8,10},{10,8},{12,14},{14,12},{16,18},{18,... | collective-permute-start | bytes 1327112 | tf_op jit(solution)/shard_map/ppermute | solution.py:356
  54.3 22.3 %collective-permute-start.4 = (bf16[4,48,1152]{2,1,0:T(8,128)(2,1)S(1)}, bf16[4,48,1152]{2,1,0:T(8,128)(2,1)S(1)}, u32[]{:S(2)}, u32[]{:S(2)}) collective-permute-start(bf16[4,48,1152]{2,1,0:T(8,128)(2,1)S(1)} %pad_maximum_fusion.own_ref), channel_id=1, source_target_pairs={{0,4},{2,6},{4,0},{6,2},{8,12},{10,14},{12,8},{14,10},{16,20},{18,... | collective-permute-start | bytes 1327112 | tf_op jit(solution)/shard_map/ppermute | solution.py:356
  55.8 41.0 %collective-permute-start.5 = (bf16[4,48,1152]{2,1,0:T(8,128)(2,1)S(1)}, bf16[4,48,1152]{2,1,0:T(8,128)(2,1)S(1)}, u32[]{:S(2)}, u32[]{:S(2)}) collective-permute-start(bf16[4,48,1152]{2,1,0:T(8,128)(2,1)S(1)} %pad_maximum_fusion.own_ref), channel_id=1, source_target_pairs={{0,6},{2,4},{4,2},{6,0},{8,14},{10,12},{12,10},{14,8},{16,22},{18,... | collective-permute-start | bytes 1327112 | tf_op jit(solution)/shard_map/ppermute | solution.py:356
  76.6 20.2 %copy-start.42 = (bf16[4,48,1152]{2,1,0:T(8,128)(2,1)}, bf16[4,48,1152]{2,1,0:T(8,128)(2,1)S(1)}, u32[]{:S(2)}) copy-start(bf16[4,48,1152]{2,1,0:T(8,128)(2,1)S(1)} %collective-permute-done.3.first_ref) | copy-start | bytes 1327108
  76.6 20.2 %copy-start.43 = (bf16[4,48,1152]{2,1,0:T(8,128)(2,1)}, bf16[4,48,1152]{2,1,0:T(8,128)(2,1)S(1)}, u32[]{:S(2)}) copy-start(bf16[4,48,1152]{2,1,0:T(8,128)(2,1)S(1)} %collective-permute-done.4.second_ref) | copy-start | bytes 1327108
  102.0 25.0 %collective-permute-start.6 = (bf16[768,1152]{1,0:T(8,128)(2,1)}, bf16[768,1152]{1,0:T(8,128)(2,1)}, u32[]{:S(2)}, u32[]{:S(2)}) collective-permute-start(bf16[768,1152]{1,0:T(8,128)(2,1)} %bitcast.210), channel_id=1, source_target_pairs={{0,1},{1,0},{2,3},{3,2},{4,5},{5,4},{6,7},{7,6},{8,9},{9,8},{10,11... | collective-permute-start | bytes 5308424 | tf_op jit(solution)/shard_map/ppermute | solution.py:352
  109.4 54.6 %copy-start.45 = (bf16[2,128,768]{2,1,0:T(8,128)(2,1)}, bf16[2,128,768]{2,1,0:T(8,128)(2,1)S(1)}, u32[]{:S(2)}) copy-start(bf16[2,128,768]{2,1,0:T(8,128)(2,1)S(1)} %pad_maximum_fusion.1) | copy-start | bytes 1179652
  115.6 19.7 %copy-start.8 = (bf16[28,32,768]{2,1,0:T(8,128)(2,1)}, bf16[28,32,768]{2,1,0:T(8,128)(2,1)S(1)}, u32[]{:S(2)}) copy-start(bf16[28,32,768]{2,1,0:T(8,128)(2,1)S(1)} %broadcast_select_fusion.5) | copy-start | bytes 4128772
  117.3 20.8 %collective-permute-start.10 = (bf16[896,384]{1,0:T(8,128)(2,1)}, bf16[896,384]{1,0:T(8,128)(2,1)}, u32[]{:S(2)}, u32[]{:S(2)}) collective-permute-start(bf16[896,384]{1,0:T(8,128)(2,1)} %convolution_convert_fusion.5.refs_0_), channel_id=1, source_target_pairs={{0,1},{1,0},{2,3},{3,2},{4,5},{5,4},{6,7},{7,6},{8,9},{9,8},{10,11... | collective-permute-start | bytes 2064392 | tf_op jit(solution)/shard_map/ppermute | solution.py:352
  117.8 53.3 %all-to-all-start.1 = ((bf16[32,32,768]{2,1,0:T(8,128)(2,1)}), bf16[32,32,768]{2,1,0:T(8,128)(2,1)}, u32[]{:S(2)}, u32[]{:S(2)}) async-start(bf16[32,32,768]{2,1,0:T(8,128)(2,1)} %get-tuple-element.58), calls=%async_computation.1 | async-start | bytes 3145728 | tf_op jit(solution)/shard_map/all_to_all | solution.py:508
  126.9 11.2 %collective-permute-start.11 = (bf16[896,384]{1,0:T(8,128)(2,1)}, bf16[896,384]{1,0:T(8,128)(2,1)}, u32[]{:S(2)}, u32[]{:S(2)}) collective-permute-start(bf16[896,384]{1,0:T(8,128)(2,1)} %fusion.42.refs_2_), channel_id=1, source_target_pairs={{0,1},{1,0},{2,3},{3,2},{4,5},{5,4},{6,7},{7,6},{8,9},{9,8},{10,11... | collective-permute-start | bytes 2064392 | tf_op jit(solution)/shard_map/ppermute | solution.py:352
  129.7 20.2 %collective-permute-start.7 = (bf16[896,384]{1,0:T(8,128)(2,1)}, bf16[896,384]{1,0:T(8,128)(2,1)}, u32[]{:S(2)}, u32[]{:S(2)}) collective-permute-start(bf16[896,384]{1,0:T(8,128)(2,1)} %convolution_convert_fusion.4.refs_0_), channel_id=1, source_target_pairs={{0,1},{1,0},{2,3},{3,2},{4,5},{5,4},{6,7},{7,6},{8,9},{9,8},{10,11... | collective-permute-start | bytes 2064392 | tf_op jit(solution)/shard_map/ppermute | solution.py:352
  130.2 45.1 %collective-permute-start.12 = (bf16[768,1920]{1,0:T(8,128)(2,1)}, bf16[768,1920]{1,0:T(8,128)(2,1)}, u32[]{:S(2)}, u32[]{:S(2)}) collective-permute-start(bf16[768,1920]{1,0:T(8,128)(2,1)} %all-gather.3.cloned.1.call-done), channel_id=1, source_target_pairs={{0,1},{1,0},{2,3},{3,2},{4,5},{5,4},{6,7},{7,6},{8,9},{9,8},{10,11... | collective-permute-start | bytes 8847368 | tf_op jit(solution)/shard_map/ppermute | solution.py:352
  133.1 16.8 %collective-permute-start.9 = (bf16[896,384]{1,0:T(8,128)(2,1)}, bf16[896,384]{1,0:T(8,128)(2,1)}, u32[]{:S(2)}, u32[]{:S(2)}) collective-permute-start(bf16[896,384]{1,0:T(8,128)(2,1)} %fusion.43.refs_2_), channel_id=1, source_target_pairs={{0,1},{1,0},{2,3},{3,2},{4,5},{5,4},{6,7},{7,6},{8,9},{9,8},{10,11... | collective-permute-start | bytes 2064392 | tf_op jit(solution)/shard_map/ppermute | solution.py:352
  180.0 23.6 %copy-start.53 = (f32[768]{0:T(1024)S(1)}, f32[768]{0:T(1024)}, u32[]{:S(2)}) copy-start(f32[768]{0:T(1024)} %get-tuple-element.146) | copy-start | bytes 9220
  180.4 24.7 %copy-start.73 = (f32[384]{0:T(512)S(1)}, f32[384]{0:T(512)}, u32[]{:S(2)}) copy-start(f32[384]{0:T(512)} %get-tuple-element.157) | copy-start | bytes 4612
  203.6 40.4 %collective-permute-start.14 = (bf16[768,3072]{1,0:T(8,128)(2,1)}, bf16[768,3072]{1,0:T(8,128)(2,1)}, u32[]{:S(2)}, u32[]{:S(2)}) collective-permute-start(bf16[768,3072]{1,0:T(8,128)(2,1)} %all-gather.5.cloned.1.call-done), channel_id=1, source_target_pairs={{0,1},{1,0},{2,3},{3,2},{4,5},{5,4},{6,7},{7,6},{8,9},{9,8},{10,11... | collective-permute-start | bytes 14155784 | tf_op jit(solution)/shard_map/ppermute | solution.py:352
  280.5 51.5 %collective-permute-start.15 = (bf16[768,3072]{1,0:T(8,128)(2,1)}, bf16[768,3072]{1,0:T(8,128)(2,1)}, u32[]{:S(2)}, u32[]{:S(2)}) collective-permute-start(bf16[768,3072]{1,0:T(8,128)(2,1)} %weight_grads.6), channel_id=1, source_target_pairs={{0,1},{1,0},{2,3},{3,2},{4,5},{5,4},{6,7},{7,6},{8,9},{9,8},{10,11... | collective-permute-start | bytes 14155784 | tf_op jit(solution)/shard_map/ppermute | solution.py:352
  313.8 64.9 %collective-permute-start.16 = (bf16[2,64,384]{2,1,0:T(8,128)(2,1)}, bf16[2,64,384]{2,1,0:T(8,128)(2,1)}, u32[]{:S(2)}, u32[]{:S(2)}) collective-permute-start(bf16[2,64,384]{2,1,0:T(8,128)(2,1)} %fusion.112), channel_id=1, source_target_pairs={{0,1},{1,0},{2,3},{3,2},{4,5},{5,4},{6,7},{7,6},{8,9},{9,8},{10,11... | collective-permute-start | bytes 294920 | tf_op jit(solution)/shard_map/ppermute | solution.py:352
  315.4 60.1 %collective-permute-start.17 = (bf16[2,64,384]{2,1,0:T(8,128)(2,1)}, bf16[2,64,384]{2,1,0:T(8,128)(2,1)}, u32[]{:S(2)}, u32[]{:S(2)}) collective-permute-start(bf16[2,64,384]{2,1,0:T(8,128)(2,1)} %fusion.113), channel_id=1, source_target_pairs={{0,1},{1,0},{2,3},{3,2},{4,5},{5,4},{6,7},{7,6},{8,9},{9,8},{10,11... | collective-permute-start | bytes 294920 | tf_op jit(solution)/shard_map/ppermute | solution.py:352
  322.0 80.3 %all-to-all-start.2 = ((bf16[32,32,768]{2,1,0:T(8,128)(2,1)}), bf16[32,32,768]{2,1,0:T(8,128)(2,1)}, u32[]{:S(2)}, u32[]{:S(2)}) async-start(bf16[32,32,768]{2,1,0:T(8,128)(2,1)} %select_select_fusion.1), calls=%async_computation.2 | async-start | bytes 3145728 | tf_op jit(solution)/shard_map/all_to_all | solution.py:502
  328.6 262.7 %reduce-scatter.2.cloned.1.call-start = ((), (), s32[]{:S(2)}) async-start(), calls=%async_computation.7 | async-start | bytes 5013504 | tf_op jit(solution)/shard_map/reduce_scatter | solution.py:409
  360.7 4.1 collective-permute-start.18
  361.7 3.7 collective-permute-start.19
  375.2 16.8 %collective-permute-start.20 = (bf16[4,4,48,1920]{3,2,1,0:T(8,128)(2,1)}, bf16[4,4,48,1920]{3,2,1,0:T(8,128)(2,1)}, u32[]{:S(2)}, u32[]{:S(2)}) collective-permute-start(bf16[4,4,48,1920]{3,2,1,0:T(8,128)(2,1)} %weight_grads.8), channel_id=1, source_target_pairs={{0,1},{1,0},{2,3},{3,2},{4,5},{5,4},{6,7},{7,6},{8,9},{9,8},{10,11... | collective-permute-start | bytes 8847368 | tf_op jit(solution)/shard_map/ppermute | solution.py:352
  405.2 24.3 %collective-permute-start.23 = (bf16[4,48,1920]{2,1,0:T(8,128)(2,1)}, bf16[4,48,1920]{2,1,0:T(8,128)(2,1)S(1)}, u32[]{:S(2)}, u32[]{:S(2)}) collective-permute-start(bf16[4,48,1920]{2,1,0:T(8,128)(2,1)} %get-tuple-element.179), channel_id=1, source_target_pairs={{0,6},{2,4},{4,2},{6,0},{8,14},{10,12},{12,10},{14,8},{16,22},{18,... | collective-permute-start | bytes 2211848 | tf_op jit(solution)/shard_map/ppermute | solution.py:356
  408.0 37.7 %collective-permute-start.22 = (bf16[4,48,1920]{2,1,0:T(8,128)(2,1)}, bf16[4,48,1920]{2,1,0:T(8,128)(2,1)S(1)}, u32[]{:S(2)}, u32[]{:S(2)}) collective-permute-start(bf16[4,48,1920]{2,1,0:T(8,128)(2,1)} %get-tuple-element.180), channel_id=1, source_target_pairs={{0,4},{2,6},{4,0},{6,2},{8,12},{10,14},{12,8},{14,10},{16,20},{18,... | collective-permute-start | bytes 2211848 | tf_op jit(solution)/shard_map/ppermute | solution.py:356
  408.6 37.3 %collective-permute-start.21 = (bf16[4,48,1920]{2,1,0:T(8,128)(2,1)S(1)}, bf16[4,48,1920]{2,1,0:T(8,128)(2,1)S(1)}, u32[]{:S(2)}, u32[]{:S(2)}) collective-permute-start(bf16[4,48,1920]{2,1,0:T(8,128)(2,1)S(1)} %get-tuple-element.178), channel_id=1, source_target_pairs={{0,2},{2,0},{4,6},{6,4},{8,10},{10,8},{12,14},{14,12},{16,18},{18,... | collective-permute-start | bytes 2211848 | tf_op jit(solution)/shard_map/ppermute | solution.py:356
  425.6 45.3 %collective-permute-start.25 = (bf16[896,384]{1,0:T(8,128)(2,1)}, bf16[896,384]{1,0:T(8,128)(2,1)}, u32[]{:S(2)}, u32[]{:S(2)}) collective-permute-start(bf16[896,384]{1,0:T(8,128)(2,1)} %get-tuple-element.81), channel_id=1, source_target_pairs={{0,1},{1,0},{2,3},{3,2},{4,5},{5,4},{6,7},{7,6},{8,9},{9,8},{10,11... | collective-permute-start | bytes 2064392 | tf_op jit(solution)/shard_map/ppermute | solution.py:352
  425.7 47.1 %collective-permute-start.27 = (bf16[896,384]{1,0:T(8,128)(2,1)}, bf16[896,384]{1,0:T(8,128)(2,1)}, u32[]{:S(2)}, u32[]{:S(2)}) collective-permute-start(bf16[896,384]{1,0:T(8,128)(2,1)} %get-tuple-element.85), channel_id=1, source_target_pairs={{0,1},{1,0},{2,3},{3,2},{4,5},{5,4},{6,7},{7,6},{8,9},{9,8},{10,11... | collective-permute-start | bytes 2064392 | tf_op jit(solution)/shard_map/ppermute | solution.py:352
  464.5 32.9 %collective-permute-start.26 = (bf16[896,384]{1,0:T(8,128)(2,1)}, bf16[896,384]{1,0:T(8,128)(2,1)}, u32[]{:S(2)}, u32[]{:S(2)}) collective-permute-start(bf16[896,384]{1,0:T(8,128)(2,1)} %get-tuple-element.83), channel_id=1, source_target_pairs={{0,1},{1,0},{2,3},{3,2},{4,5},{5,4},{6,7},{7,6},{8,9},{9,8},{10,11... | collective-permute-start | bytes 2064392 | tf_op jit(solution)/shard_map/ppermute | solution.py:352
  464.6 36.3 %collective-permute-start.24 = (bf16[896,384]{1,0:T(8,128)(2,1)}, bf16[896,384]{1,0:T(8,128)(2,1)}, u32[]{:S(2)}, u32[]{:S(2)}) collective-permute-start(bf16[896,384]{1,0:T(8,128)(2,1)} %get-tuple-element.79), channel_id=1, source_target_pairs={{0,1},{1,0},{2,3},{3,2},{4,5},{5,4},{6,7},{7,6},{8,9},{9,8},{10,11... | collective-permute-start | bytes 2064392 | tf_op jit(solution)/shard_map/ppermute | solution.py:352
  465.9 27.0 %collective-permute-start.37 = (bf16[48,1920]{1,0:T(8,128)(2,1)}, bf16[48,1920]{1,0:T(8,128)(2,1)}, u32[]{:S(2)}, u32[]{:S(2)}) collective-permute-start(bf16[48,1920]{1,0:T(8,128)(2,1)} %get-tuple-element.186), channel_id=1, source_target_pairs={{0,24},{2,26},{4,28},{6,30},{8,16},{10,18},{12,20},{14,22},{16,8},... | collective-permute-start | bytes 552968 | tf_op jit(solution)/shard_map/ppermute | solution.py:356
  470.9 22.2 %collective-permute-start.36 = (bf16[48,1920]{1,0:T(8,128)(2,1)}, bf16[48,1920]{1,0:T(8,128)(2,1)}, u32[]{:S(2)}, u32[]{:S(2)}) collective-permute-start(bf16[48,1920]{1,0:T(8,128)(2,1)} %get-tuple-element.187), channel_id=1, source_target_pairs={{0,16},{2,18},{4,20},{6,22},{8,24},{10,26},{12,28},{14,30},{16,0},... | collective-permute-start | bytes 552968 | tf_op jit(solution)/shard_map/ppermute | solution.py:356
  472.8 20.2 %collective-permute-start.35 = (bf16[48,1920]{1,0:T(8,128)(2,1)}, bf16[48,1920]{1,0:T(8,128)(2,1)}, u32[]{:S(2)}, u32[]{:S(2)}) collective-permute-start(bf16[48,1920]{1,0:T(8,128)(2,1)} %get-tuple-element.185), channel_id=1, source_target_pairs={{0,8},{2,10},{4,12},{6,14},{8,0},{10,2},{12,4},{14,6},{16,24},{18,... | collective-permute-start | bytes 552968 | tf_op jit(solution)/shard_map/ppermute | solution.py:356
  493.0 34.9 %collective-permute-start.28 = (bf16[4,4,48,1152]{3,2,1,0:T(8,128)(2,1)}, bf16[4,4,48,1152]{3,2,1,0:T(8,128)(2,1)}, u32[]{:S(2)}, u32[]{:S(2)}) collective-permute-start(bf16[4,4,48,1152]{3,2,1,0:T(8,128)(2,1)} %weight_grads.10), channel_id=1, source_target_pairs={{0,1},{1,0},{2,3},{3,2},{4,5},{5,4},{6,7},{7,6},{8,9},{9,8},{10,11... | collective-permute-start | bytes 5308424 | tf_op jit(solution)/shard_map/ppermute | solution.py:352
  500.4 4.2 collective-permute-start.38
  504.7 9.7 %collective-permute-start.41 = (f32[13056]{0:T(1024)S(1)}, f32[13056]{0:T(1024)S(1)}, u32[]{:S(2)}, u32[]{:S(2)}) collective-permute-start(f32[13056]{0:T(1024)S(1)} %add.710), channel_id=1, source_target_pairs={{0,6},{2,4},{4,2},{6,0},{8,14},{10,12},{12,10},{14,8},{16,22},{18,... | collective-permute-start | bytes 156680 | tf_op jit(solution)/shard_map/ppermute | solution.py:356
  508.0 6.4 %collective-permute-start.40 = (f32[13056]{0:T(1024)S(1)}, f32[13056]{0:T(1024)S(1)}, u32[]{:S(2)}, u32[]{:S(2)}) collective-permute-start(f32[13056]{0:T(1024)S(1)} %add.710), channel_id=1, source_target_pairs={{0,4},{2,6},{4,0},{6,2},{8,12},{10,14},{12,8},{14,10},{16,20},{18,... | collective-permute-start | bytes 156680 | tf_op jit(solution)/shard_map/ppermute | solution.py:356
  508.4 6.0 collective-permute-start.39
  514.4 13.4 %collective-permute-start.44 = (f32[13056]{0:T(1024)S(1)}, f32[13056]{0:T(1024)S(1)}, u32[]{:S(2)}, u32[]{:S(2)}) collective-permute-start(f32[13056]{0:T(1024)S(1)} %add_add_fusion.5), channel_id=1, source_target_pairs={{0,24},{2,26},{4,28},{6,30},{8,16},{10,18},{12,20},{14,22},{16,8},... | collective-permute-start | bytes 156680 | tf_op jit(solution)/shard_map/ppermute | solution.py:356
  518.3 9.5 %collective-permute-start.43 = (f32[13056]{0:T(1024)S(1)}, f32[13056]{0:T(1024)S(1)}, u32[]{:S(2)}, u32[]{:S(2)}) collective-permute-start(f32[13056]{0:T(1024)S(1)} %add_add_fusion.5), channel_id=1, source_target_pairs={{0,16},{2,18},{4,20},{6,22},{8,24},{10,26},{12,28},{14,30},{16,0},... | collective-permute-start | bytes 156680 | tf_op jit(solution)/shard_map/ppermute | solution.py:356
  518.3 9.5 %collective-permute-start.42 = (f32[13056]{0:T(1024)S(1)}, f32[13056]{0:T(1024)S(1)}, u32[]{:S(2)}, u32[]{:S(2)}) collective-permute-start(f32[13056]{0:T(1024)S(1)} %add_add_fusion.5), channel_id=1, source_target_pairs={{0,8},{2,10},{4,12},{6,14},{8,0},{10,2},{12,4},{14,6},{16,24},{18,... | collective-permute-start | bytes 156680 | tf_op jit(solution)/shard_map/ppermute | solution.py:356
  520.4 64.9 %all-to-all-start.3 = ((bf16[32,32,768]{2,1,0:T(8,128)(2,1)}), bf16[32,32,768]{2,1,0:T(8,128)(2,1)S(1)}, u32[]{:S(2)}, u32[]{:S(2)}) async-start(bf16[32,32,768]{2,1,0:T(8,128)(2,1)} %select_select_fusion), calls=%async_computation.3 | async-start | bytes 3145728 | tf_op jit(solution)/shard_map/all_to_all | solution.py:502
  537.0 27.3 %collective-permute-start.31 = (bf16[4,48,1152]{2,1,0:T(8,128)(2,1)}, bf16[4,48,1152]{2,1,0:T(8,128)(2,1)S(1)}, u32[]{:S(2)}, u32[]{:S(2)}) collective-permute-start(bf16[4,48,1152]{2,1,0:T(8,128)(2,1)} %get-tuple-element.183), channel_id=1, source_target_pairs={{0,6},{2,4},{4,2},{6,0},{8,14},{10,12},{12,10},{14,8},{16,22},{18,... | collective-permute-start | bytes 1327112 | tf_op jit(solution)/shard_map/ppermute | solution.py:356
  539.8 27.1 %collective-permute-start.30 = (bf16[4,48,1152]{2,1,0:T(8,128)(2,1)}, bf16[4,48,1152]{2,1,0:T(8,128)(2,1)S(1)}, u32[]{:S(2)}, u32[]{:S(2)}) collective-permute-start(bf16[4,48,1152]{2,1,0:T(8,128)(2,1)} %get-tuple-element.184), channel_id=1, source_target_pairs={{0,4},{2,6},{4,0},{6,2},{8,12},{10,14},{12,8},{14,10},{16,20},{18,... | collective-permute-start | bytes 1327112 | tf_op jit(solution)/shard_map/ppermute | solution.py:356
  540.3 30.9 %collective-permute-start.29 = (bf16[4,48,1152]{2,1,0:T(8,128)(2,1)S(1)}, bf16[4,48,1152]{2,1,0:T(8,128)(2,1)}, u32[]{:S(2)}, u32[]{:S(2)}) collective-permute-start(bf16[4,48,1152]{2,1,0:T(8,128)(2,1)S(1)} %get-tuple-element.182), channel_id=1, source_target_pairs={{0,2},{2,0},{4,6},{6,4},{8,10},{10,8},{12,14},{14,12},{16,18},{18,... | collective-permute-start | bytes 1327112 | tf_op jit(solution)/shard_map/ppermute | solution.py:356
  572.6 14.8 %copy-start.80 = (pred[32]{0:T(512)(128)(4,1)S(1)}, pred[32]{0:T(512)(128)(4,1)}, u32[]{:S(2)}) copy-start(pred[32]{0:T(512)(128)(4,1)} %compare_and_fusion) | copy-start | bytes 100
  572.6 7.7 %collective-permute-start.34 = (bf16[48,1152]{1,0:T(8,128)(2,1)S(1)}, bf16[48,1152]{1,0:T(8,128)(2,1)S(1)}, u32[]{:S(2)}, u32[]{:S(2)}) collective-permute-start(bf16[48,1152]{1,0:T(8,128)(2,1)S(1)} %get-tuple-element.189), channel_id=1, source_target_pairs={{0,24},{2,26},{4,28},{6,30},{8,16},{10,18},{12,20},{14,22},{16,8},... | collective-permute-start | bytes 331784 | tf_op jit(solution)/shard_map/ppermute | solution.py:356
  575.6 8.9 %collective-permute-start.33 = (bf16[48,1152]{1,0:T(8,128)(2,1)S(1)}, bf16[48,1152]{1,0:T(8,128)(2,1)S(1)}, u32[]{:S(2)}, u32[]{:S(2)}) collective-permute-start(bf16[48,1152]{1,0:T(8,128)(2,1)S(1)} %get-tuple-element.190), channel_id=1, source_target_pairs={{0,16},{2,18},{4,20},{6,22},{8,24},{10,26},{12,28},{14,30},{16,0},... | collective-permute-start | bytes 331784 | tf_op jit(solution)/shard_map/ppermute | solution.py:356
  577.5 7.0 %collective-permute-start.32 = (bf16[48,1152]{1,0:T(8,128)(2,1)S(1)}, bf16[48,1152]{1,0:T(8,128)(2,1)S(1)}, u32[]{:S(2)}, u32[]{:S(2)}) collective-permute-start(bf16[48,1152]{1,0:T(8,128)(2,1)S(1)} %get-tuple-element.188), channel_id=1, source_target_pairs={{0,8},{2,10},{4,12},{6,14},{8,0},{10,2},{12,4},{14,6},{16,24},{18,... | collective-permute-start | bytes 331784 | tf_op jit(solution)/shard_map/ppermute | solution.py:356
  (75 other events, 414.6 us)
Sparse Core Ops, SparseCore 0:
  11.4 93.2 all-gather.2
  108.0 95.5 all-gather.4
  375.6 165.2 reduce-scatter.1

commit v3 on v2

--- a/solution.py
+++ b/solution.py
@@ -12,6 +12,8 @@
 EPSILON = 1e-05
 MASKED = -1e30
 BLOCK = 128
+LIGHT = 1000
+GROUP = 4
 PAIR = 2 * HD
 F32 = jnp.float32
 BF16 = jnp.bfloat16
@@ -187,16 +189,16 @@
             dv_out[part][...] = dv_sum[part][...].astype(dv_out[part].dtype)
 
 
-def row_spec(width):
-    return pl.BlockSpec((BLOCK, width), lambda block, meta: (block, 0))
+def row_spec(width, rows=BLOCK):
+    return pl.BlockSpec((rows, width), lambda block, meta: (block, 0))
 
 
 def whole_spec(rows, width):
     return pl.BlockSpec((rows, width), lambda block, meta: (0, 0))
 
 
-def lse_spec():
-    return pl.BlockSpec((1, 8, 2 * BLOCK), lambda block, meta: (block, 0, 0))
+def lse_spec(group=1):
+    return pl.BlockSpec((group, 8, 2 * BLOCK), lambda block, meta: (block, 0, 0))
 
 
 def attend_forward(meta, queries, keys, values, causal, piece, spans):
@@ -219,7 +221,7 @@
             jax.ShapeDtypeStruct((blocks, 8, 2 * BLOCK), F32),
         ],
         cost_estimate=pl.CostEstimate(
-            flops=4 * work, bytes_accessed=8 * rows * width, transcendentals=work // 256
+            flops=(4 * work) // LIGHT, bytes_accessed=(8 * rows * width) // LIGHT, transcendentals=work // 256
         ),
         name="attend_forward",
     )(meta, queries, *keys, *values)
@@ -245,7 +247,7 @@
         out_shape=[jax.ShapeDtypeStruct((rows, width), BF16)]
         + [jax.ShapeDtypeStruct((key_rows, width), kind) for kind in kinds + kinds],
         cost_estimate=pl.CostEstimate(
-            flops=10 * work, bytes_accessed=16 * rows * width, transcendentals=work // 256
+            flops=(10 * work) // LIGHT, bytes_accessed=(16 * rows * width) // LIGHT, transcendentals=work // 256
         ),
         name="attend_backward",
     )(meta, queries, grads, lse, *keys, *values)
@@ -257,21 +259,14 @@
     rights = refs[len(lefts) : len(lefts) + len(counts)]
     rest = refs[len(lefts) + len(counts) :]
     extra_ref = rest[0] if extra else None
-    out_ref = rest[1] if extra else rest[0]
-    flipped = rest[2:] if extra else rest[1:]
+    out_ref = rest[-1]
     step = pl.program_id(0)
-
-    @pl.when(step == 0)
-    def _():
-        for left, flip in zip(lefts, flipped):
-            flip[...] = left[...].astype(F32).T.astype(BF16)
-
     begin = 0
     for index, count in enumerate(counts):
 
         @pl.when((step >= begin) & (step < begin + count))
         def _(index=index):
-            result = dot_nn(flipped[sides[index]][...], rights[index][...])
+            result = dot_tn(lefts[sides[index]][...], rights[index][...])
             if factors[index] != 1.0:
                 result = result * factors[index]
             if not grouped:
@@ -293,8 +288,10 @@
 
 
 def weight_grads(meta, lefts, rights, sides, factors, extra, grouped):
-    chunk = 384
-    counts = [right.shape[1] // chunk for right in rights]
+    chunk = min(2 * 384, rights[0].shape[1])
+    shifts = [right[1] if isinstance(right, tuple) else 0 for right in rights]
+    counts = [1 if isinstance(right, tuple) else right.shape[1] // chunk for right in rights]
+    rights = [right[0] if isinstance(right, tuple) else right for right in rights]
     width = lefts[0].shape[1]
     total = sum(counts) * chunk
     begins = [sum(counts[:i]) for i in range(len(counts))]
@@ -302,7 +299,10 @@
     def right_spec(index):
         return pl.BlockSpec(
             (rights[index].shape[0], chunk),
-            lambda step, meta: (0, jnp.clip(step - begins[index], 0, counts[index] - 1)),
+            lambda step, meta: (
+                0,
+                shifts[index] + jnp.clip(step - begins[index], 0, counts[index] - 1),
+            ),
         )
 
     if grouped:
@@ -311,7 +311,7 @@
     else:
         shape = (width, total)
         out_spec = pl.BlockSpec((width, chunk), lambda step, meta: (0, step))
-    flops = sum(2 * right.shape[0] * width * right.shape[1] for right in rights)
+    flops = 2 * rights[0].shape[0] * width * total
     return pl.pallas_call(
         functools.partial(grads_kernel, sides, counts, factors, extra is not None, grouped),
         grid_spec=pltpu.PrefetchScalarGridSpec(
@@ -321,11 +321,10 @@
             + [right_spec(index) for index in range(len(rights))]
             + ([out_spec] if extra is not None else []),
             out_specs=out_spec,
-            scratch_shapes=[pltpu.VMEM((width, left.shape[0]), BF16) for left in lefts],
         ),
         out_shape=jax.ShapeDtypeStruct(shape, BF16),
         cost_estimate=pl.CostEstimate(
-            flops=flops, bytes_accessed=flops // 256, transcendentals=0
+            flops=flops // LIGHT, bytes_accessed=flops // 256 // LIGHT, transcendentals=0
         ),
         name="weight_grads",
     )(meta, *lefts, *rights, *([extra] if extra is not None else []))
@@ -339,13 +338,404 @@
     return unit * gain + shift, unit, scale
 
 
-def norm_backward(grad, unit, scale, gain):
-    gain_grad = jnp.sum(grad * unit, 0)
-    shift_grad = jnp.sum(grad, 0)
+def norm_gradient(grad, unit, scale, gain):
     inner = grad * gain
     mean_inner = jnp.mean(inner, -1, keepdims=True)
     mean_unit = jnp.mean(inner * unit, -1, keepdims=True)
-    return scale * (inner - mean_inner - unit * mean_unit), gain_grad, shift_grad
+    return scale * (inner - mean_inner - unit * mean_unit)
+
+
+def norm_backward(grad, unit, scale, gain):
+    return norm_gradient(grad, unit, scale, gain), jnp.sum(grad * unit, 0), jnp.sum(grad, 0)
+
+
+def sub_blocks(meta, keys_each, run, skip):
+    def one(sub, carry):
+        block = pl.program_id(0) * GROUP + sub
+        second = (block >= meta[0]).astype(jnp.int32)
+        place = pl.ds(pl.multiple_of(second * keys_each, keys_each), keys_each)
+        rows = pl.ds(pl.multiple_of(sub * BLOCK, BLOCK), BLOCK)
+        pl.when(block < meta[1])(functools.partial(run, sub, rows, place))
+        pl.when(block >= meta[1])(functools.partial(skip, sub, rows))
+        return carry
+
+    lax.fori_loop(0, GROUP, one, 0)
+
+
+def mid_forward_kernel(score_scale, meta, x_ref, attn0, attn1, memory_ref, *refs):
+    attn = (attn0, attn1)
+    self_out, query_w, memory_k, memory_v, cross_out = [refs[2 * i : 2 * i + 2] for i in range(5)]
+    bias0, bias1, out_bias, gain, shift = refs[10:15]
+    unit1_ref, scale1_ref, unit2_ref, scale2_ref, cross_in_ref, hidden_ref, lse_ref = refs[15:22]
+    cq_refs, cattn_refs, ck_refs, cv_refs = [refs[22 + 2 * i : 24 + 2 * i] for i in range(4)]
+    flipped = refs[30:32]
+    half = attn0.shape[1]
+    keys_each = memory_ref.shape[0] // 2
+
+    @pl.when(pl.program_id(0) == 0)
+    def _():
+        for h, bias in enumerate((bias0, bias1)):
+            ck_refs[h][...] = dot_nn(memory_ref[...], memory_k[h][...]).astype(BF16)
+            value = dot_nn(memory_ref[...], memory_v[h][...]) + bias[3:4, :]
+            cv_refs[h][...] = value.astype(BF16)
+            flipped[h][...] = value.T.astype(BF16)
+
+    branch = dot_nt(attn[0][...], self_out[0][...]) + dot_nt(attn[1][...], self_out[1][...])
+    n1, unit1, scale1 = norm_forward(
+        x_ref[...].astype(F32) + branch + out_bias[0:1, :], gain[0:1, :], shift[0:1, :]
+    )
+    unit1_ref[...] = unit1
+    scale1_ref[...] = scale1
+    cross_in = n1.astype(BF16)
+    cross_in_ref[...] = cross_in
+    for h, bias in enumerate((bias0, bias1)):
+        query = (dot_nn(cross_in, query_w[h][...]) + bias[2:3, :]) * score_scale
+        cq_refs[h][...] = query.astype(BF16)
+
+    def run(sub, rows, place):
+        for h in range(2):
+            for pair in range(half // PAIR):
+                cols = pair_columns(pair)
+                tile = dot_nt(ck_refs[h][place, cols], stack_heads(cq_refs[h][rows, cols]))
+                top = jnp.max(tile, 0, keepdims=True)
+                exps = jnp.exp(tile - top)
+                total = jnp.sum(exps, 0, keepdims=True)
+                result = dot_nn(flipped[h][cols, place], exps.astype(BF16))
+                cattn_refs[h][rows, cols] = unstack_heads(result / total).astype(BF16)
+                row = h * (half // PAIR) + pair
+                lse_ref[sub, row : row + 1, :] = top + jnp.log(total)
+
+    def skip(sub, rows):
+        lse_ref[sub] = jnp.zeros(lse_ref.shape[1:], F32)
+        for h in range(2):
+            cattn_refs[h][rows, :] = jnp.zeros((BLOCK, half), BF16)
+
+    sub_blocks(meta, keys_each, run, skip)
+    branch = dot_nt(cattn_refs[0][...], cross_out[0][...]) + dot_nt(
+        cattn_refs[1][...], cross_out[1][...]
+    )
+    n1 = unit1_ref[...] * gain[0:1, :] + shift[0:1, :]
+    n2, unit2, scale2 = norm_forward(n1 + branch + out_bias[1:2, :], gain[1:2, :], shift[1:2, :])
+    unit2_ref[...] = unit2
+    scale2_ref[...] = scale2
+    hidden_ref[...] = n2.astype(BF16)
+
+
+def mid_backward_kernel(score_scale, total_rows, meta, dn2_ref, unit2_ref, scale2_ref, unit1_ref, scale1_ref, lse_ref, *refs):
+    cq_refs, ck_refs, cv_refs = [refs[2 * i : 2 * i + 2] for i in range(3)]
+    self_out, query_w, cross_out = [refs[6 + 2 * i : 8 + 2 * i] for i in range(3)]
+    gain = refs[12]
+    dy2_ref, dh1_ref, dy_ref, sums_ref = refs[13:17]
+    dcq_refs, da_refs = refs[17:19], refs[19:21]
+    near_ref, far_ref = refs[21:23]
+    dca_refs, flipped, dck_refs, dcv_refs = [refs[23 + 2 * i : 25 + 2 * i] for i in range(4)]
+    half = cq_refs[0].shape[1]
+    keys_each = ck_refs[0].shape[0] // 2
+    here = pl.program_id(0) * GROUP * BLOCK + lax.broadcasted_iota(
+        jnp.int32, (GROUP * BLOCK, 1), 0
+    )
+    inside = here < total_rows
+
+    def load(ref):
+        return jnp.where(inside, ref[...], 0.0)
+
+    @pl.when(pl.program_id(0) == 0)
+    def _():
+        sums_ref[...] = jnp.zeros_like(sums_ref)
+        for h in range(2):
+            flipped[h][...] = ck_refs[h][...].astype(F32).T.astype(BF16)
+            dck_refs[h][...] = jnp.zeros_like(dck_refs[h])
+            dcv_refs[h][...] = jnp.zeros_like(dcv_refs[h])
+
+    dn2 = load(dn2_ref)
+    unit2 = load(unit2_ref)
+    dh2 = norm_gradient(dn2, unit2, load(scale2_ref), gain[1:2, :])
+    dh1_ref[...] = dh2
+    dy2 = dh2.astype(BF16)
+    dy2_ref[...] = dy2
+    sums_ref[0:1, :] += jnp.sum(dn2 * unit2, 0, keepdims=True)
+    sums_ref[1:2, :] += jnp.sum(dn2, 0, keepdims=True)
+    sums_ref[2:3, :] += jnp.sum(dy2.astype(F32), 0, keepdims=True)
+    for h in range(2):
+        dca_refs[h][...] = dot_nn(dy2, cross_out[h][...]).astype(BF16)
+
+    def run(sub, rows, place):
+        for h in range(2):
+            for pair in range(half // PAIR):
+                cols = pair_columns(pair)
+                row = h * (half // PAIR) + pair
+                queries = stack_heads(cq_refs[h][rows, cols])
+                grads = stack_heads(dca_refs[h][rows, cols])
+                tile = dot_nt(ck_refs[h][place, cols], queries)
+                probs = jnp.exp(tile - lse_ref[sub, row : row + 1, :])
+                grad_probs = dot_nt(cv_refs[h][place, cols], grads)
+                row_dot = jnp.sum(probs * grad_probs, 0, keepdims=True)
+                grad_score = (probs * (grad_probs - row_dot)).astype(BF16)
+                dcv_refs[h][place, cols] += dot_nn(probs.astype(BF16), grads)
+                dck_refs[h][place, cols] += dot_nn(grad_score, queries)
+                term = dot_nn(flipped[h][cols, place], grad_score)
+                dcq_refs[h][rows, cols] = unstack_heads(term).astype(BF16)
+
+    def skip(sub, rows):
+        for h in range(2):
+            dcq_refs[h][rows, :] = jnp.zeros((BLOCK, half), BF16)
+
+    sub_blocks(meta, keys_each, run, skip)
+    dn1 = dh1_ref[...]
+    for h in range(2):
+        dcq = dcq_refs[h][...]
+        dn1 = dn1 + score_scale * dot_nt(dcq, query_w[h][...])
+        sums_ref[6:7, h * half : (h + 1) * half] += jnp.sum(dcq.astype(F32), 0, keepdims=True)
+    unit1 = load(unit1_ref)
+    dh1 = norm_gradient(dn1, unit1, load(scale1_ref), gain[0:1, :])
+    dy = dh1.astype(BF16)
+    dh1_ref[...] = dh1
+    dy_ref[...] = dy
+    sums_ref[3:4, :] += jnp.sum(dn1 * unit1, 0, keepdims=True)
+    sums_ref[4:5, :] += jnp.sum(dn1, 0, keepdims=True)
+    sums_ref[5:6, :] += jnp.sum(dy.astype(F32), 0, keepdims=True)
+    for h in range(2):
+        da_refs[h][...] = dot_nn(dy, self_out[h][...]).astype(BF16)
+
+    @pl.when(pl.program_id(0) == pl.num_programs(0) - 1)
+    def _():
+        own = keys_each // 2
+        for index, ref in enumerate((dck_refs[0], dck_refs[1], dcv_refs[0], dcv_refs[1])):
+            near = slice(index * half, (index + 1) * half)
+            far = slice((index ^ 1) * half, ((index ^ 1) + 1) * half)
+            for seq in range(2):
+                rows = slice(seq * own, (seq + 1) * own)
+                base = seq * keys_each
+                near_ref[rows, near] = ref[base : base + own, :]
+                far_ref[rows, far] = ref[base + own : base + keys_each, :].astype(BF16)
+
+
+def memory_backward_kernel(near_ref, got_ref, wk0, wv0, wk1, wv1, sum_ref, encoder_ref, bias_ref):
+    total = (near_ref[...] + got_ref[...].astype(F32)).astype(BF16)
+    sum_ref[...] = total
+    half = wk0.shape[1]
+    grad = dot_nt(total[:, :half], wk0[...]) + dot_nt(total[:, half : 2 * half], wk1[...])
+    grad = grad + dot_nt(total[:, 2 * half : 3 * half], wv0[...])
+    encoder_ref[...] = (grad + dot_nt(total[:, 3 * half :], wv1[...])).astype(BF16)
+    bias = jnp.sum(total[:, 2 * half :].astype(F32), 0, keepdims=True)
+    bias_ref[...] = jnp.broadcast_to(bias, bias_ref.shape)
+
+
+def memory_backward(near, got, mid):
+    rows, span = near.shape
+    half = span // 4
+    width = mid[0].shape[0]
+    columns = [plain_fixed((width, half), 0, 2), plain_fixed((width, half), 0, 3)]
+    return pl.pallas_call(
+        memory_backward_kernel,
+        grid=(1,),
+        in_specs=[plain_fixed((rows, span))] * 2 + columns * 2,
+        out_specs=[plain_fixed((rows, span)), plain_fixed((rows, width)), plain_fixed((8, 2 * half))],
+        out_shape=[kept((rows, span), BF16), kept((rows, width), BF16), kept((8, 2 * half), F32)],
+        cost_estimate=pl.CostEstimate(flops=1000, bytes_accessed=1000, transcendentals=0),
+        name="memory_backward",
+    )(near, got, mid[0], mid[0], mid[1], mid[1])
+
+
+def ffn_backward_kernel(h3_ref, cot_ref, valid_ref, slope0, slope1, in0, in1, out0, out1, gain, shift, n3_ref, dz_ref, dn2_ref, sums_ref, du0, du1, usum0, usum1):
+    @pl.when(pl.program_id(0) == 0)
+    def _():
+        for ref in (sums_ref, usum0, usum1):
+            ref[...] = jnp.zeros_like(ref)
+
+    n3, unit, scale = norm_forward(h3_ref[...], gain[2:3, :], shift[2:3, :])
+    valid = valid_ref[...] > 0.5
+    n3_ref[...] = jnp.where(valid, n3, 0.0).astype(BF16)
+    dn3 = jnp.where(valid, cot_ref[...].astype(F32), 0.0)
+    dh3 = norm_gradient(dn3, unit, scale, gain[2:3, :])
+    dz = dh3.astype(BF16)
+    dz_ref[...] = dz
+    sums_ref[0:1, :] += jnp.sum(dn3 * unit, 0, keepdims=True)
+    sums_ref[1:2, :] += jnp.sum(dn3, 0, keepdims=True)
+    sums_ref[2:3, :] += jnp.sum(dz.astype(F32), 0, keepdims=True)
+    total = dh3
+    sides = ((slope0, out0, in0, du0, usum0), (slope1, out1, in1, du1, usum1))
+    for slope, reduce, expand, du_ref, usum in sides:
+        du = (dot_nn(dz, reduce[...]) * slope[...].astype(F32)).astype(BF16)
+        du_ref[...] = du
+        usum[0:1, :] += jnp.sum(du.astype(F32), 0, keepdims=True)
+        total = total + dot_nt(du, expand[...])
+    dn2_ref[...] = total
+
+
+def ffn_backward(h3, cot, valid, slope, ffn, gain, shift):
+    rows, width = h3.shape
+    units = slope[0].shape[1]
+    wide, thin, long = [plain_rows(rows // 2, w) for w in (width, 1, units)]
+
+    def side(column):
+        return pl.BlockSpec(
+            (width, units), lambda step: (0, column), pipeline_mode=pl.Buffered(1)
+        )
+
+    return pl.pallas_call(
+        ffn_backward_kernel,
+        grid=(2,),
+        in_specs=[wide, wide, thin, long, long, side(0), side(0), side(1), side(1)]
+        + [plain_fixed((3, width))] * 2,
+        out_specs=[wide, wide, wide, plain_fixed((8, width)), long, long]
+        + [plain_fixed((8, units))] * 2,
+        out_shape=[
+            kept((rows, width), BF16),
+            kept((rows, width), BF16),
+            kept((rows, width), F32),
+            kept((8, width), F32),
+            kept((rows, units), BF16),
+            kept((rows, units), BF16),
+            kept((8, units), F32),
+            kept((8, units), F32),
+        ],
+        cost_estimate=pl.CostEstimate(flops=1000, bytes_accessed=1000, transcendentals=0),
+        name="ffn_backward",
+    )(h3, cot, valid, *slope, ffn[0], ffn[1], ffn[0], ffn[1], gain, shift)
+
+
+def fixed_spec(shape, *index):
+    place = index or (0,) * len(shape)
+    return pl.BlockSpec(shape, lambda block, meta: place)
+
+
+def kept(shape, kind):
+    return jax.ShapeDtypeStruct(shape, kind)
+
+
+def mid_forward(meta, inputs, attn, memory, mid, in_pair, out_bias, gain, shift, score_scale):
+    rows, width = inputs.shape
+    half = attn[0].shape[1]
+    blocks = rows // BLOCK
+    memory_rows = memory.shape[0]
+    weights = [fixed_spec((width, half), 0, column) for column in range(5) for _ in range(2)]
+    tall = GROUP * BLOCK
+    wide, thin, narrow = row_spec(width, tall), row_spec(1, tall), row_spec(half, tall)
+    memory_spec = fixed_spec((memory_rows, half))
+    outs = pl.pallas_call(
+        functools.partial(mid_forward_kernel, score_scale),
+        grid_spec=pltpu.PrefetchScalarGridSpec(
+            num_scalar_prefetch=1,
+            grid=(pl.cdiv(blocks, GROUP),),
+            in_specs=[wide, narrow, narrow, fixed_spec(memory.shape)]
+            + weights
+            + [fixed_spec((4, half))] * 2
+            + [fixed_spec((3, width))] * 3,
+            out_specs=[wide, thin, wide, thin, wide, wide, lse_spec(GROUP)]
+            + [narrow] * 4
+            + [memory_spec] * 4,
+            scratch_shapes=[pltpu.VMEM((half, memory_rows), BF16)] * 2,
+        ),
+        out_shape=[
+            kept((rows, width), F32),
+            kept((rows, 1), F32),
+            kept((rows, width), F32),
+            kept((rows, 1), F32),
+            kept((rows, width), BF16),
+            kept((rows, width), BF16),
+            kept((blocks, 8, 2 * BLOCK), F32),
+        ]
+        + [kept((rows, half), BF16)] * 4
+        + [kept((memory_rows, half), BF16)] * 4,
+        cost_estimate=pl.CostEstimate(
+            flops=(24 * rows * width * half) // LIGHT, bytes_accessed=(20 * rows * width) // LIGHT, transcendentals=0
+        ),
+        name="mid_forward",
+    )(meta, inputs, *attn, memory, *[mid[h] for _ in range(5) for h in range(2)], *in_pair, out_bias, gain, shift)
+    return outs[:7], outs[7:9], outs[9:11], outs[11:13], outs[13:15]
+
+
+def mid_backward(meta, dn2, saved, cq, ck, cv, mid, gain, score_scale):
+    unit1, scale1, unit2, scale2, lse = saved
+    rows, width = dn2.shape
+    half = cq[0].shape[1]
+    blocks = rows // BLOCK
+    memory_rows = ck[0].shape[0]
+    tall = GROUP * BLOCK
+    wide, thin, narrow = row_spec(width, tall), row_spec(1, tall), row_spec(half, tall)
+    memory_spec = fixed_spec((memory_rows, half))
+    weights = [fixed_spec((width, half), 0, column) for column in (0, 1, 4) for _ in range(2)]
+    outs = pl.pallas_call(
+        functools.partial(mid_backward_kernel, score_scale, rows),
+        grid_spec=pltpu.PrefetchScalarGridSpec(
+            num_scalar_prefetch=1,
+            grid=(pl.cdiv(blocks, GROUP),),
+            in_specs=[wide, wide, thin, wide, thin, lse_spec(GROUP)]
+            + [narrow] * 2
+            + [memory_spec] * 4
+            + weights
+            + [fixed_spec((3, width))],
+            out_specs=[wide, wide, wide, fixed_spec((8, width))]
+            + [narrow] * 4
+            + [fixed_spec((memory_rows // 2, 4 * half))] * 2,
+            scratch_shapes=[pltpu.VMEM((tall, half), BF16)] * 2
+            + [pltpu.VMEM((half, memory_rows), BF16)] * 2
+            + [pltpu.VMEM((memory_rows, half), F32)] * 4,
+        ),
+        out_shape=[
+            kept((rows, width), BF16),
+            kept((rows, width), F32),
+            kept((rows, width), BF16),
+            kept((8, width), F32),
+        ]
+        + [kept((rows, half), BF16)] * 4
+        + [kept((memory_rows // 2, 4 * half), F32), kept((memory_rows // 2, 4 * half), BF16)],
+        cost_estimate=pl.CostEstimate(
+            flops=(24 * rows * width * half) // LIGHT, bytes_accessed=(20 * rows * width) // LIGHT, transcendentals=0
+        ),
+        name="mid_backward",
+    )(meta, dn2, unit2, scale2, unit1, scale1, lse, *cq, *ck, *cv, *[mid[h] for _ in range(3) for h in range(2)], gain)
+    return outs[:4], outs[4:6], outs[6:8], outs[8], outs[9]
+
+
+def input_backward_kernel(score_scale, base_ref, dq_ref, dk_own, dk_got, dv_own, dv_got, wq, wk, wv, dx_ref, dk_ref, dv_ref, sums_ref):
+    @pl.when(pl.program_id(0) == 0)
+    def _():
+        sums_ref[...] = jnp.zeros_like(sums_ref)
+
+    dk = (dk_own[...] + dk_got[...].astype(F32)).astype(BF16)
+    dv = (dv_own[...] + dv_got[...].astype(F32)).astype(BF16)
+    dk_ref[...] = dk
+    dv_ref[...] = dv
+    dq = dq_ref[...]
+    sums_ref[0:1, :] += score_scale * jnp.sum(dq.astype(F32), 0, keepdims=True)
+    sums_ref[1:2, :] += jnp.sum(dv.astype(F32), 0, keepdims=True)
+    total = score_scale * dot_nt(dq, wq[...]) + dot_nt(dk, wk[...]) + dot_nt(dv, wv[...])
+    dx_ref[...] = (base_ref[...] + total).astype(dx_ref.dtype)
+
+
+def plain_rows(rows, width):
+    return pl.BlockSpec((rows, width), lambda step: (step, 0))
+
+
+def plain_fixed(shape, *index):
+    place = index or (0,) * len(shape)
+    return pl.BlockSpec(shape, lambda step: place)
+
+
+def input_backward(base, dq, dk, dk_got, dv, dv_got, weight, score_scale, kind):
+    rows, width = base.shape
+    half = dq.shape[1]
+    wide, narrow = plain_rows(rows // 2, width), plain_rows(rows // 2, half)
+    return pl.pallas_call(
+        functools.partial(input_backward_kernel, score_scale),
+        grid=(2,),
+        in_specs=[wide] + [narrow] * 5 + [plain_fixed((width, half), 0, i) for i in range(3)],
+        out_specs=[wide, narrow, narrow, plain_fixed((8, half))],
+        out_shape=[
+            kept((rows, width), kind),
+            kept((rows, half), BF16),
+            kept((rows, half), BF16),
+            kept((8, half), F32),
+        ],
+        cost_estimate=pl.CostEstimate(
+            flops=(6 * rows * width * half) // LIGHT,
+            bytes_accessed=(12 * rows * width) // LIGHT,
+            transcendentals=0,
+        ),
+        name="input_backward",
+    )(base, dq, dk, dk_got, dv, dv_got, weight, weight, weight)
 
 
 def swap(value):
@@ -361,11 +751,12 @@
         out_ref[0, pl.ds(meta[1] ^ low, 1)] = ref[...]
 
 
-def quick_gather(value):
+def quick_gather(value, later):
     if lax.axis_size("dp") != 16:
-        return lax.all_gather(value, "dp", axis=0, tiled=True)
+        return lax.all_gather(value, "dp", axis=0, tiled=True), later
     rows, count = value.shape
     line = jnp.stack([value, hop(value, 4), hop(value, 8), hop(value, 12)])
+    line, later = tie(line, later)
     index = lax.axis_index("dp")
     meta = jnp.stack([index // 4, index % 4]).astype(jnp.int32)
     spec = pl.BlockSpec((1, rows, count), lambda i, meta: (i ^ meta[0], 0, 0))
@@ -379,11 +770,11 @@
         ),
         out_shape=jax.ShapeDtypeStruct((4, 4, rows, count), value.dtype),
         cost_estimate=pl.CostEstimate(
-            flops=0, bytes_accessed=64 * rows * count, transcendentals=0
+            flops=(0) // LIGHT, bytes_accessed=(64 * rows * count) // LIGHT, transcendentals=0
         ),
         name="assemble",
     )(meta, line, hop(line, 1), hop(line, 2), hop(line, 3))
-    return full.reshape(16 * rows, count)
+    return full.reshape(16 * rows, count), later
 
 
 def total_of(parts):
@@ -416,6 +807,10 @@
     for unit in (1, 4):
         value = total_of([value] + [hop(value, unit * bits) for bits in (1, 2, 3)])
     return value
+
+
+def rows_at(value, ids):
+    return value.at[ids].get(mode="promise_in_bounds")
 
 
 def tie(*values):
@@ -458,7 +853,7 @@
     per_block = BLOCK // piece
 
     pair_ids = lax.dynamic_slice_in_dim(deal, 2 * dp_index, 2)
-    pair_len = jnp.take(lengths, pair_ids)
+    pair_len = rows_at(lengths, pair_ids)
     pieces_used = (pair_len + 2 * piece - 1) // (2 * piece)
     blocks_used = (pieces_used * piece + BLOCK - 1) // BLOCK
     first_blocks = blocks_used[0]
@@ -494,41 +889,44 @@
     send_valid = (send_pos < pair_len[None, :, None]).reshape(2 * dp_count, piece, 1)
     inverse = jnp.zeros_like(deal).at[deal].set(jnp.arange(deal.shape[0], dtype=jnp.int32))
 
-    def send_home(value):
+    def home_pieces(value):
         pieces = value.reshape(rows // piece, piece, width)
-        outgoing = jnp.where(
-            send_valid, jnp.take(pieces, send_ids.reshape(-1), axis=0), jnp.zeros((), value.dtype)
+        return jnp.where(
+            send_valid, rows_at(pieces, send_ids.reshape(-1)), jnp.zeros((), value.dtype)
         )
+
+    def go_home(outgoing):
         return lax.all_to_all(outgoing, "dp", split_axis=0, concat_axis=0, tiled=True)
 
     def order(value):
-        return jnp.take(value, deal, axis=0)
+        return rows_at(value, deal)
 
     def arrive(ordered):
         return lax.all_to_all(ordered, "dp", split_axis=0, concat_axis=0, tiled=True)
 
     def pack(arrived):
-        return jnp.take(arrived, piece_ids, axis=0).reshape(rows, width)
-
-    arrived = arrive(order(tokens))
+        return rows_at(arrived, piece_ids).reshape(rows, width)
+
+    qkv_own, ordered = quick_gather(self_project.reshape(shard, 3 * half), order(tokens))
+    qkv_weight = (qkv_own, swap(qkv_own))
+    arrived = arrive(ordered)
     ordered_cot, arrived = tie(order(cotangent), arrived)
     inputs = pack(arrived)
     arrived_cot = arrive(ordered_cot)
 
     quick = dp_count == 16
 
-    def gather(value):
-        own = lax.all_gather(value, "dp", axis=0, tiled=True)
-        return (own, swap(own))
-
-    qkv_own = quick_gather(self_project.reshape(shard, 3 * half))
-    qkv_weight = (qkv_own, swap(qkv_own))
-    mid_weight = gather(
+    mid_own = lax.all_gather(
         jnp.concatenate(
             [self_output.T, cross_query, cross_memory.reshape(shard, 2 * half), cross_output.T], 1
-        )
-    )
-    ffn_weight = gather(jnp.concatenate([hidden_in, hidden_out.T], 1))
+        ),
+        "dp",
+        axis=0,
+        tiled=True,
+    )
+    ffn_own = lax.all_gather(
+        jnp.concatenate([hidden_in, hidden_out.T], 1), "dp", axis=0, tiled=True
+    )
     both = (0, 1)
 
     def columns(pair, start, count):
@@ -537,20 +935,10 @@
     project_q = columns(qkv_weight, 0, half)
     project_k = columns(qkv_weight, half, half)
     project_v = columns(qkv_weight, 2 * half, half)
-    self_out = columns(mid_weight, 0, half)
-    query_w = columns(mid_weight, half, half)
-    memory_k = columns(mid_weight, 2 * half, half)
-    memory_v = columns(mid_weight, 3 * half, half)
-    cross_out = columns(mid_weight, 4 * half, half)
-    expand = columns(ffn_weight, 0, units)
-    reduce = columns(ffn_weight, units, units)
-
     biases = jnp.concatenate([in_bias.reshape(-1), hidden_bias])
     bias_pair = (biases, swap(biases))
     in_pair = [b[: 4 * half].reshape(4, half) for b in bias_pair]
     hidden_pair = [b[4 * half :] for b in bias_pair]
-
-    cot = jnp.where(row_valid, pack(arrived_cot), jnp.zeros((), BF16)).astype(F32)
 
     memory_full = jnp.concatenate([encoder, swap(encoder)], 1).reshape(4 * memory_rows, width)
 
@@ -569,23 +957,18 @@
         )
         attn.append(result[0])
         lse.append(result[1])
-    branch = dot_nt(attn[0], self_out[0]) + dot_nt(attn[1], self_out[1]) + out_bias[0]
-    n1, unit1, scale1 = norm_forward(inputs.astype(F32) + branch, norm_gain[0], norm_bias[0])
-    cross_in = n1.astype(BF16)
-    cqs = [
-        ((dot_nn(cross_in, query_w[h]) + in_pair[h][2]) * score_scale).astype(BF16) for h in both
-    ]
-    cks = [dot_nn(memory_full, memory_k[h]).astype(BF16) for h in both]
-    cvs = [(dot_nn(memory_full, memory_v[h]) + in_pair[h][3]).astype(BF16) for h in both]
-    cattn = []
-    clse = []
-    for h in both:
-        result = attend_forward(meta, cqs[h], [cks[h]], [cvs[h]], False, piece, spans)
-        cattn.append(result[0])
-        clse.append(result[1])
-    branch = dot_nt(cattn[0], cross_out[0]) + dot_nt(cattn[1], cross_out[1]) + out_bias[1]
-    n2, unit2, scale2 = norm_forward(n1 + branch, norm_gain[1], norm_bias[1])
-    hidden = n2.astype(BF16)
+        if h == 0:
+            mid_own, attn[0] = tie(mid_own, attn[0])
+            mid_weight = (mid_own, swap(mid_own))
+    saved, cqs, cattn, cks, cvs = mid_forward(
+        meta, inputs, attn, memory_full, mid_weight, in_pair, out_bias, norm_gain, norm_bias, score_scale
+    )
+    unit1, scale1, unit2, scale2, cross_in, hidden, clse = saved
+    ffn_own, hidden, arrived_cot = tie(ffn_own, hidden, arrived_cot)
+    ffn_weight = (ffn_own, swap(ffn_own))
+    expand = columns(ffn_weight, 0, units)
+    reduce = columns(ffn_weight, units, units)
+    n2 = unit2 * norm_gain[1] + norm_bias[1]
     act = []
     slope = []
     for h in both:
@@ -595,8 +978,11 @@
         density = jnp.exp(-0.5 * pre * pre) * (1.0 / math.sqrt(2.0 * math.pi))
         slope.append((phi + pre * density).astype(BF16))
     branch = dot_nt(act[0], reduce[0]) + dot_nt(act[1], reduce[1]) + out_bias[2]
-    n3, unit3, scale3 = norm_forward(n2 + branch, norm_gain[2], norm_bias[2])
-    output_back = send_home(n3.astype(BF16))
+    n3, dz, dn2, sums3, du0, du1, usum0, usum1 = ffn_backward(
+        n2 + branch, pack(arrived_cot), row_valid.astype(F32), slope, ffn_weight, norm_gain, norm_bias
+    )
+    du = (du0, du1)
+    output_back = go_home(home_pieces(n3))
 
     low_meta = jnp.reshape(dp_index % 4, (1,)).astype(jnp.int32)
 
@@ -604,61 +990,33 @@
         far = weight_grads(low_meta, lefts, rights[1], sides, factors, None, grouped)
         return weight_grads(low_meta, lefts, rights[0], sides, factors, swap(far), grouped)
 
-    dh3, gain3, shift3 = norm_backward(cot, unit3, scale3, norm_gain[2])
-    dz = dh3.astype(BF16)
-    du = [(dot_nn(dz, reduce[h]) * slope[h].astype(F32)).astype(BF16) for h in both]
     ffn_grads = chip_grads(
         [hidden, dz], [[du[h], act[h]] for h in both], (0, 1), (1.0, 1.0), False
     )
-    dn2 = dh3 + dot_nt(du[0], expand[0]) + dot_nt(du[1], expand[1])
-    dh2, gain2, shift2 = norm_backward(dn2, unit2, scale2, norm_gain[1])
-    dy2 = dh2.astype(BF16)
-    dca = [dot_nn(dy2, cross_out[h]).astype(BF16) for h in both]
-    ffn_grads, dca[0] = tie(ffn_grads, dca[0])
+    ffn_grads, dn2 = tie(ffn_grads, dn2)
     ffn_shard = slow_scatter(ffn_grads)
-    dcq = []
-    dck = []
-    dcv = []
-    for h in both:
-        result = attend_backward(
-            meta, cqs[h], dca[h], clse[h], [cks[h]], [cvs[h]], False, piece, spans, [F32]
-        )
-        dcq.append(result[0])
-        dck.append(result[1][0].reshape(2, 2, memory_rows, half))
-        dcv.append(result[2][0].reshape(2, 2, memory_rows, half))
-    dck_sum = [
-        (dck[h][:, 0] + swap(dck[1 - h][:, 1].astype(BF16)).astype(F32))
-        .astype(BF16)
-        .reshape(2 * memory_rows, half)
-        for h in both
-    ]
-    dcv_sum = [
-        (dcv[h][:, 0] + swap(dcv[1 - h][:, 1].astype(BF16)).astype(F32))
-        .astype(BF16)
-        .reshape(2 * memory_rows, half)
-        for h in both
-    ]
+    rows_back, dcq, da, memory_near, memory_far = mid_backward(
+        meta, dn2, (unit1, scale1, unit2, scale2, clse), cqs, cks, cvs, mid_weight, norm_gain, score_scale
+    )
+    dy2, dh1, dy, sums = rows_back
+    da = list(da)
+    memory_far, output_back = tie(memory_far, output_back)
+    memory_sum, grad_memory, memory_bias = memory_backward(
+        memory_near, swap(memory_far), mid_weight
+    )
+    grad_encoder = grad_memory.reshape(2, memory_rows, width)
     memory_own = encoder.reshape(2 * memory_rows, width)
-    grad_memory = (
-        dot_nt(dck_sum[0], memory_k[0])
-        + dot_nt(dck_sum[1], memory_k[1])
-        + dot_nt(dcv_sum[0], memory_v[0])
-        + dot_nt(dcv_sum[1], memory_v[1])
-    )
-    grad_encoder = grad_memory.astype(BF16).reshape(2, memory_rows, width)
-    dn1 = dh2 + (dot_nt(dcq[0], query_w[0]) + dot_nt(dcq[1], query_w[1])) * score_scale
-    dh1, gain1, shift1 = norm_backward(dn1, unit1, scale1, norm_gain[0])
-    dy = dh1.astype(BF16)
-    da = [dot_nn(dy, self_out[h]).astype(BF16) for h in both]
     mid_grads = chip_grads(
         [dy, cross_in, memory_own, dy2],
-        [[attn[h], dcq[h], dck_sum[h], dcv_sum[h], cattn[h]] for h in both],
+        [
+            [attn[h], dcq[h], (memory_sum, h), (memory_sum, 2 + h), cattn[h]]
+            for h in both
+        ],
         (0, 1, 2, 2, 3),
         (1.0, score_scale, 1.0, 1.0, 1.0),
         quick,
     )
-    mid_grads, da[0], output_back = tie(mid_grads, da[0], output_back)
-    output = jnp.take(output_back, inverse, axis=0)
+    mid_grads, da[0], da[1] = tie(mid_grads, da[0], da[1])
     mid_line = scatter_low(mid_grads) if quick else None
     dq = []
     dk = []
@@ -676,36 +1034,36 @@
             spans,
             [F32, BF16],
         )
-        if h == 0 and quick:
-            mid_line, dq_first = tie(mid_line, result[0])
-            result = (dq_first, result[1], result[2])
-            da[1], mid_line = tie(da[1], mid_line)
         dq.append(result[0])
         dk.append(result[1])
         dv.append(result[2])
-    mid_shard = scatter_plane(mid_line) if quick else slow_scatter(mid_grads)
-    dk = [(dk[h][0] + swap(dk[1 - h][1]).astype(F32)).astype(BF16) for h in both]
-    dv = [(dv[h][0] + swap(dv[1 - h][1]).astype(F32)).astype(BF16) for h in both]
-    qkv_grads = chip_grads(
-        [inputs],
-        [[dq[h], dk[h], dv[h]] for h in both],
-        (0, 0, 0),
-        (score_scale, 1.0, 1.0),
-        quick,
-    )
-    qkv_shard = scatter_plane(scatter_low(qkv_grads)) if quick else slow_scatter(qkv_grads)
-    grad_inputs = (
-        dh1
-        + (dot_nt(dq[0], project_q[0]) + dot_nt(dq[1], project_q[1])) * score_scale
-        + dot_nt(dk[0], project_k[0])
-        + dot_nt(dk[1], project_k[1])
-        + dot_nt(dv[0], project_v[0])
-        + dot_nt(dv[1], project_v[1])
-    )
-    grad_tokens = jnp.take(send_home(grad_inputs.astype(BF16)), inverse, axis=0)
-
-    def rows_sum(value):
-        return jnp.sum(value, 0, dtype=F32)
+    factors = (score_scale, 1.0, 1.0)
+    near = [swap(dk[1][1]), swap(dv[1][1])]
+    if quick:
+        mid_line, dh1 = tie(mid_line, dh1)
+        mid_shard = scatter_plane(mid_line)
+    else:
+        mid_shard = slow_scatter(mid_grads)
+    dx_far, dk_far, dv_far, sums_far = input_backward(
+        dh1, dq[1], dk[1][0], swap(dk[0][1]), dv[1][0], swap(dv[0][1]), qkv_weight[1], score_scale, F32
+    )
+    far_grads = weight_grads(
+        low_meta, [inputs], [dq[1], dk_far, dv_far], (0, 0, 0), factors, None, quick
+    )
+    far_grads, dx_far, near[0], near[1], mid_shard = tie(far_grads, dx_far, *near, mid_shard)
+    far_grads = swap(far_grads)
+    dx, dk_near, dv_near, sums_near = input_backward(
+        dx_far, dq[0], dk[0][0], near[0], dv[0][0], near[1], qkv_weight[0], score_scale, BF16
+    )
+    grad_out = home_pieces(dx)
+    grad_out, far_grads, output_back = tie(grad_out, far_grads, output_back)
+    output = rows_at(output_back, inverse)
+    grad_back = go_home(grad_out)
+    far_grads, ffn_shard = tie(far_grads, ffn_shard)
+    qkv_grads = weight_grads(
+        low_meta, [inputs], [dq[0], dk_near, dv_near], (0, 0, 0), factors, far_grads, quick
+    )
+    sums_qkv = [sums_near, sums_far]
 
     def global_order(pair):
         own_first = jnp.concatenate(pair, -1)
@@ -716,30 +1074,36 @@
         [
             jnp.stack(
                 [
-                    score_scale * rows_sum(dq[h]),
-                    rows_sum(dv[h]),
-                    score_scale * rows_sum(dcq[h]),
-                    rows_sum(dcv_sum[h]),
+                    sums_qkv[h][0],
+                    sums_qkv[h][1],
+                    score_scale * sums[6, h * half : (h + 1) * half],
+                    memory_bias[0, h * half : (h + 1) * half],
                 ]
             )
             for h in both
         ]
     )
-    hidden_row = global_order([rows_sum(du[h]) for h in both])
-    out_rows = jnp.stack([rows_sum(dy), rows_sum(dy2), rows_sum(dz)])
-    gain_rows = jnp.stack([gain1, gain2, gain3])
-    shift_rows = jnp.stack([shift1, shift2, shift3])
-    small = sum_everywhere(
-        jnp.concatenate(
-            [
-                in_rows.reshape(-1),
-                hidden_row,
-                out_rows.reshape(-1),
-                gain_rows.reshape(-1),
-                shift_rows.reshape(-1),
-            ]
-        )
-    )
+    hidden_row = global_order([usum0[0], usum1[0]])
+    out_rows = jnp.stack([sums[5], sums[2], sums3[2]])
+    gain_rows = jnp.stack([sums[3], sums[0], sums3[0]])
+    shift_rows = jnp.stack([sums[4], sums[1], sums3[1]])
+    small = jnp.concatenate(
+        [
+            in_rows.reshape(-1),
+            hidden_row,
+            out_rows.reshape(-1),
+            gain_rows.reshape(-1),
+            shift_rows.reshape(-1),
+        ]
+    )
+    small, qkv_grads = tie(small, qkv_grads)
+    small = sum_everywhere(small)
+    if quick:
+        qkv_line, grad_back = tie(scatter_low(qkv_grads), grad_back)
+        qkv_shard = scatter_plane(qkv_line)
+    else:
+        qkv_shard = slow_scatter(qkv_grads)
+    grad_tokens = rows_at(grad_back, inverse)
     in_end = 8 * half
     hidden_end = in_end + 2 * units
     in_total = small[:in_end].reshape(4, 2 * half)

time: 610 us -> 535 us (0.88)
  matrix products: 117 us -> 32 us
  other arithmetic: 64.5 us -> 21.2 us
  Pallas kernels: 154 us -> 196 us
  starting transfers between devices: 68.1 us -> 84.4 us
  local copies, waits for them, and re-layouts: 61.7 us -> 51 us
    pallas_call x0 -> x6, Pallas kernels: none -> 83.3 us  [the longest x1 25.8 us: mid_backward(): pl.pallas_call(functools.partial(mid_backward_kernel, score_scale, rows),...]
    dot_general x20 -> x2, matrix products: 52.8 us -> 8.94 us  [dot_nt(): lax.dot_general(left, right, (((1,), (1,)), ((), ())), preferred_element_...]
    dot_general x20 -> x8, matrix products: 64.3 us -> 23.1 us  [dot_nn(): lax.dot_general(left, right, (((1,), (0,)), ((), ())), preferred_element_...]
    ppermute x24, waiting for transfers between devices: 89.6 us -> 68.2 us  [hop(): return lax.ppermute(value, 'dp', [(i, i ^ bits) for i in range(16)])]
    reduce_sum x16 -> x0, other arithmetic: 20.4 us -> none  [the longest x11 14.7 us: rows_sum(): return jnp.sum(value, 0, dtype=F32)]
    pallas_call x4 -> x2, Pallas kernels: 51.5 us -> 34.1 us  [attend_backward(): pl.pallas_call(functools.partial(backward_kernel, parts, pairs, causal, p...]
    pallas_call x4 -> x2, Pallas kernels: 39.5 us -> 23.5 us  [attend_forward(): pl.pallas_call(functools.partial(forward_kernel, parts, pairs, causal, pi...]
    ppermute x24, starting transfers between devices: 34.7 us -> 48.5 us  [hop(): return lax.ppermute(value, 'dp', [(i, i ^ bits) for i in range(16)])]
  transfers between devices with their start and end apart: 52 -> 49, of which waited for: 11 -> 18; matrix products, arithmetic and copies ran while one was open for 35% -> 16% of each run, Pallas kernels for 24% -> 32%
where the time goes in v3:
time: 535 us; the launch traced here: 524 us
  Pallas kernels  196 us (37%)
  waiting for transfers between devices  122 us (23%)
  starting transfers between devices  84.4 us (16%)
  local copies, waits for them, and re-layouts  51 us (10%)
  matrix products  32 us (6%)
  other arithmetic  21.2 us (4%)
  between operations  17.6 us (3%)
    ppermute x24, waiting for transfers between devices, hop(): return lax.ppermute(value, 'dp', [(i, i ^ bits) for i in range(16)])  68.2 us
    pallas_call x6, Pallas kernels, weight_grads(): pl.pallas_call(functools.partial(grads_kernel, sides, counts, factors, ex...  51.2 us
    ppermute x24, starting transfers between devices, hop(): return lax.ppermute(value, 'dp', [(i, i ^ bits) for i in range(16)])  48.5 us
    pallas_call x2, Pallas kernels, attend_backward(): pl.pallas_call(functools.partial(backward_kernel, parts, pairs, causal, p...  34.1 us
    all_gather x1, waiting for transfers between devices, body(): lax.all_gather(jnp.concatenate([hidden_in, hidden_out.T], 1), 'dp', axis=...  32.2 us
    pallas_call x1, Pallas kernels, mid_backward(): pl.pallas_call(functools.partial(mid_backward_kernel, score_scale, rows),...  25.8 us
    pallas_call x2, Pallas kernels, attend_forward(): pl.pallas_call(functools.partial(forward_kernel, parts, pairs, causal, pi...  23.5 us
    dot_general x8, matrix products, dot_nn(): lax.dot_general(left, right, (((1,), (0,)), ((), ())), preferred_element_...  23.1 us
  transfers between devices with their start and end apart: 49, of which 18 were waited for; matrix products, arithmetic and copies ran while one was open for 16% of the time, Pallas kernels for 32%

profile of v3, /device:TPU:0, one launch (start us, length us, event | category | flops | bytes accessed | tf_op | source)
XLA Modules:
  0.0 524.4 jit_solution(2334549162270790877)
XLA Ops:
  9.8 1.7 pad_maximum_fusion.2
  12.5 3.1 collective-permute-start
  15.6 2.6 collective-permute-start.1
  18.4 1.8 gather_fusion.2
  20.2 7.2 %collective-permute-done.1 = bf16[48,1152]{1,0:T(8,128)(2,1)S(1)} collective-permute-done((bf16[48,1152]{1,0:T(8,128)(2,1)S(1)}, bf16[48,1152]{1,0:T(8,128)(2,1)S(1)}, u32[]{:S(2)}, u32[]{:S(2)}) %collective-permute-start.1) | collective-permute-done | bytes 110624 | tf_op jit(solution)/shard_map/ppermute | solution.py:746
  27.5 7.7 %all-to-all-start = ((bf16[32,32,768]{2,1,0:T(8,128)(2,1)}), bf16[32,32,768]{2,1,0:T(8,128)(2,1)}, u32[]{:S(2)}, u32[]{:S(2)}) async-start(bf16[32,32,768]{2,1,0:T(8,128)(2,1)} %gather_fusion.2), calls=%async_computation | async-start | bytes 3145728 | tf_op jit(solution)/shard_map/all_to_all | solution.py:905
  35.2 1.9 collective-permute-start.3
  39.5 26.7 %collective-permute-done.3.first_ref = bf16[4,48,1152]{2,1,0:T(8,128)(2,1)S(1)} collective-permute-done((bf16[4,48,1152]{2,1,0:T(8,128)(2,1)S(1)}, bf16[4,48,1152]{2,1,0:T(8,128)(2,1)S(1)}, u32[]{:S(2)}, u32[]{:S(2)}) %collective-permute-start.3) | collective-permute-done | bytes 442400 | tf_op jit(solution)/shard_map/ppermute | solution.py:746
  66.2 17.4 %collective-permute-done.5.third_ref = bf16[4,48,1152]{2,1,0:T(8,128)(2,1)S(1)} collective-permute-done((bf16[4,48,1152]{2,1,0:T(8,128)(2,1)S(1)}, bf16[4,48,1152]{2,1,0:T(8,128)(2,1)S(1)}, u32[]{:S(2)}, u32[]{:S(2)}) %collective-permute-start.5) | collective-permute-done | bytes 442400 | tf_op jit(solution)/shard_map/ppermute | solution.py:746
  84.4 4.4 assemble.1
  94.3 3.2 gather_fusion.1
  97.5 2.0 gather_fusion.3
  102.3 1.7 convolution_convert_fusion.1.refs_0_
  104.1 1.7 fusion.23.refs_2_
  105.8 1.7 fusion.25.q_ref
  108.4 11.7 %attend_forward.2 = (bf16[896,384]{1,0:T(8,128)(2,1)}, f32[7,8,256]{2,1,0:T(8,128)}) custom-call(s32[3]{0:T(128)} %pad_add_fusion.meta, bf16[896,384]{1,0:T(8,128)(2,1)} %fusion.25.q_ref, bf16[896,384]{1,0:T(8,128)(2,1)} %convolution_convert_fusion.1.refs_0_, bf16[896,384]{1,0:T(8,128)(2,1)} %collective-permute-done.8.refs_1_, ...), custom_call_target="tpu_custom_call" | custom-call | flops 5637144 | bytes 2752 | tf_op jit(solution)/shard_map/attend_forward/pallas_call | solution.py:210
  120.7 4.9 all-to-all-start.1
  129.2 3.2 fusion.26.q_ref
  132.4 11.7 %attend_forward.3 = (bf16[896,384]{1,0:T(8,128)(2,1)}, f32[7,8,256]{2,1,0:T(8,128)}) custom-call(s32[3]{0:T(128)} %pad_add_fusion.meta, bf16[896,384]{1,0:T(8,128)(2,1)} %fusion.26.q_ref, bf16[896,384]{1,0:T(8,128)(2,1)} %copy-done.29, bf16[896,384]{1,0:T(8,128)(2,1)} %collective-permute-done.10.refs_1_, bf16[896,384]{1,0:T(8,128)(2,1)} %copy-done.28, ...), custom_call_target="tpu_custom_call" | custom-call | flops 5637144 | bytes 2752 | tf_op jit(solution)/shard_map/attend_forward/pallas_call | solution.py:210
  145.7 22.0 %mid_forward.1 = (f32[896,768]{1,0:T(8,128)}, f32[896,1]{1,0:T(8,128)}, f32[896,768]{1,0:T(8,128)}, f32[896,1]{1,0:T(8,128)}, bf16[896,768]{1,0:T(8,128)(2,1)}, ...) custom-call(s32[3]{0:T(128)} %pad_add_fusion.meta, ...), custom_call_target="tpu_custom_call" | custom-call | flops 6341787 | bytes 13762 | tf_op jit(solution)/shard_map/mid_forward/pallas_call | solution.py:616
  167.7 4.4 all-to-all-done.1
  172.2 32.2 %all-gather.3.cloned.1.call-done.in0.out0 = bf16[768,3072]{1,0:T(8,128)(2,1)} async-done(((bf16[48,3072]{1,0:T(8,128)(2,1)}), bf16[768,3072]{1,0:T(8,128)(2,1)}) %all-gather.3.cloned.1.call-update) | async-done | bytes 4718608 | tf_op jit(solution)/shard_map/all_gather | solution.py:927
  205.0 1.9 compare_select_fusion.5
  210.7 3.2 gather_fusion.4
  213.9 6.6 %fusion.4 = (bf16[896,1536]{1,0:T(8,128)(2,1)}, bf16[896,1536]{1,0:T(8,128)(2,1)S(1)}) fusion(f32[1536]{0:T(1024)S(1)} %copy-done.27, bf16[896,768]{1,0:T(8,128)(2,1)S(1)} %copy-done.8, bf16[768,3072]{1,0:T(8,128)(2,1)} %all-gather.3.cloned.1.call-done.in0.out0), kind=kOutput, calls=%fused_computation.16 | convolution fusion | flops 2130444288 | bytes 9246720 | tf_op jit(solution)/shard_map/dot_general | solution.py:23
  220.5 2.3 fusion.14
  222.9 6.4 %fusion.9 = (bf16[896,1536]{1,0:T(8,128)(2,1)}, bf16[896,1536]{1,0:T(8,128)(2,1)S(1)}) fusion(f32[1536]{0:T(1024)S(1)} %get-tuple-element.296, bf16[896,768]{1,0:T(8,128)(2,1)S(1)} %copy-done.8, bf16[768,3072]{1,0:T(8,128)(2,1)} %collective-permute-done.14.in1.out1), kind=kOutput, calls=%fused_computation.21 | convolution fusion | flops 2130444288 | bytes 9246720 | tf_op jit(solution)/shard_map/dot_general | solution.py:23
  229.2 6.6 %add_add_fusion.h3_ref = f32[896,768]{1,0:T(8,128)} fusion(f32[896,768]{1,0:T(8,128)S(1)} %fusion.14, f32[896,768]{1,0:T(8,128)S(1)} %copy-done.11, f32[768]{0:T(1024)S(1)} %get-tuple-element.308, f32[768]{0:T(1024)S(1)} %get-tuple-element.309, f32[768]{0:T(1024)S(1)} %slice_reduce_fusion.4, bf16[896,1536]{1,0:T(8,128)(2,1)S(1)} %get-tuple-element.258.refs_3_, ...), kind=kOutput, calls=%fused_computation.26 | convolution fusion | flops 2117369856 | bytes 13378560 | tf_op jit(solution)/shard_map/dot_general | solution.py:27
  235.8 18.4 %ffn_backward.1 = (bf16[896,768]{1,0:T(8,128)(2,1)}, bf16[896,768]{1,0:T(8,128)(2,1)}, f32[896,768]{1,0:T(8,128)}, f32[8,768]{1,0:T(8,128)}, bf16[896,1536]{1,0:...) custom-call(f32[896,768]{1,0:T(8,128)} %add_add_fusion.h3_ref, ...), custom_call_target="tpu_custom_call" | custom-call | flops 1000 | bytes 1000 | tf_op jit(solution)/shard_map/ffn_backward/pallas_call | solution.py:576
  254.3 10.1 %weight_grads.6 = bf16[768,3072]{1,0:T(8,128)(2,1)} custom-call(s32[1]{0:T(128)} %bitcast.1.meta, bf16[896,768]{1,0:T(8,128)(2,1)} %get-tuple-element.114.refs_0_, bf16[896,768]{1,0:T(8,128)(2,1)} %get-tuple-element.118.refs_1_, bf16[896,1536]{1,0:T(8,128)(2,1)} %get-tuple-element.120.refs_2_, bf16[896,1536]{1,0:T(8,128)(2,1)} %copy-done.10), custom_call_target="tpu_custom_call" | custom-call | flops 4227858 | bytes 16515 | tf_op jit(solution)/shard_map/weight_grads/pallas_call | solution.py:315
  269.3 3.7 all-to-all-start.2
  273.1 11.2 %weight_grads.7 = bf16[768,3072]{1,0:T(8,128)(2,1)} custom-call(s32[1]{0:T(128)} %bitcast.1.meta, bf16[896,768]{1,0:T(8,128)(2,1)} %get-tuple-element.114.refs_0_, bf16[896,768]{1,0:T(8,128)(2,1)} %get-tuple-element.118.refs_1_, bf16[896,1536]{1,0:T(8,128)(2,1)} %get-tuple-element.119.refs_2_, bf16[896,1536]{1,0:T(8,128)(2,1)} %copy-done.9, ...), custom_call_target="tpu_custom_call" | custom-call | flops 4227858 | bytes 16515 | tf_op jit(solution)/shard_map/weight_grads/pallas_call | solution.py:315
  284.2 25.8 %mid_backward.1 = (bf16[896,768]{1,0:T(8,128)(2,1)}, f32[896,768]{1,0:T(8,128)}, bf16[896,768]{1,0:T(8,128)(2,1)}, f32[8,768]{1,0:T(8,128)}, bf16[896,384]{1,0:T...) custom-call(s32[3]{0:T(128)} %pad_add_fusion.meta, ...), custom_call_target="tpu_custom_call" | custom-call | flops 6341787 | bytes 13762 | tf_op jit(solution)/shard_map/mid_backward/pallas_call | solution.py:659
  310.0 5.2 all-to-all-done.2
  315.2 1.9 collective-permute-done.16.got_ref
  317.9 3.5 memory_backward.1
  321.4 8.2 %weight_grads.8 = bf16[4,4,48,1920]{3,2,1,0:T(8,128)(2,1)} custom-call(s32[1]{0:T(128)} %bitcast.1.meta, bf16[896,768]{1,0:T(8,128)(2,1)} %get-tuple-element.133.refs_0_, bf16[896,768]{1,0:T(8,128)(2,1)} %get-tuple-element.134.refs_1_, bf16[128,768]{1,0:T(8,128)(2,1)} %bitcast.156, bf16[896,768]{1,0:T(8,128)(2,1)} %get-tuple-element.135.refs_3_, ...), custom_call_target="tpu_custom_call" | custom-call | flops 2642411 | bytes 10321 | tf_op jit(solution)/shard_map/weight_grads/pallas_call | solution.py:315
  329.9 5.5 %collective-permute-done.17.refs_9_ = bf16[4,4,48,1920]{3,2,1,0:T(8,128)(2,1)} collective-permute-done((bf16[4,4,48,1920]{3,2,1,0:T(8,128)(2,1)}, bf16[4,4,48,1920]{3,2,1,0:T(8,128)(2,1)}, u32[]{:S(2)}, u32[]{:S(2)}) %collective-permute-start.17) | collective-permute-done | bytes 2949152 | tf_op jit(solution)/shard_map/ppermute | solution.py:742
  335.3 9.3 %weight_grads.9 = bf16[4,4,48,1920]{3,2,1,0:T(8,128)(2,1)} custom-call(s32[1]{0:T(128)} %bitcast.1.meta, bf16[896,768]{1,0:T(8,128)(2,1)} %get-tuple-element.133.refs_0_, bf16[896,768]{1,0:T(8,128)(2,1)} %get-tuple-element.134.refs_1_, bf16[128,768]{1,0:T(8,128)(2,1)} %bitcast.157, bf16[896,768]{1,0:T(8,128)(2,1)} %get-tuple-element.135.refs_3_, ...), custom_call_target="tpu_custom_call" | custom-call | flops 2642411 | bytes 10321 | tf_op jit(solution)/shard_map/weight_grads/pallas_call | solution.py:315
  344.7 3.0 slice_bitcast_fusion.2
  349.1 3.4 collective-permute-start.19
  355.3 16.9 %attend_backward.3 = (bf16[896,384]{1,0:T(8,128)(2,1)}, f32[896,384]{1,0:T(8,128)}, bf16[896,384]{1,0:T(8,128)(2,1)}, f32[896,384]{1,0:T(8,128)}, bf16[896,384]{1,0:T(8,128)(2,1)}) custom-call(s32[3]{0:T(128)} %pad_add_fusion.meta, bf16[896,384]{1,0:T(8,128)(2,1)} %fusion.25.q_ref, bf16[896,384]{1,0:T(8,128)(2,1)} %get-tuple-element.154.g_ref, ...), custom_call_target="tpu_custom_call" | custom-call | flops 14092861 | bytes 5505 | tf_op jit(solution)/shard_map/attend_backward/pallas_call | solution.py:236
  372.7 17.1 %attend_backward.2 = (bf16[896,384]{1,0:T(8,128)(2,1)}, f32[896,384]{1,0:T(8,128)}, bf16[896,384]{1,0:T(8,128)(2,1)}, f32[896,384]{1,0:T(8,128)}, bf16[896,384]{1,0:T(8,128)(2,1)}) custom-call(s32[3]{0:T(128)} %pad_add_fusion.meta, bf16[896,384]{1,0:T(8,128)(2,1)} %fusion.26.q_ref, bf16[896,384]{1,0:T(8,128)(2,1)} %get-tuple-element.147.g_ref, ...), custom_call_target="tpu_custom_call" | custom-call | flops 14092861 | bytes 5505 | tf_op jit(solution)/shard_map/attend_backward/pallas_call | solution.py:236
  391.6 1.9 fusion.20
  393.6 7.3 %collective-permute-start.25 = (bf16[48,1920]{1,0:T(8,128)(2,1)S(1)}, bf16[48,1920]{1,0:T(8,128)(2,1)S(1)}, u32[]{:S(2)}, u32[]{:S(2)}) collective-permute-start(bf16[48,1920]{1,0:T(8,128)(2,1)S(1)} %get-tuple-element.267), channel_id=1, source_target_pairs={{0,8},{2,10},{4,12},{6,14},{8,0},{10,2},{12,4},{14,6},{16,24},{18,... | collective-permute-start | bytes 552968 | tf_op jit(solution)/shard_map/ppermute | solution.py:746
  400.8 2.4 collective-permute-start.27
  404.1 7.1 %input_backward.2 = (f32[896,768]{1,0:T(8,128)}, bf16[896,384]{1,0:T(8,128)(2,1)}, bf16[896,384]{1,0:T(8,128)(2,1)}, f32[8,384]{1,0:T(8,128)}) custom-call(f32[896,768]{1,0:T(8,128)} %get-tuple-element.152.base_ref, bf16[896,384]{1,0:T(8,128)(2,1)} %get-tuple-element.149.dq_ref.refs_1_, f32[896,384]{1,0:T(8,128)} %get-tuple-element.153.dk_own, ...), custom_call_target="tpu_custom_call" | custom-call | flops 1585446 | bytes 8257 | tf_op jit(solution)/shard_map/input_backward/pallas_call | solution.py:721
  411.3 6.1 %weight_grads.10 = bf16[4,4,48,1152]{3,2,1,0:T(8,128)(2,1)} custom-call(s32[1]{0:T(128)} %bitcast.1.meta, bf16[896,768]{1,0:T(8,128)(2,1)} %bitcast.149, bf16[896,384]{1,0:T(8,128)(2,1)} %get-tuple-element.149.dq_ref.refs_1_, bf16[896,384]{1,0:T(8,128)(2,1)} %get-tuple-element.159.refs_2_, bf16[896,384]{1,0:T(8,128)(2,1)} %get-tuple-element.160.refs_3_), custom_call_target="tpu_custom_call" | custom-call | flops 1585446 | bytes 6193 | tf_op jit(solution)/shard_map/weight_grads/pallas_call | solution.py:315
  417.4 5.3 %collective-permute-done.26 = bf16[48,1920]{1,0:T(8,128)(2,1)S(1)} collective-permute-done((bf16[48,1920]{1,0:T(8,128)(2,1)S(1)}, bf16[48,1920]{1,0:T(8,128)(2,1)S(1)}, u32[]{:S(2)}, u32[]{:S(2)}) %collective-permute-start.26) | collective-permute-done | bytes 184352 | tf_op jit(solution)/shard_map/ppermute | solution.py:746
  425.1 6.4 %input_backward.3 = (bf16[896,768]{1,0:T(8,128)(2,1)}, bf16[896,384]{1,0:T(8,128)(2,1)}, bf16[896,384]{1,0:T(8,128)(2,1)}, f32[8,384]{1,0:T(8,128)}) custom-call(f32[896,768]{1,0:T(8,128)} %get-tuple-element.165.base_ref, bf16[896,384]{1,0:T(8,128)(2,1)} %get-tuple-element.166.dq_ref.refs_1_, f32[896,384]{1,0:T(8,128)} %get-tuple-element.167.dk_own, ...), custom_call_target="tpu_custom_call" | custom-call | flops 1585446 | bytes 8257 | tf_op jit(solution)/shard_map/input_backward/pallas_call | solution.py:721
  431.5 2.0 gather_fusion.6
  435.7 16.1 %all-to-all-start.3 = ((bf16[32,32,768]{2,1,0:T(8,128)(2,1)}), bf16[32,32,768]{2,1,0:T(8,128)(2,1)}, u32[]{:S(2)}, u32[]{:S(2)}) async-start(bf16[32,32,768]{2,1,0:T(8,128)(2,1)} %broadcast_select_fusion), calls=%async_computation.4 | async-start | bytes 3145728 | tf_op jit(solution)/shard_map/all_to_all | solution.py:899
  451.8 2.6 reduce-scatter.2.cloned.1.call-done
  454.4 1.9 convert_element_type.135
  456.3 6.4 %weight_grads.11 = bf16[4,4,48,1152]{3,2,1,0:T(8,128)(2,1)} custom-call(s32[1]{0:T(128)} %bitcast.1.meta, bf16[896,768]{1,0:T(8,128)(2,1)} %bitcast.150, bf16[896,384]{1,0:T(8,128)(2,1)} %get-tuple-element.166.dq_ref.refs_1_, bf16[896,384]{1,0:T(8,128)(2,1)} %get-tuple-element.182.refs_2_, bf16[896,384]{1,0:T(8,128)(2,1)} %get-tuple-element.183.refs_3_, ...), custom_call_target="tpu_custom_call" | custom-call | flops 1585446 | bytes 6193 | tf_op jit(solution)/shard_map/weight_grads/pallas_call | solution.py:315
  464.1 1.8 gather_fusion.7
  473.8 4.0 collective-permute-done.36
  478.2 1.8 collective-permute-start.39
  480.0 7.3 %collective-permute-start.40 = (f32[13056]{0:T(1024)S(1)}, f32[13056]{0:T(1024)S(1)}, u32[]{:S(2)}, u32[]{:S(2)}) collective-permute-start(f32[13056]{0:T(1024)S(1)} %add_add_fusion.2), channel_id=1, source_target_pairs={{0,16},{2,18},{4,20},{6,22},{8,24},{10,26},{12,28},{14,30},{16,0},... | collective-permute-start | bytes 156680 | tf_op jit(solution)/shard_map/ppermute | solution.py:746
  489.5 1.9 collective-permute-start.31
  491.5 2.0 collective-permute-done.40
  504.2 4.0 collective-permute-start.33
  509.5 3.2 gather_fusion.8
  512.7 4.0 collective-permute-done.34
  (251 shorter events, 66.0 us)
Async XLA Ops:
  7.2 11.2 %copy-start = (bf16[32,32,768]{2,1,0:T(8,128)(2,1)S(1)}, bf16[32,32,768]{2,1,0:T(8,128)(2,1)}, u32[]{:S(2)}) copy-start(bf16[32,32,768]{2,1,0:T(8,128)(2,1)} %param.17) | copy-start | bytes 4718596
  7.2 11.0 %copy-start.18 = (bf16[48,3,384]{2,0,1:T(8,128)(2,1)S(1)}, bf16[48,3,384]{2,0,1:T(8,128)(2,1)}, u32[]{:S(2)}) copy-start(bf16[48,3,384]{2,0,1:T(8,128)(2,1)} %param.21) | copy-start | bytes 331780
  7.2 11.1 %copy-start.31 = (s32[32]{0:T(128)S(1)}, s32[32]{0:T(128)}, u32[]{:S(2)}) copy-start(s32[32]{0:T(128)} %param.20) | copy-start | bytes 388
  7.2 112.9 %all-gather.5.cloned.1.call-start = ((), (), s32[]{:S(2)}) async-start(), calls=%async_computation.6 | async-start | bytes 3133440 | tf_op jit(solution)/shard_map/all_gather | solution.py:919
  9.8 194.6 %all-gather.3.cloned.1.call-start = ((), (), s32[]{:S(2)}) async-start(), calls=%async_computation.5 | async-start | bytes 5013504 | tf_op jit(solution)/shard_map/all_gather | solution.py:927
  12.5 7.7 %collective-permute-start = (bf16[48,1152]{1,0:T(8,128)(2,1)S(1)}, bf16[48,1152]{1,0:T(8,128)(2,1)S(1)}, u32[]{:S(2)}, u32[]{:S(2)}) collective-permute-start(bf16[48,1152]{1,0:T(8,128)(2,1)S(1)} %bitcast.165), channel_id=1, source_target_pairs={{0,8},{2,10},{4,12},{6,14},{8,0},{10,2},{12,4},{14,6},{16,24},{18,... | collective-permute-start | bytes 331784 | tf_op jit(solution)/shard_map/ppermute | solution.py:746
  15.6 11.8 %collective-permute-start.1 = (bf16[48,1152]{1,0:T(8,128)(2,1)S(1)}, bf16[48,1152]{1,0:T(8,128)(2,1)S(1)}, u32[]{:S(2)}, u32[]{:S(2)}) collective-permute-start(bf16[48,1152]{1,0:T(8,128)(2,1)S(1)} %bitcast.166), channel_id=1, source_target_pairs={{0,16},{2,18},{4,20},{6,22},{8,24},{10,26},{12,28},{14,30},{16,0},... | collective-permute-start | bytes 331784 | tf_op jit(solution)/shard_map/ppermute | solution.py:746
  18.2 9.2 %collective-permute-start.2 = (bf16[48,1152]{1,0:T(8,128)(2,1)S(1)}, bf16[48,1152]{1,0:T(8,128)(2,1)S(1)}, u32[]{:S(2)}, u32[]{:S(2)}) collective-permute-start(bf16[48,1152]{1,0:T(8,128)(2,1)S(1)} %bitcast.167), channel_id=1, source_target_pairs={{0,24},{2,26},{4,28},{6,30},{8,16},{10,18},{12,20},{14,22},{16,8},... | collective-permute-start | bytes 331784 | tf_op jit(solution)/shard_map/ppermute | solution.py:746
  27.5 56.1 %copy-start.14 = (bf16[4,48,1152]{2,1,0:T(8,128)(2,1)}, bf16[4,48,1152]{2,1,0:T(8,128)(2,1)S(1)}, u32[]{:S(2)}) copy-start(bf16[4,48,1152]{2,1,0:T(8,128)(2,1)S(1)} %pad_maximum_fusion.own_ref) | copy-start | bytes 1327108
  27.5 11.2 %copy-start.24 = (f32[4,384]{1,0:T(4,128)S(1)}, f32[4,384]{1,0:T(4,128)}, u32[]{:S(2)}) copy-start(f32[4,384]{1,0:T(4,128)} %refs_10_.1) | copy-start | bytes 18436
  27.5 11.2 %copy-start.27 = (f32[1536]{0:T(1024)S(1)}, f32[1536]{0:T(1024)}, u32[]{:S(2)}) copy-start(f32[1536]{0:T(1024)} %param.30) | copy-start | bytes 18436
  27.5 69.9 %all-to-all-start = ((bf16[32,32,768]{2,1,0:T(8,128)(2,1)}), bf16[32,32,768]{2,1,0:T(8,128)(2,1)}, u32[]{:S(2)}, u32[]{:S(2)}) async-start(bf16[32,32,768]{2,1,0:T(8,128)(2,1)} %gather_fusion.2), calls=%async_computation | async-start | bytes 3145728 | tf_op jit(solution)/shard_map/all_to_all | solution.py:905
  35.2 31.0 %collective-permute-start.3 = (bf16[4,48,1152]{2,1,0:T(8,128)(2,1)S(1)}, bf16[4,48,1152]{2,1,0:T(8,128)(2,1)S(1)}, u32[]{:S(2)}, u32[]{:S(2)}) collective-permute-start(bf16[4,48,1152]{2,1,0:T(8,128)(2,1)S(1)} %pad_maximum_fusion.own_ref), channel_id=1, source_target_pairs={{0,2},{2,0},{4,6},{6,4},{8,10},{10,8},{12,14},{14,12},{16,18},{18,... | collective-permute-start | bytes 1327112 | tf_op jit(solution)/shard_map/ppermute | solution.py:746
  37.1 29.1 %collective-permute-start.4 = (bf16[4,48,1152]{2,1,0:T(8,128)(2,1)S(1)}, bf16[4,48,1152]{2,1,0:T(8,128)(2,1)S(1)}, u32[]{:S(2)}, u32[]{:S(2)}) collective-permute-start(bf16[4,48,1152]{2,1,0:T(8,128)(2,1)S(1)} %pad_maximum_fusion.own_ref), channel_id=1, source_target_pairs={{0,4},{2,6},{4,0},{6,2},{8,12},{10,14},{12,8},{14,10},{16,20},{18,... | collective-permute-start | bytes 1327112 | tf_op jit(solution)/shard_map/ppermute | solution.py:746
  38.5 45.0 %collective-permute-start.5 = (bf16[4,48,1152]{2,1,0:T(8,128)(2,1)S(1)}, bf16[4,48,1152]{2,1,0:T(8,128)(2,1)S(1)}, u32[]{:S(2)}, u32[]{:S(2)}) collective-permute-start(bf16[4,48,1152]{2,1,0:T(8,128)(2,1)S(1)} %pad_maximum_fusion.own_ref), channel_id=1, source_target_pairs={{0,6},{2,4},{4,2},{6,0},{8,14},{10,12},{12,10},{14,8},{16,22},{18,... | collective-permute-start | bytes 1327112 | tf_op jit(solution)/shard_map/ppermute | solution.py:746
  38.8 58.7 %collective-permute-start.7 = (f32[3072]{0:T(1024)S(1)}, f32[3072]{0:T(1024)S(1)}, u32[]{:S(2)}, u32[]{:S(2)}) collective-permute-start(f32[3072]{0:T(1024)S(1)} %pad_maximum_fusion.4), channel_id=1, source_target_pairs={{0,1},{1,0},{2,3},{3,2},{4,5},{5,4},{6,7},{7,6},{8,9},{9,8},{10,11... | collective-permute-start | bytes 36872 | tf_op jit(solution)/shard_map/ppermute | solution.py:742
  39.5 49.4 %copy-start.2 = (s32[32]{0:T(128)S(1)}, s32[32]{0:T(128)}, u32[]{:S(2)}) copy-start(s32[32]{0:T(128)} %param.19) | copy-start | bytes 388
  66.2 17.4 %copy-start.19 = (bf16[4,48,1152]{2,1,0:T(8,128)(2,1)}, bf16[4,48,1152]{2,1,0:T(8,128)(2,1)S(1)}, u32[]{:S(2)}) copy-start(bf16[4,48,1152]{2,1,0:T(8,128)(2,1)S(1)} %collective-permute-done.3.first_ref) | copy-start | bytes 1327108
  66.2 17.4 %copy-start.20 = (bf16[4,48,1152]{2,1,0:T(8,128)(2,1)}, bf16[4,48,1152]{2,1,0:T(8,128)(2,1)S(1)}, u32[]{:S(2)}) copy-start(bf16[4,48,1152]{2,1,0:T(8,128)(2,1)S(1)} %collective-permute-done.4.second_ref) | copy-start | bytes 1327108
  88.8 10.7 %collective-permute-start.6 = (bf16[768,1152]{1,0:T(8,128)(2,1)}, bf16[768,1152]{1,0:T(8,128)(2,1)S(1)}, u32[]{:S(2)}, u32[]{:S(2)}) collective-permute-start(bf16[768,1152]{1,0:T(8,128)(2,1)} %bitcast.135), channel_id=1, source_target_pairs={{0,1},{1,0},{2,3},{3,2},{4,5},{5,4},{6,7},{7,6},{8,9},{9,8},{10,11... | collective-permute-start | bytes 5308424 | tf_op jit(solution)/shard_map/ppermute | solution.py:742
  100.5 7.1 %collective-permute-start.9 = (bf16[896,384]{1,0:T(8,128)(2,1)S(1)}, bf16[896,384]{1,0:T(8,128)(2,1)S(1)}, u32[]{:S(2)}, u32[]{:S(2)}) collective-permute-start(bf16[896,384]{1,0:T(8,128)(2,1)S(1)} %fusion.24.refs_2_), channel_id=1, source_target_pairs={{0,1},{1,0},{2,3},{3,2},{4,5},{5,4},{6,7},{7,6},{8,9},{9,8},{10,11... | collective-permute-start | bytes 2064392 | tf_op jit(solution)/shard_map/ppermute | solution.py:742
  101.9 6.5 %collective-permute-start.8 = (bf16[896,384]{1,0:T(8,128)(2,1)S(1)}, bf16[896,384]{1,0:T(8,128)(2,1)}, u32[]{:S(2)}, u32[]{:S(2)}) collective-permute-start(bf16[896,384]{1,0:T(8,128)(2,1)S(1)} %convolution_convert_fusion.refs_0_), channel_id=1, source_target_pairs={{0,1},{1,0},{2,3},{3,2},{4,5},{5,4},{6,7},{7,6},{8,9},{9,8},{10,11... | collective-permute-start | bytes 2064392 | tf_op jit(solution)/shard_map/ppermute | solution.py:742
  120.2 23.9 %collective-permute-start.13 = (bf16[768,1920]{1,0:T(8,128)(2,1)}, bf16[768,1920]{1,0:T(8,128)(2,1)S(1)}, u32[]{:S(2)}, u32[]{:S(2)}) collective-permute-start(bf16[768,1920]{1,0:T(8,128)(2,1)} %all-gather.5.cloned.1.call-done.refs_0_.refs_2_.refs_4_.refs_6_.refs_8_.refs_10_.wk0.wv0), channel_id=1, source_target_pairs={{0,1},{1,0},{2,3},{3,2},{4,5},{5,4},{6,7},{7,6},{8,9},{9,8},{10,11... | collective-permute-start | bytes 8847368 | tf_op jit(solution)/shard_map/ppermute | solution.py:742
  120.7 51.4 %all-to-all-start.1 = ((bf16[32,32,768]{2,1,0:T(8,128)(2,1)}), bf16[32,32,768]{2,1,0:T(8,128)(2,1)}, u32[]{:S(2)}, u32[]{:S(2)}) async-start(bf16[32,32,768]{2,1,0:T(8,128)(2,1)} %gather_fusion.1), calls=%async_computation.1 | async-start | bytes 3145728 | tf_op jit(solution)/shard_map/all_to_all | solution.py:905
  125.6 6.8 %collective-permute-start.11 = (bf16[896,384]{1,0:T(8,128)(2,1)}, bf16[896,384]{1,0:T(8,128)(2,1)}, u32[]{:S(2)}, u32[]{:S(2)}) collective-permute-start(bf16[896,384]{1,0:T(8,128)(2,1)} %fusion.23.refs_2_), channel_id=1, source_target_pairs={{0,1},{1,0},{2,3},{3,2},{4,5},{5,4},{6,7},{7,6},{8,9},{9,8},{10,11... | collective-permute-start | bytes 2064392 | tf_op jit(solution)/shard_map/ppermute | solution.py:742
  125.7 6.7 %collective-permute-start.10 = (bf16[896,384]{1,0:T(8,128)(2,1)}, bf16[896,384]{1,0:T(8,128)(2,1)}, u32[]{:S(2)}, u32[]{:S(2)}) collective-permute-start(bf16[896,384]{1,0:T(8,128)(2,1)} %convolution_convert_fusion.1.refs_0_), channel_id=1, source_target_pairs={{0,1},{1,0},{2,3},{3,2},{4,5},{5,4},{6,7},{7,6},{8,9},{9,8},{10,11... | collective-permute-start | bytes 2064392 | tf_op jit(solution)/shard_map/ppermute | solution.py:742
  126.2 2.2 collective-permute-start.12
  204.4 18.5 %collective-permute-start.14 = (bf16[768,3072]{1,0:T(8,128)(2,1)}, bf16[768,3072]{1,0:T(8,128)(2,1)}, u32[]{:S(2)}, u32[]{:S(2)}) collective-permute-start(bf16[768,3072]{1,0:T(8,128)(2,1)} %all-gather.3.cloned.1.call-done.in0.out0), channel_id=1, source_target_pairs={{0,1},{1,0},{2,3},{3,2},{4,5},{5,4},{6,7},{7,6},{8,9},{9,8},{10,11... | collective-permute-start | bytes 14155784 | tf_op jit(solution)/shard_map/ppermute | solution.py:742
  210.7 9.8 %slice-start = ((s8[4718592]{0:T(1024)(128)(4,1)}), s8[524288]{0:T(1024)(128)(4,1)S(1)}, s32[]{:S(2)}) async-start(s8[4718592]{0:T(1024)(128)(4,1)} %bitcast.151), calls=%async_computation.8 | async-start | bytes 1048576
  254.3 13.0 %copy-start.13 = (bf16[896,768]{1,0:T(8,128)(2,1)S(1)}, bf16[896,768]{1,0:T(8,128)(2,1)}, u32[]{:S(2)}) copy-start(bf16[896,768]{1,0:T(8,128)(2,1)} %get-tuple-element.139) | copy-start | bytes 4128772
  264.4 8.7 %collective-permute-start.15 = (bf16[768,3072]{1,0:T(8,128)(2,1)}, bf16[768,3072]{1,0:T(8,128)(2,1)}, u32[]{:S(2)}, u32[]{:S(2)}) collective-permute-start(bf16[768,3072]{1,0:T(8,128)(2,1)} %weight_grads.6), channel_id=1, source_target_pairs={{0,1},{1,0},{2,3},{3,2},{4,5},{5,4},{6,7},{7,6},{8,9},{9,8},{10,11... | collective-permute-start | bytes 14155784 | tf_op jit(solution)/shard_map/ppermute | solution.py:742
  269.3 45.9 %all-to-all-start.2 = ((bf16[32,32,768]{2,1,0:T(8,128)(2,1)}), bf16[32,32,768]{2,1,0:T(8,128)(2,1)S(1)}, u32[]{:S(2)}, u32[]{:S(2)}) async-start(bf16[32,32,768]{2,1,0:T(8,128)(2,1)} %broadcast_select_fusion.1), calls=%async_computation.2 | async-start | bytes 3145728 | tf_op jit(solution)/shard_map/all_to_all | solution.py:899
  273.0 181.4 %reduce-scatter.2.cloned.1.call-start = ((), (), s32[]{:S(2)}) async-start(), calls=%async_computation.7 | async-start | bytes 5013504 | tf_op jit(solution)/shard_map/reduce_scatter | solution.py:800
  315.2 1.9 collective-permute-start.16
  329.6 5.7 %collective-permute-start.17 = (bf16[4,4,48,1920]{3,2,1,0:T(8,128)(2,1)}, bf16[4,4,48,1920]{3,2,1,0:T(8,128)(2,1)}, u32[]{:S(2)}, u32[]{:S(2)}) collective-permute-start(bf16[4,4,48,1920]{3,2,1,0:T(8,128)(2,1)} %weight_grads.8), channel_id=1, source_target_pairs={{0,1},{1,0},{2,3},{3,2},{4,5},{5,4},{6,7},{7,6},{8,9},{9,8},{10,11... | collective-permute-start | bytes 8847368 | tf_op jit(solution)/shard_map/ppermute | solution.py:742
  347.6 42.2 %collective-permute-start.18 = (bf16[4,48,1920]{2,1,0:T(8,128)(2,1)}, bf16[4,48,1920]{2,1,0:T(8,128)(2,1)S(1)}, u32[]{:S(2)}, u32[]{:S(2)}) collective-permute-start(bf16[4,48,1920]{2,1,0:T(8,128)(2,1)} %get-tuple-element.261), channel_id=1, source_target_pairs={{0,2},{2,0},{4,6},{6,4},{8,10},{10,8},{12,14},{14,12},{16,18},{18,... | collective-permute-start | bytes 2211848 | tf_op jit(solution)/shard_map/ppermute | solution.py:746
  349.1 41.3 %collective-permute-start.19 = (bf16[4,48,1920]{2,1,0:T(8,128)(2,1)}, bf16[4,48,1920]{2,1,0:T(8,128)(2,1)S(1)}, u32[]{:S(2)}, u32[]{:S(2)}) collective-permute-start(bf16[4,48,1920]{2,1,0:T(8,128)(2,1)} %get-tuple-element.263), channel_id=1, source_target_pairs={{0,4},{2,6},{4,0},{6,2},{8,12},{10,14},{12,8},{14,10},{16,20},{18,... | collective-permute-start | bytes 2211848 | tf_op jit(solution)/shard_map/ppermute | solution.py:746
  352.5 39.1 %collective-permute-start.20 = (bf16[4,48,1920]{2,1,0:T(8,128)(2,1)}, bf16[4,48,1920]{2,1,0:T(8,128)(2,1)}, u32[]{:S(2)}, u32[]{:S(2)}) collective-permute-start(bf16[4,48,1920]{2,1,0:T(8,128)(2,1)} %get-tuple-element.262), channel_id=1, source_target_pairs={{0,6},{2,4},{4,2},{6,0},{8,14},{10,12},{12,10},{14,8},{16,22},{18,... | collective-permute-start | bytes 2211848 | tf_op jit(solution)/shard_map/ppermute | solution.py:746
  372.2 28.7 %collective-permute-start.21 = (bf16[896,384]{1,0:T(8,128)(2,1)}, bf16[896,384]{1,0:T(8,128)(2,1)}, u32[]{:S(2)}, u32[]{:S(2)}) collective-permute-start(bf16[896,384]{1,0:T(8,128)(2,1)} %get-tuple-element.156), channel_id=1, source_target_pairs={{0,1},{1,0},{2,3},{3,2},{4,5},{5,4},{6,7},{7,6},{8,9},{9,8},{10,11... | collective-permute-start | bytes 2064392 | tf_op jit(solution)/shard_map/ppermute | solution.py:742
  372.2 28.6 %collective-permute-start.22 = (bf16[896,384]{1,0:T(8,128)(2,1)}, bf16[896,384]{1,0:T(8,128)(2,1)}, u32[]{:S(2)}, u32[]{:S(2)}) collective-permute-start(bf16[896,384]{1,0:T(8,128)(2,1)} %get-tuple-element.158), channel_id=1, source_target_pairs={{0,1},{1,0},{2,3},{3,2},{4,5},{5,4},{6,7},{7,6},{8,9},{9,8},{10,11... | collective-permute-start | bytes 2064392 | tf_op jit(solution)/shard_map/ppermute | solution.py:742
  389.9 33.6 %collective-permute-start.23 = (bf16[896,384]{1,0:T(8,128)(2,1)}, bf16[896,384]{1,0:T(8,128)(2,1)}, u32[]{:S(2)}, u32[]{:S(2)}) collective-permute-start(bf16[896,384]{1,0:T(8,128)(2,1)} %get-tuple-element.162), channel_id=1, source_target_pairs={{0,1},{1,0},{2,3},{3,2},{4,5},{5,4},{6,7},{7,6},{8,9},{9,8},{10,11... | collective-permute-start | bytes 2064392 | tf_op jit(solution)/shard_map/ppermute | solution.py:742
  390.4 33.1 %collective-permute-start.24 = (bf16[896,384]{1,0:T(8,128)(2,1)}, bf16[896,384]{1,0:T(8,128)(2,1)}, u32[]{:S(2)}, u32[]{:S(2)}) collective-permute-start(bf16[896,384]{1,0:T(8,128)(2,1)} %get-tuple-element.163), channel_id=1, source_target_pairs={{0,1},{1,0},{2,3},{3,2},{4,5},{5,4},{6,7},{7,6},{8,9},{9,8},{10,11... | collective-permute-start | bytes 2064392 | tf_op jit(solution)/shard_map/ppermute | solution.py:742
  393.6 23.8 %collective-permute-start.25 = (bf16[48,1920]{1,0:T(8,128)(2,1)S(1)}, bf16[48,1920]{1,0:T(8,128)(2,1)S(1)}, u32[]{:S(2)}, u32[]{:S(2)}) collective-permute-start(bf16[48,1920]{1,0:T(8,128)(2,1)S(1)} %get-tuple-element.267), channel_id=1, source_target_pairs={{0,8},{2,10},{4,12},{6,14},{8,0},{10,2},{12,4},{14,6},{16,24},{18,... | collective-permute-start | bytes 552968 | tf_op jit(solution)/shard_map/ppermute | solution.py:746
  400.8 21.8 %collective-permute-start.26 = (bf16[48,1920]{1,0:T(8,128)(2,1)S(1)}, bf16[48,1920]{1,0:T(8,128)(2,1)S(1)}, u32[]{:S(2)}, u32[]{:S(2)}) collective-permute-start(bf16[48,1920]{1,0:T(8,128)(2,1)S(1)} %get-tuple-element.269), channel_id=1, source_target_pairs={{0,16},{2,18},{4,20},{6,22},{8,24},{10,26},{12,28},{14,30},{16,0},... | collective-permute-start | bytes 552968 | tf_op jit(solution)/shard_map/ppermute | solution.py:746
  400.8 21.8 %collective-permute-start.27 = (bf16[48,1920]{1,0:T(8,128)(2,1)S(1)}, bf16[48,1920]{1,0:T(8,128)(2,1)S(1)}, u32[]{:S(2)}, u32[]{:S(2)}) collective-permute-start(bf16[48,1920]{1,0:T(8,128)(2,1)S(1)} %get-tuple-element.268), channel_id=1, source_target_pairs={{0,24},{2,26},{4,28},{6,30},{8,16},{10,18},{12,20},{14,22},{16,8},... | collective-permute-start | bytes 552968 | tf_op jit(solution)/shard_map/ppermute | solution.py:746
  411.3 12.2 %copy-start.26 = (f32[8,768]{1,0:T(8,128)S(1)}, f32[8,768]{1,0:T(8,128)}, u32[]{:S(2)}) copy-start(f32[8,768]{1,0:T(8,128)} %get-tuple-element.176) | copy-start | bytes 73732
  423.5 12.2 %collective-permute-start.28 = (bf16[4,4,48,1152]{3,2,1,0:T(8,128)(2,1)}, bf16[4,4,48,1152]{3,2,1,0:T(8,128)(2,1)}, u32[]{:S(2)}, u32[]{:S(2)}) collective-permute-start(bf16[4,4,48,1152]{3,2,1,0:T(8,128)(2,1)} %weight_grads.10), channel_id=1, source_target_pairs={{0,1},{1,0},{2,3},{3,2},{4,5},{5,4},{6,7},{7,6},{8,9},{9,8},{10,11... | collective-permute-start | bytes 5308424 | tf_op jit(solution)/shard_map/ppermute | solution.py:742
  435.7 67.4 %all-to-all-start.3 = ((bf16[32,32,768]{2,1,0:T(8,128)(2,1)}), bf16[32,32,768]{2,1,0:T(8,128)(2,1)}, u32[]{:S(2)}, u32[]{:S(2)}) async-start(bf16[32,32,768]{2,1,0:T(8,128)(2,1)} %broadcast_select_fusion), calls=%async_computation.4 | async-start | bytes 3145728 | tf_op jit(solution)/shard_map/all_to_all | solution.py:899
  462.7 3.2 collective-permute-start.35
  465.9 22.8 %copy-start.12 = (f32[48,3072]{1,0:T(8,128)S(1)}, f32[48,3072]{1,0:T(8,128)}, u32[]{:S(2)}) copy-start(f32[48,3072]{1,0:T(8,128)} %convert_element_type.135) | copy-start | bytes 1769476
  466.8 11.0 %collective-permute-start.36 = (f32[13056]{0:T(1024)S(1)}, f32[13056]{0:T(1024)S(1)}, u32[]{:S(2)}, u32[]{:S(2)}) collective-permute-start(f32[13056]{0:T(1024)S(1)} %add.502), channel_id=1, source_target_pairs={{0,2},{2,0},{4,6},{6,4},{8,10},{10,8},{12,14},{14,12},{16,18},{18,... | collective-permute-start | bytes 156680 | tf_op jit(solution)/shard_map/ppermute | solution.py:746
  468.1 9.6 %collective-permute-start.37 = (f32[13056]{0:T(1024)S(1)}, f32[13056]{0:T(1024)S(1)}, u32[]{:S(2)}, u32[]{:S(2)}) collective-permute-start(f32[13056]{0:T(1024)S(1)} %add.502), channel_id=1, source_target_pairs={{0,4},{2,6},{4,0},{6,2},{8,12},{10,14},{12,8},{14,10},{16,20},{18,... | collective-permute-start | bytes 156680 | tf_op jit(solution)/shard_map/ppermute | solution.py:746
  469.4 8.7 %collective-permute-start.38 = (f32[13056]{0:T(1024)S(1)}, f32[13056]{0:T(1024)S(1)}, u32[]{:S(2)}, u32[]{:S(2)}) collective-permute-start(f32[13056]{0:T(1024)S(1)} %add.502), channel_id=1, source_target_pairs={{0,6},{2,4},{4,2},{6,0},{8,14},{10,12},{12,10},{14,8},{16,22},{18,... | collective-permute-start | bytes 156680 | tf_op jit(solution)/shard_map/ppermute | solution.py:746
  471.1 30.1 %collective-permute-start.29 = (bf16[4,48,1152]{2,1,0:T(8,128)(2,1)}, bf16[4,48,1152]{2,1,0:T(8,128)(2,1)S(1)}, u32[]{:S(2)}, u32[]{:S(2)}) collective-permute-start(bf16[4,48,1152]{2,1,0:T(8,128)(2,1)} %get-tuple-element.264), channel_id=1, source_target_pairs={{0,2},{2,0},{4,6},{6,4},{8,10},{10,8},{12,14},{14,12},{16,18},{18,... | collective-permute-start | bytes 1327112 | tf_op jit(solution)/shard_map/ppermute | solution.py:746
  472.5 28.8 %collective-permute-start.30 = (bf16[4,48,1152]{2,1,0:T(8,128)(2,1)S(1)}, bf16[4,48,1152]{2,1,0:T(8,128)(2,1)S(1)}, u32[]{:S(2)}, u32[]{:S(2)}) collective-permute-start(bf16[4,48,1152]{2,1,0:T(8,128)(2,1)S(1)} %get-tuple-element.266), channel_id=1, source_target_pairs={{0,4},{2,6},{4,0},{6,2},{8,12},{10,14},{12,8},{14,10},{16,20},{18,... | collective-permute-start | bytes 1327112 | tf_op jit(solution)/shard_map/ppermute | solution.py:746
  478.2 11.4 %collective-permute-start.39 = (f32[13056]{0:T(1024)S(1)}, f32[13056]{0:T(1024)S(1)}, u32[]{:S(2)}, u32[]{:S(2)}) collective-permute-start(f32[13056]{0:T(1024)S(1)} %add_add_fusion.2), channel_id=1, source_target_pairs={{0,8},{2,10},{4,12},{6,14},{8,0},{10,2},{12,4},{14,6},{16,24},{18,... | collective-permute-start | bytes 156680 | tf_op jit(solution)/shard_map/ppermute | solution.py:746
  480.0 13.5 %collective-permute-start.40 = (f32[13056]{0:T(1024)S(1)}, f32[13056]{0:T(1024)S(1)}, u32[]{:S(2)}, u32[]{:S(2)}) collective-permute-start(f32[13056]{0:T(1024)S(1)} %add_add_fusion.2), channel_id=1, source_target_pairs={{0,16},{2,18},{4,20},{6,22},{8,24},{10,26},{12,28},{14,30},{16,0},... | collective-permute-start | bytes 156680 | tf_op jit(solution)/shard_map/ppermute | solution.py:746
  487.3 6.2 %collective-permute-start.41 = (f32[13056]{0:T(1024)S(1)}, f32[13056]{0:T(1024)S(1)}, u32[]{:S(2)}, u32[]{:S(2)}) collective-permute-start(f32[13056]{0:T(1024)S(1)} %add_add_fusion.2), channel_id=1, source_target_pairs={{0,24},{2,26},{4,28},{6,30},{8,16},{10,18},{12,20},{14,22},{16,8},... | collective-permute-start | bytes 156680 | tf_op jit(solution)/shard_map/ppermute | solution.py:746
  489.5 12.3 %collective-permute-start.31 = (bf16[4,48,1152]{2,1,0:T(8,128)(2,1)S(1)}, bf16[4,48,1152]{2,1,0:T(8,128)(2,1)}, u32[]{:S(2)}, u32[]{:S(2)}) collective-permute-start(bf16[4,48,1152]{2,1,0:T(8,128)(2,1)S(1)} %get-tuple-element.265), channel_id=1, source_target_pairs={{0,6},{2,4},{4,2},{6,0},{8,14},{10,12},{12,10},{14,8},{16,22},{18,... | collective-permute-start | bytes 1327112 | tf_op jit(solution)/shard_map/ppermute | solution.py:746
  499.9 9.0 %copy-start.25 = (f32[4,768]{1,0:T(4,128)S(1)}, f32[4,768]{1,0:T(4,128)}, u32[]{:S(2)}) copy-start(f32[4,768]{1,0:T(4,128)} %slice.306) | copy-start | bytes 36868
  503.1 9.6 %collective-permute-start.32 = (bf16[48,1152]{1,0:T(8,128)(2,1)S(1)}, bf16[48,1152]{1,0:T(8,128)(2,1)S(1)}, u32[]{:S(2)}, u32[]{:S(2)}) collective-permute-start(bf16[48,1152]{1,0:T(8,128)(2,1)S(1)} %get-tuple-element.272), channel_id=1, source_target_pairs={{0,8},{2,10},{4,12},{6,14},{8,0},{10,2},{12,4},{14,6},{16,24},{18,... | collective-permute-start | bytes 331784 | tf_op jit(solution)/shard_map/ppermute | solution.py:746
  504.2 8.5 %collective-permute-start.33 = (bf16[48,1152]{1,0:T(8,128)(2,1)S(1)}, bf16[48,1152]{1,0:T(8,128)(2,1)S(1)}, u32[]{:S(2)}, u32[]{:S(2)}) collective-permute-start(bf16[48,1152]{1,0:T(8,128)(2,1)S(1)} %get-tuple-element.274), channel_id=1, source_target_pairs={{0,16},{2,18},{4,20},{6,22},{8,24},{10,26},{12,28},{14,30},{16,0},... | collective-permute-start | bytes 331784 | tf_op jit(solution)/shard_map/ppermute | solution.py:746
  508.2 8.4 %collective-permute-start.34 = (bf16[48,1152]{1,0:T(8,128)(2,1)S(1)}, bf16[48,1152]{1,0:T(8,128)(2,1)S(1)}, u32[]{:S(2)}, u32[]{:S(2)}) collective-permute-start(bf16[48,1152]{1,0:T(8,128)(2,1)S(1)} %get-tuple-element.273), channel_id=1, source_target_pairs={{0,24},{2,26},{4,28},{6,30},{8,16},{10,18},{12,20},{14,22},{16,8},... | collective-permute-start | bytes 331784 | tf_op jit(solution)/shard_map/ppermute | solution.py:746
  508.9 8.5 %copy-start.1 = (bf16[32,32,768]{2,1,0:T(8,128)(2,1)S(1)}, bf16[32,32,768]{2,1,0:T(8,128)(2,1)}, u32[]{:S(2)}) copy-start(bf16[32,32,768]{2,1,0:T(8,128)(2,1)} %param.17) | copy-start | bytes 4718596
  (20 other events, 80.2 us)
Sparse Core Ops, SparseCore 0:
  11.4 87.5 all-gather.4
  102.4 101.8 all-gather.2
  284.4 170.0 reduce-scatter.1

commit v4 on v3

--- a/solution.py
+++ b/solution.py
@@ -13,7 +13,10 @@
 MASKED = -1e30
 BLOCK = 128
 LIGHT = 1000
+LOW_GROUPS = [[4 * plane + low for low in range(4)] for plane in range(4)]
+PLANE_GROUPS = [[low + 4 * plane for plane in range(4)] for low in range(4)]
 GROUP = 4
+FIXED = 2
 PAIR = 2 * HD
 F32 = jnp.float32
 BF16 = jnp.bfloat16
@@ -76,52 +79,46 @@
     return slice(pair * PAIR, (pair + 1) * PAIR)
 
 
-def run_spans(causal, spans, local, start, second, active, run):
-    if causal:
-        base = pl.multiple_of(start * BLOCK, BLOCK)
-        for step in range(spans):
-            pl.when(active & (local == step))(functools.partial(run, base, (step + 1) * BLOCK))
-    else:
-        pl.when(active)(functools.partial(run, pl.multiple_of(second * BLOCK, BLOCK), BLOCK))
-
-
-def forward_kernel(parts, pairs, causal, piece, spans, meta, q_ref, *refs):
-    keys = refs[:parts]
-    values = refs[parts : 2 * parts]
-    out_ref, lse_ref = refs[2 * parts : 2 * parts + 2]
-    flipped = refs[2 * parts + 2 :]
-    block, local, start, second, active = block_place(meta)
+def run_spans(spans, local, start, active, run):
+    base = pl.multiple_of(start * BLOCK, BLOCK)
+    for step in range(spans):
+        pl.when(active & (local == step))(functools.partial(run, base, (step + 1) * BLOCK))
+
+
+def forward_kernel(piece, spans, meta, q_ref, *refs):
+    pairs_in = refs[:2]
+    out_ref, lse_ref = refs[2:4]
+    flipped = refs[4:6]
+    block, local, start, _, active = block_place(meta)
+    half = q_ref.shape[1]
 
     @pl.when(block == 0)
     def _():
-        for part in range(parts):
-            flipped[part][...] = values[part][...].astype(F32).T.astype(BF16)
+        for part in range(2):
+            flipped[part][...] = pairs_in[part][:, half:].astype(F32).T.astype(BF16)
 
     def run(base, span):
-        masks = [diagonal_mask(part == 0, piece, meta[2]) for part in range(parts)]
-        for pair in range(pairs):
+        place = pl.ds(base, span)
+        masks = [diagonal_mask(part == 0, piece, meta[2]) for part in range(2)]
+        for pair in range(half // PAIR):
             cols = pair_columns(pair)
             stacked = stack_heads(q_ref[:, cols])
-            scores = []
-            for part in range(parts):
-                tile = dot_nt(keys[part][pl.ds(base, span), cols], stacked)
-                scores.append(mask_scores(tile, masks[part]) if causal else tile)
-            top = functools.reduce(
-                jnp.maximum, [jnp.max(tile, 0, keepdims=True) for tile in scores]
+            scores = [
+                mask_scores(dot_nt(pairs_in[part][place, cols], stacked), masks[part])
+                for part in range(2)
+            ]
+            top = jnp.maximum(
+                jnp.max(scores[0], 0, keepdims=True), jnp.max(scores[1], 0, keepdims=True)
             )
             exps = [jnp.exp(tile - top) for tile in scores]
-            total = functools.reduce(jnp.add, [jnp.sum(tile, 0, keepdims=True) for tile in exps])
-            result = functools.reduce(
-                jnp.add,
-                [
-                    dot_nn(flipped[part][cols, pl.ds(base, span)], exps[part].astype(BF16))
-                    for part in range(parts)
-                ],
+            total = jnp.sum(exps[0], 0, keepdims=True) + jnp.sum(exps[1], 0, keepdims=True)
+            result = dot_nn(flipped[0][cols, place], exps[0].astype(BF16)) + dot_nn(
+                flipped[1][cols, place], exps[1].astype(BF16)
             )
             out_ref[:, cols] = unstack_heads(result / total).astype(BF16)
             lse_ref[0, pair : pair + 1, :] = top + jnp.log(total)
 
-    run_spans(causal, spans, local, start, second, active, run)
+    run_spans(spans, local, start, active, run)
 
     @pl.when(jnp.logical_not(active))
     def _():
@@ -129,54 +126,49 @@
         lse_ref[...] = jnp.zeros_like(lse_ref)
 
 
-def backward_kernel(parts, pairs, causal, piece, spans, meta, q_ref, g_ref, lse_ref, *refs):
-    keys = refs[:parts]
-    values = refs[parts : 2 * parts]
-    dq_ref = refs[2 * parts]
-    dk_out = refs[2 * parts + 1 : 3 * parts + 1]
-    dv_out = refs[3 * parts + 1 : 4 * parts + 1]
-    flipped = refs[4 * parts + 1 : 5 * parts + 1]
-    dk_sum = refs[5 * parts + 1 : 6 * parts + 1]
-    dv_sum = refs[6 * parts + 1 : 7 * parts + 1]
-    block, local, start, second, active = block_place(meta)
+def backward_kernel(piece, spans, meta, q_ref, g_ref, lse_ref, *refs):
+    pairs_in = refs[:2]
+    dq_ref = refs[2]
+    outs = refs[3:5]
+    flipped = refs[5:7]
+    sums = refs[7:9]
+    block, local, start, _, active = block_place(meta)
+    half = q_ref.shape[1]
 
     @pl.when(block == 0)
     def _():
-        for part in range(parts):
-            flipped[part][...] = keys[part][...].astype(F32).T.astype(BF16)
-            dk_sum[part][...] = jnp.zeros_like(dk_sum[part])
-            dv_sum[part][...] = jnp.zeros_like(dv_sum[part])
+        for part in range(2):
+            flipped[part][...] = pairs_in[part][:, :half].astype(F32).T.astype(BF16)
+            sums[part][...] = jnp.zeros_like(sums[part])
 
     def run(base, span):
         place = pl.ds(base, span)
-        masks = [diagonal_mask(part == 0, piece, meta[2]) for part in range(parts)]
-        for pair in range(pairs):
+        masks = [diagonal_mask(part == 0, piece, meta[2]) for part in range(2)]
+        for pair in range(half // PAIR):
             cols = pair_columns(pair)
+            value_cols = slice(half + pair * PAIR, half + (pair + 1) * PAIR)
             queries = stack_heads(q_ref[:, cols])
             grads = stack_heads(g_ref[:, cols])
             lse = lse_ref[0, pair : pair + 1, :]
             probs = []
             grad_probs = []
-            for part in range(parts):
-                tile = dot_nt(keys[part][place, cols], queries)
-                if causal:
-                    tile = mask_scores(tile, masks[part])
+            for part in range(2):
+                tile = mask_scores(dot_nt(pairs_in[part][place, cols], queries), masks[part])
                 probs.append(jnp.exp(tile - lse))
-                grad_probs.append(dot_nt(values[part][place, cols], grads))
-            row_dot = functools.reduce(
-                jnp.add,
-                [jnp.sum(p * g, 0, keepdims=True) for p, g in zip(probs, grad_probs)],
+                grad_probs.append(dot_nt(pairs_in[part][place, value_cols], grads))
+            row_dot = jnp.sum(probs[0] * grad_probs[0], 0, keepdims=True) + jnp.sum(
+                probs[1] * grad_probs[1], 0, keepdims=True
             )
             grad_query = None
-            for part in range(parts):
+            for part in range(2):
                 grad_score = (probs[part] * (grad_probs[part] - row_dot)).astype(BF16)
-                dv_sum[part][place, cols] += dot_nn(probs[part].astype(BF16), grads)
-                dk_sum[part][place, cols] += dot_nn(grad_score, queries)
+                sums[part][place, value_cols] += dot_nn(probs[part].astype(BF16), grads)
+                sums[part][place, cols] += dot_nn(grad_score, queries)
                 term = dot_nn(flipped[part][cols, place], grad_score)
                 grad_query = term if grad_query is None else grad_query + term
             dq_ref[:, cols] = unstack_heads(grad_query).astype(BF16)
 
-    run_spans(causal, spans, local, start, second, active, run)
+    run_spans(spans, local, start, active, run)
 
     @pl.when(jnp.logical_not(active))
     def _():
@@ -184,9 +176,8 @@
 
     @pl.when(block == pl.num_programs(0) - 1)
     def _():
-        for part in range(parts):
-            dk_out[part][...] = dk_sum[part][...].astype(dk_out[part].dtype)
-            dv_out[part][...] = dv_sum[part][...].astype(dv_out[part].dtype)
+        for part in range(2):
+            outs[part][...] = sums[part][...].astype(outs[part].dtype)
 
 
 def row_spec(width, rows=BLOCK):
@@ -201,57 +192,77 @@
     return pl.BlockSpec((group, 8, 2 * BLOCK), lambda block, meta: (block, 0, 0))
 
 
-def attend_forward(meta, queries, keys, values, causal, piece, spans):
-    rows, width = queries.shape
-    parts = len(keys)
-    pairs, blocks = width // PAIR, rows // BLOCK
-    key_rows = keys[0].shape[0]
-    work = pairs * blocks * parts * 4 * BLOCK * 2 * BLOCK * (2 * BLOCK if causal else BLOCK)
+def kept(shape, kind):
+    return jax.ShapeDtypeStruct(shape, kind)
+
+
+def light_cost():
+    return pl.CostEstimate(flops=1000, bytes_accessed=1000, transcendentals=0)
+
+
+def attend_forward(meta, queries, near, far, piece, spans):
+    rows, half = queries.shape
+    blocks = rows // BLOCK
     return pl.pallas_call(
-        functools.partial(forward_kernel, parts, pairs, causal, piece, spans),
+        functools.partial(forward_kernel, piece, spans),
         grid_spec=pltpu.PrefetchScalarGridSpec(
             num_scalar_prefetch=1,
             grid=(blocks,),
-            in_specs=[row_spec(width)] + [whole_spec(key_rows, width)] * (2 * parts),
-            out_specs=[row_spec(width), lse_spec()],
-            scratch_shapes=[pltpu.VMEM((width, key_rows), BF16)] * parts,
+            in_specs=[row_spec(half)] + [whole_spec(rows, 2 * half)] * 2,
+            out_specs=[row_spec(half), lse_spec()],
+            scratch_shapes=[pltpu.VMEM((half, rows), BF16)] * 2,
+        ),
+        out_shape=[kept((rows, half), BF16), kept((blocks, 8, 2 * BLOCK), F32)],
+        cost_estimate=light_cost(),
+        name="attend_forward",
+    )(meta, queries, near, far)
+
+
+def attend_backward(meta, queries, grads, lse, near, far, piece, spans):
+    rows, half = queries.shape
+    return pl.pallas_call(
+        functools.partial(backward_kernel, piece, spans),
+        grid_spec=pltpu.PrefetchScalarGridSpec(
+            num_scalar_prefetch=1,
+            grid=(rows // BLOCK,),
+            in_specs=[row_spec(half), row_spec(half), lse_spec()]
+            + [whole_spec(rows, 2 * half)] * 2,
+            out_specs=[row_spec(half)] + [whole_spec(rows, 2 * half)] * 2,
+            scratch_shapes=[pltpu.VMEM((half, rows), BF16)] * 2
+            + [pltpu.VMEM((rows, 2 * half), F32)] * 2,
         ),
         out_shape=[
-            jax.ShapeDtypeStruct((rows, width), BF16),
-            jax.ShapeDtypeStruct((blocks, 8, 2 * BLOCK), F32),
+            kept((rows, half), BF16),
+            kept((rows, 2 * half), F32),
+            kept((rows, 2 * half), BF16),
         ],
-        cost_estimate=pl.CostEstimate(
-            flops=(4 * work) // LIGHT, bytes_accessed=(8 * rows * width) // LIGHT, transcendentals=work // 256
-        ),
-        name="attend_forward",
-    )(meta, queries, *keys, *values)
-
-
-def attend_backward(meta, queries, grads, lse, keys, values, causal, piece, spans, kinds):
-    rows, width = queries.shape
-    parts = len(keys)
-    pairs, blocks = width // PAIR, rows // BLOCK
-    key_rows = keys[0].shape[0]
-    work = pairs * blocks * parts * 4 * BLOCK * 2 * BLOCK * (2 * BLOCK if causal else BLOCK)
-    results = pl.pallas_call(
-        functools.partial(backward_kernel, parts, pairs, causal, piece, spans),
-        grid_spec=pltpu.PrefetchScalarGridSpec(
-            num_scalar_prefetch=1,
-            grid=(blocks,),
-            in_specs=[row_spec(width), row_spec(width), lse_spec()]
-            + [whole_spec(key_rows, width)] * (2 * parts),
-            out_specs=[row_spec(width)] + [whole_spec(key_rows, width)] * (2 * parts),
-            scratch_shapes=[pltpu.VMEM((width, key_rows), BF16)] * parts
-            + [pltpu.VMEM((key_rows, width), F32)] * (2 * parts),
-        ),
-        out_shape=[jax.ShapeDtypeStruct((rows, width), BF16)]
-        + [jax.ShapeDtypeStruct((key_rows, width), kind) for kind in kinds + kinds],
-        cost_estimate=pl.CostEstimate(
-            flops=(10 * work) // LIGHT, bytes_accessed=(16 * rows * width) // LIGHT, transcendentals=work // 256
-        ),
+        cost_estimate=light_cost(),
         name="attend_backward",
-    )(meta, queries, grads, lse, *keys, *values)
-    return results[0], results[1 : 1 + parts], results[1 + parts :]
+    )(meta, queries, grads, lse, near, far)
+
+
+def project_kernel(score_scale, x_ref, wq, wk, wv, bias, q_ref, pair_ref):
+    rows = x_ref[...]
+    half = q_ref.shape[1]
+    q_ref[...] = ((dot_nn(rows, wq[...]) + bias[0:1, :]) * score_scale).astype(BF16)
+    pair_ref[:, :half] = dot_nn(rows, wk[...]).astype(BF16)
+    pair_ref[:, half:] = (dot_nn(rows, wv[...]) + bias[1:2, :]).astype(BF16)
+
+
+def project(inputs, weight, bias, score_scale):
+    rows, width = inputs.shape
+    half = bias.shape[1]
+    return pl.pallas_call(
+        functools.partial(project_kernel, score_scale),
+        grid=(2,),
+        in_specs=[plain_rows(rows // 2, width)]
+        + [plain_fixed((width, half), 0, i) for i in range(3)]
+        + [plain_fixed((4, half))],
+        out_specs=[plain_rows(rows // 2, half), plain_rows(rows // 2, 2 * half)],
+        out_shape=[kept((rows, half), BF16), kept((rows, 2 * half), BF16)],
+        cost_estimate=light_cost(),
+        name="project",
+    )(inputs, weight, weight, weight, bias)
 
 
 def grads_kernel(sides, counts, factors, extra, grouped, meta, *refs):
@@ -278,7 +289,7 @@
             for plane in range(4):
                 for low in range(4):
                     row = (plane * 4 + low) * size
-                    place = pl.ds(meta[0] ^ low, 1)
+                    place = pl.ds(low if grouped == FIXED else meta[0] ^ low, 1)
                     part = result[row : row + size]
                     if extra:
                         part = part + extra_ref[place, plane].astype(F32)[0]
@@ -537,6 +548,46 @@
     )(near, got, mid[0], mid[0], mid[1], mid[1])
 
 
+def ffn_forward_kernel(first, hidden_ref, base_ref, expand, reduce, bias, gain, shift, act_ref, slope_ref, total_ref):
+    pre = dot_nn(hidden_ref[...], expand[...]) + bias[0:1, :]
+    phi = 0.5 * (1.0 + lax.erf(pre * (1.0 / math.sqrt(2.0))))
+    density = jnp.exp(-0.5 * pre * pre) * (1.0 / math.sqrt(2.0 * math.pi))
+    act = (pre * phi).astype(BF16)
+    act_ref[...] = act
+    slope_ref[...] = (phi + pre * density).astype(BF16)
+    base = base_ref[...]
+    if first:
+        base = base * gain[0:1, :] + shift[0:1, :]
+    total_ref[...] = base + dot_nt(act, reduce[...])
+
+
+def ffn_forward(first, hidden, base, weight, bias, gain, shift):
+    rows, width = hidden.shape
+    units = bias.shape[1]
+    tall = rows // 4
+    wide, long = plain_rows(tall, width), plain_rows(tall, units)
+
+    def side(column):
+        return pl.BlockSpec(
+            (width, units), lambda step: (0, column), pipeline_mode=pl.Buffered(1)
+        )
+
+    return pl.pallas_call(
+        functools.partial(ffn_forward_kernel, first),
+        grid=(4,),
+        in_specs=[wide, wide, side(0), side(1), plain_fixed((1, units))]
+        + [plain_fixed((1, width))] * 2,
+        out_specs=[long, long, wide],
+        out_shape=[
+            kept((rows, units), BF16),
+            kept((rows, units), BF16),
+            kept((rows, width), F32),
+        ],
+        cost_estimate=light_cost(),
+        name="ffn_forward",
+    )(hidden, base, weight, weight, bias, gain, shift)
+
+
 def ffn_backward_kernel(h3_ref, cot_ref, valid_ref, slope0, slope1, in0, in1, out0, out1, gain, shift, n3_ref, dz_ref, dn2_ref, sums_ref, du0, du1, usum0, usum1):
     @pl.when(pl.program_id(0) == 0)
     def _():
@@ -598,10 +649,6 @@
 def fixed_spec(shape, *index):
     place = index or (0,) * len(shape)
     return pl.BlockSpec(shape, lambda block, meta: place)
-
-
-def kept(shape, kind):
-    return jax.ShapeDtypeStruct(shape, kind)
 
 
 def mid_forward(meta, inputs, attn, memory, mid, in_pair, out_bias, gain, shift, score_scale):
@@ -689,16 +736,16 @@
     return outs[:4], outs[4:6], outs[6:8], outs[8], outs[9]
 
 
-def input_backward_kernel(score_scale, base_ref, dq_ref, dk_own, dk_got, dv_own, dv_got, wq, wk, wv, dx_ref, dk_ref, dv_ref, sums_ref):
+def input_backward_kernel(score_scale, base_ref, dq_ref, own_ref, got_ref, wq, wk, wv, dx_ref, pair_ref, sums_ref):
     @pl.when(pl.program_id(0) == 0)
     def _():
         sums_ref[...] = jnp.zeros_like(sums_ref)
 
-    dk = (dk_own[...] + dk_got[...].astype(F32)).astype(BF16)
-    dv = (dv_own[...] + dv_got[...].astype(F32)).astype(BF16)
-    dk_ref[...] = dk
-    dv_ref[...] = dv
+    half = dq_ref.shape[1]
+    pair = (own_ref[...] + got_ref[...].astype(F32)).astype(BF16)
+    pair_ref[...] = pair
     dq = dq_ref[...]
+    dk, dv = pair[:, :half], pair[:, half:]
     sums_ref[0:1, :] += score_scale * jnp.sum(dq.astype(F32), 0, keepdims=True)
     sums_ref[1:2, :] += jnp.sum(dv.astype(F32), 0, keepdims=True)
     total = score_scale * dot_nt(dq, wq[...]) + dot_nt(dk, wk[...]) + dot_nt(dv, wv[...])
@@ -714,28 +761,25 @@
     return pl.BlockSpec(shape, lambda step: place)
 
 
-def input_backward(base, dq, dk, dk_got, dv, dv_got, weight, score_scale, kind):
+def input_backward(base, dq, own, got, weight, score_scale, kind):
     rows, width = base.shape
     half = dq.shape[1]
-    wide, narrow = plain_rows(rows // 2, width), plain_rows(rows // 2, half)
+    tall = rows // 2
     return pl.pallas_call(
         functools.partial(input_backward_kernel, score_scale),
         grid=(2,),
-        in_specs=[wide] + [narrow] * 5 + [plain_fixed((width, half), 0, i) for i in range(3)],
-        out_specs=[wide, narrow, narrow, plain_fixed((8, half))],
+        in_specs=[plain_rows(tall, width), plain_rows(tall, half)]
+        + [plain_rows(tall, 2 * half)] * 2
+        + [plain_fixed((width, half), 0, i) for i in range(3)],
+        out_specs=[plain_rows(tall, width), plain_rows(tall, 2 * half), plain_fixed((8, half))],
         out_shape=[
             kept((rows, width), kind),
-            kept((rows, half), BF16),
-            kept((rows, half), BF16),
+            kept((rows, 2 * half), BF16),
             kept((8, half), F32),
         ],
-        cost_estimate=pl.CostEstimate(
-            flops=(6 * rows * width * half) // LIGHT,
-            bytes_accessed=(12 * rows * width) // LIGHT,
-            transcendentals=0,
-        ),
+        cost_estimate=light_cost(),
         name="input_backward",
-    )(base, dq, dk, dk_got, dv, dv_got, weight, weight, weight)
+    )(base, dq, own, got, weight, weight, weight)
 
 
 def swap(value):
@@ -751,12 +795,16 @@
         out_ref[0, pl.ds(meta[1] ^ low, 1)] = ref[...]
 
 
-def quick_gather(value, later):
-    if lax.axis_size("dp") != 16:
-        return lax.all_gather(value, "dp", axis=0, tiled=True), later
-    rows, count = value.shape
-    line = jnp.stack([value, hop(value, 4), hop(value, 8), hop(value, 12)])
-    line, later = tie(line, later)
+def plane_line(value):
+    return jnp.stack([value, hop(value, 4), hop(value, 8), hop(value, 12)])
+
+
+def low_groups(line):
+    return (line, hop(line, 1), hop(line, 2), hop(line, 3))
+
+
+def assemble(groups):
+    rows, count = groups[0].shape[1:]
     index = lax.axis_index("dp")
     meta = jnp.stack([index // 4, index % 4]).astype(jnp.int32)
     spec = pl.BlockSpec((1, rows, count), lambda i, meta: (i ^ meta[0], 0, 0))
@@ -768,13 +816,11 @@
             in_specs=[spec] * 4,
             out_specs=pl.BlockSpec((1, 4, rows, count), lambda i, meta: (i, 0, 0, 0)),
         ),
-        out_shape=jax.ShapeDtypeStruct((4, 4, rows, count), value.dtype),
-        cost_estimate=pl.CostEstimate(
-            flops=(0) // LIGHT, bytes_accessed=(64 * rows * count) // LIGHT, transcendentals=0
-        ),
+        out_shape=kept((4, 4, rows, count), groups[0].dtype),
+        cost_estimate=light_cost(),
         name="assemble",
-    )(meta, line, hop(line, 1), hop(line, 2), hop(line, 3))
-    return full.reshape(16 * rows, count), later
+    )(meta, *groups)
+    return full.reshape(16 * rows, count)
 
 
 def total_of(parts):
@@ -796,17 +842,18 @@
     return total_of([pick(0)] + received)
 
 
-def slow_scatter(value):
-    return lax.psum_scatter(value, "dp", scatter_dimension=0, tiled=True).astype(F32)
-
-
-def sum_everywhere(value):
-    if lax.axis_size("dp") != 16:
-        return lax.psum(value, ("dp", "tensor"))
-    value = value + swap(value)
-    for unit in (1, 4):
-        value = total_of([value] + [hop(value, unit * bits) for bits in (1, 2, 3)])
-    return value
+def wide_scatter(value, groups=None):
+    return lax.psum_scatter(
+        value, "dp", scatter_dimension=0, tiled=True, axis_index_groups=groups
+    )
+
+
+def sum_low(value):
+    return total_of([value] + [hop(value, bits) for bits in (1, 2, 3)])
+
+
+def sum_planes(value):
+    return total_of([value] + [hop(value, 4 * bits) for bits in (1, 2, 3)])
 
 
 def rows_at(value, ids):
@@ -907,34 +954,38 @@
     def pack(arrived):
         return rows_at(arrived, piece_ids).reshape(rows, width)
 
-    qkv_own, ordered = quick_gather(self_project.reshape(shard, 3 * half), order(tokens))
+    quick = dp_count == 16
+    ordered = order(tokens)
+    qkv_shard_in = self_project.reshape(shard, 3 * half)
+    mid_shard_in = jnp.concatenate(
+        [self_output.T, cross_query, cross_memory.reshape(shard, 2 * half), cross_output.T], 1
+    )
+
+    def slow_gather(value):
+        return lax.all_gather(value, "dp", axis=0, tiled=True)
+
+    ordered_cot = order(cotangent)
+    if quick:
+        qkv_line = plane_line(qkv_shard_in)
+        qkv_line, ordered = tie(qkv_line, ordered)
+        qkv_groups = low_groups(qkv_line)
+        arrived = arrive(ordered)
+        ordered_cot, arrived, qkv_groups = tie(ordered_cot, arrived, qkv_groups)
+        qkv_own = assemble(qkv_groups)
+    else:
+        arrived = arrive(ordered)
+        qkv_own = slow_gather(qkv_shard_in)
     qkv_weight = (qkv_own, swap(qkv_own))
-    arrived = arrive(ordered)
-    ordered_cot, arrived = tie(order(cotangent), arrived)
     inputs = pack(arrived)
     arrived_cot = arrive(ordered_cot)
 
-    quick = dp_count == 16
-
-    mid_own = lax.all_gather(
-        jnp.concatenate(
-            [self_output.T, cross_query, cross_memory.reshape(shard, 2 * half), cross_output.T], 1
-        ),
-        "dp",
-        axis=0,
-        tiled=True,
-    )
-    ffn_own = lax.all_gather(
-        jnp.concatenate([hidden_in, hidden_out.T], 1), "dp", axis=0, tiled=True
-    )
+    mid_own = slow_gather(mid_shard_in)
+    ffn_own = slow_gather(jnp.concatenate([hidden_in, hidden_out.T], 1))
     both = (0, 1)
 
     def columns(pair, start, count):
         return [lax.slice_in_dim(pair[h], start, start + count, axis=1) for h in both]
 
-    project_q = columns(qkv_weight, 0, half)
-    project_k = columns(qkv_weight, half, half)
-    project_v = columns(qkv_weight, 2 * half, half)
     biases = jnp.concatenate([in_bias.reshape(-1), hidden_bias])
     bias_pair = (biases, swap(biases))
     in_pair = [b[: 4 * half].reshape(4, half) for b in bias_pair]
@@ -942,44 +993,39 @@
 
     memory_full = jnp.concatenate([encoder, swap(encoder)], 1).reshape(4 * memory_rows, width)
 
-    queries = [
-        ((dot_nn(inputs, project_q[h]) + in_pair[h][0]) * score_scale).astype(BF16) for h in both
-    ]
-    keys = [dot_nn(inputs, project_k[h]).astype(BF16) for h in both]
-    values = [(dot_nn(inputs, project_v[h]) + in_pair[h][1]).astype(BF16) for h in both]
-    keys_far = [swap(keys[1 - h]) for h in both]
-    values_far = [swap(values[1 - h]) for h in both]
-    attn = []
-    lse = []
+    queries = [None, None]
+    near = [None, None]
+    attn = [None, None]
+    lse = [None, None]
     for h in both:
-        result = attend_forward(
-            meta, queries[h], [keys[h], keys_far[h]], [values[h], values_far[h]], True, piece, spans
-        )
-        attn.append(result[0])
-        lse.append(result[1])
-        if h == 0:
-            mid_own, attn[0] = tie(mid_own, attn[0])
-            mid_weight = (mid_own, swap(mid_own))
+        queries[h], near[h] = project(inputs, qkv_weight[h], in_pair[h], score_scale)
+    far = [swap(near[1 - h]) for h in both]
+    attn[1], lse[1] = attend_forward(meta, queries[1], near[1], far[1], piece, spans)
+    mid_own, attn[1], queries[0], valid_rows = tie(
+        mid_own, attn[1], queries[0], row_valid.astype(F32)
+    )
+    mid_weight = (mid_own, swap(mid_own))
+    attn[0], lse[0] = attend_forward(meta, queries[0], near[0], far[0], piece, spans)
     saved, cqs, cattn, cks, cvs = mid_forward(
         meta, inputs, attn, memory_full, mid_weight, in_pair, out_bias, norm_gain, norm_bias, score_scale
     )
     unit1, scale1, unit2, scale2, cross_in, hidden, clse = saved
-    ffn_own, hidden, arrived_cot = tie(ffn_own, hidden, arrived_cot)
-    ffn_weight = (ffn_own, swap(ffn_own))
-    expand = columns(ffn_weight, 0, units)
-    reduce = columns(ffn_weight, units, units)
-    n2 = unit2 * norm_gain[1] + norm_bias[1]
-    act = []
-    slope = []
-    for h in both:
-        pre = dot_nn(hidden, expand[h]) + hidden_pair[h]
-        phi = 0.5 * (1.0 + lax.erf(pre * (1.0 / math.sqrt(2.0))))
-        act.append((pre * phi).astype(BF16))
-        density = jnp.exp(-0.5 * pre * pre) * (1.0 / math.sqrt(2.0 * math.pi))
-        slope.append((phi + pre * density).astype(BF16))
-    branch = dot_nt(act[0], reduce[0]) + dot_nt(act[1], reduce[1]) + out_bias[2]
+    hidden, ffn_own = tie(hidden, ffn_own)
+    ffn_far = swap(ffn_own)
+    act = [None, None]
+    slope = [None, None]
+    affine = (norm_gain[1:2], norm_bias[1:2] + out_bias[2:3])
+    act[0], slope[0], total = ffn_forward(
+        True, hidden, unit2, ffn_own, hidden_pair[0][None], *affine
+    )
+    ffn_far, total = tie(ffn_far, total)
+    act[1], slope[1], total = ffn_forward(
+        False, hidden, total, ffn_far, hidden_pair[1][None], *affine
+    )
+    arrived_cot, total = tie(arrived_cot, total)
+    ffn_weight = (ffn_own, ffn_far)
     n3, dz, dn2, sums3, du0, du1, usum0, usum1 = ffn_backward(
-        n2 + branch, pack(arrived_cot), row_valid.astype(F32), slope, ffn_weight, norm_gain, norm_bias
+        total, pack(arrived_cot), valid_rows, slope, ffn_weight, norm_gain, norm_bias
     )
     du = (du0, du1)
     output_back = go_home(home_pieces(n3))
@@ -991,10 +1037,10 @@
         return weight_grads(low_meta, lefts, rights[0], sides, factors, swap(far), grouped)
 
     ffn_grads = chip_grads(
-        [hidden, dz], [[du[h], act[h]] for h in both], (0, 1), (1.0, 1.0), False
+        [hidden, dz], [[du[h], act[h]] for h in both], (0, 1), (1.0, 1.0), FIXED if quick else 0
     )
     ffn_grads, dn2 = tie(ffn_grads, dn2)
-    ffn_shard = slow_scatter(ffn_grads)
+    ffn_line = wide_scatter(ffn_grads.reshape(width, 2 * units), LOW_GROUPS if quick else None)
     rows_back, dcq, da, memory_near, memory_far = mid_backward(
         meta, dn2, (unit1, scale1, unit2, scale2, clse), cqs, cks, cvs, mid_weight, norm_gain, score_scale
     )
@@ -1014,54 +1060,42 @@
         ],
         (0, 1, 2, 2, 3),
         (1.0, score_scale, 1.0, 1.0, 1.0),
-        quick,
+        FIXED if quick else 0,
     )
     mid_grads, da[0], da[1] = tie(mid_grads, da[0], da[1])
-    mid_line = scatter_low(mid_grads) if quick else None
-    dq = []
-    dk = []
-    dv = []
+    mid_line = wide_scatter(mid_grads.reshape(width, 5 * half), LOW_GROUPS if quick else None)
+    dq = [None, None]
+    own = [None, None]
+    out = [None, None]
     for h in both:
-        result = attend_backward(
-            meta,
-            queries[h],
-            da[h],
-            lse[h],
-            [keys[h], keys_far[h]],
-            [values[h], values_far[h]],
-            True,
-            piece,
-            spans,
-            [F32, BF16],
+        dq[h], own[h], out[h] = attend_backward(
+            meta, queries[h], da[h], lse[h], near[h], far[h], piece, spans
         )
-        dq.append(result[0])
-        dk.append(result[1])
-        dv.append(result[2])
+        if h == 0:
+            da[1], dq[0], ffn_line = tie(da[1], dq[0], ffn_line)
     factors = (score_scale, 1.0, 1.0)
-    near = [swap(dk[1][1]), swap(dv[1][1])]
-    if quick:
-        mid_line, dh1 = tie(mid_line, dh1)
-        mid_shard = scatter_plane(mid_line)
-    else:
-        mid_shard = slow_scatter(mid_grads)
-    dx_far, dk_far, dv_far, sums_far = input_backward(
-        dh1, dq[1], dk[1][0], swap(dk[0][1]), dv[1][0], swap(dv[0][1]), qkv_weight[1], score_scale, F32
+    got_far, got_near = swap(out[0]), swap(out[1])
+    dx_far, pair_far, sums_far = input_backward(
+        dh1, dq[1], own[1], got_far, qkv_weight[1], score_scale, F32
     )
     far_grads = weight_grads(
-        low_meta, [inputs], [dq[1], dk_far, dv_far], (0, 0, 0), factors, None, quick
-    )
-    far_grads, dx_far, near[0], near[1], mid_shard = tie(far_grads, dx_far, *near, mid_shard)
+        low_meta, [inputs], [dq[1], (pair_far, 0), (pair_far, 1)], (0, 0, 0), factors, None, quick
+    )
+    far_grads, dx_far, got_near, ffn_line = tie(far_grads, dx_far, got_near, ffn_line)
     far_grads = swap(far_grads)
-    dx, dk_near, dv_near, sums_near = input_backward(
-        dx_far, dq[0], dk[0][0], near[0], dv[0][0], near[1], qkv_weight[0], score_scale, BF16
+    dx, pair_near, sums_near = input_backward(
+        dx_far, dq[0], own[0], got_near, qkv_weight[0], score_scale, BF16
     )
     grad_out = home_pieces(dx)
     grad_out, far_grads, output_back = tie(grad_out, far_grads, output_back)
     output = rows_at(output_back, inverse)
     grad_back = go_home(grad_out)
-    far_grads, ffn_shard = tie(far_grads, ffn_shard)
+    far_grads, mid_line = tie(far_grads, mid_line)
+    ffn_shard = wide_scatter(ffn_line, PLANE_GROUPS) if quick else ffn_line
+    mid_shard = wide_scatter(mid_line, PLANE_GROUPS) if quick else mid_line
+    ffn_shard, mid_shard = ffn_shard.astype(F32), mid_shard.astype(F32)
     qkv_grads = weight_grads(
-        low_meta, [inputs], [dq[0], dk_near, dv_near], (0, 0, 0), factors, far_grads, quick
+        low_meta, [inputs], [dq[0], (pair_near, 0), (pair_near, 1)], (0, 0, 0), factors, far_grads, quick
     )
     sums_qkv = [sums_near, sums_far]
 
@@ -1096,13 +1130,19 @@
             shift_rows.reshape(-1),
         ]
     )
-    small, qkv_grads = tie(small, qkv_grads)
-    small = sum_everywhere(small)
     if quick:
-        qkv_line, grad_back = tie(scatter_low(qkv_grads), grad_back)
+        small = small + swap(small)
+        small, qkv_grads = tie(small, qkv_grads)
+        qkv_line = scatter_low(qkv_grads)
+        small = sum_low(small)
+        qkv_line, grad_back, mid_shard, ffn_shard, small = tie(
+            qkv_line, grad_back, mid_shard, ffn_shard, small
+        )
         qkv_shard = scatter_plane(qkv_line)
+        small = sum_planes(small)
     else:
-        qkv_shard = slow_scatter(qkv_grads)
+        qkv_shard = wide_scatter(qkv_grads).astype(F32)
+        small = lax.psum(small, ("dp", "tensor"))
     grad_tokens = rows_at(grad_back, inverse)
     in_end = 8 * half
     hidden_end = in_end + 2 * units

time: 535 us -> 512 us (0.957)
  matrix products: 32 us -> 0 us
  Pallas kernels: 196 us -> 218 us
  starting transfers between devices: 84.4 us -> 64 us
  waiting for transfers between devices: 122 us -> 136 us
  local copies, waits for them, and re-layouts: 51 us -> 43.2 us
    dot_general x10 -> x0, matrix products: 32 us -> none  [the longest x8 23.1 us: dot_nn(): lax.dot_general(left, right, (((1,), (0,)), ((), ())), preferred_element_...]
    pallas_call x5 -> x9, Pallas kernels: 61.9 us -> 86.5 us  [the longest x2 30.4 us: attend_backward(): pl.pallas_call(functools.partial(backward_kernel, piece, spans), grid_spe...]
    ppermute x24 -> x18, starting transfers between devices: 48.5 us -> 25.4 us  [hop(): return lax.ppermute(value, 'dp', [(i, i ^ bits) for i in range(16)])]
    all_gather x2, waiting for transfers between devices: 32.2 us -> 12.7 us  [slow_gather(): return lax.all_gather(value, 'dp', axis=0, tiled=True)]
    ppermute x18 -> x14, waiting for transfers between devices: 8.94 us -> 23.2 us  [swap(): return lax.ppermute(value, 'tensor', [(0, 1), (1, 0)])]
    ppermute x24 -> x18, waiting for transfers between devices: 68.2 us -> 81 us  [hop(): return lax.ppermute(value, 'dp', [(i, i ^ bits) for i in range(16)])]
    all_to_all x2, waiting for transfers between devices: 4.43 us -> 10.3 us  [arrive(): lax.all_to_all(ordered, 'dp', split_axis=0, concat_axis=0, tiled=True)]
  transfers between devices with their start and end apart: 49 -> 42, of which waited for: 18 -> 16; matrix products, arithmetic and copies ran while one was open for 16% -> 11% of each run, Pallas kernels for 32% -> 36%
where the time goes in v4:
time: 512 us; the launch traced here: 502 us
  Pallas kernels  218 us (43%)
  waiting for transfers between devices  136 us (27%)
  starting transfers between devices  64 us (12%)
  local copies, waits for them, and re-layouts  43.2 us (8%)
  other arithmetic  23.2 us (5%)
  between operations  18 us (4%)
    ppermute x18, waiting for transfers between devices, hop(): return lax.ppermute(value, 'dp', [(i, i ^ bits) for i in range(16)])  81 us
    pallas_call x6, Pallas kernels, weight_grads(): pl.pallas_call(functools.partial(grads_kernel, sides, counts, factors, ex...  50.1 us
    pallas_call x2, Pallas kernels, attend_backward(): pl.pallas_call(functools.partial(backward_kernel, piece, spans), grid_spe...  30.4 us
    ppermute x18, starting transfers between devices, hop(): return lax.ppermute(value, 'dp', [(i, i ^ bits) for i in range(16)])  25.4 us
    pallas_call x1, Pallas kernels, mid_backward(): pl.pallas_call(functools.partial(mid_backward_kernel, score_scale, rows),...  25 us
    all_to_all x2, starting transfers between devices, go_home(): lax.all_to_all(outgoing, 'dp', split_axis=0, concat_axis=0, tiled=True)  24.1 us
    ppermute x14, waiting for transfers between devices, swap(): return lax.ppermute(value, 'tensor', [(0, 1), (1, 0)])  23.2 us
    pallas_call x1, Pallas kernels, mid_forward(): pl.pallas_call(functools.partial(mid_forward_kernel, score_scale), grid_s...  21.7 us
  transfers between devices with their start and end apart: 42, of which 16 were waited for; matrix products, arithmetic and copies ran while one was open for 11% of the time, Pallas kernels for 36%

profile of v4, /device:TPU:0, one launch (start us, length us, event | category | flops | bytes accessed | tf_op | source)
XLA Modules:
  0.0 502.1 jit_solution(11876009218904991756)
XLA Ops:
  8.3 1.5 pad_maximum_fusion.3
  9.8 1.7 pad_maximum_fusion.2
  11.6 3.1 collective-permute-start
  14.7 2.6 collective-permute-start.1
  17.5 1.8 gather_fusion.2
  19.3 6.8 %collective-permute-done.1 = bf16[48,1152]{1,0:T(8,128)(2,1)S(1)} collective-permute-done((bf16[48,1152]{1,0:T(8,128)(2,1)S(1)}, bf16[48,1152]{1,0:T(8,128)(2,1)S(1)}, u32[]{:S(2)}, u32[]{:S(2)}) %collective-permute-start.1) | collective-permute-done | bytes 110624 | tf_op jit(solution)/shard_map/ppermute | solution.py:790
  26.2 7.6 %all-to-all-start = ((bf16[32,32,768]{2,1,0:T(8,128)(2,1)}), bf16[32,32,768]{2,1,0:T(8,128)(2,1)S(1)}, u32[]{:S(2)}, u32[]{:S(2)}) async-start(bf16[32,32,768]{2,1,0:T(8,128)(2,1)} %gather_fusion.2), calls=%async_computation | async-start | bytes 3145728 | tf_op jit(solution)/shard_map/all_to_all | solution.py:952
  33.9 3.2 gather_fusion.1
  40.4 2.0 collective-permute-start.3
  42.4 1.5 collective-permute-start.4
  44.1 21.3 %collective-permute-done.3.first_ref = bf16[4,48,1152]{2,1,0:T(8,128)(2,1)S(1)} collective-permute-done((bf16[4,48,1152]{2,1,0:T(8,128)(2,1)S(1)}, bf16[4,48,1152]{2,1,0:T(8,128)(2,1)S(1)}, u32[]{:S(2)}, u32[]{:S(2)}) %collective-permute-start.3) | collective-permute-done | bytes 442400 | tf_op jit(solution)/shard_map/ppermute | solution.py:790
  65.5 21.5 %collective-permute-done.5.third_ref = bf16[4,48,1152]{2,1,0:T(8,128)(2,1)} collective-permute-done((bf16[4,48,1152]{2,1,0:T(8,128)(2,1)S(1)}, bf16[4,48,1152]{2,1,0:T(8,128)(2,1)}, u32[]{:S(2)}, u32[]{:S(2)}) %collective-permute-start.5) | collective-permute-done | bytes 442400 | tf_op jit(solution)/shard_map/ppermute | solution.py:790
  87.0 4.4 assemble.1
  92.0 2.0 compare_select_fusion.5
  94.0 1.7 gather_fusion.3
  95.8 5.0 project.3
  105.8 2.5 fusion.13.valid_ref
  111.5 5.0 project.2
  117.6 10.7 %attend_forward.2 = (bf16[896,384]{1,0:T(8,128)(2,1)}, f32[7,8,256]{2,1,0:T(8,128)}) custom-call(s32[3]{0:T(128)} %pad_add_fusion.meta, bf16[896,384]{1,0:T(8,128)(2,1)} %get-tuple-element.128.q_ref, bf16[896,768]{1,0:T(8,128)(2,1)} %get-tuple-element.129.refs_0_, bf16[896,768]{1,0:T(8,128)(2,1)} %copy-done.5), custom_call_target="tpu_custom_call" | custom-call | flops 1000 | bytes 1000 | tf_op jit(solution)/shard_map/attend_forward/pallas_call | solution.py:206
  128.9 5.8 %collective-permute-done.10 = bf16[2,64,768]{2,1,0:T(8,128)(2,1)S(1)} collective-permute-done((bf16[2,64,768]{2,1,0:T(8,128)(2,1)S(1)}, bf16[2,64,768]{2,1,0:T(8,128)(2,1)S(1)}, u32[]{:S(2)}, u32[]{:S(2)}) %collective-permute-start.10) | collective-permute-done | bytes 196640 | tf_op jit(solution)/shard_map/ppermute | solution.py:786
  136.0 10.8 %attend_forward.3 = (bf16[896,384]{1,0:T(8,128)(2,1)}, f32[7,8,256]{2,1,0:T(8,128)}) custom-call(s32[3]{0:T(128)} %pad_add_fusion.meta, bf16[896,384]{1,0:T(8,128)(2,1)} %get-tuple-element.133.q_ref, bf16[896,768]{1,0:T(8,128)(2,1)} %get-tuple-element.130.refs_0_, bf16[896,768]{1,0:T(8,128)(2,1)} %collective-permute-done.9.refs_1_), custom_call_target="tpu_custom_call" | custom-call | flops 1000 | bytes 1000 | tf_op jit(solution)/shard_map/attend_forward/pallas_call | solution.py:206
  146.8 1.6 copy-done.3
  148.4 21.7 %mid_forward.1 = (f32[896,768]{1,0:T(8,128)}, f32[896,1]{1,0:T(8,128)}, f32[896,768]{1,0:T(8,128)}, f32[896,1]{1,0:T(8,128)}, bf16[896,768]{1,0:T(8,128)(2,1)}, ...) custom-call(s32[3]{0:T(128)} %pad_add_fusion.meta, ...), custom_call_target="tpu_custom_call" | custom-call | flops 6341787 | bytes 13762 | tf_op jit(solution)/shard_map/mid_forward/pallas_call | solution.py:663
  170.0 12.7 %all-gather.5.cloned.1.call-done.expand.reduce.in0.out0 = bf16[768,3072]{1,0:T(8,128)(2,1)} async-done(((bf16[48,3072]{1,0:T(8,128)(2,1)}), bf16[768,3072]{1,0:T(8,128)(2,1)}) %all-gather.5.cloned.1.call-update) | async-done | bytes 4718608 | tf_op jit(solution)/shard_map/all_gather | solution.py:965
  182.7 4.3 all-to-all-start.1
  190.8 10.2 %ffn_forward.2 = (bf16[896,1536]{1,0:T(8,128)(2,1)}, bf16[896,1536]{1,0:T(8,128)(2,1)}, f32[896,768]{1,0:T(8,128)}) custom-call(bf16[896,768]{1,0:T(8,128)(2,1)} %get-tuple-element.138.hidden_ref.refs_0_, f32[896,768]{1,0:T(8,128)} %get-tuple-element.141.base_ref.unit2_ref, bf16[768,3072]{1,0:T(8,128)(2,1)} %all-gather.5.cloned.1.call-done.expand.reduce.in0.out0, ...), custom_call_target="tpu_custom_call" | custom-call | flops 1000 | bytes 1000 | tf_op jit(solution)/shard_map/ffn_forward/pallas_call | solution.py:575
  201.0 10.0 %ffn_forward.3 = (bf16[896,1536]{1,0:T(8,128)(2,1)}, bf16[896,1536]{1,0:T(8,128)(2,1)}, f32[896,768]{1,0:T(8,128)}) custom-call(bf16[896,768]{1,0:T(8,128)(2,1)} %get-tuple-element.138.hidden_ref.refs_0_, f32[896,768]{1,0:T(8,128)} %get-tuple-element.143.base_ref, bf16[768,3072]{1,0:T(8,128)(2,1)} %collective-permute-done.12.expand.reduce.in1.out1, ...), custom_call_target="tpu_custom_call" | custom-call | flops 1000 | bytes 1000 | tf_op jit(solution)/shard_map/ffn_forward/pallas_call | solution.py:575
  211.0 10.3 %all-to-all-done.1 = bf16[32,32,768]{2,1,0:T(8,128)(2,1)S(1)} async-done(((bf16[32,32,768]{2,1,0:T(8,128)(2,1)}), bf16[32,32,768]{2,1,0:T(8,128)(2,1)S(1)}, u32[]{:S(2)}, u32[]{:S(2)}) %all-to-all-start.1) | async-done | bytes 1572896 | tf_op jit(solution)/shard_map/all_to_all | solution.py:952
  221.2 1.7 gather_fusion.4
  223.0 18.3 %ffn_backward.1 = (bf16[896,768]{1,0:T(8,128)(2,1)}, bf16[896,768]{1,0:T(8,128)(2,1)}, f32[896,768]{1,0:T(8,128)}, f32[8,768]{1,0:T(8,128)}, bf16[896,1536]{1,0:...) custom-call(f32[896,768]{1,0:T(8,128)} %get-tuple-element.146.h3_ref, ...), custom_call_target="tpu_custom_call" | custom-call | flops 1000 | bytes 1000 | tf_op jit(solution)/shard_map/ffn_backward/pallas_call | solution.py:627
  241.3 9.9 %weight_grads.6 = bf16[4,4,48,3072]{3,2,1,0:T(8,128)(2,1)} custom-call(s32[1]{0:T(128)} %bitcast.1.meta, bf16[896,768]{1,0:T(8,128)(2,1)} %get-tuple-element.138.hidden_ref.refs_0_, bf16[896,768]{1,0:T(8,128)(2,1)} %get-tuple-element.151.refs_1_, bf16[896,1536]{1,0:T(8,128)(2,1)} %get-tuple-element.154.refs_2_, bf16[896,1536]{1,0:T(8,128)(2,1)} %get-tuple-element.155.refs_3_), custom_call_target="tpu_custom_call" | custom-call | flops 4227858 | bytes 16515 | tf_op jit(solution)/shard_map/weight_grads/pallas_call | solution.py:326
  251.2 8.2 %collective-permute-done.13.refs_4_ = bf16[4,4,48,3072]{3,2,1,0:T(8,128)(2,1)} collective-permute-done((bf16[4,4,48,3072]{3,2,1,0:T(8,128)(2,1)}, bf16[4,4,48,3072]{3,2,1,0:T(8,128)(2,1)}, u32[]{:S(2)}, u32[]{:S(2)}) %collective-permute-start.13) | collective-permute-done | bytes 4718624 | tf_op jit(solution)/shard_map/ppermute | solution.py:786
  259.5 10.7 %weight_grads.7 = bf16[4,4,48,3072]{3,2,1,0:T(8,128)(2,1)} custom-call(s32[1]{0:T(128)} %bitcast.1.meta, bf16[896,768]{1,0:T(8,128)(2,1)} %get-tuple-element.138.hidden_ref.refs_0_, bf16[896,768]{1,0:T(8,128)(2,1)} %get-tuple-element.151.refs_1_, bf16[896,1536]{1,0:T(8,128)(2,1)} %get-tuple-element.152.refs_2_, ...), custom_call_target="tpu_custom_call" | custom-call | flops 4227858 | bytes 16515 | tf_op jit(solution)/shard_map/weight_grads/pallas_call | solution.py:326
  274.8 8.5 %all-to-all-start.2 = ((bf16[32,32,768]{2,1,0:T(8,128)(2,1)}), bf16[32,32,768]{2,1,0:T(8,128)(2,1)S(1)}, u32[]{:S(2)}, u32[]{:S(2)}) async-start(bf16[32,32,768]{2,1,0:T(8,128)(2,1)} %broadcast_select_fusion.1), calls=%async_computation.2 | async-start | bytes 3145728 | tf_op jit(solution)/shard_map/all_to_all | solution.py:946
  283.3 25.0 %mid_backward.1 = (bf16[896,768]{1,0:T(8,128)(2,1)}, f32[896,768]{1,0:T(8,128)}, bf16[896,768]{1,0:T(8,128)(2,1)}, f32[8,768]{1,0:T(8,128)}, bf16[896,384]{1,0:T...) custom-call(s32[3]{0:T(128)} %pad_add_fusion.meta, ...), custom_call_target="tpu_custom_call" | custom-call | flops 6341787 | bytes 13762 | tf_op jit(solution)/shard_map/mid_backward/pallas_call | solution.py:706
  308.3 8.9 %all-to-all-done.2 = bf16[32,32,768]{2,1,0:T(8,128)(2,1)S(1)} async-done(((bf16[32,32,768]{2,1,0:T(8,128)(2,1)}), bf16[32,32,768]{2,1,0:T(8,128)(2,1)S(1)}, u32[]{:S(2)}, u32[]{:S(2)}) %all-to-all-start.2) | async-done | bytes 1572896 | tf_op jit(solution)/shard_map/all_to_all | solution.py:946
  317.2 1.9 collective-permute-done.14.got_ref
  319.9 3.5 memory_backward.1
  323.3 8.2 %weight_grads.8 = bf16[4,4,48,1920]{3,2,1,0:T(8,128)(2,1)} custom-call(s32[1]{0:T(128)} %bitcast.1.meta, bf16[896,768]{1,0:T(8,128)(2,1)} %get-tuple-element.168.refs_0_, bf16[896,768]{1,0:T(8,128)(2,1)} %get-tuple-element.169.refs_1_, bf16[128,768]{1,0:T(8,128)(2,1)} %bitcast.126, bf16[896,768]{1,0:T(8,128)(2,1)} %get-tuple-element.170.refs_3_, ...), custom_call_target="tpu_custom_call" | custom-call | flops 2642411 | bytes 10321 | tf_op jit(solution)/shard_map/weight_grads/pallas_call | solution.py:326
  331.7 5.6 %collective-permute-done.15.refs_9_ = bf16[4,4,48,1920]{3,2,1,0:T(8,128)(2,1)} collective-permute-done((bf16[4,4,48,1920]{3,2,1,0:T(8,128)(2,1)}, bf16[4,4,48,1920]{3,2,1,0:T(8,128)(2,1)}, u32[]{:S(2)}, u32[]{:S(2)}) %collective-permute-start.15) | collective-permute-done | bytes 2949152 | tf_op jit(solution)/shard_map/ppermute | solution.py:786
  337.3 9.1 %weight_grads.9 = bf16[4,4,48,1920]{3,2,1,0:T(8,128)(2,1)} custom-call(s32[1]{0:T(128)} %bitcast.1.meta, bf16[896,768]{1,0:T(8,128)(2,1)} %get-tuple-element.168.refs_0_, bf16[896,768]{1,0:T(8,128)(2,1)} %get-tuple-element.169.refs_1_, bf16[128,768]{1,0:T(8,128)(2,1)} %bitcast.127, bf16[896,768]{1,0:T(8,128)(2,1)} %get-tuple-element.170.refs_3_, ...), custom_call_target="tpu_custom_call" | custom-call | flops 2642411 | bytes 10321 | tf_op jit(solution)/shard_map/weight_grads/pallas_call | solution.py:326
  346.6 15.1 %attend_backward.2 = (bf16[896,384]{1,0:T(8,128)(2,1)}, f32[896,768]{1,0:T(8,128)}, bf16[896,768]{1,0:T(8,128)(2,1)}) custom-call(s32[3]{0:T(128)} %pad_add_fusion.meta, bf16[896,384]{1,0:T(8,128)(2,1)} %get-tuple-element.133.q_ref, bf16[896,384]{1,0:T(8,128)(2,1)} %get-tuple-element.183.g_ref, f32[7,8,256]{2,1,0:T(8,128)} %get-tuple-element.184.lse_ref, ...), custom_call_target="tpu_custom_call" | custom-call | flops 1000 | bytes 1000 | tf_op jit(solution)/shard_map/attend_backward/pallas_call | solution.py:223
  361.7 15.3 %attend_backward.3 = (bf16[896,384]{1,0:T(8,128)(2,1)}, f32[896,768]{1,0:T(8,128)}, bf16[896,768]{1,0:T(8,128)(2,1)}) custom-call(s32[3]{0:T(128)} %pad_add_fusion.meta, bf16[896,384]{1,0:T(8,128)(2,1)} %get-tuple-element.128.q_ref, bf16[896,384]{1,0:T(8,128)(2,1)} %get-tuple-element.187.g_ref, f32[7,8,256]{2,1,0:T(8,128)} %get-tuple-element.188.lse_ref, ...), custom_call_target="tpu_custom_call" | custom-call | flops 1000 | bytes 1000 | tf_op jit(solution)/shard_map/attend_backward/pallas_call | solution.py:223
  377.6 6.4 %input_backward.2 = (f32[896,768]{1,0:T(8,128)}, bf16[896,768]{1,0:T(8,128)(2,1)}, f32[8,384]{1,0:T(8,128)}) custom-call(f32[896,768]{1,0:T(8,128)} %get-tuple-element.190.base_ref, bf16[896,384]{1,0:T(8,128)(2,1)} %get-tuple-element.189.dq_ref.refs_1_, f32[896,768]{1,0:T(8,128)} %get-tuple-element.191.own_ref, ...), custom_call_target="tpu_custom_call" | custom-call | flops 1000 | bytes 1000 | tf_op jit(solution)/shard_map/input_backward/pallas_call | solution.py:768
  384.0 5.9 %weight_grads.10 = bf16[4,4,48,1152]{3,2,1,0:T(8,128)(2,1)} custom-call(s32[1]{0:T(128)} %bitcast.1.meta, bf16[896,768]{1,0:T(8,128)(2,1)} %bitcast.119, bf16[896,384]{1,0:T(8,128)(2,1)} %get-tuple-element.189.dq_ref.refs_1_, bf16[896,768]{1,0:T(8,128)(2,1)} %get-tuple-element.193.refs_2_.refs_3_, bf16[896,768]{1,0:T(8,128)(2,1)} %get-tuple-element.193.refs_2_.refs_3_), custom_call_target="tpu_custom_call" | custom-call | flops 1585446 | bytes 6193 | tf_op jit(solution)/shard_map/weight_grads/pallas_call | solution.py:326
  393.6 6.2 %input_backward.3 = (bf16[896,768]{1,0:T(8,128)(2,1)}, bf16[896,768]{1,0:T(8,128)(2,1)}, f32[8,384]{1,0:T(8,128)}) custom-call(f32[896,768]{1,0:T(8,128)} %get-tuple-element.197.base_ref, bf16[896,384]{1,0:T(8,128)(2,1)} %get-tuple-element.198.dq_ref.refs_1_, f32[896,768]{1,0:T(8,128)} %get-tuple-element.199.own_ref, bf16[896,768]{1,0:T(8,128)(2,1)} %copy-done.10, ...), custom_call_target="tpu_custom_call" | custom-call | flops 1000 | bytes 1000 | tf_op jit(solution)/shard_map/input_backward/pallas_call | solution.py:768
  399.8 2.0 gather_fusion.6
  403.1 15.6 %all-to-all-start.3 = ((bf16[32,32,768]{2,1,0:T(8,128)(2,1)}), bf16[32,32,768]{2,1,0:T(8,128)(2,1)S(1)}, u32[]{:S(2)}, u32[]{:S(2)}) async-start(bf16[32,32,768]{2,1,0:T(8,128)(2,1)} %broadcast_select_fusion), calls=%async_computation.5 | async-start | bytes 3145728 | tf_op jit(solution)/shard_map/all_to_all | solution.py:946
  422.5 6.3 %weight_grads.11 = bf16[4,4,48,1152]{3,2,1,0:T(8,128)(2,1)} custom-call(s32[1]{0:T(128)} %bitcast.1.meta, bf16[896,768]{1,0:T(8,128)(2,1)} %bitcast.120, bf16[896,384]{1,0:T(8,128)(2,1)} %get-tuple-element.198.dq_ref.refs_1_, bf16[896,768]{1,0:T(8,128)(2,1)} %get-tuple-element.212.refs_2_.refs_3_, bf16[896,768]{1,0:T(8,128)(2,1)} %get-tuple-element.212.refs_2_.refs_3_, ...), custom_call_target="tpu_custom_call" | custom-call | flops 1585446 | bytes 6193 | tf_op jit(solution)/shard_map/weight_grads/pallas_call | solution.py:326
  428.8 1.9 collective-permute-start.23
  430.7 1.5 collective-permute-start.24
  432.3 2.4 slice_bitcast_fusion.2
  434.7 1.9 collective-permute-start.20
  436.6 1.5 collective-permute-start.21
  438.1 1.8 gather_fusion.7
  440.0 16.5 %collective-permute-done.20 = bf16[4,48,1152]{2,1,0:T(8,128)(2,1)} collective-permute-done((bf16[4,48,1152]{2,1,0:T(8,128)(2,1)}, bf16[4,48,1152]{2,1,0:T(8,128)(2,1)}, u32[]{:S(2)}, u32[]{:S(2)}) %collective-permute-start.20) | collective-permute-done | bytes 442400 | tf_op jit(solution)/shard_map/ppermute | solution.py:790
  456.6 2.7 collective-permute-done.21
  459.2 10.9 %collective-permute-done.22 = bf16[4,48,1152]{2,1,0:T(8,128)(2,1)S(1)} collective-permute-done((bf16[4,48,1152]{2,1,0:T(8,128)(2,1)}, bf16[4,48,1152]{2,1,0:T(8,128)(2,1)S(1)}, u32[]{:S(2)}, u32[]{:S(2)}) %collective-permute-start.22) | collective-permute-done | bytes 442400 | tf_op jit(solution)/shard_map/ppermute | solution.py:790
  470.1 1.5 fusion.2
  473.8 2.2 collective-permute-start.29
  477.2 1.5 collective-permute-start.31
  480.9 2.1 collective-permute-start.27
  483.8 1.8 gather_fusion.8
  486.3 1.5 collective-permute-start.28
  (200 shorter events, 47.2 us)
Async XLA Ops:
  7.2 10.3 %copy-start = (bf16[32,32,768]{2,1,0:T(8,128)(2,1)S(1)}, bf16[32,32,768]{2,1,0:T(8,128)(2,1)}, u32[]{:S(2)}) copy-start(bf16[32,32,768]{2,1,0:T(8,128)(2,1)} %param.17) | copy-start | bytes 4718596
  7.2 4.4 copy-start.11
  7.2 10.3 %copy-start.18 = (s32[32]{0:T(128)S(1)}, s32[32]{0:T(128)}, u32[]{:S(2)}) copy-start(s32[32]{0:T(128)} %param.20) | copy-start | bytes 388
  7.2 121.1 %all-gather.3.cloned.1.call-start = ((), (), s32[]{:S(2)}) async-start(), calls=%async_computation.8 | async-start | bytes 3133440 | tf_op jit(solution)/shard_map/all_gather | solution.py:965
  9.8 172.9 %all-gather.5.cloned.1.call-start = ((), (), s32[]{:S(2)}) async-start(), calls=%async_computation.9 | async-start | bytes 5013504 | tf_op jit(solution)/shard_map/all_gather | solution.py:965
  11.6 7.7 %collective-permute-start = (bf16[48,1152]{1,0:T(8,128)(2,1)S(1)}, bf16[48,1152]{1,0:T(8,128)(2,1)S(1)}, u32[]{:S(2)}, u32[]{:S(2)}) collective-permute-start(bf16[48,1152]{1,0:T(8,128)(2,1)S(1)} %bitcast.135), channel_id=1, source_target_pairs={{0,8},{2,10},{4,12},{6,14},{8,0},{10,2},{12,4},{14,6},{16,24},{18,... | collective-permute-start | bytes 331784 | tf_op jit(solution)/shard_map/ppermute | solution.py:790
  14.7 11.4 %collective-permute-start.1 = (bf16[48,1152]{1,0:T(8,128)(2,1)S(1)}, bf16[48,1152]{1,0:T(8,128)(2,1)S(1)}, u32[]{:S(2)}, u32[]{:S(2)}) collective-permute-start(bf16[48,1152]{1,0:T(8,128)(2,1)S(1)} %bitcast.136), channel_id=1, source_target_pairs={{0,16},{2,18},{4,20},{6,22},{8,24},{10,26},{12,28},{14,30},{16,0},... | collective-permute-start | bytes 331784 | tf_op jit(solution)/shard_map/ppermute | solution.py:790
  17.3 8.8 %collective-permute-start.2 = (bf16[48,1152]{1,0:T(8,128)(2,1)S(1)}, bf16[48,1152]{1,0:T(8,128)(2,1)S(1)}, u32[]{:S(2)}, u32[]{:S(2)}) collective-permute-start(bf16[48,1152]{1,0:T(8,128)(2,1)S(1)} %bitcast.137), channel_id=1, source_target_pairs={{0,24},{2,26},{4,28},{6,30},{8,16},{10,18},{12,20},{14,22},{16,8},... | collective-permute-start | bytes 331784 | tf_op jit(solution)/shard_map/ppermute | solution.py:790
  26.1 17.7 %copy-start.8 = (bf16[4,48,1152]{2,1,0:T(8,128)(2,1)}, bf16[4,48,1152]{2,1,0:T(8,128)(2,1)S(1)}, u32[]{:S(2)}) copy-start(bf16[4,48,1152]{2,1,0:T(8,128)(2,1)S(1)} %pad_maximum_fusion.own_ref) | copy-start | bytes 1327108
  26.1 7.6 %copy-start.15 = (f32[4,384]{1,0:T(4,128)S(1)}, f32[4,384]{1,0:T(4,128)}, u32[]{:S(2)}) copy-start(f32[4,384]{1,0:T(4,128)} %refs_10_.1) | copy-start | bytes 18436
  26.2 7.6 %copy-start.16 = (f32[1536]{0:T(1024)S(1)}, f32[1536]{0:T(1024)}, u32[]{:S(2)}) copy-start(f32[1536]{0:T(1024)} %param.30) | copy-start | bytes 18436
  26.2 60.8 %all-to-all-start = ((bf16[32,32,768]{2,1,0:T(8,128)(2,1)}), bf16[32,32,768]{2,1,0:T(8,128)(2,1)S(1)}, u32[]{:S(2)}, u32[]{:S(2)}) async-start(bf16[32,32,768]{2,1,0:T(8,128)(2,1)} %gather_fusion.2), calls=%async_computation | async-start | bytes 3145728 | tf_op jit(solution)/shard_map/all_to_all | solution.py:952
  33.8 75.8 %collective-permute-start.7 = (f32[3072]{0:T(1024)S(1)}, f32[3072]{0:T(1024)S(1)}, u32[]{:S(2)}, u32[]{:S(2)}) collective-permute-start(f32[3072]{0:T(1024)S(1)} %pad_maximum_fusion.4), channel_id=1, source_target_pairs={{0,1},{1,0},{2,3},{3,2},{4,5},{5,4},{6,7},{7,6},{8,9},{9,8},{10,11... | collective-permute-start | bytes 36872 | tf_op jit(solution)/shard_map/ppermute | solution.py:786
  33.9 3.8 copy-start.2
  40.4 25.1 %collective-permute-start.3 = (bf16[4,48,1152]{2,1,0:T(8,128)(2,1)S(1)}, bf16[4,48,1152]{2,1,0:T(8,128)(2,1)S(1)}, u32[]{:S(2)}, u32[]{:S(2)}) collective-permute-start(bf16[4,48,1152]{2,1,0:T(8,128)(2,1)S(1)} %pad_maximum_fusion.own_ref), channel_id=1, source_target_pairs={{0,2},{2,0},{4,6},{6,4},{8,10},{10,8},{12,14},{14,12},{16,18},{18,... | collective-permute-start | bytes 1327112 | tf_op jit(solution)/shard_map/ppermute | solution.py:790
  42.4 23.1 %collective-permute-start.4 = (bf16[4,48,1152]{2,1,0:T(8,128)(2,1)S(1)}, bf16[4,48,1152]{2,1,0:T(8,128)(2,1)S(1)}, u32[]{:S(2)}, u32[]{:S(2)}) collective-permute-start(bf16[4,48,1152]{2,1,0:T(8,128)(2,1)S(1)} %pad_maximum_fusion.own_ref), channel_id=1, source_target_pairs={{0,4},{2,6},{4,0},{6,2},{8,12},{10,14},{12,8},{14,10},{16,20},{18,... | collective-permute-start | bytes 1327112 | tf_op jit(solution)/shard_map/ppermute | solution.py:790
  43.9 43.2 %collective-permute-start.5 = (bf16[4,48,1152]{2,1,0:T(8,128)(2,1)S(1)}, bf16[4,48,1152]{2,1,0:T(8,128)(2,1)}, u32[]{:S(2)}, u32[]{:S(2)}) collective-permute-start(bf16[4,48,1152]{2,1,0:T(8,128)(2,1)S(1)} %pad_maximum_fusion.own_ref), channel_id=1, source_target_pairs={{0,6},{2,4},{4,2},{6,0},{8,14},{10,12},{12,10},{14,8},{16,22},{18,... | collective-permute-start | bytes 1327112 | tf_op jit(solution)/shard_map/ppermute | solution.py:790
  65.5 21.6 %copy-start.12 = (bf16[4,48,1152]{2,1,0:T(8,128)(2,1)}, bf16[4,48,1152]{2,1,0:T(8,128)(2,1)S(1)}, u32[]{:S(2)}) copy-start(bf16[4,48,1152]{2,1,0:T(8,128)(2,1)S(1)} %collective-permute-done.3.first_ref) | copy-start | bytes 1327108
  65.5 21.6 %copy-start.13 = (bf16[4,48,1152]{2,1,0:T(8,128)(2,1)}, bf16[4,48,1152]{2,1,0:T(8,128)(2,1)S(1)}, u32[]{:S(2)}) copy-start(bf16[4,48,1152]{2,1,0:T(8,128)(2,1)S(1)} %collective-permute-done.4.second_ref) | copy-start | bytes 1327108
  91.4 18.8 %collective-permute-start.6 = (bf16[768,1152]{1,0:T(8,128)(2,1)}, bf16[768,1152]{1,0:T(8,128)(2,1)S(1)}, u32[]{:S(2)}, u32[]{:S(2)}) collective-permute-start(bf16[768,1152]{1,0:T(8,128)(2,1)} %bitcast.109), channel_id=1, source_target_pairs={{0,1},{1,0},{2,3},{3,2},{4,5},{5,4},{6,7},{7,6},{8,9},{9,8},{10,11... | collective-permute-start | bytes 5308424 | tf_op jit(solution)/shard_map/ppermute | solution.py:786
  100.8 15.7 %collective-permute-start.8 = (bf16[896,768]{1,0:T(8,128)(2,1)}, bf16[896,768]{1,0:T(8,128)(2,1)S(1)}, u32[]{:S(2)}, u32[]{:S(2)}) collective-permute-start(bf16[896,768]{1,0:T(8,128)(2,1)} %get-tuple-element.130.refs_0_), channel_id=1, source_target_pairs={{0,1},{1,0},{2,3},{3,2},{4,5},{5,4},{6,7},{7,6},{8,9},{9,8},{10,11... | collective-permute-start | bytes 4128776 | tf_op jit(solution)/shard_map/ppermute | solution.py:786
  110.2 1.2 copy-start.4
  116.5 1.1 copy-start.5
  117.6 11.3 %copy-start.9 = (bf16[2,64,768]{2,1,0:T(8,128)(2,1)S(1)}, bf16[2,64,768]{2,1,0:T(8,128)(2,1)}, u32[]{:S(2)}) copy-start(bf16[2,64,768]{2,1,0:T(8,128)(2,1)} %param.18) | copy-start | bytes 589828
  128.3 18.4 %collective-permute-start.11 = (bf16[768,1920]{1,0:T(8,128)(2,1)}, bf16[768,1920]{1,0:T(8,128)(2,1)S(1)}, u32[]{:S(2)}, u32[]{:S(2)}) collective-permute-start(bf16[768,1920]{1,0:T(8,128)(2,1)} %all-gather.3.cloned.1.call-done.refs_0_.refs_2_.refs_4_.refs_6_.refs_8_.refs_10_.wk0.wv0), channel_id=1, source_target_pairs={{0,1},{1,0},{2,3},{3,2},{4,5},{5,4},{6,7},{7,6},{8,9},{9,8},{10,11... | collective-permute-start | bytes 8847368 | tf_op jit(solution)/shard_map/ppermute | solution.py:786
  128.4 7.6 %collective-permute-start.9 = (bf16[896,768]{1,0:T(8,128)(2,1)}, bf16[896,768]{1,0:T(8,128)(2,1)}, u32[]{:S(2)}, u32[]{:S(2)}) collective-permute-start(bf16[896,768]{1,0:T(8,128)(2,1)} %get-tuple-element.129.refs_0_), channel_id=1, source_target_pairs={{0,1},{1,0},{2,3},{3,2},{4,5},{5,4},{6,7},{7,6},{8,9},{9,8},{10,11... | collective-permute-start | bytes 4128776 | tf_op jit(solution)/shard_map/ppermute | solution.py:786
  128.8 5.9 %collective-permute-start.10 = (bf16[2,64,768]{2,1,0:T(8,128)(2,1)S(1)}, bf16[2,64,768]{2,1,0:T(8,128)(2,1)S(1)}, u32[]{:S(2)}, u32[]{:S(2)}) collective-permute-start(bf16[2,64,768]{2,1,0:T(8,128)(2,1)S(1)} %copy-done.9), channel_id=1, source_target_pairs={{0,1},{1,0},{2,3},{3,2},{4,5},{5,4},{6,7},{7,6},{8,9},{9,8},{10,11... | collective-permute-start | bytes 589832 | tf_op jit(solution)/shard_map/ppermute | solution.py:786
  146.8 1.6 copy-start.3
  182.7 18.3 %collective-permute-start.12 = (bf16[768,3072]{1,0:T(8,128)(2,1)}, bf16[768,3072]{1,0:T(8,128)(2,1)}, u32[]{:S(2)}, u32[]{:S(2)}) collective-permute-start(bf16[768,3072]{1,0:T(8,128)(2,1)} %all-gather.5.cloned.1.call-done.expand.reduce.in0.out0), channel_id=1, source_target_pairs={{0,1},{1,0},{2,3},{3,2},{4,5},{5,4},{6,7},{7,6},{8,9},{9,8},{10,11... | collective-permute-start | bytes 14155784 | tf_op jit(solution)/shard_map/ppermute | solution.py:786
  182.7 38.5 %all-to-all-start.1 = ((bf16[32,32,768]{2,1,0:T(8,128)(2,1)}), bf16[32,32,768]{2,1,0:T(8,128)(2,1)S(1)}, u32[]{:S(2)}, u32[]{:S(2)}) async-start(bf16[32,32,768]{2,1,0:T(8,128)(2,1)} %gather_fusion.1), calls=%async_computation.1 | async-start | bytes 3145728 | tf_op jit(solution)/shard_map/all_to_all | solution.py:952
  187.0 174.7 %reduce-scatter.5.cloned.1.call-start = ((), (), s32[]{:S(2)}) async-start(), calls=%async_computation.10 | async-start | bytes 5898240 | tf_op jit(solution)/shard_map/reduce_scatter | solution.py:846
  251.2 8.3 %collective-permute-start.13 = (bf16[4,4,48,3072]{3,2,1,0:T(8,128)(2,1)}, bf16[4,4,48,3072]{3,2,1,0:T(8,128)(2,1)}, u32[]{:S(2)}, u32[]{:S(2)}) collective-permute-start(bf16[4,4,48,3072]{3,2,1,0:T(8,128)(2,1)} %weight_grads.6), channel_id=1, source_target_pairs={{0,1},{1,0},{2,3},{3,2},{4,5},{5,4},{6,7},{7,6},{8,9},{9,8},{10,11... | collective-permute-start | bytes 14155784 | tf_op jit(solution)/shard_map/ppermute | solution.py:786
  270.1 2.7 copy-start.6
  274.8 42.4 %all-to-all-start.2 = ((bf16[32,32,768]{2,1,0:T(8,128)(2,1)}), bf16[32,32,768]{2,1,0:T(8,128)(2,1)S(1)}, u32[]{:S(2)}, u32[]{:S(2)}) async-start(bf16[32,32,768]{2,1,0:T(8,128)(2,1)} %broadcast_select_fusion.1), calls=%async_computation.2 | async-start | bytes 3145728 | tf_op jit(solution)/shard_map/all_to_all | solution.py:946
  283.3 139.2 %reduce-scatter.7.cloned.1.call-start = ((), (), s32[]{:S(2)}) async-start(), calls=%async_computation.11 | async-start | bytes 3686400 | tf_op jit(solution)/shard_map/reduce_scatter | solution.py:846
  317.2 1.9 collective-permute-start.14
  319.1 0.7 copy-start.14
  331.6 5.7 %collective-permute-start.15 = (bf16[4,4,48,1920]{3,2,1,0:T(8,128)(2,1)}, bf16[4,4,48,1920]{3,2,1,0:T(8,128)(2,1)}, u32[]{:S(2)}, u32[]{:S(2)}) collective-permute-start(bf16[4,4,48,1920]{3,2,1,0:T(8,128)(2,1)} %weight_grads.8), channel_id=1, source_target_pairs={{0,1},{1,0},{2,3},{3,2},{4,5},{5,4},{6,7},{7,6},{8,9},{9,8},{10,11... | collective-permute-start | bytes 8847368 | tf_op jit(solution)/shard_map/ppermute | solution.py:786
  346.4 125.3 %reduce-scatter.11.cloned.1.call-start = ((), (), s32[]{:S(2)}) async-start(), calls=%async_computation.13 | async-start | bytes 1474560 | tf_op jit(solution)/shard_map/reduce_scatter | solution.py:846
  361.7 15.9 %collective-permute-start.16 = (bf16[896,768]{1,0:T(8,128)(2,1)}, bf16[896,768]{1,0:T(8,128)(2,1)}, u32[]{:S(2)}, u32[]{:S(2)}) collective-permute-start(bf16[896,768]{1,0:T(8,128)(2,1)} %get-tuple-element.192), channel_id=1, source_target_pairs={{0,1},{1,0},{2,3},{3,2},{4,5},{5,4},{6,7},{7,6},{8,9},{9,8},{10,11... | collective-permute-start | bytes 4128776 | tf_op jit(solution)/shard_map/ppermute | solution.py:786
  377.1 12.8 %collective-permute-start.17 = (bf16[896,768]{1,0:T(8,128)(2,1)}, bf16[896,768]{1,0:T(8,128)(2,1)S(1)}, u32[]{:S(2)}, u32[]{:S(2)}) collective-permute-start(bf16[896,768]{1,0:T(8,128)(2,1)} %get-tuple-element.195), channel_id=1, source_target_pairs={{0,1},{1,0},{2,3},{3,2},{4,5},{5,4},{6,7},{7,6},{8,9},{9,8},{10,11... | collective-permute-start | bytes 4128776 | tf_op jit(solution)/shard_map/ppermute | solution.py:786
  384.0 9.5 %copy-start.17 = (f32[8,768]{1,0:T(8,128)S(1)}, f32[8,768]{1,0:T(8,128)}, u32[]{:S(2)}) copy-start(f32[8,768]{1,0:T(8,128)} %get-tuple-element.206) | copy-start | bytes 73732
  389.9 3.6 copy-start.10
  389.9 13.2 %collective-permute-start.18 = (bf16[4,4,48,1152]{3,2,1,0:T(8,128)(2,1)}, bf16[4,4,48,1152]{3,2,1,0:T(8,128)(2,1)}, u32[]{:S(2)}, u32[]{:S(2)}) collective-permute-start(bf16[4,4,48,1152]{3,2,1,0:T(8,128)(2,1)} %weight_grads.10), channel_id=1, source_target_pairs={{0,1},{1,0},{2,3},{3,2},{4,5},{5,4},{6,7},{7,6},{8,9},{9,8},{10,11... | collective-permute-start | bytes 5308424 | tf_op jit(solution)/shard_map/ppermute | solution.py:786
  403.1 70.7 %all-to-all-start.3 = ((bf16[32,32,768]{2,1,0:T(8,128)(2,1)}), bf16[32,32,768]{2,1,0:T(8,128)(2,1)S(1)}, u32[]{:S(2)}, u32[]{:S(2)}) async-start(bf16[32,32,768]{2,1,0:T(8,128)(2,1)} %broadcast_select_fusion), calls=%async_computation.5 | async-start | bytes 3145728 | tf_op jit(solution)/shard_map/all_to_all | solution.py:946
  418.7 54.1 %reduce-scatter.9.cloned.1.call-start = ((), (), s32[]{:S(2)}) async-start(), calls=%async_computation.12 | async-start | bytes 921600 | tf_op jit(solution)/shard_map/reduce_scatter | solution.py:846
  421.1 1.3 collective-permute-start.19
  428.8 11.1 %collective-permute-start.23 = (f32[13056]{0:T(1024)S(1)}, f32[13056]{0:T(1024)S(1)}, u32[]{:S(2)}, u32[]{:S(2)}) collective-permute-start(f32[13056]{0:T(1024)S(1)} %add.357), channel_id=1, source_target_pairs={{0,2},{2,0},{4,6},{6,4},{8,10},{10,8},{12,14},{14,12},{16,18},{18,... | collective-permute-start | bytes 156680 | tf_op jit(solution)/shard_map/ppermute | solution.py:790
  430.7 9.3 %collective-permute-start.24 = (f32[13056]{0:T(1024)S(1)}, f32[13056]{0:T(1024)S(1)}, u32[]{:S(2)}, u32[]{:S(2)}) collective-permute-start(f32[13056]{0:T(1024)S(1)} %add.357), channel_id=1, source_target_pairs={{0,4},{2,6},{4,0},{6,2},{8,12},{10,14},{12,8},{14,10},{16,20},{18,... | collective-permute-start | bytes 156680 | tf_op jit(solution)/shard_map/ppermute | solution.py:790
  432.2 7.8 %collective-permute-start.25 = (f32[13056]{0:T(1024)S(1)}, f32[13056]{0:T(1024)S(1)}, u32[]{:S(2)}, u32[]{:S(2)}) collective-permute-start(f32[13056]{0:T(1024)S(1)} %add.357), channel_id=1, source_target_pairs={{0,6},{2,4},{4,2},{6,0},{8,14},{10,12},{12,10},{14,8},{16,22},{18,... | collective-permute-start | bytes 156680 | tf_op jit(solution)/shard_map/ppermute | solution.py:790
  434.7 21.9 %collective-permute-start.20 = (bf16[4,48,1152]{2,1,0:T(8,128)(2,1)}, bf16[4,48,1152]{2,1,0:T(8,128)(2,1)}, u32[]{:S(2)}, u32[]{:S(2)}) collective-permute-start(bf16[4,48,1152]{2,1,0:T(8,128)(2,1)} %get-tuple-element.287), channel_id=1, source_target_pairs={{0,2},{2,0},{4,6},{6,4},{8,10},{10,8},{12,14},{14,12},{16,18},{18,... | collective-permute-start | bytes 1327112 | tf_op jit(solution)/shard_map/ppermute | solution.py:790
  436.6 22.6 %collective-permute-start.21 = (bf16[4,48,1152]{2,1,0:T(8,128)(2,1)}, bf16[4,48,1152]{2,1,0:T(8,128)(2,1)}, u32[]{:S(2)}, u32[]{:S(2)}) collective-permute-start(bf16[4,48,1152]{2,1,0:T(8,128)(2,1)} %get-tuple-element.289), channel_id=1, source_target_pairs={{0,4},{2,6},{4,0},{6,2},{8,12},{10,14},{12,8},{14,10},{16,20},{18,... | collective-permute-start | bytes 1327112 | tf_op jit(solution)/shard_map/ppermute | solution.py:790
  439.9 30.3 %collective-permute-start.22 = (bf16[4,48,1152]{2,1,0:T(8,128)(2,1)}, bf16[4,48,1152]{2,1,0:T(8,128)(2,1)S(1)}, u32[]{:S(2)}, u32[]{:S(2)}) collective-permute-start(bf16[4,48,1152]{2,1,0:T(8,128)(2,1)} %get-tuple-element.288), channel_id=1, source_target_pairs={{0,6},{2,4},{4,2},{6,0},{8,14},{10,12},{12,10},{14,8},{16,22},{18,... | collective-permute-start | bytes 1327112 | tf_op jit(solution)/shard_map/ppermute | solution.py:790
  471.6 7.7 %copy-start.7 = (bf16[4,48,1152]{2,1,0:T(8,128)(2,1)}, bf16[4,48,1152]{2,1,0:T(8,128)(2,1)S(1)}, u32[]{:S(2)}) copy-start(bf16[4,48,1152]{2,1,0:T(8,128)(2,1)S(1)} %fusion.2) | copy-start | bytes 1327108
  473.8 12.5 %collective-permute-start.29 = (f32[13056]{0:T(1024)S(1)}, f32[13056]{0:T(1024)S(1)}, u32[]{:S(2)}, u32[]{:S(2)}) collective-permute-start(f32[13056]{0:T(1024)S(1)} %add_add_fusion.1), channel_id=1, source_target_pairs={{0,8},{2,10},{4,12},{6,14},{8,0},{10,2},{12,4},{14,6},{16,24},{18,... | collective-permute-start | bytes 156680 | tf_op jit(solution)/shard_map/ppermute | solution.py:790
  476.0 11.8 %collective-permute-start.30 = (f32[13056]{0:T(1024)S(1)}, f32[13056]{0:T(1024)}, u32[]{:S(2)}, u32[]{:S(2)}) collective-permute-start(f32[13056]{0:T(1024)S(1)} %add_add_fusion.1), channel_id=1, source_target_pairs={{0,16},{2,18},{4,20},{6,22},{8,24},{10,26},{12,28},{14,30},{16,0},... | collective-permute-start | bytes 156680 | tf_op jit(solution)/shard_map/ppermute | solution.py:790
  477.2 10.6 %collective-permute-start.31 = (f32[13056]{0:T(1024)S(1)}, f32[13056]{0:T(1024)}, u32[]{:S(2)}, u32[]{:S(2)}) collective-permute-start(f32[13056]{0:T(1024)S(1)} %add_add_fusion.1), channel_id=1, source_target_pairs={{0,24},{2,26},{4,28},{6,30},{8,16},{10,18},{12,20},{14,22},{16,8},... | collective-permute-start | bytes 156680 | tf_op jit(solution)/shard_map/ppermute | solution.py:790
  480.0 11.8 %collective-permute-start.26 = (bf16[48,1152]{1,0:T(8,128)(2,1)}, bf16[48,1152]{1,0:T(8,128)(2,1)}, u32[]{:S(2)}, u32[]{:S(2)}) collective-permute-start(bf16[48,1152]{1,0:T(8,128)(2,1)} %get-tuple-element.292), channel_id=1, source_target_pairs={{0,8},{2,10},{4,12},{6,14},{8,0},{10,2},{12,4},{14,6},{16,24},{18,... | collective-permute-start | bytes 331784 | tf_op jit(solution)/shard_map/ppermute | solution.py:790
  480.9 10.9 %collective-permute-start.27 = (bf16[48,1152]{1,0:T(8,128)(2,1)}, bf16[48,1152]{1,0:T(8,128)(2,1)}, u32[]{:S(2)}, u32[]{:S(2)}) collective-permute-start(bf16[48,1152]{1,0:T(8,128)(2,1)} %get-tuple-element.294), channel_id=1, source_target_pairs={{0,16},{2,18},{4,20},{6,22},{8,24},{10,26},{12,28},{14,30},{16,0},... | collective-permute-start | bytes 331784 | tf_op jit(solution)/shard_map/ppermute | solution.py:790
  483.8 10.9 %copy-start.1 = (bf16[32,32,768]{2,1,0:T(8,128)(2,1)S(1)}, bf16[32,32,768]{2,1,0:T(8,128)(2,1)}, u32[]{:S(2)}) copy-start(bf16[32,32,768]{2,1,0:T(8,128)(2,1)} %param.17) | copy-start | bytes 4718596
  486.3 6.7 %collective-permute-start.28 = (bf16[48,1152]{1,0:T(8,128)(2,1)S(1)}, bf16[48,1152]{1,0:T(8,128)(2,1)S(1)}, u32[]{:S(2)}, u32[]{:S(2)}) collective-permute-start(bf16[48,1152]{1,0:T(8,128)(2,1)S(1)} %get-tuple-element.293), channel_id=1, source_target_pairs={{0,24},{2,26},{4,28},{6,30},{8,16},{10,18},{12,20},{14,22},{16,8},... | collective-permute-start | bytes 331784 | tf_op jit(solution)/shard_map/ppermute | solution.py:790
Sparse Core Ops, SparseCore 0:
  11.4 88.6 all-gather.2
  103.5 79.1 all-gather.4
  270.3 76.8 reduce-scatter.4
  350.0 42.3 reduce-scatter.6
  394.6 44.5 reduce-scatter.10
  441.3 29.9 reduce-scatter.8

commit v5 on v4

--- a/solution.py
+++ b/solution.py
@@ -16,6 +16,8 @@
 LOW_GROUPS = [[4 * plane + low for low in range(4)] for plane in range(4)]
 PLANE_GROUPS = [[low + 4 * plane for plane in range(4)] for low in range(4)]
 GROUP = 4
+PLAIN = 0
+RELATIVE = 1
 FIXED = 2
 PAIR = 2 * HD
 F32 = jnp.float32
@@ -265,22 +267,22 @@
     )(inputs, weight, weight, weight, bias)
 
 
-def grads_kernel(sides, counts, factors, extra, grouped, meta, *refs):
+def grads_kernel(sides, counts, factors, extra_steps, fills, kind, meta, *refs):
     lefts = refs[: max(sides) + 1]
     rights = refs[len(lefts) : len(lefts) + len(counts)]
-    rest = refs[len(lefts) + len(counts) :]
-    extra_ref = rest[0] if extra else None
-    out_ref = rest[-1]
+    extra_ref = refs[len(lefts) + len(counts)]
+    out_ref = refs[-1]
     step = pl.program_id(0)
     begin = 0
     for index, count in enumerate(counts):
+        extra = begin < extra_steps
 
         @pl.when((step >= begin) & (step < begin + count))
-        def _(index=index):
+        def _(index=index, extra=extra):
             result = dot_tn(lefts[sides[index]][...], rights[index][...])
             if factors[index] != 1.0:
                 result = result * factors[index]
-            if not grouped:
+            if kind == PLAIN:
                 if extra:
                     result = result + extra_ref[...].astype(F32)
                 out_ref[...] = result.astype(BF16)
@@ -289,7 +291,7 @@
             for plane in range(4):
                 for low in range(4):
                     row = (plane * 4 + low) * size
-                    place = pl.ds(low if grouped == FIXED else meta[0] ^ low, 1)
+                    place = pl.ds(low if kind == FIXED else meta[0] ^ low, 1)
                     part = result[row : row + size]
                     if extra:
                         part = part + extra_ref[place, plane].astype(F32)[0]
@@ -298,13 +300,15 @@
         begin += count
 
 
-def weight_grads(meta, lefts, rights, sides, factors, extra, grouped):
+def weight_grads(meta, lefts, rights, sides, factors, kind, extra=None, room=None, into=None):
     chunk = min(2 * 384, rights[0].shape[1])
     shifts = [right[1] if isinstance(right, tuple) else 0 for right in rights]
     counts = [1 if isinstance(right, tuple) else right.shape[1] // chunk for right in rights]
     rights = [right[0] if isinstance(right, tuple) else right for right in rights]
     width = lefts[0].shape[1]
-    total = sum(counts) * chunk
+    steps = sum(counts)
+    total = room or steps * chunk
+    start = total // chunk - steps if into is not None else 0
     begins = [sum(counts[:i]) for i in range(len(counts))]
 
     def right_spec(index):
@@ -316,29 +320,40 @@
             ),
         )
 
-    if grouped:
-        shape = (4, 4, width // 16, total)
-        out_spec = pl.BlockSpec((4, 4, width // 16, chunk), lambda step, meta: (0, 0, 0, step))
-    else:
-        shape = (width, total)
-        out_spec = pl.BlockSpec((width, chunk), lambda step, meta: (0, step))
-    flops = 2 * rights[0].shape[0] * width * total
+    def tile_spec(place):
+        if kind == PLAIN:
+            return pl.BlockSpec((width, chunk), lambda step, meta: (0, place(step)))
+        return pl.BlockSpec(
+            (4, 4, width // 16, chunk), lambda step, meta: (0, 0, 0, place(step))
+        )
+
+    extra_steps = extra.shape[-1] // chunk if extra is not None else 0
+    operands = [*lefts, *rights]
+    specs = [pl.BlockSpec(left.shape, lambda step, meta: (0, 0)) for left in lefts]
+    specs += [right_spec(index) for index in range(len(rights))]
+    if extra is not None:
+        operands.append(extra)
+        specs.append(tile_spec(lambda step: jnp.minimum(step, extra_steps - 1)))
+    if into is not None:
+        operands.append(into)
+        specs.append(pl.BlockSpec(memory_space=pl.ANY))
     return pl.pallas_call(
-        functools.partial(grads_kernel, sides, counts, factors, extra is not None, grouped),
+        functools.partial(
+            grads_kernel, sides, counts, factors, extra_steps, into is not None, kind
+        ),
         grid_spec=pltpu.PrefetchScalarGridSpec(
             num_scalar_prefetch=1,
-            grid=(sum(counts),),
-            in_specs=[pl.BlockSpec(left.shape, lambda step, meta: (0, 0)) for left in lefts]
-            + [right_spec(index) for index in range(len(rights))]
-            + ([out_spec] if extra is not None else []),
-            out_specs=out_spec,
+            grid=(steps,),
+            in_specs=specs,
+            out_specs=tile_spec(lambda step: start + step),
         ),
-        out_shape=jax.ShapeDtypeStruct(shape, BF16),
-        cost_estimate=pl.CostEstimate(
-            flops=flops // LIGHT, bytes_accessed=flops // 256 // LIGHT, transcendentals=0
+        out_shape=jax.ShapeDtypeStruct(
+            (width, total) if kind == PLAIN else (4, 4, width // 16, total), BF16
         ),
+        input_output_aliases={len(operands): 0} if into is not None else {},
+        cost_estimate=light_cost(),
         name="weight_grads",
-    )(meta, *lefts, *rights, *([extra] if extra is not None else []))
+    )(meta, *operands)
 
 
 def norm_forward(hidden, gain, shift):
@@ -512,40 +527,51 @@
     def _():
         own = keys_each // 2
         for index, ref in enumerate((dck_refs[0], dck_refs[1], dcv_refs[0], dcv_refs[1])):
-            near = slice(index * half, (index + 1) * half)
+            near_ref[:, index * half : (index + 1) * half] = ref[...]
             far = slice((index ^ 1) * half, ((index ^ 1) + 1) * half)
             for seq in range(2):
-                rows = slice(seq * own, (seq + 1) * own)
                 base = seq * keys_each
-                near_ref[rows, near] = ref[base : base + own, :]
-                far_ref[rows, far] = ref[base + own : base + keys_each, :].astype(BF16)
+                middle, end = base + own, base + keys_each
+                far_ref[middle:end, far] = ref[base:middle, :].astype(BF16)
+                far_ref[base:middle, far] = ref[middle:end, :].astype(BF16)
 
 
 def memory_backward_kernel(near_ref, got_ref, wk0, wv0, wk1, wv1, sum_ref, encoder_ref, bias_ref):
     total = (near_ref[...] + got_ref[...].astype(F32)).astype(BF16)
-    sum_ref[...] = total
     half = wk0.shape[1]
-    grad = dot_nt(total[:, :half], wk0[...]) + dot_nt(total[:, half : 2 * half], wk1[...])
-    grad = grad + dot_nt(total[:, 2 * half : 3 * half], wv0[...])
-    encoder_ref[...] = (grad + dot_nt(total[:, 3 * half :], wv1[...])).astype(BF16)
-    bias = jnp.sum(total[:, 2 * half :].astype(F32), 0, keepdims=True)
+    sum_ref[:, :half] = total[:, :half]
+    sum_ref[:, half:] = total[:, 2 * half : 3 * half]
+    own = total.shape[0] // 4
+    mine = jnp.concatenate([total[:own], total[2 * own : 3 * own]], 0)
+    grad = dot_nt(mine[:, :half], wk0[...]) + dot_nt(mine[:, half : 2 * half], wk1[...])
+    grad = grad + dot_nt(mine[:, 2 * half : 3 * half], wv0[...])
+    encoder_ref[...] = (grad + dot_nt(mine[:, 3 * half :], wv1[...])).astype(BF16)
+    bias = jnp.sum(mine[:, 2 * half :].astype(F32), 0, keepdims=True)
     bias_ref[...] = jnp.broadcast_to(bias, bias_ref.shape)
 
 
 def memory_backward(near, got, mid):
     rows, span = near.shape
     half = span // 4
-    width = mid[0].shape[0]
-    columns = [plain_fixed((width, half), 0, 2), plain_fixed((width, half), 0, 3)]
+    width = mid[0][0].shape[0]
+    columns = [plain_fixed((width, half), 0, m[1] + c) for m in mid for c in (3, 4)]
     return pl.pallas_call(
         memory_backward_kernel,
         grid=(1,),
-        in_specs=[plain_fixed((rows, span))] * 2 + columns * 2,
-        out_specs=[plain_fixed((rows, span)), plain_fixed((rows, width)), plain_fixed((8, 2 * half))],
-        out_shape=[kept((rows, span), BF16), kept((rows, width), BF16), kept((8, 2 * half), F32)],
-        cost_estimate=pl.CostEstimate(flops=1000, bytes_accessed=1000, transcendentals=0),
+        in_specs=[plain_fixed((rows, span))] * 2 + columns,
+        out_specs=[
+            plain_fixed((rows, 2 * half)),
+            plain_fixed((rows // 2, width)),
+            plain_fixed((8, 2 * half)),
+        ],
+        out_shape=[
+            kept((rows, 2 * half), BF16),
+            kept((rows // 2, width), BF16),
+            kept((8, 2 * half), F32),
+        ],
+        cost_estimate=light_cost(),
         name="memory_backward",
-    )(near, got, mid[0], mid[0], mid[1], mid[1])
+    )(near, got, *[m[0] for m in mid for _ in range(2)])
 
 
 def ffn_forward_kernel(first, hidden_ref, base_ref, expand, reduce, bias, gain, shift, act_ref, slope_ref, total_ref):
@@ -656,7 +682,7 @@
     half = attn[0].shape[1]
     blocks = rows // BLOCK
     memory_rows = memory.shape[0]
-    weights = [fixed_spec((width, half), 0, column) for column in range(5) for _ in range(2)]
+    weights = [fixed_spec((width, half), 0, m[1] + c) for c in (0, 1, 3, 4, 2) for m in mid]
     tall = GROUP * BLOCK
     wide, thin, narrow = row_spec(width, tall), row_spec(1, tall), row_spec(half, tall)
     memory_spec = fixed_spec((memory_rows, half))
@@ -689,7 +715,7 @@
             flops=(24 * rows * width * half) // LIGHT, bytes_accessed=(20 * rows * width) // LIGHT, transcendentals=0
         ),
         name="mid_forward",
-    )(meta, inputs, *attn, memory, *[mid[h] for _ in range(5) for h in range(2)], *in_pair, out_bias, gain, shift)
+    )(meta, inputs, *attn, memory, *[m[0] for _ in range(5) for m in mid], *in_pair, out_bias, gain, shift)
     return outs[:7], outs[7:9], outs[9:11], outs[11:13], outs[13:15]
 
 
@@ -702,7 +728,7 @@
     tall = GROUP * BLOCK
     wide, thin, narrow = row_spec(width, tall), row_spec(1, tall), row_spec(half, tall)
     memory_spec = fixed_spec((memory_rows, half))
-    weights = [fixed_spec((width, half), 0, column) for column in (0, 1, 4) for _ in range(2)]
+    weights = [fixed_spec((width, half), 0, m[1] + c) for c in (0, 1, 2) for m in mid]
     outs = pl.pallas_call(
         functools.partial(mid_backward_kernel, score_scale, rows),
         grid_spec=pltpu.PrefetchScalarGridSpec(
@@ -715,7 +741,7 @@
             + [fixed_spec((3, width))],
             out_specs=[wide, wide, wide, fixed_spec((8, width))]
             + [narrow] * 4
-            + [fixed_spec((memory_rows // 2, 4 * half))] * 2,
+            + [fixed_spec((memory_rows, 4 * half))] * 2,
             scratch_shapes=[pltpu.VMEM((tall, half), BF16)] * 2
             + [pltpu.VMEM((half, memory_rows), BF16)] * 2
             + [pltpu.VMEM((memory_rows, half), F32)] * 4,
@@ -727,12 +753,12 @@
             kept((8, width), F32),
         ]
         + [kept((rows, half), BF16)] * 4
-        + [kept((memory_rows // 2, 4 * half), F32), kept((memory_rows // 2, 4 * half), BF16)],
+        + [kept((memory_rows, 4 * half), F32), kept((memory_rows, 4 * half), BF16)],
         cost_estimate=pl.CostEstimate(
             flops=(24 * rows * width * half) // LIGHT, bytes_accessed=(20 * rows * width) // LIGHT, transcendentals=0
         ),
         name="mid_backward",
-    )(meta, dn2, unit2, scale2, unit1, scale1, lse, *cq, *ck, *cv, *[mid[h] for _ in range(3) for h in range(2)], gain)
+    )(meta, dn2, unit2, scale2, unit1, scale1, lse, *cq, *ck, *cv, *[m[0] for _ in range(3) for m in mid], gain)
     return outs[:4], outs[4:6], outs[6:8], outs[8], outs[9]
 
 
@@ -922,25 +948,19 @@
     ).reshape(rows, 1)
 
     send_piece = jnp.arange(dp_count, dtype=jnp.int32)
-    send_block = send_piece // per_block
-    send_ids = jnp.stack(
-        [
-            jnp.minimum(send_block, blocks_used[0] - 1) * per_block,
-            (first_blocks + jnp.minimum(send_block, blocks_used[1] - 1)) * per_block,
-        ],
-        1,
-    ) + (send_piece % per_block)[:, None]
-    send_pos = (send_piece[:, None, None] * 2 + tensor_index) * piece + jnp.arange(
-        piece, dtype=jnp.int32
-    )[None, None, :]
-    send_valid = (send_pos < pair_len[None, :, None]).reshape(2 * dp_count, piece, 1)
+    spare = jnp.where(
+        pieces_used[0] % per_block != 0, first_blocks * per_block - 1, rows // piece - 1
+    )
+    send_start = jnp.stack([0 * first_blocks, first_blocks * per_block])
+    send_ids = jnp.where(
+        send_piece[:, None] < pieces_used[None, :],
+        send_start[None, :] + send_piece[:, None],
+        spare,
+    ).reshape(-1)
     inverse = jnp.zeros_like(deal).at[deal].set(jnp.arange(deal.shape[0], dtype=jnp.int32))
 
     def home_pieces(value):
-        pieces = value.reshape(rows // piece, piece, width)
-        return jnp.where(
-            send_valid, rows_at(pieces, send_ids.reshape(-1)), jnp.zeros((), value.dtype)
-        )
+        return rows_at(value.reshape(rows // piece, piece, width), send_ids)
 
     def go_home(outgoing):
         return lax.all_to_all(outgoing, "dp", split_axis=0, concat_axis=0, tiled=True)
@@ -951,14 +971,23 @@
     def arrive(ordered):
         return lax.all_to_all(ordered, "dp", split_axis=0, concat_axis=0, tiled=True)
 
-    def pack(arrived):
-        return rows_at(arrived, piece_ids).reshape(rows, width)
+    def pack(arrived, ids):
+        return rows_at(arrived, ids).reshape(rows, width)
 
     quick = dp_count == 16
+    both = (0, 1)
+    biases = jnp.concatenate([in_bias.reshape(-1), hidden_bias])
+    bias_pair = (biases, swap(biases))
+    in_pair = [b[: 4 * half].reshape(4, half) for b in bias_pair]
+    hidden_pair = [b[None, 4 * half :] for b in bias_pair]
+
+    memory_full = jnp.concatenate([encoder, swap(encoder)], 1).reshape(4 * memory_rows, width)
+    affine = (norm_gain[1:2], norm_bias[1:2] + out_bias[2:3])
+    early = (row_valid.astype(F32), affine, in_pair, hidden_pair, meta, piece_ids, memory_full, send_ids, inverse)
     ordered = order(tokens)
     qkv_shard_in = self_project.reshape(shard, 3 * half)
     mid_shard_in = jnp.concatenate(
-        [self_output.T, cross_query, cross_memory.reshape(shard, 2 * half), cross_output.T], 1
+        [self_output.T, cross_query, cross_output.T, cross_memory.reshape(shard, 2 * half)], 1
     )
 
     def slow_gather(value):
@@ -970,28 +999,22 @@
         qkv_line, ordered = tie(qkv_line, ordered)
         qkv_groups = low_groups(qkv_line)
         arrived = arrive(ordered)
-        ordered_cot, arrived, qkv_groups = tie(ordered_cot, arrived, qkv_groups)
+        ordered_cot, arrived, qkv_groups, early = tie(ordered_cot, arrived, qkv_groups, early)
         qkv_own = assemble(qkv_groups)
     else:
         arrived = arrive(ordered)
         qkv_own = slow_gather(qkv_shard_in)
     qkv_weight = (qkv_own, swap(qkv_own))
-    inputs = pack(arrived)
+    valid_rows, affine, in_pair, hidden_pair, meta, piece_ids, memory_full = early[:7]
+    send_ids, inverse = early[7:]
+    inputs = pack(arrived, piece_ids)
     arrived_cot = arrive(ordered_cot)
 
-    mid_own = slow_gather(mid_shard_in)
-    ffn_own = slow_gather(jnp.concatenate([hidden_in, hidden_out.T], 1))
-    both = (0, 1)
+    rest_own = slow_gather(jnp.concatenate([hidden_in, hidden_out.T, mid_shard_in], 1))
 
     def columns(pair, start, count):
         return [lax.slice_in_dim(pair[h], start, start + count, axis=1) for h in both]
 
-    biases = jnp.concatenate([in_bias.reshape(-1), hidden_bias])
-    bias_pair = (biases, swap(biases))
-    in_pair = [b[: 4 * half].reshape(4, half) for b in bias_pair]
-    hidden_pair = [b[4 * half :] for b in bias_pair]
-
-    memory_full = jnp.concatenate([encoder, swap(encoder)], 1).reshape(4 * memory_rows, width)
 
     queries = [None, None]
     near = [None, None]
@@ -1001,43 +1024,42 @@
         queries[h], near[h] = project(inputs, qkv_weight[h], in_pair[h], score_scale)
     far = [swap(near[1 - h]) for h in both]
     attn[1], lse[1] = attend_forward(meta, queries[1], near[1], far[1], piece, spans)
-    mid_own, attn[1], queries[0], valid_rows = tie(
-        mid_own, attn[1], queries[0], row_valid.astype(F32)
-    )
-    mid_weight = (mid_own, swap(mid_own))
+    attn[1], queries[0], far[0] = tie(attn[1], queries[0], far[0])
     attn[0], lse[0] = attend_forward(meta, queries[0], near[0], far[0], piece, spans)
+    rest_own, attn[0] = tie(rest_own, attn[0])
+    rest_far = swap(rest_own)
+    mid_weight = [(rest, 2 * units // half) for rest in (rest_own, rest_far)]
     saved, cqs, cattn, cks, cvs = mid_forward(
         meta, inputs, attn, memory_full, mid_weight, in_pair, out_bias, norm_gain, norm_bias, score_scale
     )
     unit1, scale1, unit2, scale2, cross_in, hidden, clse = saved
-    hidden, ffn_own = tie(hidden, ffn_own)
-    ffn_far = swap(ffn_own)
     act = [None, None]
     slope = [None, None]
-    affine = (norm_gain[1:2], norm_bias[1:2] + out_bias[2:3])
     act[0], slope[0], total = ffn_forward(
-        True, hidden, unit2, ffn_own, hidden_pair[0][None], *affine
-    )
-    ffn_far, total = tie(ffn_far, total)
+        True, hidden, unit2, rest_own, hidden_pair[0], *affine
+    )
     act[1], slope[1], total = ffn_forward(
-        False, hidden, total, ffn_far, hidden_pair[1][None], *affine
+        False, hidden, total, rest_far, hidden_pair[1], *affine
     )
     arrived_cot, total = tie(arrived_cot, total)
-    ffn_weight = (ffn_own, ffn_far)
+    ffn_weight = (rest_own, rest_far)
     n3, dz, dn2, sums3, du0, du1, usum0, usum1 = ffn_backward(
-        total, pack(arrived_cot), valid_rows, slope, ffn_weight, norm_gain, norm_bias
+        total, pack(arrived_cot, piece_ids), valid_rows, slope, ffn_weight, norm_gain, norm_bias
     )
     du = (du0, du1)
     output_back = go_home(home_pieces(n3))
 
     low_meta = jnp.reshape(dp_index % 4, (1,)).astype(jnp.int32)
 
-    def chip_grads(lefts, rights, sides, factors, grouped):
-        far = weight_grads(low_meta, lefts, rights[1], sides, factors, None, grouped)
-        return weight_grads(low_meta, lefts, rights[0], sides, factors, swap(far), grouped)
-
-    ffn_grads = chip_grads(
-        [hidden, dz], [[du[h], act[h]] for h in both], (0, 1), (1.0, 1.0), FIXED if quick else 0
+    fixed = FIXED if quick else PLAIN
+    one = (0,)
+    far_in = weight_grads(low_meta, [hidden], [du[1]], one, (1.0,), fixed)
+    far_out = weight_grads(low_meta, [dz], [act[1]], one, (1.0,), fixed)
+    ffn_grads = weight_grads(
+        low_meta, [hidden], [du[0]], one, (1.0,), fixed, swap(far_in), 2 * units
+    )
+    ffn_grads = weight_grads(
+        low_meta, [dz], [act[0]], one, (1.0,), fixed, swap(far_out), 2 * units, ffn_grads
     )
     ffn_grads, dn2 = tie(ffn_grads, dn2)
     ffn_line = wide_scatter(ffn_grads.reshape(width, 2 * units), LOW_GROUPS if quick else None)
@@ -1051,16 +1073,23 @@
         memory_near, swap(memory_far), mid_weight
     )
     grad_encoder = grad_memory.reshape(2, memory_rows, width)
-    memory_own = encoder.reshape(2 * memory_rows, width)
-    mid_grads = chip_grads(
-        [dy, cross_in, memory_own, dy2],
-        [
-            [attn[h], dcq[h], (memory_sum, h), (memory_sum, 2 + h), cattn[h]]
-            for h in both
-        ],
-        (0, 1, 2, 2, 3),
-        (1.0, score_scale, 1.0, 1.0, 1.0),
-        FIXED if quick else 0,
+    mid_factors = (1.0, score_scale, 1.0, 1.0, 1.0)
+    far_mid = weight_grads(
+        low_meta,
+        [dy, cross_in, dy2],
+        [attn[1], dcq[1], cattn[1]],
+        (0, 1, 2),
+        mid_factors[:3],
+        fixed,
+    )
+    mid_grads = weight_grads(
+        low_meta,
+        [dy, cross_in, dy2, memory_full],
+        [attn[0], dcq[0], cattn[0], (memory_sum, 0), (memory_sum, 1)],
+        (0, 1, 2, 3, 3),
+        mid_factors,
+        fixed,
+        swap(far_mid),
     )
     mid_grads, da[0], da[1] = tie(mid_grads, da[0], da[1])
     mid_line = wide_scatter(mid_grads.reshape(width, 5 * half), LOW_GROUPS if quick else None)
@@ -1078,8 +1107,9 @@
     dx_far, pair_far, sums_far = input_backward(
         dh1, dq[1], own[1], got_far, qkv_weight[1], score_scale, F32
     )
+    relative = RELATIVE if quick else PLAIN
     far_grads = weight_grads(
-        low_meta, [inputs], [dq[1], (pair_far, 0), (pair_far, 1)], (0, 0, 0), factors, None, quick
+        low_meta, [inputs], [dq[1], (pair_far, 0), (pair_far, 1)], (0, 0, 0), factors, relative
     )
     far_grads, dx_far, got_near, ffn_line = tie(far_grads, dx_far, got_near, ffn_line)
     far_grads = swap(far_grads)
@@ -1089,14 +1119,23 @@
     grad_out = home_pieces(dx)
     grad_out, far_grads, output_back = tie(grad_out, far_grads, output_back)
     output = rows_at(output_back, inverse)
-    grad_back = go_home(grad_out)
     far_grads, mid_line = tie(far_grads, mid_line)
     ffn_shard = wide_scatter(ffn_line, PLANE_GROUPS) if quick else ffn_line
     mid_shard = wide_scatter(mid_line, PLANE_GROUPS) if quick else mid_line
     ffn_shard, mid_shard = ffn_shard.astype(F32), mid_shard.astype(F32)
     qkv_grads = weight_grads(
-        low_meta, [inputs], [dq[0], (pair_near, 0), (pair_near, 1)], (0, 0, 0), factors, far_grads, quick
-    )
+        low_meta,
+        [inputs],
+        [dq[0], (pair_near, 0), (pair_near, 1)],
+        (0, 0, 0),
+        factors,
+        relative,
+        far_grads,
+    )
+    sums, sums3, sums_near, sums_far, usum0, usum1, memory_bias, grad_out = tie(
+        sums, sums3, sums_near, sums_far, usum0, usum1, memory_bias, grad_out
+    )
+    grad_back = go_home(grad_out)
     sums_qkv = [sums_near, sums_far]
 
     def global_order(pair):
@@ -1156,8 +1195,8 @@
         qkv_shard.reshape(shard, 3, half),
         mid_shard[:, :half].T,
         mid_shard[:, half : 2 * half],
-        mid_shard[:, 2 * half : 4 * half].reshape(shard, 2, half),
-        mid_shard[:, 4 * half :].T,
+        mid_shard[:, 3 * half :].reshape(shard, 2, half),
+        mid_shard[:, 2 * half : 3 * half].T,
         ffn_shard[:, :units],
         ffn_shard[:, units:].T,
         lax.dynamic_slice_in_dim(in_total, tensor_index * half, half, 1),

time: 512 us -> 478 us (0.934)
  waiting for transfers between devices: 136 us -> 102 us
  other arithmetic: 23.2 us -> 14 us
  local copies, waits for them, and re-layouts: 43.2 us -> 50.6 us
    ppermute x18, waiting for transfers between devices: 81 us -> 67.5 us  [hop(): return lax.ppermute(value, 'dp', [(i, i ^ bits) for i in range(16)])]
    ppermute x14, waiting for transfers between devices: 23.2 us -> 12.1 us  [swap(): return lax.ppermute(value, 'tensor', [(0, 1), (1, 0)])]
    all_to_all x2, waiting for transfers between devices: 10.3 us -> 0.01 us  [arrive(): lax.all_to_all(ordered, 'dp', split_axis=0, concat_axis=0, tiled=True)]
    all_to_all x2, waiting for transfers between devices: 8.87 us -> 1.61 us  [go_home(): lax.all_to_all(outgoing, 'dp', split_axis=0, concat_axis=0, tiled=True)]
    unnamed x51 -> x62, local copies, waits for them, and re-layouts: 8.25 us -> 14.7 us
    all_gather x2 -> x1, waiting for transfers between devices: 12.7 us -> 17 us  [slow_gather(): return lax.all_gather(value, 'dp', axis=0, tiled=True)]
    pallas_call x6 -> x8, Pallas kernels: 50.1 us -> 51.7 us  [weight_grads(): pl.pallas_call(functools.partial(grads_kernel, sides, counts, factors, ex...]
  transfers between devices with their start and end apart: 42 -> 41, of which waited for: 16 -> 13; matrix products, arithmetic and copies ran while one was open for 11% -> 10% of each run, Pallas kernels for 36% -> 40%
where the time goes in v5:
time: 478 us; the launch traced here: 471 us
  Pallas kernels  220 us (46%)
  waiting for transfers between devices  102 us (21%)
  starting transfers between devices  68.4 us (14%)
  local copies, waits for them, and re-layouts  50.6 us (11%)
  between operations  16.7 us (3%)
  other arithmetic  14 us (3%)
    ppermute x18, waiting for transfers between devices, hop(): return lax.ppermute(value, 'dp', [(i, i ^ bits) for i in range(16)])  67.5 us
    pallas_call x8, Pallas kernels, weight_grads(): pl.pallas_call(functools.partial(grads_kernel, sides, counts, factors, ex...  51.7 us
    pallas_call x2, Pallas kernels, attend_backward(): pl.pallas_call(functools.partial(backward_kernel, piece, spans), grid_spe...  30.5 us
    ppermute x18, starting transfers between devices, hop(): return lax.ppermute(value, 'dp', [(i, i ^ bits) for i in range(16)])  27 us
    pallas_call x1, Pallas kernels, mid_backward(): pl.pallas_call(functools.partial(mid_backward_kernel, score_scale, rows),...  25.2 us
    all_to_all x2, starting transfers between devices, go_home(): lax.all_to_all(outgoing, 'dp', split_axis=0, concat_axis=0, tiled=True)  23.3 us
    pallas_call x2, Pallas kernels, attend_forward(): pl.pallas_call(functools.partial(forward_kernel, piece, spans), grid_spec...  21.2 us
    pallas_call x1, Pallas kernels, mid_forward(): pl.pallas_call(functools.partial(mid_forward_kernel, score_scale), grid_s...  21 us
  transfers between devices with their start and end apart: 41, of which 13 were waited for; matrix products, arithmetic and copies ran while one was open for 10% of the time, Pallas kernels for 40%

profile of v5, /device:TPU:0, one launch (start us, length us, event | category | flops | bytes accessed | tf_op | source)
XLA Modules:
  0.0 471.2 jit_solution(18222622341804448521)
XLA Ops:
  13.3 3.1 collective-permute-start
  16.4 2.6 collective-permute-start.1
  21.2 1.8 gather_fusion.1
  23.0 4.8 %collective-permute-done.1 = bf16[48,1152]{1,0:T(8,128)(2,1)S(1)} collective-permute-done((bf16[48,1152]{1,0:T(8,128)(2,1)S(1)}, bf16[48,1152]{1,0:T(8,128)(2,1)S(1)}, u32[]{:S(2)}, u32[]{:S(2)}) %collective-permute-start.1) | collective-permute-done | bytes 110624 | tf_op jit(solution)/shard_map/ppermute | solution.py:816
  27.9 11.6 %all-to-all-start = ((bf16[32,32,768]{2,1,0:T(8,128)(2,1)}), bf16[32,32,768]{2,1,0:T(8,128)(2,1)S(1)}, u32[]{:S(2)}, u32[]{:S(2)}) async-start(bf16[32,32,768]{2,1,0:T(8,128)(2,1)} %gather_fusion.1), calls=%async_computation | async-start | bytes 3145728 | tf_op jit(solution)/shard_map/all_to_all | solution.py:972
  41.3 1.9 compare_select_fusion.5
  47.7 1.3 slice_add_fusion.shift
  50.3 1.9 collective-permute-start.3
  52.3 1.5 collective-permute-start.4
  53.8 1.3 pad_add_fusion.meta
  55.9 3.2 gather_fusion
  62.8 1.8 pad_maximum_fusion.1
  64.6 16.9 %collective-permute-done.3.first_ref = bf16[4,48,1152]{2,1,0:T(8,128)(2,1)S(1)} collective-permute-done((bf16[4,48,1152]{2,1,0:T(8,128)(2,1)S(1)}, bf16[4,48,1152]{2,1,0:T(8,128)(2,1)S(1)}, u32[]{:S(2)}, u32[]{:S(2)}) %collective-permute-start.3) | collective-permute-done | bytes 442400 | tf_op jit(solution)/shard_map/ppermute | solution.py:816
  81.5 10.8 %collective-permute-done.5.third_ref = bf16[4,48,1152]{2,1,0:T(8,128)(2,1)S(1)} collective-permute-done((bf16[4,48,1152]{2,1,0:T(8,128)(2,1)S(1)}, bf16[4,48,1152]{2,1,0:T(8,128)(2,1)S(1)}, u32[]{:S(2)}, u32[]{:S(2)}) %collective-permute-start.5) | collective-permute-done | bytes 442400 | tf_op jit(solution)/shard_map/ppermute | solution.py:816
  93.1 4.4 assemble.1
  97.6 1.7 gather_fusion.3
  99.3 5.0 %project.3 = (bf16[896,384]{1,0:T(8,128)(2,1)}, bf16[896,768]{1,0:T(8,128)(2,1)}) custom-call(bf16[896,768]{1,0:T(8,128)(2,1)} %bitcast.116, bf16[768,1152]{1,0:T(8,128)(2,1)} %bitcast.110, bf16[768,1152]{1,0:T(8,128)(2,1)} %bitcast.111, bf16[768,1152]{1,0:T(8,128)(2,1)} %bitcast.112, f32[4,384]{1,0:T(4,128)} %refs_10_), custom_call_target="tpu_custom_call" | custom-call | flops 1000 | bytes 1000 | tf_op jit(solution)/shard_map/project/pallas_call | solution.py:257
  106.0 5.0 %project.2 = (bf16[896,384]{1,0:T(8,128)(2,1)}, bf16[896,768]{1,0:T(8,128)(2,1)}) custom-call(bf16[896,768]{1,0:T(8,128)(2,1)} %bitcast.117, bf16[768,1152]{1,0:T(8,128)(2,1)} %copy-done.3, bf16[768,1152]{1,0:T(8,128)(2,1)} %copy-done.3, bf16[768,1152]{1,0:T(8,128)(2,1)} %copy-done.3, f32[4,384]{1,0:T(4,128)} %slice.201.bias.refs_11_), custom_call_target="tpu_custom_call" | custom-call | flops 1000 | bytes 1000 | tf_op jit(solution)/shard_map/project/pallas_call | solution.py:257
  112.1 10.6 %attend_forward.2 = (bf16[896,384]{1,0:T(8,128)(2,1)}, f32[7,8,256]{2,1,0:T(8,128)}) custom-call(s32[3]{0:T(128)} %pad_add_fusion.meta, bf16[896,384]{1,0:T(8,128)(2,1)} %get-tuple-element.148.q_ref, bf16[896,768]{1,0:T(8,128)(2,1)} %get-tuple-element.150.refs_0_, bf16[896,768]{1,0:T(8,128)(2,1)} %copy-done.5), custom_call_target="tpu_custom_call" | custom-call | flops 1000 | bytes 1000 | tf_op jit(solution)/shard_map/attend_forward/pallas_call | solution.py:208
  123.9 10.6 %attend_forward.3 = (bf16[896,384]{1,0:T(8,128)(2,1)}, f32[7,8,256]{2,1,0:T(8,128)}) custom-call(s32[3]{0:T(128)} %pad_add_fusion.meta, bf16[896,384]{1,0:T(8,128)(2,1)} %get-tuple-element.155.q_ref, bf16[896,768]{1,0:T(8,128)(2,1)} %get-tuple-element.152.refs_0_, bf16[896,768]{1,0:T(8,128)(2,1)} %copy-done.6), custom_call_target="tpu_custom_call" | custom-call | flops 1000 | bytes 1000 | tf_op jit(solution)/shard_map/attend_forward/pallas_call | solution.py:208
  134.5 17.0 %all-gather.2.cloned.1.call-done.refs_0_.refs_2_.refs_4_.refs_6_.refs_8_.expand.reduce.in0.out0.refs_10_.wk0.wv0 = bf16[768,4992]{1,0:T(8,128)(2,1)} async-done(((bf16[48,4992]{1,0:T(8,128)(2,1)}), bf16[768,4992]{1,0:T(8,128)(2,1)}) %all-gather.2.cloned.1.call-update) | async-done | bytes 7667728 | tf_op jit(solution)/shard_map/all_gather | solution.py:994
  151.5 3.7 all-to-all-start.1
  155.5 8.5 %collective-permute-done.11.refs_1_.refs_3_.refs_5_.refs_7_.refs_9_.expand.reduce.in1.out1.refs_11_.wk1.wv1 = bf16[768,4992]{1,0:T(8,128)(2,1)} collective-permute-done((bf16[768,4992]{1,0:T(8,128)(2,1)}, bf16[768,4992]{1,0:T(8,128)(2,1)}, u32[]{:S(2)}, u32[]{:S(2)}) %collective-permute-start.11) | collective-permute-done | bytes 7667744 | tf_op jit(solution)/shard_map/ppermute | solution.py:812
  164.0 21.0 %mid_forward.1 = (f32[896,768]{1,0:T(8,128)}, f32[896,1]{1,0:T(8,128)}, f32[896,768]{1,0:T(8,128)}, f32[896,1]{1,0:T(8,128)}, bf16[896,768]{1,0:T(8,128)(2,1)}, ...) custom-call(s32[3]{0:T(128)} %pad_add_fusion.meta, ...), custom_call_target="tpu_custom_call" | custom-call | flops 6341787 | bytes 13762 | tf_op jit(solution)/shard_map/mid_forward/pallas_call | solution.py:689
  185.0 10.0 %ffn_forward.2 = (bf16[896,1536]{1,0:T(8,128)(2,1)}, bf16[896,1536]{1,0:T(8,128)(2,1)}, f32[896,768]{1,0:T(8,128)}) custom-call(bf16[896,768]{1,0:T(8,128)(2,1)} %get-tuple-element.162.hidden_ref.refs_0_, f32[896,768]{1,0:T(8,128)} %get-tuple-element.163.base_ref.unit2_ref, ...), custom_call_target="tpu_custom_call" | custom-call | flops 1000 | bytes 1000 | tf_op jit(solution)/shard_map/ffn_forward/pallas_call | solution.py:601
  195.0 10.0 %ffn_forward.3 = (bf16[896,1536]{1,0:T(8,128)(2,1)}, bf16[896,1536]{1,0:T(8,128)(2,1)}, f32[896,768]{1,0:T(8,128)}) custom-call(bf16[896,768]{1,0:T(8,128)(2,1)} %get-tuple-element.162.hidden_ref.refs_0_, f32[896,768]{1,0:T(8,128)} %get-tuple-element.167.base_ref, ...), custom_call_target="tpu_custom_call" | custom-call | flops 1000 | bytes 1000 | tf_op jit(solution)/shard_map/ffn_forward/pallas_call | solution.py:601
  205.0 1.7 gather_fusion.4
  206.7 18.5 %ffn_backward.1 = (bf16[896,768]{1,0:T(8,128)(2,1)}, bf16[896,768]{1,0:T(8,128)(2,1)}, f32[896,768]{1,0:T(8,128)}, f32[8,768]{1,0:T(8,128)}, bf16[896,1536]{1,0:...) custom-call(f32[896,768]{1,0:T(8,128)} %get-tuple-element.170.h3_ref, ...), custom_call_target="tpu_custom_call" | custom-call | flops 1000 | bytes 1000 | tf_op jit(solution)/shard_map/ffn_backward/pallas_call | solution.py:653
  225.2 5.7 %weight_grads.9 = bf16[4,4,48,1536]{3,2,1,0:T(8,128)(2,1)} custom-call(s32[1]{0:T(128)} %bitcast.meta, bf16[896,768]{1,0:T(8,128)(2,1)} %get-tuple-element.162.hidden_ref.refs_0_, bf16[896,1536]{1,0:T(8,128)(2,1)} %get-tuple-element.179.refs_1_), custom_call_target="tpu_custom_call" | custom-call | flops 1000 | bytes 1000 | tf_op jit(solution)/shard_map/weight_grads/pallas_call | solution.py:340
  231.1 5.7 %weight_grads.8 = bf16[4,4,48,1536]{3,2,1,0:T(8,128)(2,1)} custom-call(s32[1]{0:T(128)} %bitcast.meta, bf16[896,768]{1,0:T(8,128)(2,1)} %get-tuple-element.175.refs_0_, bf16[896,1536]{1,0:T(8,128)(2,1)} %get-tuple-element.177.refs_1_), custom_call_target="tpu_custom_call" | custom-call | flops 1000 | bytes 1000 | tf_op jit(solution)/shard_map/weight_grads/pallas_call | solution.py:340
  237.2 6.1 %weight_grads.10.refs_3_ = bf16[4,4,48,3072]{3,2,1,0:T(8,128)(2,1)} custom-call(s32[1]{0:T(128)} %bitcast.meta, bf16[896,768]{1,0:T(8,128)(2,1)} %get-tuple-element.162.hidden_ref.refs_0_, bf16[896,1536]{1,0:T(8,128)(2,1)} %get-tuple-element.178.refs_1_, bf16[4,4,48,1536]{3,2,1,0:T(8,128)(2,1)} %collective-permute-done.13.refs_2_), custom_call_target="tpu_custom_call" | custom-call | flops 1000 | bytes 1000 | tf_op jit(solution)/shard_map/weight_grads/pallas_call | solution.py:340
  243.3 6.1 %weight_grads.11 = bf16[4,4,48,3072]{3,2,1,0:T(8,128)(2,1)} custom-call(s32[1]{0:T(128)} %bitcast.meta, bf16[896,768]{1,0:T(8,128)(2,1)} %get-tuple-element.175.refs_0_, bf16[896,1536]{1,0:T(8,128)(2,1)} %get-tuple-element.176.refs_1_, bf16[4,4,48,1536]{3,2,1,0:T(8,128)(2,1)} %collective-permute-done.12.refs_2_, ...), custom_call_target="tpu_custom_call", output_to_operand_aliasing={{}: (4, {})} | custom-call | flops 1000 | bytes 1000 | tf_op jit(solution)/shard_map/weight_grads/pallas_call | solution.py:340
  250.8 1.8 gather_fusion.5
  252.5 5.3 %all-to-all-start.2 = ((bf16[32,32,768]{2,1,0:T(8,128)(2,1)}), bf16[32,32,768]{2,1,0:T(8,128)(2,1)S(1)}, u32[]{:S(2)}, u32[]{:S(2)}) async-start(bf16[32,32,768]{2,1,0:T(8,128)(2,1)} %gather_fusion.5), calls=%async_computation.2 | async-start | bytes 3145728 | tf_op jit(solution)/shard_map/all_to_all | solution.py:966
  257.9 25.2 %mid_backward.1 = (bf16[896,768]{1,0:T(8,128)(2,1)}, f32[896,768]{1,0:T(8,128)}, bf16[896,768]{1,0:T(8,128)(2,1)}, f32[8,768]{1,0:T(8,128)}, bf16[896,384]{1,0:T...) custom-call(s32[3]{0:T(128)} %pad_add_fusion.meta, ...), custom_call_target="tpu_custom_call" | custom-call | flops 6341787 | bytes 13762 | tf_op jit(solution)/shard_map/mid_backward/pallas_call | solution.py:732
  283.1 7.0 %weight_grads.12 = bf16[4,4,48,1152]{3,2,1,0:T(8,128)(2,1)} custom-call(s32[1]{0:T(128)} %bitcast.meta, bf16[896,768]{1,0:T(8,128)(2,1)} %get-tuple-element.192.refs_0_, bf16[896,768]{1,0:T(8,128)(2,1)} %get-tuple-element.193.refs_1_, bf16[896,768]{1,0:T(8,128)(2,1)} %get-tuple-element.194.refs_2_, bf16[896,384]{1,0:T(8,128)(2,1)} %get-tuple-element.159.attn1.refs_3_, ...), custom_call_target="tpu_custom_call" | custom-call | flops 1000 | bytes 1000 | tf_op jit(solution)/shard_map/weight_grads/pallas_call | solution.py:340
  290.2 1.6 all-to-all-done.2
  291.8 3.5 collective-permute-done.14.got_ref
  295.3 4.0 memory_backward.1
  300.5 8.8 %weight_grads.13 = bf16[4,4,48,1920]{3,2,1,0:T(8,128)(2,1)} custom-call(s32[1]{0:T(128)} %bitcast.meta, bf16[896,768]{1,0:T(8,128)(2,1)} %get-tuple-element.192.refs_0_, bf16[896,768]{1,0:T(8,128)(2,1)} %get-tuple-element.193.refs_1_, bf16[896,768]{1,0:T(8,128)(2,1)} %get-tuple-element.194.refs_2_, bf16[256,768]{1,0:T(8,128)(2,1)} %bitcast.125, ...), custom_call_target="tpu_custom_call" | custom-call | flops 1000 | bytes 1000 | tf_op jit(solution)/shard_map/weight_grads/pallas_call | solution.py:340
  309.3 15.2 %attend_backward.2 = (bf16[896,384]{1,0:T(8,128)(2,1)}, f32[896,768]{1,0:T(8,128)}, bf16[896,768]{1,0:T(8,128)(2,1)}) custom-call(s32[3]{0:T(128)} %pad_add_fusion.meta, bf16[896,384]{1,0:T(8,128)(2,1)} %get-tuple-element.155.q_ref, bf16[896,384]{1,0:T(8,128)(2,1)} %get-tuple-element.208.g_ref, f32[7,8,256]{2,1,0:T(8,128)} %get-tuple-element.209.lse_ref, ...), custom_call_target="tpu_custom_call" | custom-call | flops 1000 | bytes 1000 | tf_op jit(solution)/shard_map/attend_backward/pallas_call | solution.py:225
  324.7 15.2 %attend_backward.3 = (bf16[896,384]{1,0:T(8,128)(2,1)}, f32[896,768]{1,0:T(8,128)}, bf16[896,768]{1,0:T(8,128)(2,1)}) custom-call(s32[3]{0:T(128)} %pad_add_fusion.meta, bf16[896,384]{1,0:T(8,128)(2,1)} %get-tuple-element.148.q_ref, bf16[896,384]{1,0:T(8,128)(2,1)} %get-tuple-element.212.g_ref, f32[7,8,256]{2,1,0:T(8,128)} %get-tuple-element.213.lse_ref, ...), custom_call_target="tpu_custom_call" | custom-call | flops 1000 | bytes 1000 | tf_op jit(solution)/shard_map/attend_backward/pallas_call | solution.py:225
  340.3 6.7 %input_backward.2 = (f32[896,768]{1,0:T(8,128)}, bf16[896,768]{1,0:T(8,128)(2,1)}, f32[8,384]{1,0:T(8,128)}) custom-call(f32[896,768]{1,0:T(8,128)} %get-tuple-element.215.base_ref, bf16[896,384]{1,0:T(8,128)(2,1)} %get-tuple-element.214.dq_ref.refs_1_, f32[896,768]{1,0:T(8,128)} %get-tuple-element.216.own_ref, ...), custom_call_target="tpu_custom_call" | custom-call | flops 1000 | bytes 1000 | tf_op jit(solution)/shard_map/input_backward/pallas_call | solution.py:794
  347.0 5.9 %weight_grads.14 = bf16[4,4,48,1152]{3,2,1,0:T(8,128)(2,1)} custom-call(s32[1]{0:T(128)} %bitcast.meta, bf16[896,768]{1,0:T(8,128)(2,1)} %bitcast.119, bf16[896,384]{1,0:T(8,128)(2,1)} %get-tuple-element.214.dq_ref.refs_1_, bf16[896,768]{1,0:T(8,128)(2,1)} %get-tuple-element.218.refs_2_.refs_3_, bf16[896,768]{1,0:T(8,128)(2,1)} %get-tuple-element.218.refs_2_.refs_3_), custom_call_target="tpu_custom_call" | custom-call | flops 1000 | bytes 1000 | tf_op jit(solution)/shard_map/weight_grads/pallas_call | solution.py:340
  354.1 6.6 %input_backward.3 = (bf16[896,768]{1,0:T(8,128)(2,1)}, bf16[896,768]{1,0:T(8,128)(2,1)}, f32[8,384]{1,0:T(8,128)}) custom-call(f32[896,768]{1,0:T(8,128)} %get-tuple-element.222.base_ref, bf16[896,384]{1,0:T(8,128)(2,1)} %get-tuple-element.223.dq_ref.refs_1_, f32[896,768]{1,0:T(8,128)} %get-tuple-element.224.own_ref, bf16[896,768]{1,0:T(8,128)(2,1)} %copy-done.12, ...), custom_call_target="tpu_custom_call" | custom-call | flops 1000 | bytes 1000 | tf_op jit(solution)/shard_map/input_backward/pallas_call | solution.py:794
  360.7 3.1 gather_fusion.6
  366.3 18.0 %all-to-all-start.3 = ((bf16[32,32,768]{2,1,0:T(8,128)(2,1)}), bf16[32,32,768]{2,1,0:T(8,128)(2,1)}, u32[]{:S(2)}, u32[]{:S(2)}) async-start(bf16[32,32,768]{2,1,0:T(8,128)(2,1)} %gather_fusion.6), calls=%async_computation.5 | async-start | bytes 3145728 | tf_op jit(solution)/shard_map/all_to_all | solution.py:966
  387.0 6.3 %weight_grads.15 = bf16[4,4,48,1152]{3,2,1,0:T(8,128)(2,1)} custom-call(s32[1]{0:T(128)} %bitcast.meta, bf16[896,768]{1,0:T(8,128)(2,1)} %bitcast.120, bf16[896,384]{1,0:T(8,128)(2,1)} %get-tuple-element.223.dq_ref.refs_1_, bf16[896,768]{1,0:T(8,128)(2,1)} %get-tuple-element.246.refs_2_.refs_3_, bf16[896,768]{1,0:T(8,128)(2,1)} %get-tuple-element.246.refs_2_.refs_3_, ...), custom_call_target="tpu_custom_call" | custom-call | flops 1000 | bytes 1000 | tf_op jit(solution)/shard_map/weight_grads/pallas_call | solution.py:340
  393.3 1.8 gather_fusion.7
  395.1 1.9 collective-permute-start.23
  397.0 1.5 collective-permute-start.24
  398.8 1.9 collective-permute-start.20
  400.7 1.5 collective-permute-start.21
  402.4 1.7 collective-permute-done.25
  404.1 17.0 %collective-permute-done.20 = bf16[4,48,1152]{2,1,0:T(8,128)(2,1)S(1)} collective-permute-done((bf16[4,48,1152]{2,1,0:T(8,128)(2,1)S(1)}, bf16[4,48,1152]{2,1,0:T(8,128)(2,1)S(1)}, u32[]{:S(2)}, u32[]{:S(2)}) %collective-permute-start.20) | collective-permute-done | bytes 442400 | tf_op jit(solution)/shard_map/ppermute | solution.py:816
  421.1 6.0 %collective-permute-done.21 = bf16[4,48,1152]{2,1,0:T(8,128)(2,1)S(1)} collective-permute-done((bf16[4,48,1152]{2,1,0:T(8,128)(2,1)S(1)}, bf16[4,48,1152]{2,1,0:T(8,128)(2,1)S(1)}, u32[]{:S(2)}, u32[]{:S(2)}) %collective-permute-start.21) | collective-permute-done | bytes 442400 | tf_op jit(solution)/shard_map/ppermute | solution.py:816
  427.1 8.2 %collective-permute-done.22 = bf16[4,48,1152]{2,1,0:T(8,128)(2,1)S(1)} collective-permute-done((bf16[4,48,1152]{2,1,0:T(8,128)(2,1)S(1)}, bf16[4,48,1152]{2,1,0:T(8,128)(2,1)S(1)}, u32[]{:S(2)}, u32[]{:S(2)}) %collective-permute-start.22) | collective-permute-done | bytes 442400 | tf_op jit(solution)/shard_map/ppermute | solution.py:816
  436.7 3.5 reduce-scatter.9.cloned.1.call-done
  441.2 3.5 collective-permute-start.29
  446.0 1.5 collective-permute-start.31
  449.0 2.2 collective-permute-start.27
  452.1 3.3 gather_fusion.8
  456.1 1.5 collective-permute-start.28
  460.7 2.0 collective-permute-done.28
  (198 shorter events, 45.2 us)
Async XLA Ops:
  7.2 14.0 %copy-start = (bf16[32,32,768]{2,1,0:T(8,128)(2,1)S(1)}, bf16[32,32,768]{2,1,0:T(8,128)(2,1)}, u32[]{:S(2)}) copy-start(bf16[32,32,768]{2,1,0:T(8,128)(2,1)} %param.17) | copy-start | bytes 4718596
  7.2 6.1 %copy-start.14 = (bf16[48,3,384]{2,0,1:T(8,128)(2,1)S(1)}, bf16[48,3,384]{2,0,1:T(8,128)(2,1)}, u32[]{:S(2)}) copy-start(bf16[48,3,384]{2,0,1:T(8,128)(2,1)} %param.21) | copy-start | bytes 331780
  7.2 11.8 %copy-start.18 = (f32[4,384]{1,0:T(4,128)S(1)}, f32[4,384]{1,0:T(4,128)}, u32[]{:S(2)}) copy-start(f32[4,384]{1,0:T(4,128)} %refs_10_) | copy-start | bytes 18436
  7.2 11.8 %copy-start.19 = (f32[1536]{0:T(1024)S(1)}, f32[1536]{0:T(1024)}, u32[]{:S(2)}) copy-start(f32[1536]{0:T(1024)} %param.30) | copy-start | bytes 18436
  7.2 12.4 %copy-start.21 = (s32[32]{0:T(128)S(1)}, s32[32]{0:T(128)}, u32[]{:S(2)}) copy-start(s32[32]{0:T(128)} %param.20) | copy-start | bytes 388
  7.2 13.0 %copy-start.2 = (s32[32]{0:T(128)S(1)}, s32[32]{0:T(128)}, u32[]{:S(2)}) copy-start(s32[32]{0:T(128)} %param.19) | copy-start | bytes 388
  7.2 144.2 %all-gather.2.cloned.1.call-start = ((), (), s32[]{:S(2)}) async-start(), calls=%async_computation.8 | async-start | bytes 8146944 | tf_op jit(solution)/shard_map/all_gather | solution.py:994
  12.5 0.8 copy-start.13
  13.3 9.7 %collective-permute-start = (bf16[48,1152]{1,0:T(8,128)(2,1)S(1)}, bf16[48,1152]{1,0:T(8,128)(2,1)S(1)}, u32[]{:S(2)}, u32[]{:S(2)}) collective-permute-start(bf16[48,1152]{1,0:T(8,128)(2,1)S(1)} %bitcast.133), channel_id=1, source_target_pairs={{0,8},{2,10},{4,12},{6,14},{8,0},{10,2},{12,4},{14,6},{16,24},{18,... | collective-permute-start | bytes 331784 | tf_op jit(solution)/shard_map/ppermute | solution.py:816
  16.4 11.3 %collective-permute-start.1 = (bf16[48,1152]{1,0:T(8,128)(2,1)S(1)}, bf16[48,1152]{1,0:T(8,128)(2,1)S(1)}, u32[]{:S(2)}, u32[]{:S(2)}) collective-permute-start(bf16[48,1152]{1,0:T(8,128)(2,1)S(1)} %bitcast.134), channel_id=1, source_target_pairs={{0,16},{2,18},{4,20},{6,22},{8,24},{10,26},{12,28},{14,30},{16,0},... | collective-permute-start | bytes 331784 | tf_op jit(solution)/shard_map/ppermute | solution.py:816
  19.0 8.8 %collective-permute-start.2 = (bf16[48,1152]{1,0:T(8,128)(2,1)S(1)}, bf16[48,1152]{1,0:T(8,128)(2,1)S(1)}, u32[]{:S(2)}, u32[]{:S(2)}) collective-permute-start(bf16[48,1152]{1,0:T(8,128)(2,1)S(1)} %bitcast.135), channel_id=1, source_target_pairs={{0,24},{2,26},{4,28},{6,30},{8,16},{10,18},{12,20},{14,22},{16,8},... | collective-permute-start | bytes 331784 | tf_op jit(solution)/shard_map/ppermute | solution.py:816
  19.1 42.6 %collective-permute-start.6 = (f32[3072]{0:T(1024)S(1)}, f32[3072]{0:T(1024)S(1)}, u32[]{:S(2)}, u32[]{:S(2)}) collective-permute-start(f32[3072]{0:T(1024)S(1)} %pad_maximum_fusion.2), channel_id=1, source_target_pairs={{0,1},{1,0},{2,3},{3,2},{4,5},{5,4},{6,7},{7,6},{8,9},{9,8},{10,11... | collective-permute-start | bytes 36872 | tf_op jit(solution)/shard_map/ppermute | solution.py:812
  19.1 43.7 %collective-permute-start.7 = (bf16[2,64,768]{2,1,0:T(8,128)(2,1)}, bf16[2,64,768]{2,1,0:T(8,128)(2,1)}, u32[]{:S(2)}, u32[]{:S(2)}) collective-permute-start(bf16[2,64,768]{2,1,0:T(8,128)(2,1)} %param.18), channel_id=1, source_target_pairs={{0,1},{1,0},{2,3},{3,2},{4,5},{5,4},{6,7},{7,6},{8,9},{9,8},{10,11... | collective-permute-start | bytes 589832 | tf_op jit(solution)/shard_map/ppermute | solution.py:812
  27.9 25.9 %copy-start.11 = (bf16[4,48,1152]{2,1,0:T(8,128)(2,1)}, bf16[4,48,1152]{2,1,0:T(8,128)(2,1)S(1)}, u32[]{:S(2)}) copy-start(bf16[4,48,1152]{2,1,0:T(8,128)(2,1)S(1)} %pad_maximum_fusion.own_ref) | copy-start | bytes 1327108
  27.9 64.5 %all-to-all-start = ((bf16[32,32,768]{2,1,0:T(8,128)(2,1)}), bf16[32,32,768]{2,1,0:T(8,128)(2,1)S(1)}, u32[]{:S(2)}, u32[]{:S(2)}) async-start(bf16[32,32,768]{2,1,0:T(8,128)(2,1)} %gather_fusion.1), calls=%async_computation | async-start | bytes 3145728 | tf_op jit(solution)/shard_map/all_to_all | solution.py:972
  50.3 31.2 %collective-permute-start.3 = (bf16[4,48,1152]{2,1,0:T(8,128)(2,1)S(1)}, bf16[4,48,1152]{2,1,0:T(8,128)(2,1)S(1)}, u32[]{:S(2)}, u32[]{:S(2)}) collective-permute-start(bf16[4,48,1152]{2,1,0:T(8,128)(2,1)S(1)} %pad_maximum_fusion.own_ref), channel_id=1, source_target_pairs={{0,2},{2,0},{4,6},{6,4},{8,10},{10,8},{12,14},{14,12},{16,18},{18,... | collective-permute-start | bytes 1327112 | tf_op jit(solution)/shard_map/ppermute | solution.py:816
  52.3 29.2 %collective-permute-start.4 = (bf16[4,48,1152]{2,1,0:T(8,128)(2,1)S(1)}, bf16[4,48,1152]{2,1,0:T(8,128)(2,1)S(1)}, u32[]{:S(2)}, u32[]{:S(2)}) collective-permute-start(bf16[4,48,1152]{2,1,0:T(8,128)(2,1)S(1)} %pad_maximum_fusion.own_ref), channel_id=1, source_target_pairs={{0,4},{2,6},{4,0},{6,2},{8,12},{10,14},{12,8},{14,10},{16,20},{18,... | collective-permute-start | bytes 1327112 | tf_op jit(solution)/shard_map/ppermute | solution.py:816
  53.7 38.6 %collective-permute-start.5 = (bf16[4,48,1152]{2,1,0:T(8,128)(2,1)S(1)}, bf16[4,48,1152]{2,1,0:T(8,128)(2,1)S(1)}, u32[]{:S(2)}, u32[]{:S(2)}) collective-permute-start(bf16[4,48,1152]{2,1,0:T(8,128)(2,1)S(1)} %pad_maximum_fusion.own_ref), channel_id=1, source_target_pairs={{0,6},{2,4},{4,2},{6,0},{8,14},{10,12},{12,10},{14,8},{16,22},{18,... | collective-permute-start | bytes 1327112 | tf_op jit(solution)/shard_map/ppermute | solution.py:816
  81.5 10.8 %copy-start.15 = (bf16[4,48,1152]{2,1,0:T(8,128)(2,1)}, bf16[4,48,1152]{2,1,0:T(8,128)(2,1)S(1)}, u32[]{:S(2)}) copy-start(bf16[4,48,1152]{2,1,0:T(8,128)(2,1)S(1)} %collective-permute-done.3.first_ref) | copy-start | bytes 1327108
  81.5 10.8 %copy-start.16 = (bf16[4,48,1152]{2,1,0:T(8,128)(2,1)}, bf16[4,48,1152]{2,1,0:T(8,128)(2,1)S(1)}, u32[]{:S(2)}) copy-start(bf16[4,48,1152]{2,1,0:T(8,128)(2,1)S(1)} %collective-permute-done.4.second_ref) | copy-start | bytes 1327108
  92.3 0.8 copy-start.17
  97.5 7.3 %collective-permute-start.8 = (bf16[768,1152]{1,0:T(8,128)(2,1)}, bf16[768,1152]{1,0:T(8,128)(2,1)S(1)}, u32[]{:S(2)}, u32[]{:S(2)}) collective-permute-start(bf16[768,1152]{1,0:T(8,128)(2,1)} %bitcast.109), channel_id=1, source_target_pairs={{0,1},{1,0},{2,3},{3,2},{4,5},{5,4},{6,7},{7,6},{8,9},{9,8},{10,11... | collective-permute-start | bytes 5308424 | tf_op jit(solution)/shard_map/ppermute | solution.py:812
  104.3 6.7 %collective-permute-start.9 = (bf16[896,768]{1,0:T(8,128)(2,1)}, bf16[896,768]{1,0:T(8,128)(2,1)S(1)}, u32[]{:S(2)}, u32[]{:S(2)}) collective-permute-start(bf16[896,768]{1,0:T(8,128)(2,1)} %get-tuple-element.152.refs_0_), channel_id=1, source_target_pairs={{0,1},{1,0},{2,3},{3,2},{4,5},{5,4},{6,7},{7,6},{8,9},{9,8},{10,11... | collective-permute-start | bytes 4128776 | tf_op jit(solution)/shard_map/ppermute | solution.py:812
  104.8 1.2 copy-start.3
  111.0 11.7 %collective-permute-start.10 = (bf16[896,768]{1,0:T(8,128)(2,1)}, bf16[896,768]{1,0:T(8,128)(2,1)S(1)}, u32[]{:S(2)}, u32[]{:S(2)}) collective-permute-start(bf16[896,768]{1,0:T(8,128)(2,1)} %get-tuple-element.150.refs_0_), channel_id=1, source_target_pairs={{0,1},{1,0},{2,3},{3,2},{4,5},{5,4},{6,7},{7,6},{8,9},{9,8},{10,11... | collective-permute-start | bytes 4128776 | tf_op jit(solution)/shard_map/ppermute | solution.py:812
  111.0 1.1 copy-start.5
  122.7 1.1 copy-start.6
  151.5 12.5 %collective-permute-start.11 = (bf16[768,4992]{1,0:T(8,128)(2,1)}, bf16[768,4992]{1,0:T(8,128)(2,1)}, u32[]{:S(2)}, u32[]{:S(2)}) collective-permute-start(bf16[768,4992]{1,0:T(8,128)(2,1)} %all-gather.2.cloned.1.call-done.refs_0_.refs_2_.refs_4_.refs_6_.refs_8_.expand.reduce.in0.out0.refs_10_.wk0.wv0), channel_id=1, source_target_pairs={{0,1},{1,0},{2,3},{3,2},{4,5},{5,4},{6,7},{7,6},{8,9},{9,8},{10,11... | collective-permute-start | bytes 23003144 | tf_op jit(solution)/shard_map/ppermute | solution.py:812
  151.5 53.5 %all-to-all-start.1 = ((bf16[32,32,768]{2,1,0:T(8,128)(2,1)}), bf16[32,32,768]{2,1,0:T(8,128)(2,1)S(1)}, u32[]{:S(2)}, u32[]{:S(2)}) async-start(bf16[32,32,768]{2,1,0:T(8,128)(2,1)} %gather_fusion), calls=%async_computation.1 | async-start | bytes 3145728 | tf_op jit(solution)/shard_map/all_to_all | solution.py:972
  155.2 169.4 %reduce-scatter.5.cloned.1.call-start = ((), (), s32[]{:S(2)}) async-start(), calls=%async_computation.9 | async-start | bytes 5898240 | tf_op jit(solution)/shard_map/reduce_scatter | solution.py:872
  230.9 6.3 %collective-permute-start.13 = (bf16[4,4,48,1536]{3,2,1,0:T(8,128)(2,1)}, bf16[4,4,48,1536]{3,2,1,0:T(8,128)(2,1)}, u32[]{:S(2)}, u32[]{:S(2)}) collective-permute-start(bf16[4,4,48,1536]{3,2,1,0:T(8,128)(2,1)} %weight_grads.9), channel_id=1, source_target_pairs={{0,1},{1,0},{2,3},{3,2},{4,5},{5,4},{6,7},{7,6},{8,9},{9,8},{10,11... | collective-permute-start | bytes 7077896 | tf_op jit(solution)/shard_map/ppermute | solution.py:812
  236.8 6.5 %collective-permute-start.12 = (bf16[4,4,48,1536]{3,2,1,0:T(8,128)(2,1)}, bf16[4,4,48,1536]{3,2,1,0:T(8,128)(2,1)}, u32[]{:S(2)}, u32[]{:S(2)}) collective-permute-start(bf16[4,4,48,1536]{3,2,1,0:T(8,128)(2,1)} %weight_grads.8), channel_id=1, source_target_pairs={{0,1},{1,0},{2,3},{3,2},{4,5},{5,4},{6,7},{7,6},{8,9},{9,8},{10,11... | collective-permute-start | bytes 7077896 | tf_op jit(solution)/shard_map/ppermute | solution.py:812
  249.4 1.3 copy-start.7
  252.5 39.2 %all-to-all-start.2 = ((bf16[32,32,768]{2,1,0:T(8,128)(2,1)}), bf16[32,32,768]{2,1,0:T(8,128)(2,1)S(1)}, u32[]{:S(2)}, u32[]{:S(2)}) async-start(bf16[32,32,768]{2,1,0:T(8,128)(2,1)} %gather_fusion.5), calls=%async_computation.2 | async-start | bytes 3145728 | tf_op jit(solution)/shard_map/all_to_all | solution.py:966
  257.9 129.1 %reduce-scatter.7.cloned.1.call-start = ((), (), s32[]{:S(2)}) async-start(), calls=%async_computation.10 | async-start | bytes 3686400 | tf_op jit(solution)/shard_map/reduce_scatter | solution.py:872
  290.1 9.1 %collective-permute-start.15 = (bf16[4,4,48,1152]{3,2,1,0:T(8,128)(2,1)}, bf16[4,4,48,1152]{3,2,1,0:T(8,128)(2,1)S(1)}, u32[]{:S(2)}, u32[]{:S(2)}) collective-permute-start(bf16[4,4,48,1152]{3,2,1,0:T(8,128)(2,1)} %weight_grads.12), channel_id=1, source_target_pairs={{0,1},{1,0},{2,3},{3,2},{4,5},{5,4},{6,7},{7,6},{8,9},{9,8},{10,11... | collective-permute-start | bytes 5308424 | tf_op jit(solution)/shard_map/ppermute | solution.py:812
  291.8 3.5 collective-permute-start.14
  299.2 1.2 copy-start.9
  309.3 126.3 %reduce-scatter.11.cloned.1.call-start = ((), (), s32[]{:S(2)}) async-start(), calls=%async_computation.12 | async-start | bytes 1474560 | tf_op jit(solution)/shard_map/reduce_scatter | solution.py:872
  324.5 15.8 %collective-permute-start.16 = (bf16[896,768]{1,0:T(8,128)(2,1)}, bf16[896,768]{1,0:T(8,128)(2,1)}, u32[]{:S(2)}, u32[]{:S(2)}) collective-permute-start(bf16[896,768]{1,0:T(8,128)(2,1)} %get-tuple-element.217), channel_id=1, source_target_pairs={{0,1},{1,0},{2,3},{3,2},{4,5},{5,4},{6,7},{7,6},{8,9},{9,8},{10,11... | collective-permute-start | bytes 4128776 | tf_op jit(solution)/shard_map/ppermute | solution.py:812
  339.9 13.0 %collective-permute-start.17 = (bf16[896,768]{1,0:T(8,128)(2,1)}, bf16[896,768]{1,0:T(8,128)(2,1)S(1)}, u32[]{:S(2)}, u32[]{:S(2)}) collective-permute-start(bf16[896,768]{1,0:T(8,128)(2,1)} %get-tuple-element.220), channel_id=1, source_target_pairs={{0,1},{1,0},{2,3},{3,2},{4,5},{5,4},{6,7},{7,6},{8,9},{9,8},{10,11... | collective-permute-start | bytes 4128776 | tf_op jit(solution)/shard_map/ppermute | solution.py:812
  352.9 1.1 copy-start.12
  354.0 9.9 %collective-permute-start.18 = (bf16[4,4,48,1152]{3,2,1,0:T(8,128)(2,1)}, bf16[4,4,48,1152]{3,2,1,0:T(8,128)(2,1)S(1)}, u32[]{:S(2)}, u32[]{:S(2)}) collective-permute-start(bf16[4,4,48,1152]{3,2,1,0:T(8,128)(2,1)} %weight_grads.14), channel_id=1, source_target_pairs={{0,1},{1,0},{2,3},{3,2},{4,5},{5,4},{6,7},{7,6},{8,9},{9,8},{10,11... | collective-permute-start | bytes 5308424 | tf_op jit(solution)/shard_map/ppermute | solution.py:812
  360.7 4.0 copy-start.20
  363.8 2.4 copy-start.8
  366.3 75.0 %all-to-all-start.3 = ((bf16[32,32,768]{2,1,0:T(8,128)(2,1)}), bf16[32,32,768]{2,1,0:T(8,128)(2,1)}, u32[]{:S(2)}, u32[]{:S(2)}) async-start(bf16[32,32,768]{2,1,0:T(8,128)(2,1)} %gather_fusion.6), calls=%async_computation.5 | async-start | bytes 3145728 | tf_op jit(solution)/shard_map/all_to_all | solution.py:966
  384.2 56.0 %reduce-scatter.9.cloned.1.call-start = ((), (), s32[]{:S(2)}) async-start(), calls=%async_computation.11 | async-start | bytes 921600 | tf_op jit(solution)/shard_map/reduce_scatter | solution.py:872
  386.8 8.3 %collective-permute-start.19 = (f32[13056]{0:T(1024)S(1)}, f32[13056]{0:T(1024)S(1)}, u32[]{:S(2)}, u32[]{:S(2)}) collective-permute-start(f32[13056]{0:T(1024)S(1)} %constant_dynamic-update-slice_fusion.4), channel_id=1, source_target_pairs={{0,1},{1,0},{2,3},{3,2},{4,5},{5,4},{6,7},{7,6},{8,9},{9,8},{10,11... | collective-permute-start | bytes 156680 | tf_op jit(solution)/shard_map/ppermute | solution.py:812
  393.3 5.4 %copy-start.4 = (bf16[4,4,48,1152]{3,2,1,0:T(8,128)(2,1)S(1)}, bf16[4,4,48,1152]{3,2,1,0:T(8,128)(2,1)}, u32[]{:S(2)}) copy-start(bf16[4,4,48,1152]{3,2,1,0:T(8,128)(2,1)} %weight_grads.15) | copy-start | bytes 5308420
  395.1 7.0 %collective-permute-start.23 = (f32[13056]{0:T(1024)S(1)}, f32[13056]{0:T(1024)S(1)}, u32[]{:S(2)}, u32[]{:S(2)}) collective-permute-start(f32[13056]{0:T(1024)S(1)} %add.264), channel_id=1, source_target_pairs={{0,2},{2,0},{4,6},{6,4},{8,10},{10,8},{12,14},{14,12},{16,18},{18,... | collective-permute-start | bytes 156680 | tf_op jit(solution)/shard_map/ppermute | solution.py:816
  397.0 5.3 %collective-permute-start.24 = (f32[13056]{0:T(1024)S(1)}, f32[13056]{0:T(1024)S(1)}, u32[]{:S(2)}, u32[]{:S(2)}) collective-permute-start(f32[13056]{0:T(1024)S(1)} %add.264), channel_id=1, source_target_pairs={{0,4},{2,6},{4,0},{6,2},{8,12},{10,14},{12,8},{14,10},{16,20},{18,... | collective-permute-start | bytes 156680 | tf_op jit(solution)/shard_map/ppermute | solution.py:816
  398.5 5.6 %collective-permute-start.25 = (f32[13056]{0:T(1024)S(1)}, f32[13056]{0:T(1024)S(1)}, u32[]{:S(2)}, u32[]{:S(2)}) collective-permute-start(f32[13056]{0:T(1024)S(1)} %add.264), channel_id=1, source_target_pairs={{0,6},{2,4},{4,2},{6,0},{8,14},{10,12},{12,10},{14,8},{16,22},{18,... | collective-permute-start | bytes 156680 | tf_op jit(solution)/shard_map/ppermute | solution.py:816
  398.8 22.4 %collective-permute-start.20 = (bf16[4,48,1152]{2,1,0:T(8,128)(2,1)S(1)}, bf16[4,48,1152]{2,1,0:T(8,128)(2,1)S(1)}, u32[]{:S(2)}, u32[]{:S(2)}) collective-permute-start(bf16[4,48,1152]{2,1,0:T(8,128)(2,1)S(1)} %get-tuple-element.308), channel_id=1, source_target_pairs={{0,2},{2,0},{4,6},{6,4},{8,10},{10,8},{12,14},{14,12},{16,18},{18,... | collective-permute-start | bytes 1327112 | tf_op jit(solution)/shard_map/ppermute | solution.py:816
  400.7 26.4 %collective-permute-start.21 = (bf16[4,48,1152]{2,1,0:T(8,128)(2,1)S(1)}, bf16[4,48,1152]{2,1,0:T(8,128)(2,1)S(1)}, u32[]{:S(2)}, u32[]{:S(2)}) collective-permute-start(bf16[4,48,1152]{2,1,0:T(8,128)(2,1)S(1)} %get-tuple-element.310), channel_id=1, source_target_pairs={{0,4},{2,6},{4,0},{6,2},{8,12},{10,14},{12,8},{14,10},{16,20},{18,... | collective-permute-start | bytes 1327112 | tf_op jit(solution)/shard_map/ppermute | solution.py:816
  402.2 33.2 %collective-permute-start.22 = (bf16[4,48,1152]{2,1,0:T(8,128)(2,1)S(1)}, bf16[4,48,1152]{2,1,0:T(8,128)(2,1)S(1)}, u32[]{:S(2)}, u32[]{:S(2)}) collective-permute-start(bf16[4,48,1152]{2,1,0:T(8,128)(2,1)S(1)} %get-tuple-element.309), channel_id=1, source_target_pairs={{0,6},{2,4},{4,2},{6,0},{8,14},{10,12},{12,10},{14,8},{16,22},{18,... | collective-permute-start | bytes 1327112 | tf_op jit(solution)/shard_map/ppermute | solution.py:816
  435.6 12.6 %copy-start.10 = (bf16[4,48,1152]{2,1,0:T(8,128)(2,1)}, bf16[4,48,1152]{2,1,0:T(8,128)(2,1)S(1)}, u32[]{:S(2)}) copy-start(bf16[4,48,1152]{2,1,0:T(8,128)(2,1)S(1)} %fusion.2) | copy-start | bytes 1327108
  441.2 14.9 %collective-permute-start.29 = (f32[13056]{0:T(1024)S(1)}, f32[13056]{0:T(1024)S(1)}, u32[]{:S(2)}, u32[]{:S(2)}) collective-permute-start(f32[13056]{0:T(1024)S(1)} %add_add_fusion.1), channel_id=1, source_target_pairs={{0,8},{2,10},{4,12},{6,14},{8,0},{10,2},{12,4},{14,6},{16,24},{18,... | collective-permute-start | bytes 156680 | tf_op jit(solution)/shard_map/ppermute | solution.py:816
  444.8 12.8 %collective-permute-start.30 = (f32[13056]{0:T(1024)S(1)}, f32[13056]{0:T(1024)S(1)}, u32[]{:S(2)}, u32[]{:S(2)}) collective-permute-start(f32[13056]{0:T(1024)S(1)} %add_add_fusion.1), channel_id=1, source_target_pairs={{0,16},{2,18},{4,20},{6,22},{8,24},{10,26},{12,28},{14,30},{16,0},... | collective-permute-start | bytes 156680 | tf_op jit(solution)/shard_map/ppermute | solution.py:816
  446.0 11.6 %collective-permute-start.31 = (f32[13056]{0:T(1024)S(1)}, f32[13056]{0:T(1024)S(1)}, u32[]{:S(2)}, u32[]{:S(2)}) collective-permute-start(f32[13056]{0:T(1024)S(1)} %add_add_fusion.1), channel_id=1, source_target_pairs={{0,24},{2,26},{4,28},{6,30},{8,16},{10,18},{12,20},{14,22},{16,8},... | collective-permute-start | bytes 156680 | tf_op jit(solution)/shard_map/ppermute | solution.py:816
  448.2 12.5 %collective-permute-start.26 = (bf16[48,1152]{1,0:T(8,128)(2,1)S(1)}, bf16[48,1152]{1,0:T(8,128)(2,1)S(1)}, u32[]{:S(2)}, u32[]{:S(2)}) collective-permute-start(bf16[48,1152]{1,0:T(8,128)(2,1)S(1)} %get-tuple-element.313), channel_id=1, source_target_pairs={{0,8},{2,10},{4,12},{6,14},{8,0},{10,2},{12,4},{14,6},{16,24},{18,... | collective-permute-start | bytes 331784 | tf_op jit(solution)/shard_map/ppermute | solution.py:816
  449.0 11.7 %collective-permute-start.27 = (bf16[48,1152]{1,0:T(8,128)(2,1)S(1)}, bf16[48,1152]{1,0:T(8,128)(2,1)S(1)}, u32[]{:S(2)}, u32[]{:S(2)}) collective-permute-start(bf16[48,1152]{1,0:T(8,128)(2,1)S(1)} %get-tuple-element.315), channel_id=1, source_target_pairs={{0,16},{2,18},{4,20},{6,22},{8,24},{10,26},{12,28},{14,30},{16,0},... | collective-permute-start | bytes 331784 | tf_op jit(solution)/shard_map/ppermute | solution.py:816
  452.1 12.4 %copy-start.1 = (bf16[32,32,768]{2,1,0:T(8,128)(2,1)S(1)}, bf16[32,32,768]{2,1,0:T(8,128)(2,1)}, u32[]{:S(2)}) copy-start(bf16[32,32,768]{2,1,0:T(8,128)(2,1)} %param.17) | copy-start | bytes 4718596
  456.1 6.7 %collective-permute-start.28 = (bf16[48,1152]{1,0:T(8,128)(2,1)S(1)}, bf16[48,1152]{1,0:T(8,128)(2,1)S(1)}, u32[]{:S(2)}, u32[]{:S(2)}) collective-permute-start(bf16[48,1152]{1,0:T(8,128)(2,1)S(1)} %get-tuple-element.314), channel_id=1, source_target_pairs={{0,24},{2,26},{4,28},{6,30},{8,16},{10,18},{12,20},{14,22},{16,8},... | collective-permute-start | bytes 331784 | tf_op jit(solution)/shard_map/ppermute | solution.py:816
Sparse Core Ops, SparseCore 0:
  13.4 138.0 all-gather.1
  249.6 73.6 reduce-scatter.4
  326.3 42.3 reduce-scatter.6
  370.8 40.8 reduce-scatter.10
  413.9 26.3 reduce-scatter.8

commit v6 on v5

--- a/solution.py
+++ b/solution.py
@@ -12,7 +12,6 @@
 EPSILON = 1e-05
 MASKED = -1e30
 BLOCK = 128
-LIGHT = 1000
 LOW_GROUPS = [[4 * plane + low for low in range(4)] for plane in range(4)]
 PLANE_GROUPS = [[low + 4 * plane for plane in range(4)] for low in range(4)]
 GROUP = 4
@@ -132,15 +131,13 @@
     pairs_in = refs[:2]
     dq_ref = refs[2]
     outs = refs[3:5]
-    flipped = refs[5:7]
-    sums = refs[7:9]
+    sums = refs[5:7]
     block, local, start, _, active = block_place(meta)
     half = q_ref.shape[1]
 
     @pl.when(block == 0)
     def _():
         for part in range(2):
-            flipped[part][...] = pairs_in[part][:, :half].astype(F32).T.astype(BF16)
             sums[part][...] = jnp.zeros_like(sums[part])
 
     def run(base, span):
@@ -166,9 +163,10 @@
                 grad_score = (probs[part] * (grad_probs[part] - row_dot)).astype(BF16)
                 sums[part][place, value_cols] += dot_nn(probs[part].astype(BF16), grads)
                 sums[part][place, cols] += dot_nn(grad_score, queries)
-                term = dot_nn(flipped[part][cols, place], grad_score)
+                term = dot_tn(grad_score, pairs_in[part][place, cols])
                 grad_query = term if grad_query is None else grad_query + term
-            dq_ref[:, cols] = unstack_heads(grad_query).astype(BF16)
+            low = lane_low((BLOCK, PAIR))
+            dq_ref[:, cols] = jnp.where(low, grad_query[:BLOCK], grad_query[BLOCK:]).astype(BF16)
 
     run_spans(spans, local, start, active, run)
 
@@ -230,8 +228,7 @@
             in_specs=[row_spec(half), row_spec(half), lse_spec()]
             + [whole_spec(rows, 2 * half)] * 2,
             out_specs=[row_spec(half)] + [whole_spec(rows, 2 * half)] * 2,
-            scratch_shapes=[pltpu.VMEM((half, rows), BF16)] * 2
-            + [pltpu.VMEM((rows, 2 * half), F32)] * 2,
+            scratch_shapes=[pltpu.VMEM((rows, 2 * half), F32)] * 2,
         ),
         out_shape=[
             kept((rows, half), BF16),
@@ -371,10 +368,6 @@
     return scale * (inner - mean_inner - unit * mean_unit)
 
 
-def norm_backward(grad, unit, scale, gain):
-    return norm_gradient(grad, unit, scale, gain), jnp.sum(grad * unit, 0), jnp.sum(grad, 0)
-
-
 def sub_blocks(meta, keys_each, run, skip):
     def one(sub, carry):
         block = pl.program_id(0) * GROUP + sub
@@ -590,7 +583,7 @@
 def ffn_forward(first, hidden, base, weight, bias, gain, shift):
     rows, width = hidden.shape
     units = bias.shape[1]
-    tall = rows // 4
+    tall = rows // 2
     wide, long = plain_rows(tall, width), plain_rows(tall, units)
 
     def side(column):
@@ -600,7 +593,7 @@
 
     return pl.pallas_call(
         functools.partial(ffn_forward_kernel, first),
-        grid=(4,),
+        grid=(2,),
         in_specs=[wide, wide, side(0), side(1), plain_fixed((1, units))]
         + [plain_fixed((1, width))] * 2,
         out_specs=[long, long, wide],
@@ -711,9 +704,7 @@
         ]
         + [kept((rows, half), BF16)] * 4
         + [kept((memory_rows, half), BF16)] * 4,
-        cost_estimate=pl.CostEstimate(
-            flops=(24 * rows * width * half) // LIGHT, bytes_accessed=(20 * rows * width) // LIGHT, transcendentals=0
-        ),
+        cost_estimate=light_cost(),
         name="mid_forward",
     )(meta, inputs, *attn, memory, *[m[0] for _ in range(5) for m in mid], *in_pair, out_bias, gain, shift)
     return outs[:7], outs[7:9], outs[9:11], outs[11:13], outs[13:15]
@@ -754,9 +745,7 @@
         ]
         + [kept((rows, half), BF16)] * 4
         + [kept((memory_rows, 4 * half), F32), kept((memory_rows, 4 * half), BF16)],
-        cost_estimate=pl.CostEstimate(
-            flops=(24 * rows * width * half) // LIGHT, bytes_accessed=(20 * rows * width) // LIGHT, transcendentals=0
-        ),
+        cost_estimate=light_cost(),
         name="mid_backward",
     )(meta, dn2, unit2, scale2, unit1, scale1, lse, *cq, *ck, *cv, *[m[0] for _ in range(3) for m in mid], gain)
     return outs[:4], outs[4:6], outs[6:8], outs[8], outs[9]
@@ -814,6 +803,27 @@
 
 def hop(value, bits):
     return lax.ppermute(value, "dp", [(i, i ^ bits) for i in range(16)])
+
+
+def pack_kernel(*refs):
+    start = 0
+    for ref in refs[:-1]:
+        refs[-1][:, start : start + ref.shape[1]] = ref[...]
+        start += ref.shape[1]
+
+
+def pack_shards(*parts):
+    shard = parts[0].shape[0]
+    total = sum(part.shape[1] for part in parts)
+    return pl.pallas_call(
+        pack_kernel,
+        grid=(1,),
+        in_specs=[plain_fixed(part.shape) for part in parts],
+        out_specs=plain_fixed((shard, total)),
+        out_shape=kept((shard, total), BF16),
+        cost_estimate=light_cost(),
+        name="pack_shards",
+    )(*parts)
 
 
 def assemble_kernel(meta, own_ref, first_ref, second_ref, third_ref, out_ref):
@@ -986,10 +996,6 @@
     early = (row_valid.astype(F32), affine, in_pair, hidden_pair, meta, piece_ids, memory_full, send_ids, inverse)
     ordered = order(tokens)
     qkv_shard_in = self_project.reshape(shard, 3 * half)
-    mid_shard_in = jnp.concatenate(
-        [self_output.T, cross_query, cross_output.T, cross_memory.reshape(shard, 2 * half)], 1
-    )
-
     def slow_gather(value):
         return lax.all_gather(value, "dp", axis=0, tiled=True)
 
@@ -1010,10 +1016,16 @@
     inputs = pack(arrived, piece_ids)
     arrived_cot = arrive(ordered_cot)
 
-    rest_own = slow_gather(jnp.concatenate([hidden_in, hidden_out.T, mid_shard_in], 1))
-
-    def columns(pair, start, count):
-        return [lax.slice_in_dim(pair[h], start, start + count, axis=1) for h in both]
+    rest_own = slow_gather(
+        pack_shards(
+            hidden_in,
+            hidden_out.T,
+            self_output.T,
+            cross_query,
+            cross_output.T,
+            cross_memory.reshape(shard, 2 * half),
+        )
+    )
 
 
     queries = [None, None]
@@ -1174,9 +1186,7 @@
         small, qkv_grads = tie(small, qkv_grads)
         qkv_line = scatter_low(qkv_grads)
         small = sum_low(small)
-        qkv_line, grad_back, mid_shard, ffn_shard, small = tie(
-            qkv_line, grad_back, mid_shard, ffn_shard, small
-        )
+        qkv_line, grad_back, ffn_shard, small = tie(qkv_line, grad_back, ffn_shard, small)
         qkv_shard = scatter_plane(qkv_line)
         small = sum_planes(small)
     else:

time: 478 us -> 479 us (level)
  starting transfers between devices: 68.4 us -> 61.3 us
  Pallas kernels: 220 us -> 226 us
  waiting for transfers between devices: 102 us -> 107 us
    reduce_scatter x4, waiting for transfers between devices: 3.54 us -> 10.3 us  [wide_scatter(): lax.psum_scatter(value, 'dp', scatter_dimension=0, tiled=True, axis_index...]
    all_to_all x2, starting transfers between devices: 23.3 us -> 17.8 us  [go_home(): lax.all_to_all(outgoing, 'dp', split_axis=0, concat_axis=0, tiled=True)]
    unnamed x62 -> x55, local copies, waits for them, and re-layouts: 14.7 us -> 10.4 us
    pallas_call x2 -> x3, Pallas kernels: 20 us -> 21.1 us  [the longest x2 19.2 us: ffn_forward(): pl.pallas_call(functools.partial(ffn_forward_kernel, first), grid=(2,), i...]
  transfers between devices with their start and end apart: 41 -> 41, of which waited for: 13 -> 13; matrix products, arithmetic and copies ran while one was open for 10% -> 10% of each run, Pallas kernels for 40% -> 41%
where the time goes in v6:
time: 479 us; the launch traced here: 474 us
  Pallas kernels  226 us (47%)
  waiting for transfers between devices  107 us (22%)
  starting transfers between devices  61.3 us (13%)
  local copies, waits for them, and re-layouts  48.6 us (10%)
  between operations  16.7 us (3%)
  other arithmetic  13.9 us (3%)
    ppermute x18, waiting for transfers between devices, hop(): return lax.ppermute(value, 'dp', [(i, i ^ bits) for i in range(16)])  67.7 us
    pallas_call x8, Pallas kernels, weight_grads(): pl.pallas_call(functools.partial(grads_kernel, sides, counts, factors, ex...  51.5 us
    pallas_call x2, Pallas kernels, attend_backward(): pl.pallas_call(functools.partial(backward_kernel, piece, spans), grid_spe...  32.6 us
    pallas_call x1, Pallas kernels, mid_backward(): pl.pallas_call(functools.partial(mid_backward_kernel, score_scale, rows),...  26.7 us
    ppermute x18, starting transfers between devices, hop(): return lax.ppermute(value, 'dp', [(i, i ^ bits) for i in range(16)])  25.1 us
    pallas_call x2, Pallas kernels, attend_forward(): pl.pallas_call(functools.partial(forward_kernel, piece, spans), grid_spec...  22.5 us
    pallas_call x1, Pallas kernels, mid_forward(): pl.pallas_call(functools.partial(mid_forward_kernel, score_scale), grid_s...  21.8 us
    gather x9, local copies, waits for them, and re-layouts, rows_at(): return value.at[ids].get(mode='promise_in_bounds')  19.2 us
  transfers between devices with their start and end apart: 41, of which 13 were waited for; matrix products, arithmetic and copies ran while one was open for 10% of the time, Pallas kernels for 41%

profile of v6, /device:TPU:0, one launch (start us, length us, event | category | flops | bytes accessed | tf_op | source)
XLA Modules:
  0.0 473.8 jit_solution(7520609108282762316)
XLA Ops:
  7.3 1.6 copy.66
  8.9 1.9 pack_shards.1
  10.9 3.1 collective-permute-start
  14.0 2.6 collective-permute-start.1
  18.8 1.8 gather_fusion.1
  20.6 4.8 %collective-permute-done.1 = bf16[48,1152]{1,0:T(8,128)(2,1)S(1)} collective-permute-done((bf16[48,1152]{1,0:T(8,128)(2,1)S(1)}, bf16[48,1152]{1,0:T(8,128)(2,1)S(1)}, u32[]{:S(2)}, u32[]{:S(2)}) %collective-permute-start.1) | collective-permute-done | bytes 110624 | tf_op jit(solution)/shard_map/ppermute | solution.py:805
  25.4 11.6 %all-to-all-start = ((bf16[32,32,768]{2,1,0:T(8,128)(2,1)}), bf16[32,32,768]{2,1,0:T(8,128)(2,1)S(1)}, u32[]{:S(2)}, u32[]{:S(2)}) async-start(bf16[32,32,768]{2,1,0:T(8,128)(2,1)} %gather_fusion.1), calls=%async_computation | async-start | bytes 3145728 | tf_op jit(solution)/shard_map/all_to_all | solution.py:982
  38.9 1.9 compare_select_fusion.5
  46.6 1.3 fusion.13.valid_ref
  47.9 1.9 collective-permute-start.3
  49.8 1.5 collective-permute-start.4
  53.4 3.2 gather_fusion
  60.3 1.8 pad_maximum_fusion.1
  62.1 17.0 %collective-permute-done.3.first_ref = bf16[4,48,1152]{2,1,0:T(8,128)(2,1)S(1)} collective-permute-done((bf16[4,48,1152]{2,1,0:T(8,128)(2,1)S(1)}, bf16[4,48,1152]{2,1,0:T(8,128)(2,1)S(1)}, u32[]{:S(2)}, u32[]{:S(2)}) %collective-permute-start.3) | collective-permute-done | bytes 442400 | tf_op jit(solution)/shard_map/ppermute | solution.py:805
  79.1 10.9 %collective-permute-done.5.third_ref = bf16[4,48,1152]{2,1,0:T(8,128)(2,1)S(1)} collective-permute-done((bf16[4,48,1152]{2,1,0:T(8,128)(2,1)S(1)}, bf16[4,48,1152]{2,1,0:T(8,128)(2,1)S(1)}, u32[]{:S(2)}, u32[]{:S(2)}) %collective-permute-start.5) | collective-permute-done | bytes 442400 | tf_op jit(solution)/shard_map/ppermute | solution.py:805
  90.7 4.4 assemble.1
  95.2 1.7 gather_fusion.3
  96.9 5.0 %project.3 = (bf16[896,384]{1,0:T(8,128)(2,1)}, bf16[896,768]{1,0:T(8,128)(2,1)}) custom-call(bf16[896,768]{1,0:T(8,128)(2,1)} %bitcast.113, bf16[768,1152]{1,0:T(8,128)(2,1)} %bitcast.107, bf16[768,1152]{1,0:T(8,128)(2,1)} %bitcast.108, bf16[768,1152]{1,0:T(8,128)(2,1)} %bitcast.109, f32[4,384]{1,0:T(4,128)} %refs_10_), custom_call_target="tpu_custom_call" | custom-call | flops 1000 | bytes 1000 | tf_op jit(solution)/shard_map/project/pallas_call | solution.py:254
  103.6 5.0 %project.2 = (bf16[896,384]{1,0:T(8,128)(2,1)}, bf16[896,768]{1,0:T(8,128)(2,1)}) custom-call(bf16[896,768]{1,0:T(8,128)(2,1)} %bitcast.114, bf16[768,1152]{1,0:T(8,128)(2,1)} %copy-done.3, bf16[768,1152]{1,0:T(8,128)(2,1)} %copy-done.3, bf16[768,1152]{1,0:T(8,128)(2,1)} %copy-done.3, f32[4,384]{1,0:T(4,128)} %slice.201.bias.refs_11_), custom_call_target="tpu_custom_call" | custom-call | flops 1000 | bytes 1000 | tf_op jit(solution)/shard_map/project/pallas_call | solution.py:254
  109.7 11.3 %attend_forward.2 = (bf16[896,384]{1,0:T(8,128)(2,1)}, f32[7,8,256]{2,1,0:T(8,128)}) custom-call(s32[3]{0:T(128)} %pad_add_fusion.meta, bf16[896,384]{1,0:T(8,128)(2,1)} %get-tuple-element.147.q_ref, bf16[896,768]{1,0:T(8,128)(2,1)} %get-tuple-element.149.refs_0_, bf16[896,768]{1,0:T(8,128)(2,1)} %copy-done.5), custom_call_target="tpu_custom_call" | custom-call | flops 1000 | bytes 1000 | tf_op jit(solution)/shard_map/attend_forward/pallas_call | solution.py:206
  122.1 11.2 %attend_forward.3 = (bf16[896,384]{1,0:T(8,128)(2,1)}, f32[7,8,256]{2,1,0:T(8,128)}) custom-call(s32[3]{0:T(128)} %pad_add_fusion.meta, bf16[896,384]{1,0:T(8,128)(2,1)} %get-tuple-element.154.q_ref, bf16[896,768]{1,0:T(8,128)(2,1)} %get-tuple-element.151.refs_0_, bf16[896,768]{1,0:T(8,128)(2,1)} %copy-done.6), custom_call_target="tpu_custom_call" | custom-call | flops 1000 | bytes 1000 | tf_op jit(solution)/shard_map/attend_forward/pallas_call | solution.py:206
  133.4 15.5 %all-gather.2.cloned.1.call-done.refs_0_.refs_2_.refs_4_.refs_6_.refs_8_.expand.reduce.in0.out0.refs_10_.wk0.wv0 = bf16[768,4992]{1,0:T(8,128)(2,1)} async-done(((bf16[48,4992]{1,0:T(8,128)(2,1)}), bf16[768,4992]{1,0:T(8,128)(2,1)}) %all-gather.2.cloned.1.call-update) | async-done | bytes 7667728 | tf_op jit(solution)/shard_map/all_gather | solution.py:1000
  148.9 3.8 all-to-all-start.1
  152.9 8.4 %collective-permute-done.11.refs_1_.refs_3_.refs_5_.refs_7_.refs_9_.expand.reduce.in1.out1.refs_11_.wk1.wv1 = bf16[768,4992]{1,0:T(8,128)(2,1)} collective-permute-done((bf16[768,4992]{1,0:T(8,128)(2,1)}, bf16[768,4992]{1,0:T(8,128)(2,1)}, u32[]{:S(2)}, u32[]{:S(2)}) %collective-permute-start.11) | collective-permute-done | bytes 7667744 | tf_op jit(solution)/shard_map/ppermute | solution.py:801
  161.4 21.8 %mid_forward.1 = (f32[896,768]{1,0:T(8,128)}, f32[896,1]{1,0:T(8,128)}, f32[896,768]{1,0:T(8,128)}, f32[896,1]{1,0:T(8,128)}, bf16[896,768]{1,0:T(8,128)(2,1)}, ...) custom-call(s32[3]{0:T(128)} %pad_add_fusion.meta, ...), custom_call_target="tpu_custom_call" | custom-call | flops 1000 | bytes 1000 | tf_op jit(solution)/shard_map/mid_forward/pallas_call | solution.py:682
  183.2 9.6 %ffn_forward.2 = (bf16[896,1536]{1,0:T(8,128)(2,1)}, bf16[896,1536]{1,0:T(8,128)(2,1)}, f32[896,768]{1,0:T(8,128)}) custom-call(bf16[896,768]{1,0:T(8,128)(2,1)} %get-tuple-element.161.hidden_ref.refs_0_, f32[896,768]{1,0:T(8,128)} %get-tuple-element.162.base_ref.unit2_ref, ...), custom_call_target="tpu_custom_call" | custom-call | flops 1000 | bytes 1000 | tf_op jit(solution)/shard_map/ffn_forward/pallas_call | solution.py:594
  192.8 9.6 %ffn_forward.3 = (bf16[896,1536]{1,0:T(8,128)(2,1)}, bf16[896,1536]{1,0:T(8,128)(2,1)}, f32[896,768]{1,0:T(8,128)}) custom-call(bf16[896,768]{1,0:T(8,128)(2,1)} %get-tuple-element.161.hidden_ref.refs_0_, f32[896,768]{1,0:T(8,128)} %get-tuple-element.166.base_ref, ...), custom_call_target="tpu_custom_call" | custom-call | flops 1000 | bytes 1000 | tf_op jit(solution)/shard_map/ffn_forward/pallas_call | solution.py:594
  202.4 1.7 gather_fusion.4
  204.1 18.5 %ffn_backward.1 = (bf16[896,768]{1,0:T(8,128)(2,1)}, bf16[896,768]{1,0:T(8,128)(2,1)}, f32[896,768]{1,0:T(8,128)}, f32[8,768]{1,0:T(8,128)}, bf16[896,1536]{1,0:...) custom-call(f32[896,768]{1,0:T(8,128)} %get-tuple-element.169.h3_ref, ...), custom_call_target="tpu_custom_call" | custom-call | flops 1000 | bytes 1000 | tf_op jit(solution)/shard_map/ffn_backward/pallas_call | solution.py:646
  222.6 5.7 %weight_grads.9 = bf16[4,4,48,1536]{3,2,1,0:T(8,128)(2,1)} custom-call(s32[1]{0:T(128)} %bitcast.meta, bf16[896,768]{1,0:T(8,128)(2,1)} %get-tuple-element.161.hidden_ref.refs_0_, bf16[896,1536]{1,0:T(8,128)(2,1)} %get-tuple-element.178.refs_1_), custom_call_target="tpu_custom_call" | custom-call | flops 1000 | bytes 1000 | tf_op jit(solution)/shard_map/weight_grads/pallas_call | solution.py:337
  228.4 5.7 %weight_grads.8 = bf16[4,4,48,1536]{3,2,1,0:T(8,128)(2,1)} custom-call(s32[1]{0:T(128)} %bitcast.meta, bf16[896,768]{1,0:T(8,128)(2,1)} %get-tuple-element.174.refs_0_, bf16[896,1536]{1,0:T(8,128)(2,1)} %get-tuple-element.176.refs_1_), custom_call_target="tpu_custom_call" | custom-call | flops 1000 | bytes 1000 | tf_op jit(solution)/shard_map/weight_grads/pallas_call | solution.py:337
  234.6 6.1 %weight_grads.10.refs_3_ = bf16[4,4,48,3072]{3,2,1,0:T(8,128)(2,1)} custom-call(s32[1]{0:T(128)} %bitcast.meta, bf16[896,768]{1,0:T(8,128)(2,1)} %get-tuple-element.161.hidden_ref.refs_0_, bf16[896,1536]{1,0:T(8,128)(2,1)} %get-tuple-element.177.refs_1_, bf16[4,4,48,1536]{3,2,1,0:T(8,128)(2,1)} %collective-permute-done.13.refs_2_), custom_call_target="tpu_custom_call" | custom-call | flops 1000 | bytes 1000 | tf_op jit(solution)/shard_map/weight_grads/pallas_call | solution.py:337
  240.6 6.2 %weight_grads.11 = bf16[4,4,48,3072]{3,2,1,0:T(8,128)(2,1)} custom-call(s32[1]{0:T(128)} %bitcast.meta, bf16[896,768]{1,0:T(8,128)(2,1)} %get-tuple-element.174.refs_0_, bf16[896,1536]{1,0:T(8,128)(2,1)} %get-tuple-element.175.refs_1_, bf16[4,4,48,1536]{3,2,1,0:T(8,128)(2,1)} %collective-permute-done.12.refs_2_, ...), custom_call_target="tpu_custom_call", output_to_operand_aliasing={{}: (4, {})} | custom-call | flops 1000 | bytes 1000 | tf_op jit(solution)/shard_map/weight_grads/pallas_call | solution.py:337
  248.2 1.8 gather_fusion.5
  249.9 4.6 all-to-all-start.2
  254.6 26.7 %mid_backward.1 = (bf16[896,768]{1,0:T(8,128)(2,1)}, f32[896,768]{1,0:T(8,128)}, bf16[896,768]{1,0:T(8,128)(2,1)}, f32[8,768]{1,0:T(8,128)}, bf16[896,384]{1,0:T...) custom-call(s32[3]{0:T(128)} %pad_add_fusion.meta, ...), custom_call_target="tpu_custom_call" | custom-call | flops 1000 | bytes 1000 | tf_op jit(solution)/shard_map/mid_backward/pallas_call | solution.py:723
  281.3 6.8 %weight_grads.12 = bf16[4,4,48,1152]{3,2,1,0:T(8,128)(2,1)} custom-call(s32[1]{0:T(128)} %bitcast.meta, bf16[896,768]{1,0:T(8,128)(2,1)} %get-tuple-element.191.refs_0_, bf16[896,768]{1,0:T(8,128)(2,1)} %get-tuple-element.192.refs_1_, bf16[896,768]{1,0:T(8,128)(2,1)} %get-tuple-element.193.refs_2_, bf16[896,384]{1,0:T(8,128)(2,1)} %get-tuple-element.158.attn1.refs_3_, ...), custom_call_target="tpu_custom_call" | custom-call | flops 1000 | bytes 1000 | tf_op jit(solution)/shard_map/weight_grads/pallas_call | solution.py:337
  288.6 4.6 collective-permute-done.14.got_ref
  293.2 4.0 memory_backward.1
  298.5 8.8 %weight_grads.13 = bf16[4,4,48,1920]{3,2,1,0:T(8,128)(2,1)} custom-call(s32[1]{0:T(128)} %bitcast.meta, bf16[896,768]{1,0:T(8,128)(2,1)} %get-tuple-element.191.refs_0_, bf16[896,768]{1,0:T(8,128)(2,1)} %get-tuple-element.192.refs_1_, bf16[896,768]{1,0:T(8,128)(2,1)} %get-tuple-element.193.refs_2_, bf16[256,768]{1,0:T(8,128)(2,1)} %bitcast.122, ...), custom_call_target="tpu_custom_call" | custom-call | flops 1000 | bytes 1000 | tf_op jit(solution)/shard_map/weight_grads/pallas_call | solution.py:337
  307.4 16.3 %attend_backward.2 = (bf16[896,384]{1,0:T(8,128)(2,1)}, f32[896,768]{1,0:T(8,128)}, bf16[896,768]{1,0:T(8,128)(2,1)}) custom-call(s32[3]{0:T(128)} %pad_add_fusion.meta, bf16[896,384]{1,0:T(8,128)(2,1)} %get-tuple-element.154.q_ref, bf16[896,384]{1,0:T(8,128)(2,1)} %get-tuple-element.207.g_ref, f32[7,8,256]{2,1,0:T(8,128)} %get-tuple-element.208.lse_ref, ...), custom_call_target="tpu_custom_call" | custom-call | flops 1000 | bytes 1000 | tf_op jit(solution)/shard_map/attend_backward/pallas_call | solution.py:223
  323.8 16.3 %attend_backward.3 = (bf16[896,384]{1,0:T(8,128)(2,1)}, f32[896,768]{1,0:T(8,128)}, bf16[896,768]{1,0:T(8,128)(2,1)}) custom-call(s32[3]{0:T(128)} %pad_add_fusion.meta, bf16[896,384]{1,0:T(8,128)(2,1)} %get-tuple-element.147.q_ref, bf16[896,384]{1,0:T(8,128)(2,1)} %get-tuple-element.211.g_ref, f32[7,8,256]{2,1,0:T(8,128)} %get-tuple-element.212.lse_ref, ...), custom_call_target="tpu_custom_call" | custom-call | flops 1000 | bytes 1000 | tf_op jit(solution)/shard_map/attend_backward/pallas_call | solution.py:223
  340.5 6.6 %input_backward.2 = (f32[896,768]{1,0:T(8,128)}, bf16[896,768]{1,0:T(8,128)(2,1)}, f32[8,384]{1,0:T(8,128)}) custom-call(f32[896,768]{1,0:T(8,128)} %get-tuple-element.214.base_ref, bf16[896,384]{1,0:T(8,128)(2,1)} %get-tuple-element.213.dq_ref.refs_1_, f32[896,768]{1,0:T(8,128)} %get-tuple-element.215.own_ref, ...), custom_call_target="tpu_custom_call" | custom-call | flops 1000 | bytes 1000 | tf_op jit(solution)/shard_map/input_backward/pallas_call | solution.py:783
  347.1 5.9 %weight_grads.14 = bf16[4,4,48,1152]{3,2,1,0:T(8,128)(2,1)} custom-call(s32[1]{0:T(128)} %bitcast.meta, bf16[896,768]{1,0:T(8,128)(2,1)} %bitcast.116, bf16[896,384]{1,0:T(8,128)(2,1)} %get-tuple-element.213.dq_ref.refs_1_, bf16[896,768]{1,0:T(8,128)(2,1)} %get-tuple-element.217.refs_2_.refs_3_, bf16[896,768]{1,0:T(8,128)(2,1)} %get-tuple-element.217.refs_2_.refs_3_), custom_call_target="tpu_custom_call" | custom-call | flops 1000 | bytes 1000 | tf_op jit(solution)/shard_map/weight_grads/pallas_call | solution.py:337
  354.2 6.5 %input_backward.3 = (bf16[896,768]{1,0:T(8,128)(2,1)}, bf16[896,768]{1,0:T(8,128)(2,1)}, f32[8,384]{1,0:T(8,128)}) custom-call(f32[896,768]{1,0:T(8,128)} %get-tuple-element.221.base_ref, bf16[896,384]{1,0:T(8,128)(2,1)} %get-tuple-element.222.dq_ref.refs_1_, f32[896,768]{1,0:T(8,128)} %get-tuple-element.223.own_ref, bf16[896,768]{1,0:T(8,128)(2,1)} %copy-done.12, ...), custom_call_target="tpu_custom_call" | custom-call | flops 1000 | bytes 1000 | tf_op jit(solution)/shard_map/input_backward/pallas_call | solution.py:783
  360.7 3.2 gather_fusion.6
  366.3 13.2 %all-to-all-start.3 = ((bf16[32,32,768]{2,1,0:T(8,128)(2,1)}), bf16[32,32,768]{2,1,0:T(8,128)(2,1)}, u32[]{:S(2)}, u32[]{:S(2)}) async-start(bf16[32,32,768]{2,1,0:T(8,128)(2,1)} %gather_fusion.6), calls=%async_computation.5 | async-start | bytes 3145728 | tf_op jit(solution)/shard_map/all_to_all | solution.py:976
  382.2 6.3 %weight_grads.15 = bf16[4,4,48,1152]{3,2,1,0:T(8,128)(2,1)} custom-call(s32[1]{0:T(128)} %bitcast.meta, bf16[896,768]{1,0:T(8,128)(2,1)} %bitcast.117, bf16[896,384]{1,0:T(8,128)(2,1)} %get-tuple-element.222.dq_ref.refs_1_, bf16[896,768]{1,0:T(8,128)(2,1)} %get-tuple-element.245.refs_2_.refs_3_, bf16[896,768]{1,0:T(8,128)(2,1)} %get-tuple-element.245.refs_2_.refs_3_, ...), custom_call_target="tpu_custom_call" | custom-call | flops 1000 | bytes 1000 | tf_op jit(solution)/shard_map/weight_grads/pallas_call | solution.py:337
  388.6 1.8 gather_fusion.7
  390.4 1.9 collective-permute-start.23
  392.3 1.5 collective-permute-start.24
  394.1 1.9 collective-permute-start.20
  396.0 1.5 collective-permute-start.21
  397.6 1.8 collective-permute-done.25
  399.4 15.5 %collective-permute-done.20 = bf16[4,48,1152]{2,1,0:T(8,128)(2,1)S(1)} collective-permute-done((bf16[4,48,1152]{2,1,0:T(8,128)(2,1)S(1)}, bf16[4,48,1152]{2,1,0:T(8,128)(2,1)S(1)}, u32[]{:S(2)}, u32[]{:S(2)}) %collective-permute-start.20) | collective-permute-done | bytes 442400 | tf_op jit(solution)/shard_map/ppermute | solution.py:805
  414.9 7.2 %collective-permute-done.21 = bf16[4,48,1152]{2,1,0:T(8,128)(2,1)S(1)} collective-permute-done((bf16[4,48,1152]{2,1,0:T(8,128)(2,1)S(1)}, bf16[4,48,1152]{2,1,0:T(8,128)(2,1)S(1)}, u32[]{:S(2)}, u32[]{:S(2)}) %collective-permute-start.21) | collective-permute-done | bytes 442400 | tf_op jit(solution)/shard_map/ppermute | solution.py:805
  422.1 9.9 %collective-permute-done.22 = bf16[4,48,1152]{2,1,0:T(8,128)(2,1)S(1)} collective-permute-done((bf16[4,48,1152]{2,1,0:T(8,128)(2,1)S(1)}, bf16[4,48,1152]{2,1,0:T(8,128)(2,1)S(1)}, u32[]{:S(2)}, u32[]{:S(2)}) %collective-permute-start.22) | collective-permute-done | bytes 442400 | tf_op jit(solution)/shard_map/ppermute | solution.py:805
  433.4 10.3 %reduce-scatter.11.cloned.1.call-done = bf16[48,1920]{1,0:T(8,128)(2,1)} async-done(((bf16[192,1920]{1,0:T(8,128)(2,1)}), bf16[48,1920]{1,0:T(8,128)(2,1)}) %reduce-scatter.11.cloned.1.call-update) | async-done | bytes 184336 | tf_op jit(solution)/shard_map/reduce_scatter | solution.py:882
  446.3 1.4 slice.261
  448.4 1.6 collective-permute-start.30
  450.0 2.7 collective-permute-start.31
  452.8 1.7 collective-permute-start.27
  455.4 3.3 gather_fusion.8
  458.7 2.7 collective-permute-start.28
  (192 shorter events, 40.6 us)
Async XLA Ops:
  7.2 11.6 %copy-start = (bf16[32,32,768]{2,1,0:T(8,128)(2,1)S(1)}, bf16[32,32,768]{2,1,0:T(8,128)(2,1)}, u32[]{:S(2)}) copy-start(bf16[32,32,768]{2,1,0:T(8,128)(2,1)} %param.17) | copy-start | bytes 4718596
  7.2 3.7 copy-start.13
  7.2 9.4 %copy-start.17 = (f32[4,384]{1,0:T(4,128)S(1)}, f32[4,384]{1,0:T(4,128)}, u32[]{:S(2)}) copy-start(f32[4,384]{1,0:T(4,128)} %refs_10_) | copy-start | bytes 18436
  7.2 9.4 %copy-start.18 = (f32[1536]{0:T(1024)S(1)}, f32[1536]{0:T(1024)}, u32[]{:S(2)}) copy-start(f32[1536]{0:T(1024)} %param.30) | copy-start | bytes 18436
  7.2 10.0 %copy-start.20 = (s32[32]{0:T(128)S(1)}, s32[32]{0:T(128)}, u32[]{:S(2)}) copy-start(s32[32]{0:T(128)} %param.20) | copy-start | bytes 388
  7.2 10.5 %copy-start.2 = (s32[32]{0:T(128)S(1)}, s32[32]{0:T(128)}, u32[]{:S(2)}) copy-start(s32[32]{0:T(128)} %param.19) | copy-start | bytes 388
  7.2 141.6 %all-gather.2.cloned.1.call-start = ((), (), s32[]{:S(2)}) async-start(), calls=%async_computation.8 | async-start | bytes 8146944 | tf_op jit(solution)/shard_map/all_gather | solution.py:1000
  10.9 9.7 %collective-permute-start = (bf16[48,1152]{1,0:T(8,128)(2,1)S(1)}, bf16[48,1152]{1,0:T(8,128)(2,1)S(1)}, u32[]{:S(2)}, u32[]{:S(2)}) collective-permute-start(bf16[48,1152]{1,0:T(8,128)(2,1)S(1)} %bitcast.131), channel_id=1, source_target_pairs={{0,8},{2,10},{4,12},{6,14},{8,0},{10,2},{12,4},{14,6},{16,24},{18,... | collective-permute-start | bytes 331784 | tf_op jit(solution)/shard_map/ppermute | solution.py:805
  14.0 11.3 %collective-permute-start.1 = (bf16[48,1152]{1,0:T(8,128)(2,1)S(1)}, bf16[48,1152]{1,0:T(8,128)(2,1)S(1)}, u32[]{:S(2)}, u32[]{:S(2)}) collective-permute-start(bf16[48,1152]{1,0:T(8,128)(2,1)S(1)} %bitcast.132), channel_id=1, source_target_pairs={{0,16},{2,18},{4,20},{6,22},{8,24},{10,26},{12,28},{14,30},{16,0},... | collective-permute-start | bytes 331784 | tf_op jit(solution)/shard_map/ppermute | solution.py:805
  16.6 8.8 %collective-permute-start.2 = (bf16[48,1152]{1,0:T(8,128)(2,1)S(1)}, bf16[48,1152]{1,0:T(8,128)(2,1)S(1)}, u32[]{:S(2)}, u32[]{:S(2)}) collective-permute-start(bf16[48,1152]{1,0:T(8,128)(2,1)S(1)} %bitcast.133), channel_id=1, source_target_pairs={{0,24},{2,26},{4,28},{6,30},{8,16},{10,18},{12,20},{14,22},{16,8},... | collective-permute-start | bytes 331784 | tf_op jit(solution)/shard_map/ppermute | solution.py:805
  16.6 42.5 %collective-permute-start.6 = (f32[3072]{0:T(1024)S(1)}, f32[3072]{0:T(1024)S(1)}, u32[]{:S(2)}, u32[]{:S(2)}) collective-permute-start(f32[3072]{0:T(1024)S(1)} %pad_maximum_fusion.2), channel_id=1, source_target_pairs={{0,1},{1,0},{2,3},{3,2},{4,5},{5,4},{6,7},{7,6},{8,9},{9,8},{10,11... | collective-permute-start | bytes 36872 | tf_op jit(solution)/shard_map/ppermute | solution.py:801
  16.7 43.6 %collective-permute-start.7 = (bf16[2,64,768]{2,1,0:T(8,128)(2,1)}, bf16[2,64,768]{2,1,0:T(8,128)(2,1)}, u32[]{:S(2)}, u32[]{:S(2)}) collective-permute-start(bf16[2,64,768]{2,1,0:T(8,128)(2,1)} %param.18), channel_id=1, source_target_pairs={{0,1},{1,0},{2,3},{3,2},{4,5},{5,4},{6,7},{7,6},{8,9},{9,8},{10,11... | collective-permute-start | bytes 589832 | tf_op jit(solution)/shard_map/ppermute | solution.py:801
  25.4 25.9 %copy-start.11 = (bf16[4,48,1152]{2,1,0:T(8,128)(2,1)}, bf16[4,48,1152]{2,1,0:T(8,128)(2,1)S(1)}, u32[]{:S(2)}) copy-start(bf16[4,48,1152]{2,1,0:T(8,128)(2,1)S(1)} %pad_maximum_fusion.own_ref) | copy-start | bytes 1327108
  25.4 64.5 %all-to-all-start = ((bf16[32,32,768]{2,1,0:T(8,128)(2,1)}), bf16[32,32,768]{2,1,0:T(8,128)(2,1)S(1)}, u32[]{:S(2)}, u32[]{:S(2)}) async-start(bf16[32,32,768]{2,1,0:T(8,128)(2,1)} %gather_fusion.1), calls=%async_computation | async-start | bytes 3145728 | tf_op jit(solution)/shard_map/all_to_all | solution.py:982
  47.9 31.2 %collective-permute-start.3 = (bf16[4,48,1152]{2,1,0:T(8,128)(2,1)S(1)}, bf16[4,48,1152]{2,1,0:T(8,128)(2,1)S(1)}, u32[]{:S(2)}, u32[]{:S(2)}) collective-permute-start(bf16[4,48,1152]{2,1,0:T(8,128)(2,1)S(1)} %pad_maximum_fusion.own_ref), channel_id=1, source_target_pairs={{0,2},{2,0},{4,6},{6,4},{8,10},{10,8},{12,14},{14,12},{16,18},{18,... | collective-permute-start | bytes 1327112 | tf_op jit(solution)/shard_map/ppermute | solution.py:805
  49.8 29.2 %collective-permute-start.4 = (bf16[4,48,1152]{2,1,0:T(8,128)(2,1)S(1)}, bf16[4,48,1152]{2,1,0:T(8,128)(2,1)S(1)}, u32[]{:S(2)}, u32[]{:S(2)}) collective-permute-start(bf16[4,48,1152]{2,1,0:T(8,128)(2,1)S(1)} %pad_maximum_fusion.own_ref), channel_id=1, source_target_pairs={{0,4},{2,6},{4,0},{6,2},{8,12},{10,14},{12,8},{14,10},{16,20},{18,... | collective-permute-start | bytes 1327112 | tf_op jit(solution)/shard_map/ppermute | solution.py:805
  51.3 38.6 %collective-permute-start.5 = (bf16[4,48,1152]{2,1,0:T(8,128)(2,1)S(1)}, bf16[4,48,1152]{2,1,0:T(8,128)(2,1)S(1)}, u32[]{:S(2)}, u32[]{:S(2)}) collective-permute-start(bf16[4,48,1152]{2,1,0:T(8,128)(2,1)S(1)} %pad_maximum_fusion.own_ref), channel_id=1, source_target_pairs={{0,6},{2,4},{4,2},{6,0},{8,14},{10,12},{12,10},{14,8},{16,22},{18,... | collective-permute-start | bytes 1327112 | tf_op jit(solution)/shard_map/ppermute | solution.py:805
  79.1 10.9 %copy-start.14 = (bf16[4,48,1152]{2,1,0:T(8,128)(2,1)}, bf16[4,48,1152]{2,1,0:T(8,128)(2,1)S(1)}, u32[]{:S(2)}) copy-start(bf16[4,48,1152]{2,1,0:T(8,128)(2,1)S(1)} %collective-permute-done.3.first_ref) | copy-start | bytes 1327108
  79.1 10.9 %copy-start.15 = (bf16[4,48,1152]{2,1,0:T(8,128)(2,1)}, bf16[4,48,1152]{2,1,0:T(8,128)(2,1)S(1)}, u32[]{:S(2)}) copy-start(bf16[4,48,1152]{2,1,0:T(8,128)(2,1)S(1)} %collective-permute-done.4.second_ref) | copy-start | bytes 1327108
  89.9 0.8 copy-start.16
  95.1 7.3 %collective-permute-start.8 = (bf16[768,1152]{1,0:T(8,128)(2,1)}, bf16[768,1152]{1,0:T(8,128)(2,1)S(1)}, u32[]{:S(2)}, u32[]{:S(2)}) collective-permute-start(bf16[768,1152]{1,0:T(8,128)(2,1)} %bitcast.106), channel_id=1, source_target_pairs={{0,1},{1,0},{2,3},{3,2},{4,5},{5,4},{6,7},{7,6},{8,9},{9,8},{10,11... | collective-permute-start | bytes 5308424 | tf_op jit(solution)/shard_map/ppermute | solution.py:801
  101.9 6.7 %collective-permute-start.9 = (bf16[896,768]{1,0:T(8,128)(2,1)}, bf16[896,768]{1,0:T(8,128)(2,1)S(1)}, u32[]{:S(2)}, u32[]{:S(2)}) collective-permute-start(bf16[896,768]{1,0:T(8,128)(2,1)} %get-tuple-element.151.refs_0_), channel_id=1, source_target_pairs={{0,1},{1,0},{2,3},{3,2},{4,5},{5,4},{6,7},{7,6},{8,9},{9,8},{10,11... | collective-permute-start | bytes 4128776 | tf_op jit(solution)/shard_map/ppermute | solution.py:801
  102.4 1.2 copy-start.3
  108.6 12.4 %collective-permute-start.10 = (bf16[896,768]{1,0:T(8,128)(2,1)}, bf16[896,768]{1,0:T(8,128)(2,1)S(1)}, u32[]{:S(2)}, u32[]{:S(2)}) collective-permute-start(bf16[896,768]{1,0:T(8,128)(2,1)} %get-tuple-element.149.refs_0_), channel_id=1, source_target_pairs={{0,1},{1,0},{2,3},{3,2},{4,5},{5,4},{6,7},{7,6},{8,9},{9,8},{10,11... | collective-permute-start | bytes 4128776 | tf_op jit(solution)/shard_map/ppermute | solution.py:801
  108.6 1.1 copy-start.5
  121.0 1.1 copy-start.6
  148.9 12.5 %collective-permute-start.11 = (bf16[768,4992]{1,0:T(8,128)(2,1)}, bf16[768,4992]{1,0:T(8,128)(2,1)}, u32[]{:S(2)}, u32[]{:S(2)}) collective-permute-start(bf16[768,4992]{1,0:T(8,128)(2,1)} %all-gather.2.cloned.1.call-done.refs_0_.refs_2_.refs_4_.refs_6_.refs_8_.expand.reduce.in0.out0.refs_10_.wk0.wv0), channel_id=1, source_target_pairs={{0,1},{1,0},{2,3},{3,2},{4,5},{5,4},{6,7},{7,6},{8,9},{9,8},{10,11... | collective-permute-start | bytes 23003144 | tf_op jit(solution)/shard_map/ppermute | solution.py:801
  148.9 53.5 %all-to-all-start.1 = ((bf16[32,32,768]{2,1,0:T(8,128)(2,1)}), bf16[32,32,768]{2,1,0:T(8,128)(2,1)S(1)}, u32[]{:S(2)}, u32[]{:S(2)}) async-start(bf16[32,32,768]{2,1,0:T(8,128)(2,1)} %gather_fusion), calls=%async_computation.1 | async-start | bytes 3145728 | tf_op jit(solution)/shard_map/all_to_all | solution.py:982
  152.7 171.1 %reduce-scatter.5.cloned.1.call-start = ((), (), s32[]{:S(2)}) async-start(), calls=%async_computation.9 | async-start | bytes 5898240 | tf_op jit(solution)/shard_map/reduce_scatter | solution.py:882
  228.3 6.2 %collective-permute-start.13 = (bf16[4,4,48,1536]{3,2,1,0:T(8,128)(2,1)}, bf16[4,4,48,1536]{3,2,1,0:T(8,128)(2,1)}, u32[]{:S(2)}, u32[]{:S(2)}) collective-permute-start(bf16[4,4,48,1536]{3,2,1,0:T(8,128)(2,1)} %weight_grads.9), channel_id=1, source_target_pairs={{0,1},{1,0},{2,3},{3,2},{4,5},{5,4},{6,7},{7,6},{8,9},{9,8},{10,11... | collective-permute-start | bytes 7077896 | tf_op jit(solution)/shard_map/ppermute | solution.py:801
  234.2 6.5 %collective-permute-start.12 = (bf16[4,4,48,1536]{3,2,1,0:T(8,128)(2,1)}, bf16[4,4,48,1536]{3,2,1,0:T(8,128)(2,1)}, u32[]{:S(2)}, u32[]{:S(2)}) collective-permute-start(bf16[4,4,48,1536]{3,2,1,0:T(8,128)(2,1)} %weight_grads.8), channel_id=1, source_target_pairs={{0,1},{1,0},{2,3},{3,2},{4,5},{5,4},{6,7},{7,6},{8,9},{9,8},{10,11... | collective-permute-start | bytes 7077896 | tf_op jit(solution)/shard_map/ppermute | solution.py:801
  246.8 1.3 copy-start.7
  249.9 38.5 %all-to-all-start.2 = ((bf16[32,32,768]{2,1,0:T(8,128)(2,1)}), bf16[32,32,768]{2,1,0:T(8,128)(2,1)S(1)}, u32[]{:S(2)}, u32[]{:S(2)}) async-start(bf16[32,32,768]{2,1,0:T(8,128)(2,1)} %gather_fusion.5), calls=%async_computation.2 | async-start | bytes 3145728 | tf_op jit(solution)/shard_map/all_to_all | solution.py:976
  254.5 127.7 %reduce-scatter.7.cloned.1.call-start = ((), (), s32[]{:S(2)}) async-start(), calls=%async_computation.10 | async-start | bytes 3686400 | tf_op jit(solution)/shard_map/reduce_scatter | solution.py:882
  288.1 9.2 %collective-permute-start.15 = (bf16[4,4,48,1152]{3,2,1,0:T(8,128)(2,1)}, bf16[4,4,48,1152]{3,2,1,0:T(8,128)(2,1)S(1)}, u32[]{:S(2)}, u32[]{:S(2)}) collective-permute-start(bf16[4,4,48,1152]{3,2,1,0:T(8,128)(2,1)} %weight_grads.12), channel_id=1, source_target_pairs={{0,1},{1,0},{2,3},{3,2},{4,5},{5,4},{6,7},{7,6},{8,9},{9,8},{10,11... | collective-permute-start | bytes 5308424 | tf_op jit(solution)/shard_map/ppermute | solution.py:801
  288.4 4.8 %collective-permute-start.14 = (bf16[256,1536]{1,0:T(8,128)(2,1)}, bf16[256,1536]{1,0:T(8,128)(2,1)}, u32[]{:S(2)}, u32[]{:S(2)}) collective-permute-start(bf16[256,1536]{1,0:T(8,128)(2,1)} %get-tuple-element.200), channel_id=1, source_target_pairs={{0,1},{1,0},{2,3},{3,2},{4,5},{5,4},{6,7},{7,6},{8,9},{9,8},{10,11... | collective-permute-start | bytes 2359304 | tf_op jit(solution)/shard_map/ppermute | solution.py:801
  297.2 1.2 copy-start.9
  307.3 124.9 %reduce-scatter.9.cloned.1.call-start = ((), (), s32[]{:S(2)}) async-start(), calls=%async_computation.11 | async-start | bytes 1474560 | tf_op jit(solution)/shard_map/reduce_scatter | solution.py:882
  323.6 16.8 %collective-permute-start.16 = (bf16[896,768]{1,0:T(8,128)(2,1)}, bf16[896,768]{1,0:T(8,128)(2,1)}, u32[]{:S(2)}, u32[]{:S(2)}) collective-permute-start(bf16[896,768]{1,0:T(8,128)(2,1)} %get-tuple-element.216), channel_id=1, source_target_pairs={{0,1},{1,0},{2,3},{3,2},{4,5},{5,4},{6,7},{7,6},{8,9},{9,8},{10,11... | collective-permute-start | bytes 4128776 | tf_op jit(solution)/shard_map/ppermute | solution.py:801
  340.1 12.8 %collective-permute-start.17 = (bf16[896,768]{1,0:T(8,128)(2,1)}, bf16[896,768]{1,0:T(8,128)(2,1)S(1)}, u32[]{:S(2)}, u32[]{:S(2)}) collective-permute-start(bf16[896,768]{1,0:T(8,128)(2,1)} %get-tuple-element.219), channel_id=1, source_target_pairs={{0,1},{1,0},{2,3},{3,2},{4,5},{5,4},{6,7},{7,6},{8,9},{9,8},{10,11... | collective-permute-start | bytes 4128776 | tf_op jit(solution)/shard_map/ppermute | solution.py:801
  352.9 1.1 copy-start.12
  354.0 9.9 %collective-permute-start.18 = (bf16[4,4,48,1152]{3,2,1,0:T(8,128)(2,1)}, bf16[4,4,48,1152]{3,2,1,0:T(8,128)(2,1)S(1)}, u32[]{:S(2)}, u32[]{:S(2)}) collective-permute-start(bf16[4,4,48,1152]{3,2,1,0:T(8,128)(2,1)} %weight_grads.14), channel_id=1, source_target_pairs={{0,1},{1,0},{2,3},{3,2},{4,5},{5,4},{6,7},{7,6},{8,9},{9,8},{10,11... | collective-permute-start | bytes 5308424 | tf_op jit(solution)/shard_map/ppermute | solution.py:801
  360.7 4.1 copy-start.19
  363.9 2.4 copy-start.8
  366.3 82.0 %all-to-all-start.3 = ((bf16[32,32,768]{2,1,0:T(8,128)(2,1)}), bf16[32,32,768]{2,1,0:T(8,128)(2,1)}, u32[]{:S(2)}, u32[]{:S(2)}) async-start(bf16[32,32,768]{2,1,0:T(8,128)(2,1)} %gather_fusion.6), calls=%async_computation.5 | async-start | bytes 3145728 | tf_op jit(solution)/shard_map/all_to_all | solution.py:976
  379.5 64.1 %reduce-scatter.11.cloned.1.call-start = ((), (), s32[]{:S(2)}) async-start(), calls=%async_computation.12 | async-start | bytes 921600 | tf_op jit(solution)/shard_map/reduce_scatter | solution.py:882
  382.1 8.3 %collective-permute-start.19 = (f32[13056]{0:T(1024)S(1)}, f32[13056]{0:T(1024)S(1)}, u32[]{:S(2)}, u32[]{:S(2)}) collective-permute-start(f32[13056]{0:T(1024)S(1)} %constant_dynamic-update-slice_fusion), channel_id=1, source_target_pairs={{0,1},{1,0},{2,3},{3,2},{4,5},{5,4},{6,7},{7,6},{8,9},{9,8},{10,11... | collective-permute-start | bytes 156680 | tf_op jit(solution)/shard_map/ppermute | solution.py:801
  388.6 5.4 %copy-start.4 = (bf16[4,4,48,1152]{3,2,1,0:T(8,128)(2,1)S(1)}, bf16[4,4,48,1152]{3,2,1,0:T(8,128)(2,1)}, u32[]{:S(2)}) copy-start(bf16[4,4,48,1152]{3,2,1,0:T(8,128)(2,1)} %weight_grads.15) | copy-start | bytes 5308420
  390.4 7.1 %collective-permute-start.23 = (f32[13056]{0:T(1024)S(1)}, f32[13056]{0:T(1024)S(1)}, u32[]{:S(2)}, u32[]{:S(2)}) collective-permute-start(f32[13056]{0:T(1024)S(1)} %add.264), channel_id=1, source_target_pairs={{0,2},{2,0},{4,6},{6,4},{8,10},{10,8},{12,14},{14,12},{16,18},{18,... | collective-permute-start | bytes 156680 | tf_op jit(solution)/shard_map/ppermute | solution.py:805
  392.3 5.3 %collective-permute-start.24 = (f32[13056]{0:T(1024)S(1)}, f32[13056]{0:T(1024)S(1)}, u32[]{:S(2)}, u32[]{:S(2)}) collective-permute-start(f32[13056]{0:T(1024)S(1)} %add.264), channel_id=1, source_target_pairs={{0,4},{2,6},{4,0},{6,2},{8,12},{10,14},{12,8},{14,10},{16,20},{18,... | collective-permute-start | bytes 156680 | tf_op jit(solution)/shard_map/ppermute | solution.py:805
  393.8 5.6 %collective-permute-start.25 = (f32[13056]{0:T(1024)S(1)}, f32[13056]{0:T(1024)S(1)}, u32[]{:S(2)}, u32[]{:S(2)}) collective-permute-start(f32[13056]{0:T(1024)S(1)} %add.264), channel_id=1, source_target_pairs={{0,6},{2,4},{4,2},{6,0},{8,14},{10,12},{12,10},{14,8},{16,22},{18,... | collective-permute-start | bytes 156680 | tf_op jit(solution)/shard_map/ppermute | solution.py:805
  394.1 20.9 %collective-permute-start.20 = (bf16[4,48,1152]{2,1,0:T(8,128)(2,1)S(1)}, bf16[4,48,1152]{2,1,0:T(8,128)(2,1)S(1)}, u32[]{:S(2)}, u32[]{:S(2)}) collective-permute-start(bf16[4,48,1152]{2,1,0:T(8,128)(2,1)S(1)} %get-tuple-element.306), channel_id=1, source_target_pairs={{0,2},{2,0},{4,6},{6,4},{8,10},{10,8},{12,14},{14,12},{16,18},{18,... | collective-permute-start | bytes 1327112 | tf_op jit(solution)/shard_map/ppermute | solution.py:805
  396.0 26.1 %collective-permute-start.21 = (bf16[4,48,1152]{2,1,0:T(8,128)(2,1)S(1)}, bf16[4,48,1152]{2,1,0:T(8,128)(2,1)S(1)}, u32[]{:S(2)}, u32[]{:S(2)}) collective-permute-start(bf16[4,48,1152]{2,1,0:T(8,128)(2,1)S(1)} %get-tuple-element.308), channel_id=1, source_target_pairs={{0,4},{2,6},{4,0},{6,2},{8,12},{10,14},{12,8},{14,10},{16,20},{18,... | collective-permute-start | bytes 1327112 | tf_op jit(solution)/shard_map/ppermute | solution.py:805
  397.5 34.5 %collective-permute-start.22 = (bf16[4,48,1152]{2,1,0:T(8,128)(2,1)S(1)}, bf16[4,48,1152]{2,1,0:T(8,128)(2,1)S(1)}, u32[]{:S(2)}, u32[]{:S(2)}) collective-permute-start(bf16[4,48,1152]{2,1,0:T(8,128)(2,1)S(1)} %get-tuple-element.307), channel_id=1, source_target_pairs={{0,6},{2,4},{4,2},{6,0},{8,14},{10,12},{12,10},{14,8},{16,22},{18,... | collective-permute-start | bytes 1327112 | tf_op jit(solution)/shard_map/ppermute | solution.py:805
  432.2 20.5 %copy-start.10 = (bf16[4,48,1152]{2,1,0:T(8,128)(2,1)}, bf16[4,48,1152]{2,1,0:T(8,128)(2,1)S(1)}, u32[]{:S(2)}) copy-start(bf16[4,48,1152]{2,1,0:T(8,128)(2,1)S(1)} %fusion.2) | copy-start | bytes 1327108
  448.3 10.3 %collective-permute-start.29 = (f32[13056]{0:T(1024)S(1)}, f32[13056]{0:T(1024)S(1)}, u32[]{:S(2)}, u32[]{:S(2)}) collective-permute-start(f32[13056]{0:T(1024)S(1)} %add_add_fusion.1), channel_id=1, source_target_pairs={{0,8},{2,10},{4,12},{6,14},{8,0},{10,2},{12,4},{14,6},{16,24},{18,... | collective-permute-start | bytes 156680 | tf_op jit(solution)/shard_map/ppermute | solution.py:805
  448.4 13.0 %collective-permute-start.30 = (f32[13056]{0:T(1024)S(1)}, f32[13056]{0:T(1024)S(1)}, u32[]{:S(2)}, u32[]{:S(2)}) collective-permute-start(f32[13056]{0:T(1024)S(1)} %add_add_fusion.1), channel_id=1, source_target_pairs={{0,16},{2,18},{4,20},{6,22},{8,24},{10,26},{12,28},{14,30},{16,0},... | collective-permute-start | bytes 156680 | tf_op jit(solution)/shard_map/ppermute | solution.py:805
  450.0 11.4 %collective-permute-start.31 = (f32[13056]{0:T(1024)S(1)}, f32[13056]{0:T(1024)S(1)}, u32[]{:S(2)}, u32[]{:S(2)}) collective-permute-start(f32[13056]{0:T(1024)S(1)} %add_add_fusion.1), channel_id=1, source_target_pairs={{0,24},{2,26},{4,28},{6,30},{8,16},{10,18},{12,20},{14,22},{16,8},... | collective-permute-start | bytes 156680 | tf_op jit(solution)/shard_map/ppermute | solution.py:805
  452.8 11.8 %collective-permute-start.26 = (bf16[48,1152]{1,0:T(8,128)(2,1)S(1)}, bf16[48,1152]{1,0:T(8,128)(2,1)S(1)}, u32[]{:S(2)}, u32[]{:S(2)}) collective-permute-start(bf16[48,1152]{1,0:T(8,128)(2,1)S(1)} %get-tuple-element.311), channel_id=1, source_target_pairs={{0,8},{2,10},{4,12},{6,14},{8,0},{10,2},{12,4},{14,6},{16,24},{18,... | collective-permute-start | bytes 331784 | tf_op jit(solution)/shard_map/ppermute | solution.py:805
  452.8 11.7 %collective-permute-start.27 = (bf16[48,1152]{1,0:T(8,128)(2,1)S(1)}, bf16[48,1152]{1,0:T(8,128)(2,1)S(1)}, u32[]{:S(2)}, u32[]{:S(2)}) collective-permute-start(bf16[48,1152]{1,0:T(8,128)(2,1)S(1)} %get-tuple-element.313), channel_id=1, source_target_pairs={{0,16},{2,18},{4,20},{6,22},{8,24},{10,26},{12,28},{14,30},{16,0},... | collective-permute-start | bytes 331784 | tf_op jit(solution)/shard_map/ppermute | solution.py:805
  455.4 11.6 %copy-start.1 = (bf16[32,32,768]{2,1,0:T(8,128)(2,1)S(1)}, bf16[32,32,768]{2,1,0:T(8,128)(2,1)}, u32[]{:S(2)}) copy-start(bf16[32,32,768]{2,1,0:T(8,128)(2,1)} %param.17) | copy-start | bytes 4718596
  458.7 6.7 %collective-permute-start.28 = (bf16[48,1152]{1,0:T(8,128)(2,1)S(1)}, bf16[48,1152]{1,0:T(8,128)(2,1)S(1)}, u32[]{:S(2)}, u32[]{:S(2)}) collective-permute-start(bf16[48,1152]{1,0:T(8,128)(2,1)S(1)} %get-tuple-element.312), channel_id=1, source_target_pairs={{0,24},{2,26},{4,28},{6,30},{8,16},{10,18},{12,20},{14,22},{16,8},... | collective-permute-start | bytes 331784 | tf_op jit(solution)/shard_map/ppermute | solution.py:805
Sparse Core Ops, SparseCore 0:
  11.0 137.8 all-gather.1
  247.0 72.9 reduce-scatter.4
  323.0 42.2 reduce-scatter.6
  367.5 41.6 reduce-scatter.8
  411.3 32.3 reduce-scatter.10

commit v7 on v6

--- a/solution.py
+++ b/solution.py
@@ -1133,8 +1133,7 @@
     output = rows_at(output_back, inverse)
     far_grads, mid_line = tie(far_grads, mid_line)
     ffn_shard = wide_scatter(ffn_line, PLANE_GROUPS) if quick else ffn_line
-    mid_shard = wide_scatter(mid_line, PLANE_GROUPS) if quick else mid_line
-    ffn_shard, mid_shard = ffn_shard.astype(F32), mid_shard.astype(F32)
+    ffn_shard = ffn_shard.astype(F32)
     qkv_grads = weight_grads(
         low_meta,
         [inputs],
@@ -1186,11 +1185,17 @@
         small, qkv_grads = tie(small, qkv_grads)
         qkv_line = scatter_low(qkv_grads)
         small = sum_low(small)
-        qkv_line, grad_back, ffn_shard, small = tie(qkv_line, grad_back, ffn_shard, small)
-        qkv_shard = scatter_plane(qkv_line)
+        qkv_line, grad_back, ffn_shard, small, mid_line = tie(
+            qkv_line, grad_back, ffn_shard, small, mid_line
+        )
+        shards = scatter_plane(
+            jnp.concatenate([qkv_line, mid_line.reshape(4, shard, 5 * half)], 2)
+        )
+        qkv_shard, mid_shard = shards[:, : 3 * half], shards[:, 3 * half :]
         small = sum_planes(small)
     else:
         qkv_shard = wide_scatter(qkv_grads).astype(F32)
+        mid_shard = mid_line.astype(F32)
         small = lax.psum(small, ("dp", "tensor"))
     grad_tokens = rows_at(grad_back, inverse)
     in_end = 8 * half

time: 479 us -> 480 us (level)
  starting transfers between devices: 61.3 us -> 68.8 us
  Pallas kernels: 226 us -> 220 us
    reduce_scatter x4 -> x3, waiting for transfers between devices: 10.3 us -> 0.04 us  [wide_scatter(): lax.psum_scatter(value, 'dp', scatter_dimension=0, tiled=True, axis_index...]
    ppermute x18, waiting for transfers between devices: 67.7 us -> 75.8 us  [hop(): return lax.ppermute(value, 'dp', [(i, i ^ bits) for i in range(16)])]
    all_to_all x2, starting transfers between devices: 17.8 us -> 23 us  [go_home(): lax.all_to_all(outgoing, 'dp', split_axis=0, concat_axis=0, tiled=True)]
    unnamed x55 -> x61, local copies, waits for them, and re-layouts: 10.4 us -> 10.4 us
  transfers between devices with their start and end apart: 41 -> 40, of which waited for: 13 -> 13; matrix products, arithmetic and copies ran while one was open for 10% -> 10% of each run, Pallas kernels for 41% -> 40%
where the time goes in v7:
time: 480 us; the launch traced here: 472 us
  Pallas kernels  220 us (46%)
  waiting for transfers between devices  107 us (22%)
  starting transfers between devices  68.8 us (14%)
  local copies, waits for them, and re-layouts  46.2 us (10%)
  between operations  16.8 us (4%)
  other arithmetic  14.2 us (3%)
    ppermute x18, waiting for transfers between devices, hop(): return lax.ppermute(value, 'dp', [(i, i ^ bits) for i in range(16)])  75.8 us
    pallas_call x8, Pallas kernels, weight_grads(): pl.pallas_call(functools.partial(grads_kernel, sides, counts, factors, ex...  51.6 us
    pallas_call x2, Pallas kernels, attend_backward(): pl.pallas_call(functools.partial(backward_kernel, piece, spans), grid_spe...  29.7 us
    ppermute x18, starting transfers between devices, hop(): return lax.ppermute(value, 'dp', [(i, i ^ bits) for i in range(16)])  27.7 us
    pallas_call x1, Pallas kernels, mid_backward(): pl.pallas_call(functools.partial(mid_backward_kernel, score_scale, rows),...  25.2 us
    all_to_all x2, starting transfers between devices, go_home(): lax.all_to_all(outgoing, 'dp', split_axis=0, concat_axis=0, tiled=True)  23 us
    pallas_call x2, Pallas kernels, attend_forward(): pl.pallas_call(functools.partial(forward_kernel, piece, spans), grid_spec...  21.2 us
    pallas_call x1, Pallas kernels, mid_forward(): pl.pallas_call(functools.partial(mid_forward_kernel, score_scale), grid_s...  21 us
  transfers between devices with their start and end apart: 40, of which 13 were waited for; matrix products, arithmetic and copies ran while one was open for 10% of the time, Pallas kernels for 40%

profile of v7, /device:TPU:0, one launch (start us, length us, event | category | flops | bytes accessed | tf_op | source)
XLA Modules:
  0.0 472.2 jit_solution(17268647873551098555)
XLA Ops:
  7.3 1.6 copy.65
  8.9 1.9 pack_shards.1
  10.9 3.1 collective-permute-start
  14.0 2.6 collective-permute-start.1
  18.8 1.8 gather_fusion.1
  20.6 4.8 %collective-permute-done.1 = bf16[48,1152]{1,0:T(8,128)(2,1)S(1)} collective-permute-done((bf16[48,1152]{1,0:T(8,128)(2,1)S(1)}, bf16[48,1152]{1,0:T(8,128)(2,1)S(1)}, u32[]{:S(2)}, u32[]{:S(2)}) %collective-permute-start.1) | collective-permute-done | bytes 110624 | tf_op jit(solution)/shard_map/ppermute | solution.py:805
  25.4 11.6 %all-to-all-start = ((bf16[32,32,768]{2,1,0:T(8,128)(2,1)}), bf16[32,32,768]{2,1,0:T(8,128)(2,1)S(1)}, u32[]{:S(2)}, u32[]{:S(2)}) async-start(bf16[32,32,768]{2,1,0:T(8,128)(2,1)} %gather_fusion.1), calls=%async_computation | async-start | bytes 3145728 | tf_op jit(solution)/shard_map/all_to_all | solution.py:982
  38.9 1.9 compare_select_fusion.5
  45.3 1.3 slice_add_fusion.shift
  47.9 1.9 collective-permute-start.3
  49.8 1.5 collective-permute-start.4
  53.4 3.2 gather_fusion
  60.3 1.8 pad_maximum_fusion.1
  62.1 16.9 %collective-permute-done.3.first_ref = bf16[4,48,1152]{2,1,0:T(8,128)(2,1)S(1)} collective-permute-done((bf16[4,48,1152]{2,1,0:T(8,128)(2,1)S(1)}, bf16[4,48,1152]{2,1,0:T(8,128)(2,1)S(1)}, u32[]{:S(2)}, u32[]{:S(2)}) %collective-permute-start.3) | collective-permute-done | bytes 442400 | tf_op jit(solution)/shard_map/ppermute | solution.py:805
  79.1 10.9 %collective-permute-done.5.third_ref = bf16[4,48,1152]{2,1,0:T(8,128)(2,1)S(1)} collective-permute-done((bf16[4,48,1152]{2,1,0:T(8,128)(2,1)S(1)}, bf16[4,48,1152]{2,1,0:T(8,128)(2,1)S(1)}, u32[]{:S(2)}, u32[]{:S(2)}) %collective-permute-start.5) | collective-permute-done | bytes 442400 | tf_op jit(solution)/shard_map/ppermute | solution.py:805
  90.7 4.4 assemble.1
  95.1 1.7 gather_fusion.3
  96.9 5.0 %project.3 = (bf16[896,384]{1,0:T(8,128)(2,1)}, bf16[896,768]{1,0:T(8,128)(2,1)}) custom-call(bf16[896,768]{1,0:T(8,128)(2,1)} %bitcast.116, bf16[768,1152]{1,0:T(8,128)(2,1)} %bitcast.110, bf16[768,1152]{1,0:T(8,128)(2,1)} %bitcast.111, bf16[768,1152]{1,0:T(8,128)(2,1)} %bitcast.112, f32[4,384]{1,0:T(4,128)} %refs_10_), custom_call_target="tpu_custom_call" | custom-call | flops 1000 | bytes 1000 | tf_op jit(solution)/shard_map/project/pallas_call | solution.py:254
  103.6 5.0 %project.2 = (bf16[896,384]{1,0:T(8,128)(2,1)}, bf16[896,768]{1,0:T(8,128)(2,1)}) custom-call(bf16[896,768]{1,0:T(8,128)(2,1)} %bitcast.117, bf16[768,1152]{1,0:T(8,128)(2,1)} %copy-done.3, bf16[768,1152]{1,0:T(8,128)(2,1)} %copy-done.3, bf16[768,1152]{1,0:T(8,128)(2,1)} %copy-done.3, f32[4,384]{1,0:T(4,128)} %slice.209.bias.refs_11_), custom_call_target="tpu_custom_call" | custom-call | flops 1000 | bytes 1000 | tf_op jit(solution)/shard_map/project/pallas_call | solution.py:254
  109.7 10.6 %attend_forward.2 = (bf16[896,384]{1,0:T(8,128)(2,1)}, f32[7,8,256]{2,1,0:T(8,128)}) custom-call(s32[3]{0:T(128)} %pad_add_fusion.meta, bf16[896,384]{1,0:T(8,128)(2,1)} %get-tuple-element.148.q_ref, bf16[896,768]{1,0:T(8,128)(2,1)} %get-tuple-element.150.refs_0_, bf16[896,768]{1,0:T(8,128)(2,1)} %copy-done.5), custom_call_target="tpu_custom_call" | custom-call | flops 1000 | bytes 1000 | tf_op jit(solution)/shard_map/attend_forward/pallas_call | solution.py:206
  121.4 10.6 %attend_forward.3 = (bf16[896,384]{1,0:T(8,128)(2,1)}, f32[7,8,256]{2,1,0:T(8,128)}) custom-call(s32[3]{0:T(128)} %pad_add_fusion.meta, bf16[896,384]{1,0:T(8,128)(2,1)} %get-tuple-element.155.q_ref, bf16[896,768]{1,0:T(8,128)(2,1)} %get-tuple-element.152.refs_0_, bf16[896,768]{1,0:T(8,128)(2,1)} %copy-done.6), custom_call_target="tpu_custom_call" | custom-call | flops 1000 | bytes 1000 | tf_op jit(solution)/shard_map/attend_forward/pallas_call | solution.py:206
  132.0 16.9 %all-gather.2.cloned.1.call-done.refs_0_.refs_2_.refs_4_.refs_6_.refs_8_.expand.reduce.in0.out0.refs_10_.wk0.wv0 = bf16[768,4992]{1,0:T(8,128)(2,1)} async-done(((bf16[48,4992]{1,0:T(8,128)(2,1)}), bf16[768,4992]{1,0:T(8,128)(2,1)}) %all-gather.2.cloned.1.call-update) | async-done | bytes 7667728 | tf_op jit(solution)/shard_map/all_gather | solution.py:1000
  149.0 3.8 all-to-all-start.1
  153.0 8.5 %collective-permute-done.11.refs_1_.refs_3_.refs_5_.refs_7_.refs_9_.expand.reduce.in1.out1.refs_11_.wk1.wv1 = bf16[768,4992]{1,0:T(8,128)(2,1)} collective-permute-done((bf16[768,4992]{1,0:T(8,128)(2,1)}, bf16[768,4992]{1,0:T(8,128)(2,1)}, u32[]{:S(2)}, u32[]{:S(2)}) %collective-permute-start.11) | collective-permute-done | bytes 7667744 | tf_op jit(solution)/shard_map/ppermute | solution.py:801
  161.5 21.0 %mid_forward.1 = (f32[896,768]{1,0:T(8,128)}, f32[896,1]{1,0:T(8,128)}, f32[896,768]{1,0:T(8,128)}, f32[896,1]{1,0:T(8,128)}, bf16[896,768]{1,0:T(8,128)(2,1)}, ...) custom-call(s32[3]{0:T(128)} %pad_add_fusion.meta, ...), custom_call_target="tpu_custom_call" | custom-call | flops 1000 | bytes 1000 | tf_op jit(solution)/shard_map/mid_forward/pallas_call | solution.py:682
  182.5 9.6 %ffn_forward.2 = (bf16[896,1536]{1,0:T(8,128)(2,1)}, bf16[896,1536]{1,0:T(8,128)(2,1)}, f32[896,768]{1,0:T(8,128)}) custom-call(bf16[896,768]{1,0:T(8,128)(2,1)} %get-tuple-element.162.hidden_ref.refs_0_, f32[896,768]{1,0:T(8,128)} %get-tuple-element.163.base_ref.unit2_ref, ...), custom_call_target="tpu_custom_call" | custom-call | flops 1000 | bytes 1000 | tf_op jit(solution)/shard_map/ffn_forward/pallas_call | solution.py:594
  192.1 9.6 %ffn_forward.3 = (bf16[896,1536]{1,0:T(8,128)(2,1)}, bf16[896,1536]{1,0:T(8,128)(2,1)}, f32[896,768]{1,0:T(8,128)}) custom-call(bf16[896,768]{1,0:T(8,128)(2,1)} %get-tuple-element.162.hidden_ref.refs_0_, f32[896,768]{1,0:T(8,128)} %get-tuple-element.167.base_ref, ...), custom_call_target="tpu_custom_call" | custom-call | flops 1000 | bytes 1000 | tf_op jit(solution)/shard_map/ffn_forward/pallas_call | solution.py:594
  201.6 1.7 gather_fusion.4
  203.4 18.5 %ffn_backward.1 = (bf16[896,768]{1,0:T(8,128)(2,1)}, bf16[896,768]{1,0:T(8,128)(2,1)}, f32[896,768]{1,0:T(8,128)}, f32[8,768]{1,0:T(8,128)}, bf16[896,1536]{1,0:...) custom-call(f32[896,768]{1,0:T(8,128)} %get-tuple-element.170.h3_ref, ...), custom_call_target="tpu_custom_call" | custom-call | flops 1000 | bytes 1000 | tf_op jit(solution)/shard_map/ffn_backward/pallas_call | solution.py:646
  221.9 5.7 %weight_grads.9 = bf16[4,4,48,1536]{3,2,1,0:T(8,128)(2,1)} custom-call(s32[1]{0:T(128)} %bitcast.meta, bf16[896,768]{1,0:T(8,128)(2,1)} %get-tuple-element.162.hidden_ref.refs_0_, bf16[896,1536]{1,0:T(8,128)(2,1)} %get-tuple-element.179.refs_1_), custom_call_target="tpu_custom_call" | custom-call | flops 1000 | bytes 1000 | tf_op jit(solution)/shard_map/weight_grads/pallas_call | solution.py:337
  227.7 5.7 %weight_grads.8 = bf16[4,4,48,1536]{3,2,1,0:T(8,128)(2,1)} custom-call(s32[1]{0:T(128)} %bitcast.meta, bf16[896,768]{1,0:T(8,128)(2,1)} %get-tuple-element.175.refs_0_, bf16[896,1536]{1,0:T(8,128)(2,1)} %get-tuple-element.177.refs_1_), custom_call_target="tpu_custom_call" | custom-call | flops 1000 | bytes 1000 | tf_op jit(solution)/shard_map/weight_grads/pallas_call | solution.py:337
  233.8 6.1 %weight_grads.10.refs_3_ = bf16[4,4,48,3072]{3,2,1,0:T(8,128)(2,1)} custom-call(s32[1]{0:T(128)} %bitcast.meta, bf16[896,768]{1,0:T(8,128)(2,1)} %get-tuple-element.162.hidden_ref.refs_0_, bf16[896,1536]{1,0:T(8,128)(2,1)} %get-tuple-element.178.refs_1_, bf16[4,4,48,1536]{3,2,1,0:T(8,128)(2,1)} %collective-permute-done.13.refs_2_), custom_call_target="tpu_custom_call" | custom-call | flops 1000 | bytes 1000 | tf_op jit(solution)/shard_map/weight_grads/pallas_call | solution.py:337
  239.9 6.2 %weight_grads.11 = bf16[4,4,48,3072]{3,2,1,0:T(8,128)(2,1)} custom-call(s32[1]{0:T(128)} %bitcast.meta, bf16[896,768]{1,0:T(8,128)(2,1)} %get-tuple-element.175.refs_0_, bf16[896,1536]{1,0:T(8,128)(2,1)} %get-tuple-element.176.refs_1_, bf16[4,4,48,1536]{3,2,1,0:T(8,128)(2,1)} %collective-permute-done.12.refs_2_, ...), custom_call_target="tpu_custom_call", output_to_operand_aliasing={{}: (4, {})} | custom-call | flops 1000 | bytes 1000 | tf_op jit(solution)/shard_map/weight_grads/pallas_call | solution.py:337
  247.4 1.8 gather_fusion.5
  249.2 5.4 %all-to-all-start.2 = ((bf16[32,32,768]{2,1,0:T(8,128)(2,1)}), bf16[32,32,768]{2,1,0:T(8,128)(2,1)S(1)}, u32[]{:S(2)}, u32[]{:S(2)}) async-start(bf16[32,32,768]{2,1,0:T(8,128)(2,1)} %gather_fusion.5), calls=%async_computation.2 | async-start | bytes 3145728 | tf_op jit(solution)/shard_map/all_to_all | solution.py:976
  254.6 25.2 %mid_backward.1 = (bf16[896,768]{1,0:T(8,128)(2,1)}, f32[896,768]{1,0:T(8,128)}, bf16[896,768]{1,0:T(8,128)(2,1)}, f32[8,768]{1,0:T(8,128)}, bf16[896,384]{1,0:T...) custom-call(s32[3]{0:T(128)} %pad_add_fusion.meta, ...), custom_call_target="tpu_custom_call" | custom-call | flops 1000 | bytes 1000 | tf_op jit(solution)/shard_map/mid_backward/pallas_call | solution.py:723
  279.8 7.0 %weight_grads.12 = bf16[4,4,48,1152]{3,2,1,0:T(8,128)(2,1)} custom-call(s32[1]{0:T(128)} %bitcast.meta, bf16[896,768]{1,0:T(8,128)(2,1)} %get-tuple-element.192.refs_0_, bf16[896,768]{1,0:T(8,128)(2,1)} %get-tuple-element.193.refs_1_, bf16[896,768]{1,0:T(8,128)(2,1)} %get-tuple-element.194.refs_2_, bf16[896,384]{1,0:T(8,128)(2,1)} %get-tuple-element.159.attn1.refs_3_, ...), custom_call_target="tpu_custom_call" | custom-call | flops 1000 | bytes 1000 | tf_op jit(solution)/shard_map/weight_grads/pallas_call | solution.py:337
  286.8 1.7 all-to-all-done.2
  288.5 3.5 collective-permute-done.14.got_ref
  291.9 4.0 memory_backward.1
  297.1 8.8 %weight_grads.13 = bf16[4,4,48,1920]{3,2,1,0:T(8,128)(2,1)} custom-call(s32[1]{0:T(128)} %bitcast.meta, bf16[896,768]{1,0:T(8,128)(2,1)} %get-tuple-element.192.refs_0_, bf16[896,768]{1,0:T(8,128)(2,1)} %get-tuple-element.193.refs_1_, bf16[896,768]{1,0:T(8,128)(2,1)} %get-tuple-element.194.refs_2_, bf16[256,768]{1,0:T(8,128)(2,1)} %bitcast.125, ...), custom_call_target="tpu_custom_call" | custom-call | flops 1000 | bytes 1000 | tf_op jit(solution)/shard_map/weight_grads/pallas_call | solution.py:337
  306.0 14.8 %attend_backward.2 = (bf16[896,384]{1,0:T(8,128)(2,1)}, f32[896,768]{1,0:T(8,128)}, bf16[896,768]{1,0:T(8,128)(2,1)}) custom-call(s32[3]{0:T(128)} %pad_add_fusion.meta, bf16[896,384]{1,0:T(8,128)(2,1)} %get-tuple-element.155.q_ref, bf16[896,384]{1,0:T(8,128)(2,1)} %get-tuple-element.208.g_ref, f32[7,8,256]{2,1,0:T(8,128)} %get-tuple-element.209.lse_ref, ...), custom_call_target="tpu_custom_call" | custom-call | flops 1000 | bytes 1000 | tf_op jit(solution)/shard_map/attend_backward/pallas_call | solution.py:223
  320.9 14.9 %attend_backward.3 = (bf16[896,384]{1,0:T(8,128)(2,1)}, f32[896,768]{1,0:T(8,128)}, bf16[896,768]{1,0:T(8,128)(2,1)}) custom-call(s32[3]{0:T(128)} %pad_add_fusion.meta, bf16[896,384]{1,0:T(8,128)(2,1)} %get-tuple-element.148.q_ref, bf16[896,384]{1,0:T(8,128)(2,1)} %get-tuple-element.212.g_ref, f32[7,8,256]{2,1,0:T(8,128)} %get-tuple-element.213.lse_ref, ...), custom_call_target="tpu_custom_call" | custom-call | flops 1000 | bytes 1000 | tf_op jit(solution)/shard_map/attend_backward/pallas_call | solution.py:223
  336.2 6.7 %input_backward.2 = (f32[896,768]{1,0:T(8,128)}, bf16[896,768]{1,0:T(8,128)(2,1)}, f32[8,384]{1,0:T(8,128)}) custom-call(f32[896,768]{1,0:T(8,128)} %get-tuple-element.215.base_ref, bf16[896,384]{1,0:T(8,128)(2,1)} %get-tuple-element.214.dq_ref.refs_1_, f32[896,768]{1,0:T(8,128)} %get-tuple-element.216.own_ref, ...), custom_call_target="tpu_custom_call" | custom-call | flops 1000 | bytes 1000 | tf_op jit(solution)/shard_map/input_backward/pallas_call | solution.py:783
  342.9 5.8 %weight_grads.14 = bf16[4,4,48,1152]{3,2,1,0:T(8,128)(2,1)} custom-call(s32[1]{0:T(128)} %bitcast.meta, bf16[896,768]{1,0:T(8,128)(2,1)} %bitcast.119, bf16[896,384]{1,0:T(8,128)(2,1)} %get-tuple-element.214.dq_ref.refs_1_, bf16[896,768]{1,0:T(8,128)(2,1)} %get-tuple-element.218.refs_2_.refs_3_, bf16[896,768]{1,0:T(8,128)(2,1)} %get-tuple-element.218.refs_2_.refs_3_), custom_call_target="tpu_custom_call" | custom-call | flops 1000 | bytes 1000 | tf_op jit(solution)/shard_map/weight_grads/pallas_call | solution.py:337
  349.9 6.4 %input_backward.3 = (bf16[896,768]{1,0:T(8,128)(2,1)}, bf16[896,768]{1,0:T(8,128)(2,1)}, f32[8,384]{1,0:T(8,128)}) custom-call(f32[896,768]{1,0:T(8,128)} %get-tuple-element.222.base_ref, bf16[896,384]{1,0:T(8,128)(2,1)} %get-tuple-element.223.dq_ref.refs_1_, f32[896,768]{1,0:T(8,128)} %get-tuple-element.224.own_ref, bf16[896,768]{1,0:T(8,128)(2,1)} %copy-done.14, ...), custom_call_target="tpu_custom_call" | custom-call | flops 1000 | bytes 1000 | tf_op jit(solution)/shard_map/input_backward/pallas_call | solution.py:783
  356.4 3.1 gather_fusion.6
  362.7 17.6 %all-to-all-start.3 = ((bf16[32,32,768]{2,1,0:T(8,128)(2,1)}), bf16[32,32,768]{2,1,0:T(8,128)(2,1)}, u32[]{:S(2)}, u32[]{:S(2)}) async-start(bf16[32,32,768]{2,1,0:T(8,128)(2,1)} %gather_fusion.6), calls=%async_computation.5 | async-start | bytes 3145728 | tf_op jit(solution)/shard_map/all_to_all | solution.py:976
  382.3 6.3 %weight_grads.15 = bf16[4,4,48,1152]{3,2,1,0:T(8,128)(2,1)} custom-call(s32[1]{0:T(128)} %bitcast.meta, bf16[896,768]{1,0:T(8,128)(2,1)} %bitcast.120, bf16[896,384]{1,0:T(8,128)(2,1)} %get-tuple-element.223.dq_ref.refs_1_, bf16[896,768]{1,0:T(8,128)(2,1)} %get-tuple-element.246.refs_2_.refs_3_, bf16[896,768]{1,0:T(8,128)(2,1)} %get-tuple-element.246.refs_2_.refs_3_, ...), custom_call_target="tpu_custom_call" | custom-call | flops 1000 | bytes 1000 | tf_op jit(solution)/shard_map/weight_grads/pallas_call | solution.py:337
  388.6 1.8 gather_fusion.7
  390.4 1.9 collective-permute-start.23
  392.3 1.5 collective-permute-start.24
  394.1 1.9 collective-permute-start.20
  396.0 1.5 collective-permute-start.21
  397.6 1.8 collective-permute-done.25
  399.4 8.9 %collective-permute-done.20 = bf16[4,48,1152]{2,1,0:T(8,128)(2,1)S(1)} collective-permute-done((bf16[4,48,1152]{2,1,0:T(8,128)(2,1)S(1)}, bf16[4,48,1152]{2,1,0:T(8,128)(2,1)S(1)}, u32[]{:S(2)}, u32[]{:S(2)}) %collective-permute-start.20) | collective-permute-done | bytes 442400 | tf_op jit(solution)/shard_map/ppermute | solution.py:805
  408.4 16.1 %collective-permute-done.21 = bf16[4,48,1152]{2,1,0:T(8,128)(2,1)S(1)} collective-permute-done((bf16[4,48,1152]{2,1,0:T(8,128)(2,1)S(1)}, bf16[4,48,1152]{2,1,0:T(8,128)(2,1)S(1)}, u32[]{:S(2)}, u32[]{:S(2)}) %collective-permute-start.21) | collective-permute-done | bytes 442400 | tf_op jit(solution)/shard_map/ppermute | solution.py:805
  424.5 4.4 collective-permute-done.22
  430.2 4.6 collective-permute-start.29
  435.1 2.1 collective-permute-start.31
  440.5 3.3 gather_fusion.8
  443.8 2.1 collective-permute-start.28
  449.9 2.0 collective-permute-done.26
  451.9 10.1 %collective-permute-done.27 = bf16[48,3072]{1,0:T(8,128)(2,1)S(1)} collective-permute-done((bf16[48,3072]{1,0:T(8,128)(2,1)S(1)}, bf16[48,3072]{1,0:T(8,128)(2,1)S(1)}, u32[]{:S(2)}, u32[]{:S(2)}) %collective-permute-start.27) | collective-permute-done | bytes 294944 | tf_op jit(solution)/shard_map/ppermute | solution.py:805
  (194 shorter events, 41.3 us)
Async XLA Ops:
  7.2 11.6 %copy-start = (bf16[32,32,768]{2,1,0:T(8,128)(2,1)S(1)}, bf16[32,32,768]{2,1,0:T(8,128)(2,1)}, u32[]{:S(2)}) copy-start(bf16[32,32,768]{2,1,0:T(8,128)(2,1)} %param.17) | copy-start | bytes 4718596
  7.2 3.7 copy-start.15
  7.2 9.4 %copy-start.19 = (f32[4,384]{1,0:T(4,128)S(1)}, f32[4,384]{1,0:T(4,128)}, u32[]{:S(2)}) copy-start(f32[4,384]{1,0:T(4,128)} %refs_10_) | copy-start | bytes 18436
  7.2 9.4 %copy-start.21 = (f32[1536]{0:T(1024)S(1)}, f32[1536]{0:T(1024)}, u32[]{:S(2)}) copy-start(f32[1536]{0:T(1024)} %param.30) | copy-start | bytes 18436
  7.2 9.9 %copy-start.23 = (s32[32]{0:T(128)S(1)}, s32[32]{0:T(128)}, u32[]{:S(2)}) copy-start(s32[32]{0:T(128)} %param.20) | copy-start | bytes 388
  7.2 10.5 %copy-start.2 = (s32[32]{0:T(128)S(1)}, s32[32]{0:T(128)}, u32[]{:S(2)}) copy-start(s32[32]{0:T(128)} %param.19) | copy-start | bytes 388
  7.2 141.7 %all-gather.2.cloned.1.call-start = ((), (), s32[]{:S(2)}) async-start(), calls=%async_computation.7 | async-start | bytes 8146944 | tf_op jit(solution)/shard_map/all_gather | solution.py:1000
  10.9 9.7 %collective-permute-start = (bf16[48,1152]{1,0:T(8,128)(2,1)S(1)}, bf16[48,1152]{1,0:T(8,128)(2,1)S(1)}, u32[]{:S(2)}, u32[]{:S(2)}) collective-permute-start(bf16[48,1152]{1,0:T(8,128)(2,1)S(1)} %bitcast.136), channel_id=1, source_target_pairs={{0,8},{2,10},{4,12},{6,14},{8,0},{10,2},{12,4},{14,6},{16,24},{18,... | collective-permute-start | bytes 331784 | tf_op jit(solution)/shard_map/ppermute | solution.py:805
  14.0 11.3 %collective-permute-start.1 = (bf16[48,1152]{1,0:T(8,128)(2,1)S(1)}, bf16[48,1152]{1,0:T(8,128)(2,1)S(1)}, u32[]{:S(2)}, u32[]{:S(2)}) collective-permute-start(bf16[48,1152]{1,0:T(8,128)(2,1)S(1)} %bitcast.137), channel_id=1, source_target_pairs={{0,16},{2,18},{4,20},{6,22},{8,24},{10,26},{12,28},{14,30},{16,0},... | collective-permute-start | bytes 331784 | tf_op jit(solution)/shard_map/ppermute | solution.py:805
  16.6 8.8 %collective-permute-start.2 = (bf16[48,1152]{1,0:T(8,128)(2,1)S(1)}, bf16[48,1152]{1,0:T(8,128)(2,1)S(1)}, u32[]{:S(2)}, u32[]{:S(2)}) collective-permute-start(bf16[48,1152]{1,0:T(8,128)(2,1)S(1)} %bitcast.138), channel_id=1, source_target_pairs={{0,24},{2,26},{4,28},{6,30},{8,16},{10,18},{12,20},{14,22},{16,8},... | collective-permute-start | bytes 331784 | tf_op jit(solution)/shard_map/ppermute | solution.py:805
  16.6 42.5 %collective-permute-start.6 = (f32[3072]{0:T(1024)S(1)}, f32[3072]{0:T(1024)S(1)}, u32[]{:S(2)}, u32[]{:S(2)}) collective-permute-start(f32[3072]{0:T(1024)S(1)} %pad_maximum_fusion.2), channel_id=1, source_target_pairs={{0,1},{1,0},{2,3},{3,2},{4,5},{5,4},{6,7},{7,6},{8,9},{9,8},{10,11... | collective-permute-start | bytes 36872 | tf_op jit(solution)/shard_map/ppermute | solution.py:801
  16.7 43.6 %collective-permute-start.7 = (bf16[2,64,768]{2,1,0:T(8,128)(2,1)}, bf16[2,64,768]{2,1,0:T(8,128)(2,1)}, u32[]{:S(2)}, u32[]{:S(2)}) collective-permute-start(bf16[2,64,768]{2,1,0:T(8,128)(2,1)} %param.18), channel_id=1, source_target_pairs={{0,1},{1,0},{2,3},{3,2},{4,5},{5,4},{6,7},{7,6},{8,9},{9,8},{10,11... | collective-permute-start | bytes 589832 | tf_op jit(solution)/shard_map/ppermute | solution.py:801
  25.4 25.9 %copy-start.13 = (bf16[4,48,1152]{2,1,0:T(8,128)(2,1)}, bf16[4,48,1152]{2,1,0:T(8,128)(2,1)S(1)}, u32[]{:S(2)}) copy-start(bf16[4,48,1152]{2,1,0:T(8,128)(2,1)S(1)} %pad_maximum_fusion.own_ref) | copy-start | bytes 1327108
  25.4 64.5 %all-to-all-start = ((bf16[32,32,768]{2,1,0:T(8,128)(2,1)}), bf16[32,32,768]{2,1,0:T(8,128)(2,1)S(1)}, u32[]{:S(2)}, u32[]{:S(2)}) async-start(bf16[32,32,768]{2,1,0:T(8,128)(2,1)} %gather_fusion.1), calls=%async_computation | async-start | bytes 3145728 | tf_op jit(solution)/shard_map/all_to_all | solution.py:982
  47.9 31.2 %collective-permute-start.3 = (bf16[4,48,1152]{2,1,0:T(8,128)(2,1)S(1)}, bf16[4,48,1152]{2,1,0:T(8,128)(2,1)S(1)}, u32[]{:S(2)}, u32[]{:S(2)}) collective-permute-start(bf16[4,48,1152]{2,1,0:T(8,128)(2,1)S(1)} %pad_maximum_fusion.own_ref), channel_id=1, source_target_pairs={{0,2},{2,0},{4,6},{6,4},{8,10},{10,8},{12,14},{14,12},{16,18},{18,... | collective-permute-start | bytes 1327112 | tf_op jit(solution)/shard_map/ppermute | solution.py:805
  49.8 29.2 %collective-permute-start.4 = (bf16[4,48,1152]{2,1,0:T(8,128)(2,1)S(1)}, bf16[4,48,1152]{2,1,0:T(8,128)(2,1)S(1)}, u32[]{:S(2)}, u32[]{:S(2)}) collective-permute-start(bf16[4,48,1152]{2,1,0:T(8,128)(2,1)S(1)} %pad_maximum_fusion.own_ref), channel_id=1, source_target_pairs={{0,4},{2,6},{4,0},{6,2},{8,12},{10,14},{12,8},{14,10},{16,20},{18,... | collective-permute-start | bytes 1327112 | tf_op jit(solution)/shard_map/ppermute | solution.py:805
  51.3 38.6 %collective-permute-start.5 = (bf16[4,48,1152]{2,1,0:T(8,128)(2,1)S(1)}, bf16[4,48,1152]{2,1,0:T(8,128)(2,1)S(1)}, u32[]{:S(2)}, u32[]{:S(2)}) collective-permute-start(bf16[4,48,1152]{2,1,0:T(8,128)(2,1)S(1)} %pad_maximum_fusion.own_ref), channel_id=1, source_target_pairs={{0,6},{2,4},{4,2},{6,0},{8,14},{10,12},{12,10},{14,8},{16,22},{18,... | collective-permute-start | bytes 1327112 | tf_op jit(solution)/shard_map/ppermute | solution.py:805
  79.0 10.9 %copy-start.16 = (bf16[4,48,1152]{2,1,0:T(8,128)(2,1)}, bf16[4,48,1152]{2,1,0:T(8,128)(2,1)S(1)}, u32[]{:S(2)}) copy-start(bf16[4,48,1152]{2,1,0:T(8,128)(2,1)S(1)} %collective-permute-done.3.first_ref) | copy-start | bytes 1327108
  79.1 10.9 %copy-start.17 = (bf16[4,48,1152]{2,1,0:T(8,128)(2,1)}, bf16[4,48,1152]{2,1,0:T(8,128)(2,1)S(1)}, u32[]{:S(2)}) copy-start(bf16[4,48,1152]{2,1,0:T(8,128)(2,1)S(1)} %collective-permute-done.4.second_ref) | copy-start | bytes 1327108
  89.9 0.8 copy-start.18
  95.1 7.3 %collective-permute-start.8 = (bf16[768,1152]{1,0:T(8,128)(2,1)}, bf16[768,1152]{1,0:T(8,128)(2,1)S(1)}, u32[]{:S(2)}, u32[]{:S(2)}) collective-permute-start(bf16[768,1152]{1,0:T(8,128)(2,1)} %bitcast.109), channel_id=1, source_target_pairs={{0,1},{1,0},{2,3},{3,2},{4,5},{5,4},{6,7},{7,6},{8,9},{9,8},{10,11... | collective-permute-start | bytes 5308424 | tf_op jit(solution)/shard_map/ppermute | solution.py:801
  101.9 6.7 %collective-permute-start.9 = (bf16[896,768]{1,0:T(8,128)(2,1)}, bf16[896,768]{1,0:T(8,128)(2,1)S(1)}, u32[]{:S(2)}, u32[]{:S(2)}) collective-permute-start(bf16[896,768]{1,0:T(8,128)(2,1)} %get-tuple-element.152.refs_0_), channel_id=1, source_target_pairs={{0,1},{1,0},{2,3},{3,2},{4,5},{5,4},{6,7},{7,6},{8,9},{9,8},{10,11... | collective-permute-start | bytes 4128776 | tf_op jit(solution)/shard_map/ppermute | solution.py:801
  102.4 1.2 copy-start.3
  108.6 11.7 %collective-permute-start.10 = (bf16[896,768]{1,0:T(8,128)(2,1)}, bf16[896,768]{1,0:T(8,128)(2,1)S(1)}, u32[]{:S(2)}, u32[]{:S(2)}) collective-permute-start(bf16[896,768]{1,0:T(8,128)(2,1)} %get-tuple-element.150.refs_0_), channel_id=1, source_target_pairs={{0,1},{1,0},{2,3},{3,2},{4,5},{5,4},{6,7},{7,6},{8,9},{9,8},{10,11... | collective-permute-start | bytes 4128776 | tf_op jit(solution)/shard_map/ppermute | solution.py:801
  108.6 1.1 copy-start.5
  120.3 1.1 copy-start.6
  149.0 12.5 %collective-permute-start.11 = (bf16[768,4992]{1,0:T(8,128)(2,1)}, bf16[768,4992]{1,0:T(8,128)(2,1)}, u32[]{:S(2)}, u32[]{:S(2)}) collective-permute-start(bf16[768,4992]{1,0:T(8,128)(2,1)} %all-gather.2.cloned.1.call-done.refs_0_.refs_2_.refs_4_.refs_6_.refs_8_.expand.reduce.in0.out0.refs_10_.wk0.wv0), channel_id=1, source_target_pairs={{0,1},{1,0},{2,3},{3,2},{4,5},{5,4},{6,7},{7,6},{8,9},{9,8},{10,11... | collective-permute-start | bytes 23003144 | tf_op jit(solution)/shard_map/ppermute | solution.py:801
  149.0 52.7 %all-to-all-start.1 = ((bf16[32,32,768]{2,1,0:T(8,128)(2,1)}), bf16[32,32,768]{2,1,0:T(8,128)(2,1)S(1)}, u32[]{:S(2)}, u32[]{:S(2)}) async-start(bf16[32,32,768]{2,1,0:T(8,128)(2,1)} %gather_fusion), calls=%async_computation.1 | async-start | bytes 3145728 | tf_op jit(solution)/shard_map/all_to_all | solution.py:982
  152.8 168.2 %reduce-scatter.4.cloned.1.call-start = ((), (), s32[]{:S(2)}) async-start(), calls=%async_computation.8 | async-start | bytes 5898240 | tf_op jit(solution)/shard_map/reduce_scatter | solution.py:882
  227.6 6.2 %collective-permute-start.13 = (bf16[4,4,48,1536]{3,2,1,0:T(8,128)(2,1)}, bf16[4,4,48,1536]{3,2,1,0:T(8,128)(2,1)}, u32[]{:S(2)}, u32[]{:S(2)}) collective-permute-start(bf16[4,4,48,1536]{3,2,1,0:T(8,128)(2,1)} %weight_grads.9), channel_id=1, source_target_pairs={{0,1},{1,0},{2,3},{3,2},{4,5},{5,4},{6,7},{7,6},{8,9},{9,8},{10,11... | collective-permute-start | bytes 7077896 | tf_op jit(solution)/shard_map/ppermute | solution.py:801
  233.5 6.5 %collective-permute-start.12 = (bf16[4,4,48,1536]{3,2,1,0:T(8,128)(2,1)}, bf16[4,4,48,1536]{3,2,1,0:T(8,128)(2,1)}, u32[]{:S(2)}, u32[]{:S(2)}) collective-permute-start(bf16[4,4,48,1536]{3,2,1,0:T(8,128)(2,1)} %weight_grads.8), channel_id=1, source_target_pairs={{0,1},{1,0},{2,3},{3,2},{4,5},{5,4},{6,7},{7,6},{8,9},{9,8},{10,11... | collective-permute-start | bytes 7077896 | tf_op jit(solution)/shard_map/ppermute | solution.py:801
  246.1 1.3 copy-start.10
  249.2 39.3 %all-to-all-start.2 = ((bf16[32,32,768]{2,1,0:T(8,128)(2,1)}), bf16[32,32,768]{2,1,0:T(8,128)(2,1)S(1)}, u32[]{:S(2)}, u32[]{:S(2)}) async-start(bf16[32,32,768]{2,1,0:T(8,128)(2,1)} %gather_fusion.5), calls=%async_computation.2 | async-start | bytes 3145728 | tf_op jit(solution)/shard_map/all_to_all | solution.py:976
  254.6 127.7 %reduce-scatter.6.cloned.1.call-start = ((), (), s32[]{:S(2)}) async-start(), calls=%async_computation.9 | async-start | bytes 3686400 | tf_op jit(solution)/shard_map/reduce_scatter | solution.py:882
  286.8 9.1 %collective-permute-start.15 = (bf16[4,4,48,1152]{3,2,1,0:T(8,128)(2,1)}, bf16[4,4,48,1152]{3,2,1,0:T(8,128)(2,1)S(1)}, u32[]{:S(2)}, u32[]{:S(2)}) collective-permute-start(bf16[4,4,48,1152]{3,2,1,0:T(8,128)(2,1)} %weight_grads.12), channel_id=1, source_target_pairs={{0,1},{1,0},{2,3},{3,2},{4,5},{5,4},{6,7},{7,6},{8,9},{9,8},{10,11... | collective-permute-start | bytes 5308424 | tf_op jit(solution)/shard_map/ppermute | solution.py:801
  288.5 3.5 collective-permute-start.14
  295.9 1.2 copy-start.12
  305.9 123.2 %reduce-scatter.8.cloned.1.call-start = ((), (), s32[]{:S(2)}) async-start(), calls=%async_computation.10 | async-start | bytes 1474560 | tf_op jit(solution)/shard_map/reduce_scatter | solution.py:882
  320.8 15.4 %collective-permute-start.16 = (bf16[896,768]{1,0:T(8,128)(2,1)}, bf16[896,768]{1,0:T(8,128)(2,1)}, u32[]{:S(2)}, u32[]{:S(2)}) collective-permute-start(bf16[896,768]{1,0:T(8,128)(2,1)} %get-tuple-element.217), channel_id=1, source_target_pairs={{0,1},{1,0},{2,3},{3,2},{4,5},{5,4},{6,7},{7,6},{8,9},{9,8},{10,11... | collective-permute-start | bytes 4128776 | tf_op jit(solution)/shard_map/ppermute | solution.py:801
  335.8 12.9 %collective-permute-start.17 = (bf16[896,768]{1,0:T(8,128)(2,1)}, bf16[896,768]{1,0:T(8,128)(2,1)S(1)}, u32[]{:S(2)}, u32[]{:S(2)}) collective-permute-start(bf16[896,768]{1,0:T(8,128)(2,1)} %get-tuple-element.220), channel_id=1, source_target_pairs={{0,1},{1,0},{2,3},{3,2},{4,5},{5,4},{6,7},{7,6},{8,9},{9,8},{10,11... | collective-permute-start | bytes 4128776 | tf_op jit(solution)/shard_map/ppermute | solution.py:801
  348.7 1.1 copy-start.14
  349.8 9.7 %collective-permute-start.18 = (bf16[4,4,48,1152]{3,2,1,0:T(8,128)(2,1)}, bf16[4,4,48,1152]{3,2,1,0:T(8,128)(2,1)S(1)}, u32[]{:S(2)}, u32[]{:S(2)}) collective-permute-start(bf16[4,4,48,1152]{3,2,1,0:T(8,128)(2,1)} %weight_grads.14), channel_id=1, source_target_pairs={{0,1},{1,0},{2,3},{3,2},{4,5},{5,4},{6,7},{7,6},{8,9},{9,8},{10,11... | collective-permute-start | bytes 5308424 | tf_op jit(solution)/shard_map/ppermute | solution.py:801
  356.4 4.1 copy-start.22
  359.6 3.1 copy-start.11
  362.7 67.6 %all-to-all-start.3 = ((bf16[32,32,768]{2,1,0:T(8,128)(2,1)}), bf16[32,32,768]{2,1,0:T(8,128)(2,1)}, u32[]{:S(2)}, u32[]{:S(2)}) async-start(bf16[32,32,768]{2,1,0:T(8,128)(2,1)} %gather_fusion.6), calls=%async_computation.5 | async-start | bytes 3145728 | tf_op jit(solution)/shard_map/all_to_all | solution.py:976
  382.1 8.2 %collective-permute-start.19 = (f32[13056]{0:T(1024)S(1)}, f32[13056]{0:T(1024)S(1)}, u32[]{:S(2)}, u32[]{:S(2)}) collective-permute-start(f32[13056]{0:T(1024)S(1)} %constant_dynamic-update-slice_fusion), channel_id=1, source_target_pairs={{0,1},{1,0},{2,3},{3,2},{4,5},{5,4},{6,7},{7,6},{8,9},{9,8},{10,11... | collective-permute-start | bytes 156680 | tf_op jit(solution)/shard_map/ppermute | solution.py:801
  388.6 5.4 %copy-start.4 = (bf16[4,4,48,1152]{3,2,1,0:T(8,128)(2,1)S(1)}, bf16[4,4,48,1152]{3,2,1,0:T(8,128)(2,1)}, u32[]{:S(2)}) copy-start(bf16[4,4,48,1152]{3,2,1,0:T(8,128)(2,1)} %weight_grads.15) | copy-start | bytes 5308420
  390.4 7.1 %collective-permute-start.23 = (f32[13056]{0:T(1024)S(1)}, f32[13056]{0:T(1024)S(1)}, u32[]{:S(2)}, u32[]{:S(2)}) collective-permute-start(f32[13056]{0:T(1024)S(1)} %add.262), channel_id=1, source_target_pairs={{0,2},{2,0},{4,6},{6,4},{8,10},{10,8},{12,14},{14,12},{16,18},{18,... | collective-permute-start | bytes 156680 | tf_op jit(solution)/shard_map/ppermute | solution.py:805
  392.3 5.3 %collective-permute-start.24 = (f32[13056]{0:T(1024)S(1)}, f32[13056]{0:T(1024)S(1)}, u32[]{:S(2)}, u32[]{:S(2)}) collective-permute-start(f32[13056]{0:T(1024)S(1)} %add.262), channel_id=1, source_target_pairs={{0,4},{2,6},{4,0},{6,2},{8,12},{10,14},{12,8},{14,10},{16,20},{18,... | collective-permute-start | bytes 156680 | tf_op jit(solution)/shard_map/ppermute | solution.py:805
  393.8 5.6 %collective-permute-start.25 = (f32[13056]{0:T(1024)S(1)}, f32[13056]{0:T(1024)S(1)}, u32[]{:S(2)}, u32[]{:S(2)}) collective-permute-start(f32[13056]{0:T(1024)S(1)} %add.262), channel_id=1, source_target_pairs={{0,6},{2,4},{4,2},{6,0},{8,14},{10,12},{12,10},{14,8},{16,22},{18,... | collective-permute-start | bytes 156680 | tf_op jit(solution)/shard_map/ppermute | solution.py:805
  394.1 14.3 %collective-permute-start.20 = (bf16[4,48,1152]{2,1,0:T(8,128)(2,1)S(1)}, bf16[4,48,1152]{2,1,0:T(8,128)(2,1)S(1)}, u32[]{:S(2)}, u32[]{:S(2)}) collective-permute-start(bf16[4,48,1152]{2,1,0:T(8,128)(2,1)S(1)} %get-tuple-element.293), channel_id=1, source_target_pairs={{0,2},{2,0},{4,6},{6,4},{8,10},{10,8},{12,14},{14,12},{16,18},{18,... | collective-permute-start | bytes 1327112 | tf_op jit(solution)/shard_map/ppermute | solution.py:805
  396.0 28.5 %collective-permute-start.21 = (bf16[4,48,1152]{2,1,0:T(8,128)(2,1)S(1)}, bf16[4,48,1152]{2,1,0:T(8,128)(2,1)S(1)}, u32[]{:S(2)}, u32[]{:S(2)}) collective-permute-start(bf16[4,48,1152]{2,1,0:T(8,128)(2,1)S(1)} %get-tuple-element.295), channel_id=1, source_target_pairs={{0,4},{2,6},{4,0},{6,2},{8,12},{10,14},{12,8},{14,10},{16,20},{18,... | collective-permute-start | bytes 1327112 | tf_op jit(solution)/shard_map/ppermute | solution.py:805
  397.5 31.4 %collective-permute-start.22 = (bf16[4,48,1152]{2,1,0:T(8,128)(2,1)S(1)}, bf16[4,48,1152]{2,1,0:T(8,128)(2,1)S(1)}, u32[]{:S(2)}, u32[]{:S(2)}) collective-permute-start(bf16[4,48,1152]{2,1,0:T(8,128)(2,1)S(1)} %get-tuple-element.294), channel_id=1, source_target_pairs={{0,6},{2,4},{4,2},{6,0},{8,14},{10,12},{12,10},{14,8},{16,22},{18,... | collective-permute-start | bytes 1327112 | tf_op jit(solution)/shard_map/ppermute | solution.py:805
  399.4 37.8 %copy-start.8 = (bf16[192,1920]{1,0:T(8,128)(2,1)S(1)}, bf16[192,1920]{1,0:T(8,128)(2,1)}, u32[]{:S(2)}) copy-start(bf16[192,1920]{1,0:T(8,128)(2,1)} %reduce-scatter.6.cloned.1.call-done) | copy-start | bytes 2211844
  429.0 11.5 %copy-start.7 = (bf16[4,48,1152]{2,1,0:T(8,128)(2,1)}, bf16[4,48,1152]{2,1,0:T(8,128)(2,1)S(1)}, u32[]{:S(2)}) copy-start(bf16[4,48,1152]{2,1,0:T(8,128)(2,1)S(1)} %fusion.2) | copy-start | bytes 1327108
  430.2 13.6 %collective-permute-start.29 = (f32[13056]{0:T(1024)S(1)}, f32[13056]{0:T(1024)S(1)}, u32[]{:S(2)}, u32[]{:S(2)}) collective-permute-start(f32[13056]{0:T(1024)S(1)} %add_add_fusion.1), channel_id=1, source_target_pairs={{0,8},{2,10},{4,12},{6,14},{8,0},{10,2},{12,4},{14,6},{16,24},{18,... | collective-permute-start | bytes 156680 | tf_op jit(solution)/shard_map/ppermute | solution.py:805
  434.8 11.0 %collective-permute-start.30 = (f32[13056]{0:T(1024)S(1)}, f32[13056]{0:T(1024)}, u32[]{:S(2)}, u32[]{:S(2)}) collective-permute-start(f32[13056]{0:T(1024)S(1)} %add_add_fusion.1), channel_id=1, source_target_pairs={{0,16},{2,18},{4,20},{6,22},{8,24},{10,26},{12,28},{14,30},{16,0},... | collective-permute-start | bytes 156680 | tf_op jit(solution)/shard_map/ppermute | solution.py:805
  435.1 10.8 %collective-permute-start.31 = (f32[13056]{0:T(1024)S(1)}, f32[13056]{0:T(1024)}, u32[]{:S(2)}, u32[]{:S(2)}) collective-permute-start(f32[13056]{0:T(1024)S(1)} %add_add_fusion.1), channel_id=1, source_target_pairs={{0,24},{2,26},{4,28},{6,30},{8,16},{10,18},{12,20},{14,22},{16,8},... | collective-permute-start | bytes 156680 | tf_op jit(solution)/shard_map/ppermute | solution.py:805
  437.3 14.6 %collective-permute-start.26 = (bf16[48,3072]{1,0:T(8,128)(2,1)S(1)}, bf16[48,3072]{1,0:T(8,128)(2,1)S(1)}, u32[]{:S(2)}, u32[]{:S(2)}) collective-permute-start(bf16[48,3072]{1,0:T(8,128)(2,1)S(1)} %get-tuple-element.296), channel_id=1, source_target_pairs={{0,8},{2,10},{4,12},{6,14},{8,0},{10,2},{12,4},{14,6},{16,24},{18,... | collective-permute-start | bytes 884744 | tf_op jit(solution)/shard_map/ppermute | solution.py:805
  438.5 23.5 %collective-permute-start.27 = (bf16[48,3072]{1,0:T(8,128)(2,1)S(1)}, bf16[48,3072]{1,0:T(8,128)(2,1)S(1)}, u32[]{:S(2)}, u32[]{:S(2)}) collective-permute-start(bf16[48,3072]{1,0:T(8,128)(2,1)S(1)} %get-tuple-element.297), channel_id=1, source_target_pairs={{0,16},{2,18},{4,20},{6,22},{8,24},{10,26},{12,28},{14,30},{16,0},... | collective-permute-start | bytes 884744 | tf_op jit(solution)/shard_map/ppermute | solution.py:805
  440.5 21.4 %copy-start.9 = (bf16[192,1920]{1,0:T(8,128)(2,1)S(1)}, bf16[192,1920]{1,0:T(8,128)(2,1)}, u32[]{:S(2)}) copy-start(bf16[192,1920]{1,0:T(8,128)(2,1)} %reduce-scatter.6.cloned.1.call-done) | copy-start | bytes 2211844
  443.8 2.1 copy-start.20
  443.8 18.2 %collective-permute-start.28 = (bf16[48,3072]{1,0:T(8,128)(2,1)S(1)}, bf16[48,3072]{1,0:T(8,128)(2,1)}, u32[]{:S(2)}, u32[]{:S(2)}) collective-permute-start(bf16[48,3072]{1,0:T(8,128)(2,1)S(1)} %get-tuple-element.298), channel_id=1, source_target_pairs={{0,24},{2,26},{4,28},{6,30},{8,16},{10,18},{12,20},{14,22},{16,8},... | collective-permute-start | bytes 884744 | tf_op jit(solution)/shard_map/ppermute | solution.py:805
  462.0 3.4 copy-start.1
Sparse Core Ops, SparseCore 0:
  11.0 137.9 all-gather.1
  246.3 73.6 reduce-scatter.3
  323.0 42.3 reduce-scatter.5
  367.6 51.7 reduce-scatter.7
